TPU v7x, 32 devices: a whole 2x2x4 slice. The times are simulated.
32 devices in a mesh: seq: 8 (over z, y), head: 4 (over x, core).
Axes of the slice: x: 2, y: 2, z: 4, core: 2. Of those that a mesh axis runs over, the one named last changes fastest.
Arguments:
- inputs: bfloat16 [2, 1024, 768], P(None, 'seq'), may hold values from -6 to 6
- cotangent: float32 [2, 1024, 768], P(None, 'seq'), may hold values from -6 to 6
- lengths: int32 [2], replicated, may hold values from 256 to 1024, as said below
- ln1_gain: float32 [768], replicated, may hold values from 0.5 to 1.5
- ln1_bias: float32 [768], replicated, may hold values from -3 to 3
- query_key_value_weight: bfloat16 [3, 768, 768], P(None, None, 'head'), may hold values from -0.21875 to 0.21875
- b_qkv: float32 [3, 768], P(None, 'head'), may hold values from -3 to 3
- shift_taps: float32 [64, 768], P(None, 'head'), may hold values from -2.5 to 2.5
- shift_skip: float32 [768], P('head'), may hold values from -4 to 4
- ssm_a: float32 [768, 64], P('head'), as said below
- ssm_b: float32 [768, 64], P('head'), may hold values from -4 to 4
- ssm_c: float32 [768, 64], P('head'), may hold values from -0.75 to 0.75
- ssm_skip: float32 [768], P('head'), may hold values from -3 to 3
- ssm_step: float32 [768], P('head'), may hold values from 0.5 to 2
- output_weight: bfloat16 [768, 768], P('head'), may hold values from -0.21875 to 0.21875
- b_out: float32 [768], replicated, may hold values from -3 to 3
- ln2_gain: float32 [768], replicated, may hold values from 0.5 to 1.5
- ln2_bias: float32 [768], replicated, may hold values from -3 to 3
- up_weight: bfloat16 [768, 3072], P(None, 'head'), may hold values from -0.21875 to 0.21875
- up_bias: float32 [3072], P('head'), may hold values from -3 to 3
- down_weight: bfloat16 [3072, 768], P('head'), may hold values from -0.109375 to 0.109375
- b_down: float32 [768], replicated, may hold values from -3 to 3
Outputs:
- layer_out: float32 [2, 1024, 768], P(None, 'seq')
- grad_inputs: float32 [2, 1024, 768], P(None, 'seq')
- grad_ln1_gain: float32 [768], replicated
- grad_ln1_bias: float32 [768], replicated
- grad_w_qkv: float32 [3, 768, 768], P(None, None, 'head')
- grad_b_qkv: float32 [3, 768], P(None, 'head')
- grad_shift_taps: float32 [64, 768], P(None, 'head')
- grad_shift_skip: float32 [768], P('head')
- grad_ssm_a: float32 [768, 64], P('head')
- grad_ssm_b: float32 [768, 64], P('head')
- grad_ssm_c: float32 [768, 64], P('head')
- grad_ssm_skip: float32 [768], P('head')
- grad_ssm_step: float32 [768], P('head')
- grad_w_out: float32 [768, 768], P('head')
- grad_b_out: float32 [768], replicated
- grad_ln2_gain: float32 [768], replicated
- grad_ln2_bias: float32 [768], replicated
- up_weight_gradient: float32 [768, 3072], P(None, 'head')
- grad_b_up: float32 [3072], P('head')
- grad_w_down: float32 [3072, 768], P('head')
- grad_b_down: float32 [768], replicated
Inputs may be any that keep to these rules, and one draw needn't show every extreme that they name: `lengths`: every slot's valid tokens come first; one slot in every draw has all 1024 tokens valid. `ssm_a`: positive.
All inputs are finite; a program needn't handle non-finite values.
Results may differ from a plain program's by a relative error of at most 0.02.
Values may be sent and summed in bfloat16 or wider, within the bound.
No kernel may reach another device: no remote copies, remote signals or barrier semaphores. Data moves between devices by JAX's collectives and lax.ppermute only.
A program may use at most 128 MiB of HBM per device.

v0:
```python
import jax
import jax.numpy as jnp
from jax import lax
from jax.sharding import PartitionSpec as P

highest = lax.Precision.HIGHEST
norm_epsilon = 1e-05


def shifted_2(shard, axis, by):
    peers = lax.axis_size(axis)
    pairs = [(i, i + by) for i in range(peers) if 0 <= i + by < peers]
    return lax.ppermute(shard, axis, pairs)


def prefix(shard, axis, join, neutral):
    place = lax.axis_index(axis)
    gathered = jax.tree.map(
        lambda a, kind: lax.all_gather(a.astype(kind), axis),
        shard,
        jax.tree.map(lambda a: jnp.bfloat16 if a.dtype == jnp.float32 else a.dtype, shard),
    )
    state = jax.tree.map(lambda a, e: jnp.zeros_like(a) + jnp.asarray(e, a.dtype), shard, neutral)

    def one(lap, state):
        return join(
            state,
            jax.tree.map(
                lambda a, own: lax.dynamic_index_in_dim(a, lap, 0, False).astype(own.dtype),
                gathered,
                shard,
            ),
        )

    return lax.fori_loop(0, place, one, state)


def prefix_2(shard, axis, join, neutral):
    count = lax.axis_size(axis)
    place = lax.axis_index(axis)
    ahead = count - 1 - place
    gathered = jax.tree.map(
        lambda a, kind: lax.all_gather(a.astype(kind), axis), shard, (jnp.bfloat16, jnp.bfloat16)
    )
    state = jax.tree.map(lambda a, e: jnp.zeros_like(a) + jnp.asarray(e, a.dtype), shard, neutral)

    def one(lap, state):
        source = count - 1 - lap
        return join(
            state,
            jax.tree.map(
                lambda a, own: lax.dynamic_index_in_dim(a, source, 0, False).astype(own.dtype),
                gathered,
                shard,
            ),
        )

    return lax.fori_loop(0, ahead, one, state)


def layer_norm(rows_in, norm_gain, norm_bias):
    mean_val = jnp.mean(rows_in, axis=-1, keepdims=True)
    centred = rows_in - mean_val
    spread = jnp.mean(centred * centred, axis=-1, keepdims=True)
    return centred * lax.rsqrt(spread + norm_epsilon) * norm_gain + norm_bias


def smooth_gate(values_in):
    return jax.nn.gelu(values_in, approximate=True)


def shift_mix(extended, values, shift_taps, shift_skip):
    filters = jnp.concatenate([shift_taps[::-1], shift_skip[None]], axis=0)[:, None, :]
    shifted = lax.conv_general_dilated(
        extended,
        filters,
        (1,),
        "VALID",
        dimension_numbers=("NWC", "WIO", "NWC"),
        feature_group_count=extended.shape[2],
        precision=highest,
    )
    return shifted * values


def chain_states(earlier, later):
    return (earlier[0] * later[0], later[0][None] * earlier[1] + later[1])


def weighted_total(series, powers, outer):
    slot_count, row_count, chan_count = series.shape
    block = powers.shape[0]
    pieces = series.reshape(slot_count, row_count // block, block, chan_count)
    inner = jnp.einsum("icn,sjic->sjcn", powers, pieces, precision=highest)
    return jnp.sum(inner * outer[None], axis=1)


def ssm_local(inputs_u, ssm_a, ssm_step, ssm_b, ssm_c, ssm_skip, start_state):
    slot_count, row_count, chan_count = inputs_u.shape
    block = min(128, row_count)
    decay_rate = ssm_step[:, None] * ssm_a
    input_gain = jnp.sqrt(-jnp.expm1(-2.0 * decay_rate)) * ssm_b
    offsets = jnp.arange(block, dtype=jnp.float32)
    rising = jnp.exp(-decay_rate[None] * (offsets[:, None, None] + 1.0))
    growing = jnp.exp(decay_rate[None] * (offsets[:, None, None] + 1.0))
    falling = jnp.exp(-decay_rate[None] * (block - 1.0 - offsets[:, None, None]))
    whole_step = jnp.exp(-decay_rate * block)
    toeplitz = jnp.einsum(
        "icn,jcn->ijc", rising * (ssm_c * input_gain)[None], growing, precision=highest
    )
    lower = offsets[:, None] >= offsets[None, :]
    toeplitz = jnp.where(lower[:, :, None], toeplitz, 0.0)
    blocks_u = jnp.transpose(
        inputs_u.reshape(slot_count, row_count // block, block, chan_count), (1, 0, 2, 3)
    )

    def advance(state, piece):
        inner = jnp.einsum("ijc,sjc->sic", toeplitz, piece, precision=highest) + ssm_skip * piece
        inner = inner + jnp.einsum("icn,scn->sic", rising, ssm_c * state, precision=highest)
        state = whole_step * state + input_gain * jnp.einsum(
            "jcn,sjc->scn", falling, piece, precision=highest
        )
        return (state, inner)

    end_state, outputs = lax.scan(advance, start_state, blocks_u)
    return (
        jnp.transpose(outputs, (1, 0, 2, 3)).reshape(slot_count, row_count, chan_count),
        end_state,
    )


def shards(
    inputs,
    cotangent,
    lengths,
    ln1_gain,
    ln1_bias,
    query_key_value_weight,
    b_qkv,
    shift_taps,
    shift_skip,
    ssm_a,
    ssm_b,
    ssm_c,
    ssm_skip,
    ssm_step,
    output_weight,
    b_out,
    ln2_gain,
    ln2_bias,
    up_weight,
    up_bias,
    down_weight,
    b_down,
):
    slot_count, row_count, width_all = inputs.shape
    tap_count = shift_taps.shape[0]
    block = min(128, row_count)
    block_count = row_count // block
    places = lax.axis_index("seq") * row_count + jnp.arange(row_count, dtype=jnp.int32)
    valid_rows = (places[None, :] < lengths[:, None]).astype(jnp.float32)[:, :, None]
    residual_in = inputs.astype(jnp.float32)
    normed_one, undo_one = jax.vjp(layer_norm, residual_in, ln1_gain, ln1_bias)
    first_activation = normed_one.astype(jnp.bfloat16)
    projected = (
        jnp.einsum(
            "vbg,tgi->tvbi",
            first_activation,
            query_key_value_weight,
            preferred_element_type=jnp.float32,
        )
        + b_qkv[:, None, None, :]
    )
    queries = projected[0]
    keys_low = projected[1].astype(jnp.bfloat16)
    values = projected[2]
    edge_rows = shifted_2(keys_low[:, row_count - tap_count :, :], "seq", 1)
    extended = jnp.concatenate([edge_rows, keys_low], axis=1).astype(jnp.float32)
    mixed_u, shift_undo = jax.vjp(shift_mix, extended, values, shift_taps, shift_skip)
    decay_rate = ssm_step[:, None] * ssm_a
    input_gain = jnp.sqrt(-jnp.expm1(-2.0 * decay_rate)) * ssm_b
    offsets = jnp.arange(block, dtype=jnp.float32)[:, None, None]
    rising = jnp.exp(-decay_rate[None] * (offsets + 1.0))
    falling = jnp.exp(-decay_rate[None] * (block - 1.0 - offsets))
    block_starts = block * jnp.arange(block_count, dtype=jnp.float32)[:, None, None]
    outer_end = jnp.exp(-decay_rate[None] * (row_count - block - block_starts))
    outer_start = jnp.exp(-decay_rate[None] * block_starts)
    whole_decay = jnp.exp(-decay_rate * row_count)
    end_local = input_gain * weighted_total(mixed_u, falling, outer_end)
    identity = (jnp.ones_like(whole_decay), jnp.zeros_like(end_local))
    carried = prefix((whole_decay, end_local), "seq", chain_states, identity)
    ssm_pair, ssm_undo = jax.vjp(
        ssm_local, mixed_u, ssm_a, ssm_step, ssm_b, ssm_c, ssm_skip, carried[1]
    )
    ssm_out = ssm_pair[0]
    gated_mixture = (queries * ssm_out).astype(jnp.bfloat16)
    attention_terms = jnp.einsum(
        "upm,mq->upq", gated_mixture, output_weight, preferred_element_type=jnp.float32
    )
    attended = lax.psum(attention_terms.astype(jnp.bfloat16), "head").astype(jnp.float32) + b_out
    middle = residual_in + attended
    normed_two, undo_two = jax.vjp(layer_norm, middle, ln2_gain, ln2_bias)
    second_activation = normed_two.astype(jnp.bfloat16)
    up_projected = (
        jnp.einsum("pwu,uj->pwj", second_activation, up_weight, preferred_element_type=jnp.float32)
        + up_bias
    )
    hidden_full, gelu_undo = jax.vjp(smooth_gate, up_projected)
    hidden_activations = hidden_full.astype(jnp.bfloat16)
    down_projection_terms = jnp.einsum(
        "jiq,qx->jix", hidden_activations, down_weight, preferred_element_type=jnp.float32
    )
    feed_out = (
        lax.psum(down_projection_terms.astype(jnp.bfloat16), "head").astype(jnp.float32) + b_down
    )
    layer_out = valid_rows * (middle + feed_out)
    grad_out = cotangent * valid_rows
    grad_b_down = jnp.sum(grad_out, axis=(0, 1))
    output_lower_gradient = grad_out.astype(jnp.bfloat16)
    grad_w_down = jnp.einsum(
        "iqe,iqy->ey", hidden_activations, output_lower_gradient, preferred_element_type=jnp.float32
    )
    grad_hidden = jnp.einsum(
        "apo,io->api", output_lower_gradient, down_weight, preferred_element_type=jnp.float32
    )
    up_gradient = gelu_undo(grad_hidden)[0].astype(jnp.bfloat16)
    grad_b_up = jnp.sum(up_gradient.astype(jnp.float32), axis=(0, 1))
    up_weight_gradient = jnp.einsum(
        "bar,bak->rk", second_activation, up_gradient, preferred_element_type=jnp.float32
    )
    second_activation_terms = jnp.einsum(
        "hxe,ge->hxg", up_gradient, up_weight, preferred_element_type=jnp.float32
    )
    grad_act_two = lax.psum(second_activation_terms.astype(jnp.bfloat16), "head").astype(
        jnp.float32
    )
    grad_mid_norm, grad_ln2_gain, grad_ln2_bias = undo_two(grad_act_two)
    grad_middle = grad_out + grad_mid_norm
    mlp_parts = (
        grad_ln2_gain,
        grad_ln2_bias,
        up_weight_gradient,
        grad_b_up,
        grad_w_down,
        grad_b_down,
    )
    grad_b_out = jnp.sum(grad_middle, axis=(0, 1))
    middle_lower_gradient = grad_middle.astype(jnp.bfloat16)
    grad_w_out = jnp.einsum(
        "hxq,hxe->qe", gated_mixture, middle_lower_gradient, preferred_element_type=jnp.float32
    )
    gated_gradient = jnp.einsum(
        "ihq,zq->ihz", middle_lower_gradient, output_weight, preferred_element_type=jnp.float32
    )
    grad_queries = gated_gradient * ssm_out
    grad_ssm = gated_gradient * queries
    state_local = ssm_c * weighted_total(grad_ssm, rising, outer_start)
    future = prefix_2((whole_decay, state_local), "seq", chain_states, identity)
    ssm_grads = ssm_undo((grad_ssm, future[1]))
    grad_mixed_u = ssm_grads[0]
    grad_ext, grad_values, grad_shift_taps, grad_shift_skip = shift_undo(grad_mixed_u)
    received = shifted_2(grad_ext[:, :tap_count, :].astype(jnp.bfloat16), "seq", -1).astype(
        jnp.float32
    )
    grad_keys = grad_ext[:, tap_count:, :] + jnp.pad(
        received, ((0, 0), (row_count - tap_count, 0), (0, 0))
    )
    projected_gradient = jnp.stack([grad_queries, grad_keys, grad_values]).astype(jnp.bfloat16)
    grad_b_qkv = jnp.sum(projected_gradient.astype(jnp.float32), axis=(1, 2))
    grad_w_qkv = jnp.einsum(
        "quf,gquv->gfv", first_activation, projected_gradient, preferred_element_type=jnp.float32
    )
    act_one_terms = jnp.einsum(
        "znpu,zru->npr",
        projected_gradient,
        query_key_value_weight,
        preferred_element_type=jnp.float32,
    )
    grad_act_one = lax.psum(act_one_terms.astype(jnp.bfloat16), "head").astype(jnp.float32)
    grad_in_norm, grad_ln1_gain, grad_ln1_bias = undo_one(grad_act_one)
    grad_inputs = grad_middle + grad_in_norm
    summed_all = lax.psum(
        (
            grad_ln1_gain,
            grad_ln1_bias,
            grad_w_qkv,
            grad_b_qkv,
            grad_shift_taps,
            grad_shift_skip,
            ssm_grads[1],
            ssm_grads[3],
            ssm_grads[4],
            ssm_grads[5],
            ssm_grads[2],
            grad_w_out,
            grad_b_out,
            mlp_parts[0],
            mlp_parts[1],
            mlp_parts[2],
            mlp_parts[3],
            mlp_parts[4],
            mlp_parts[5],
        ),
        "seq",
    )
    mixer_parts = summed_all[:13]
    mlp_parts = summed_all[13:]
    return (
        layer_out,
        grad_inputs,
        mixer_parts[0],
        mixer_parts[1],
        mixer_parts[2],
        mixer_parts[3],
        mixer_parts[4],
        mixer_parts[5],
        mixer_parts[6],
        mixer_parts[7],
        mixer_parts[8],
        mixer_parts[9],
        mixer_parts[10],
        mixer_parts[11],
        mixer_parts[12],
        mlp_parts[0],
        mlp_parts[1],
        mlp_parts[2],
        mlp_parts[3],
        mlp_parts[4],
        mlp_parts[5],
    )


def solution(mesh):
    in_specs = (
        P(None, "seq", None),
        P(None, "seq", None),
        P(),
        P(),
        P(),
        P(None, None, "head"),
        P(None, "head"),
        P(None, "head"),
        P("head"),
        P("head", None),
        P("head", None),
        P("head", None),
        P("head"),
        P("head"),
        P("head", None),
        P(),
        P(),
        P(),
        P(None, "head"),
        P("head"),
        P("head", None),
        P(),
    )
    out_specs = (
        P(None, "seq", None),
        P(None, "seq", None),
        P(),
        P(),
        P(None, None, "head"),
        P(None, "head"),
        P(None, "head"),
        P("head"),
        P("head", None),
        P("head", None),
        P("head", None),
        P("head"),
        P("head"),
        P("head", None),
        P(),
        P(),
        P(),
        P(None, "head"),
        P("head"),
        P("head", None),
        P(),
    )
    return jax.shard_map(shards, mesh=mesh, in_specs=in_specs, out_specs=out_specs, check_vma=False)
```

profile of v0, /device:TPU:0, one launch (start us, length us, event | category | flops | bytes accessed | tf_op | source)
XLA Modules:
  0.0 836.6 jit_solution(12041054226291278105)
XLA Ops:
  9.7 1.8 fusion.55
  11.7 5.5 collective-permute-start
  25.1 27.2 %fusion.26 = f32[192,128,128]{2,1,0:T(8,128)} fusion(f32[192,64]{1,0:T(8,128)S(1)} %get-tuple-element.359, f32[192,64]{1,0:T(8,128)S(1)} %get-tuple-element.372, f32[128]{0:T(128)S(1)} %iota_add_fusion, f32[192,64]{1,0:T(8,128)S(1)} %get-tuple-element.361), kind=kOutput, calls=%fused_computation.38 | convolution fusion | flops 2420637696 | bytes 12730880 | tf_op jit(solution)/shard_map/jvp(icn,jcn->ijc)/dot_general | solution.py:108
  52.4 31.0 %all-gather.1 = bf16[8,192,64]{1,2,0:T(8,128)(2,1)S(1)} all-gather(bf16[1,192,64]{1,2,0:T(8,128)(2,1)S(1)} %copy.99), channel_id=2, replica_groups=mesh['seq'=8,'head'=4] {'seq'}, dimensions={0}, use_global_device_ids=true | all-gather | bytes 221184 | tf_op jit(solution)/shard_map/all_gather | solution.py:19
  84.9 1.4 fusion.153
  86.5 11.5 %fusion.107 = (bf16[1,2,192,64]{3,1,2,0:T(2,128)(2,1)S(1)}, f32[192,2,64]{2,1,0:T(2,128)}) fusion(f32[192,64]{1,0:T(8,128)} %get-tuple-element.370, f32[192,64]{1,0:T(8,128)S(1)} %get-tuple-element.360, f32[128]{0:T(128)S(1)} %iota_subtract_fusion, f32[192,64]{1,0:T(8,128)S(1)} %get-tuple-element.372, f32[2,128,192]{1,2,0:T(8,128)S(1)} %fusion.114), kind=kOutput, calls=%fused_computation.150 | convolution fusion | flops 39395328 | bytes 492032 | tf_op jit(solution)/shard_map/icn,sjic->sjcn/dot_general | solution.py:94
  98.1 31.2 %all_gather.18 = bf16[8,2,192,64]{2,3,1,0:T(8,128)(2,1)S(1)} all-gather(bf16[1,2,192,64]{2,3,1,0:T(8,128)(2,1)S(1)} %copy.101), channel_id=1, replica_groups=mesh['seq'=8,'head'=4] {'seq'}, dimensions={0}, use_global_device_ids=true | all-gather | bytes 442368 | tf_op jit(solution)/shard_map/all_gather | solution.py:19
  131.2 5.9 fusion.23
  137.1 12.8 %fusion.1 = f32[192,2,128]{2,1,0:T(2,128)S(1)} fusion(f32[192,128,128]{2,1,0:T(8,128)} %fusion.26, pred[128,128]{0,1:T(8,128)(4,1)S(1)} %iota_compare_fusion.1, f32[2,128,192]{1,2,0:T(8,128)S(1)} %fusion.114), kind=kOutput, calls=%fused_computation.8 | convolution fusion | flops 78643200 | bytes 12992512 | tf_op jit(solution)/shard_map/jvp()/while/body/eval_jaxpr/ijc,sjc->sic/dot_general | solution.py:118
  150.0 1.8 multiply_convert_fusion.4
  154.4 31.7 %all-reduce.10.cloned.1.call-done = bf16[2,128,768]{2,1,0:T(8,128)(2,1)} async-done(((bf16[2,128,768]{2,1,0:T(8,128)(2,1)}), bf16[2,128,768]{2,1,0:T(8,128)(2,1)}) %all-reduce.10.cloned.1.call-update) | async-done | bytes 393232 | tf_op jit(solution)/shard_map/psum | solution.py:200
  188.6 2.0 convolution_add_fusion
  192.1 1.5 convert_reduce_fusion.3
  193.6 2.1 convolution_bitcast_fusion
  197.1 3.1 convolution_bitcast_fusion.1
  200.2 29.6 %all-reduce.12.cloned.1.call-done = bf16[2,128,768]{2,1,0:T(8,128)(2,1)} async-done(((bf16[2,128,768]{2,1,0:T(8,128)(2,1)}), bf16[2,128,768]{2,1,0:T(8,128)(2,1)}) %all-reduce.12.cloned.1.call-update) | async-done | bytes 393232 | tf_op jit(solution)/shard_map/psum | solution.py:234
  229.8 1.9 convert_reduce_fusion.1
  231.7 2.1 fusion.92
  233.9 2.1 fusion.145
  235.9 2.0 multiply_reduce_fusion.2
  237.9 10.8 %fusion.73 = bf16[1,2,192,64]{3,1,2,0:T(2,128)(2,1)S(1)} fusion(f32[192,64]{1,0:T(8,128)S(1)} %copy-done.15, f32[128]{0:T(128)} %copy-done.50, f32[2,128,192]{1,2,0:T(8,128)S(1)} %get-tuple-element.354, f32[192,64]{1,0:T(8,128)S(1)} %copy.94, f32[192,64]{1,0:T(8,128)} %get-tuple-element.370), kind=kOutput, calls=%fused_computation.104 | convolution fusion | flops 39395328 | bytes 393728 | tf_op jit(solution)/shard_map/icn,sjic->sjcn/dot_general | solution.py:94
  248.7 22.4 %fusion = f32[192,2,128]{2,1,0:T(2,128)S(1)} fusion(f32[192,128,128]{2,1,0:T(8,128)} %fusion.26, pred[128,128]{0,1:T(8,128)(4,1)S(1)} %copy-done.37, f32[192,2,128]{2,0,1:T(8,128)S(1)} %bitcast.201), kind=kOutput, calls=%fused_computation.7 | convolution fusion | flops 78643200 | bytes 12992512 | tf_op jit(solution)/shard_map/transpose(jvp())/while/body/eval_jaxpr/ijc,sjc->sic/dot_general | solution.py:118
  271.1 19.9 %fusion.130 = f32[192,128,128]{2,1,0:T(8,128)S(1)} fusion(f32[192,2,128]{2,0,1:T(8,128)S(1)} %bitcast.202, f32[2,128,192]{1,2,0:T(8,128)S(1)} %fusion.114), kind=kOutput, calls=%fused_computation.198 | convolution fusion | flops 75497472 | bytes 12976128 | tf_op jit(solution)/shard_map/transpose(jvp())/while/body/eval_jaxpr/ijc,sjc->sic/dot_general | solution.py:118
  291.1 15.1 %fusion.10 = (f32[192,64]{1,0:T(8,128)}, f32[192,128,64]{1,2,0:T(8,128)}) fusion(f32[192,64]{1,0:T(8,128)S(1)} %copy-done.15, f32[128]{0:T(128)S(1)} %copy-done.51, f32[192,64]{1,0:T(8,128)S(1)} %get-tuple-element.361, f32[192,128,128]{2,1,0:T(8,128)S(1)} %fusion.130, pred[128,128]{1,0:T(8,128)(4,1)S(1)} %copy-done.41), kind=kOutput, calls=%fused_computation.19 | convolution fusion | flops 2425344000 | bytes 19038720 | tf_op jit(solution)/shard_map/transpose(jvp(icn,jcn->ijc))/dot_general | solution.py:108
  306.1 26.3 %fusion.12 = f32[192,64]{1,0:T(8,128)} fusion(f32[128]{0:T(128)S(1)} %copy-done.51, f32[192,64]{1,0:T(8,128)S(1)} %get-tuple-element.361, f32[192,64]{1,0:T(8,128)S(1)} %copy-done.26, f32[192,64]{1,0:T(8,128)S(1)} %copy-done.15, f32[192,128,128]{2,1,0:T(8,128)S(1)} %fusion.130, pred[128,128]{1,0:T(8,128)(4,1)S(1)} %copy-done.41), kind=kOutput, calls=%fused_computation.22 | convolution fusion | flops 2428489728 | bytes 12796416 | tf_op jit(solution)/shard_map/transpose(jvp(icn,jcn->ijc))/dot_general | solution.py:108
  332.5 33.3 %all_gather.19 = bf16[8,2,192,64]{2,3,1,0:T(8,128)(2,1)} all-gather(bf16[1,2,192,64]{2,3,1,0:T(8,128)(2,1)S(1)} %copy.108), channel_id=1, replica_groups=mesh['seq'=8,'head'=4] {'seq'}, dimensions={0}, use_global_device_ids=true | all-gather | bytes 442368 | tf_op jit(solution)/shard_map/all_gather | solution.py:43
  365.8 13.5 %while.17 = (s32[]{:T(128)}, f32[2,192,64]{2,1,0:T(8,128)S(1)}, s32[]{:T(128)}, bf16[8,192,64]{2,1,0:T(8,128)(2,1)}, bf16[8,2,192,64]{2,3,1,0:T(8,128)(2,1)}, /*index=5*/s32[]{:T(128)}, s32[]{:T(128)}, s32[]{:T(128)}, s32[]{:T(128)}) while((s32[]{:T(128)}, f32[2,192,64]{2,1,0:T(8,128)S(1)}, s32[]{:T(128)}, bf16[8,192,64]{2,1,0:T(8,128)(2,1)}, ...), condition=%wide.region_12.13_spmd, body=%wide.region_11.12_spmd.sunk | while | flops 86022 | bytes 565403 | solution.py:58
  380.1 5.9 fusion.17
  385.9 14.7 %fusion.14 = f32[192,64]{1,0:T(8,128)} fusion(f32[128]{0:T(128)} %copy-done.65, f32[192,64]{1,0:T(8,128)S(1)} %copy-done.16, f32[192,2,64]{2,0,1:T(8,128)S(1)} %get-tuple-element.367, f32[2,128,192]{1,2,0:T(8,128)S(1)} %fusion.114), kind=kOutput, calls=%fused_computation.25 | convolution fusion | flops 44027904 | bytes 393728 | tf_op jit(solution)/shard_map/transpose(jvp())/while/body/eval_jaxpr/jcn,sjc->scn/dot_general | solution.py:120
  400.7 10.6 %fusion.69 = f32[192,64]{1,0:T(8,128)} fusion(f32[192,64]{1,0:T(8,128)S(1)} %copy-done.16, f32[128]{0:T(128)S(1)} %copy-done.51, f32[2,192,64]{2,1,0:T(8,128)S(1)} %get-tuple-element.257, f32[192,2,128]{2,0,1:T(8,128)S(1)} %bitcast.203), kind=kOutput, calls=%fused_computation.98 | convolution fusion | flops 39358464 | bytes 393728 | tf_op jit(solution)/shard_map/transpose(jvp())/while/body/eval_jaxpr/icn,scn->sic/dot_general | solution.py:119
  412.5 7.9 fusion.154
  420.4 2.9 fusion.126
  426.4 17.4 %fusion.9 = f32[192,64]{1,0:T(8,128)} fusion(f32[192,128,64]{1,2,0:T(8,128)} %get-tuple-element.378, f32[192,64]{1,0:T(8,128)S(1)} %copy-done.26, f32[192,64]{1,0:T(8,128)S(1)} %copy-done.16, f32[128]{0:T(128)S(1)} %copy-done.51, f32[2,192,64]{2,1,0:T(8,128)} %copy-done.35, f32[192,2,128]{2,0,1:T(8,128)S(1)} %bitcast.204), kind=kOutput, calls=%fused_computation.18 | convolution fusion | flops 47173632 | bytes 6734336 | tf_op jit(solution)/shard_map/transpose(jvp())/while/body/eval_jaxpr/icn,scn->sic/dot_general | solution.py:119
  446.6 2.4 fusion.56
  449.2 2.4 multiply_reduce_fusion.4
  453.1 29.4 %all-reduce.18.cloned.1.call-done = (bf16[2,128,768]{2,1,0:T(8,128)(2,1)}, bf16[2,128,768]{2,1,0:T(8,128)(2,1)}) async-done(((bf16[2,128,768]{2,1,0:T(8,128)(2,1)}, bf16[2,128,768]{2,1,0:T(8,128)(2,1)}), (bf16[2,128,768]{2,1,0:T(8,128)(2,1)}, bf16[2,128,768]{2,1,0:T(8,128)(2,1)})) %all-reduce.18.cloned.1.call-update) | async-done | bytes 786448 | tf_op jit(solution)/shard_map/psum | solution.py:214
  482.5 1.9 convert_reduce_fusion
  484.4 2.2 fusion.93
  487.7 1.7 convolution_bitcast_fusion.2
  489.5 1.6 add_add_fusion.2
  491.1 75.0 %all-reduce.14.cloned.1.call-done = (f32[768]{0:T(1024)}, f32[768]{0:T(1024)}, f32[3,192]{1,0:T(4,128)}, f32[64,192]{1,0:T(8,128)}, f32[192]{0:T(256)}, /*index=...) async-done(((f32[768]{0:T(1024)}, f32[768]{0:T(1024)}, ...) | async-done | bytes 222736 | tf_op jit(solution)/shard_map/psum | solution.py:282
  566.1 1.6 copy.138
  567.7 1.6 copy.139
  569.3 1.6 copy.140
  570.9 237.2 %all-reduce.16.cloned.1.call-done = (f32[3,768,192]{1,2,0:T(8,128)}, f32[192,768]{1,0:T(8,128)}, f32[768,768]{1,0:T(8,128)}, f32[768,768]{1,0:T(8,128)}) async-done(((f32[3,768,192]{1,2,0:T(8,128)}, f32[192,768]{1,0:T(8,128)}, f32[768,768]{1,0:T(8,128)}, f32[768,768]{1,0:T(8,128)}), (f32[3,768,192]{1,2,0:T(8,128)}, f32[192,768]{1,0:T(8,128)}, f32[768,768]{1,0:T(8,128)}, ...) | async-done | bytes 7077904 | tf_op jit(solution)/shard_map/psum | solution.py:282
  810.9 2.8 copy.238
  815.0 1.5 copy.240
  820.1 1.9 copy.244
  (248 shorter events, 60.9 us)
Async XLA Ops:
  7.2 183.5 %copy-start = (bf16[768,768]{1,0:T(8,128)(2,1)S(1)}, bf16[768,768]{1,0:T(8,128)(2,1)}, u32[]{:S(2)}) copy-start(bf16[768,768]{1,0:T(8,128)(2,1)} %param.46) | copy-start | bytes 3538948
  7.2 178.9 %all-reduce.10.cloned.1.call-start = ((), (), s32[]{:S(2)}) async-start(), calls=%async_computation | async-start | bytes 786432 | tf_op jit(solution)/shard_map/psum | solution.py:200
  11.6 74.8 %copy-start.10 = (f32[3,2,128,192]{2,3,0,1:T(8,128)}, f32[3,2,128,192]{2,3,0,1:T(8,128)S(1)}, u32[]{:S(2)}) copy-start(f32[3,2,128,192]{2,3,0,1:T(8,128)S(1)} %fusion.55) | copy-start | bytes 1769476
  11.7 71.9 %collective-permute-start = (bf16[2,64,192]{1,2,0:T(8,128)(2,1)S(1)}, bf16[2,64,192]{1,2,0:T(8,128)(2,1)}, u32[]{:S(2)}, u32[]{:S(2)}) collective-permute-start(bf16[2,64,192]{1,2,0:T(8,128)(2,1)S(1)} %slice.30), channel_id=1, source_target_pairs={{0,4},{4,8},{8,12},{12,16},{16,20},{20,24},{24,28},{1,5},{5,9},{9,... | collective-permute-start | bytes 147464 | tf_op jit(solution)/shard_map/ppermute | solution.py:13
  17.3 112.6 %copy-start.50 = (f32[128]{0:T(128)}, f32[128]{0:T(128)S(1)}, u32[]{:S(2)}) copy-start(f32[128]{0:T(128)S(1)} %iota_add_fusion) | copy-start | bytes 1540
  17.3 69.2 %copy-start.65 = (f32[128]{0:T(128)}, f32[128]{0:T(128)S(1)}, u32[]{:S(2)}) copy-start(f32[128]{0:T(128)S(1)} %iota_subtract_fusion) | copy-start | bytes 1540
  17.3 119.8 %copy-start.36 = (pred[128,128]{0,1:T(8,128)(4,1)}, pred[128,128]{0,1:T(8,128)(4,1)S(1)}, u32[]{:S(2)}) copy-start(pred[128,128]{0,1:T(8,128)(4,1)S(1)} %iota_compare_fusion.1) | copy-start | bytes 49156
  19.9 32.5 %copy-start.21 = (f32[192,64]{1,0:T(8,128)}, f32[192,64]{1,0:T(8,128)S(1)}, u32[]{:S(2)}) copy-start(f32[192,64]{1,0:T(8,128)S(1)} %copy.93) | copy-start | bytes 147460
  20.8 31.5 %copy-start.23 = (f32[192,64]{1,0:T(8,128)}, f32[192,64]{1,0:T(8,128)S(1)}, u32[]{:S(2)}) copy-start(f32[192,64]{1,0:T(8,128)S(1)} %copy.92) | copy-start | bytes 147460
  21.7 30.7 %copy-start.25 = (f32[192,64]{1,0:T(8,128)}, f32[192,64]{1,0:T(8,128)S(1)}, u32[]{:S(2)}) copy-start(f32[192,64]{1,0:T(8,128)S(1)} %get-tuple-element.359) | copy-start | bytes 147460
  21.7 64.8 %copy-start.17 = (f32[192,64]{1,0:T(8,128)}, f32[192,64]{1,0:T(8,128)S(1)}, u32[]{:S(2)}) copy-start(f32[192,64]{1,0:T(8,128)S(1)} %get-tuple-element.360) | copy-start | bytes 147460
  22.4 107.4 %copy-start.14 = (f32[192,64]{1,0:T(8,128)}, f32[192,64]{1,0:T(8,128)S(1)}, u32[]{:S(2)}) copy-start(f32[192,64]{1,0:T(8,128)S(1)} %get-tuple-element.372) | copy-start | bytes 147460
  137.1 49.0 %copy-start.2 = (bf16[2,128,768]{2,1,0:T(8,128)(2,1)S(1)}, bf16[2,128,768]{2,1,0:T(8,128)(2,1)}, u32[]{:S(2)}) copy-start(bf16[2,128,768]{2,1,0:T(8,128)(2,1)} %param.26) | copy-start | bytes 1179652
  137.1 49.0 %copy-start.32 = (f32[768]{0:T(1024)S(1)}, f32[768]{0:T(1024)}, u32[]{:S(2)}) copy-start(f32[768]{0:T(1024)} %param.41) | copy-start | bytes 9220
  137.1 51.5 %copy-start.42 = (f32[768]{0:T(1024)S(1)}, f32[768]{0:T(1024)}, u32[]{:S(2)}) copy-start(f32[768]{0:T(1024)} %param.42) | copy-start | bytes 9220
  150.0 42.1 %copy-start.5 = (f32[2,128,768]{2,1,0:T(8,128)S(1)}, f32[2,128,768]{2,1,0:T(8,128)}, u32[]{:S(2)}) copy-start(f32[2,128,768]{2,1,0:T(8,128)} %param.27) | copy-start | bytes 2359300
  151.8 38.9 %copy-start.19 = (bf16[2,128,192]{1,2,0:T(8,128)(2,1)}, bf16[2,128,192]{1,2,0:T(8,128)(2,1)S(1)}, u32[]{:S(2)}) copy-start(bf16[2,128,192]{1,2,0:T(8,128)(2,1)S(1)} %get-tuple-element.357) | copy-start | bytes 294916
  152.9 76.9 %all-reduce.12.cloned.1.call-start = ((), (), s32[]{:S(2)}) async-start(), calls=%async_computation.1 | async-start | bytes 786432 | tf_op jit(solution)/shard_map/psum | solution.py:234
  193.6 38.2 %copy-start.55 = (f32[2,128]{1,0:T(2,128)S(1)}, f32[2,128]{1,0:T(2,128)}, u32[]{:S(2)}) copy-start(f32[2,128]{1,0:T(2,128)} %copy-done.54) | copy-start | bytes 3076
  195.7 40.2 %copy-start.12 = (bf16[192,768]{1,0:T(8,128)(2,1)S(1)}, bf16[192,768]{1,0:T(8,128)(2,1)}, u32[]{:S(2)}) copy-start(bf16[192,768]{1,0:T(8,128)(2,1)} %param.40) | copy-start | bytes 884740
  195.7 42.2 %copy-start.15 = (f32[192,64]{1,0:T(8,128)S(1)}, f32[192,64]{1,0:T(8,128)}, u32[]{:S(2)}) copy-start(f32[192,64]{1,0:T(8,128)} %copy-done.14) | copy-start | bytes 147460
  197.0 285.5 %all-reduce.18.cloned.1.call-start = ((), (), s32[]{:S(2)}) async-start(), calls=%async_computation.4 | async-start | bytes 1572864 | tf_op jit(solution)/shard_map/psum | solution.py:214
  229.8 19.0 %copy-start.37 = (pred[128,128]{0,1:T(8,128)(4,1)S(1)}, pred[128,128]{0,1:T(8,128)(4,1)}, u32[]{:S(2)}) copy-start(pred[128,128]{0,1:T(8,128)(4,1)} %copy-done.36) | copy-start | bytes 49156
  271.1 19.9 %copy-start.41 = (pred[128,128]{1,0:T(8,128)(4,1)S(1)}, pred[128,128]{1,0:T(8,128)(4,1)}, u32[]{:S(2)}) copy-start(pred[128,128]{1,0:T(8,128)(4,1)} %iota_compare_fusion) | copy-start | bytes 49156
  271.1 19.9 %copy-start.51 = (f32[128]{0:T(128)S(1)}, f32[128]{0:T(128)}, u32[]{:S(2)}) copy-start(f32[128]{0:T(128)} %copy-done.50) | copy-start | bytes 1540
  332.4 47.0 %copy-start.18 = (f32[192,64]{1,0:T(8,128)S(1)}, f32[192,64]{1,0:T(8,128)}, u32[]{:S(2)}) copy-start(f32[192,64]{1,0:T(8,128)} %copy-done.17) | copy-start | bytes 147460
  332.4 47.7 %copy-start.16 = (f32[192,64]{1,0:T(8,128)S(1)}, f32[192,64]{1,0:T(8,128)}, u32[]{:S(2)}) copy-start(f32[192,64]{1,0:T(8,128)} %copy-done.14) | copy-start | bytes 147460
  332.4 47.7 %copy-start.66 = (f32[128]{0:T(128)S(1)}, f32[128]{0:T(128)}, u32[]{:S(2)}) copy-start(f32[128]{0:T(128)} %copy-done.65) | copy-start | bytes 1540
  385.9 25.3 %copy-start.61 = (f32[192]{0:T(256)S(1)}, f32[192]{0:T(256)}, u32[]{:S(2)}) copy-start(f32[192]{0:T(256)} %param.38) | copy-start | bytes 2308
  424.0 19.8 %copy-start.34 = (f32[192,2,64]{2,1,0:T(2,128)S(1)}, f32[192,2,64]{2,1,0:T(2,128)}, u32[]{:S(2)}) copy-start(f32[192,2,64]{2,1,0:T(2,128)} %get-tuple-element.376) | copy-start | bytes 294916
  424.8 19.3 %copy-start.31 = (f32[2,192,192]{2,0,1:T(2,128)S(1)}, f32[2,192,192]{2,0,1:T(2,128)}, u32[]{:S(2)}) copy-start(f32[2,192,192]{2,0,1:T(2,128)} %copy-done.30) | copy-start | bytes 884740
  424.8 20.8 %collective-permute-start.1 = (bf16[2,64,192]{1,2,0:T(8,128)(2,1)}, bf16[2,64,192]{1,2,0:T(8,128)(2,1)}, u32[]{:S(2)}, u32[]{:S(2)}) collective-permute-start(bf16[2,64,192]{1,2,0:T(8,128)(2,1)} %copy.154), channel_id=1, source_target_pairs={{4,0},{8,4},{12,8},{16,12},{20,16},{24,20},{28,24},{5,1},{9,5},{13... | collective-permute-start | bytes 147464 | tf_op jit(solution)/shard_map/ppermute | solution.py:13
  426.3 22.9 %copy-start.22 = (f32[192,64]{1,0:T(8,128)S(1)}, f32[192,64]{1,0:T(8,128)}, u32[]{:S(2)}) copy-start(f32[192,64]{1,0:T(8,128)} %copy-done.21) | copy-start | bytes 147460
  426.3 22.9 %copy-start.24 = (f32[192,64]{1,0:T(8,128)S(1)}, f32[192,64]{1,0:T(8,128)}, u32[]{:S(2)}) copy-start(f32[192,64]{1,0:T(8,128)} %copy-done.23) | copy-start | bytes 147460
  426.3 22.9 %copy-start.27 = (f32[192,64]{1,0:T(8,128)S(1)}, f32[192,64]{1,0:T(8,128)}, u32[]{:S(2)}) copy-start(f32[192,64]{1,0:T(8,128)} %get-tuple-element.377) | copy-start | bytes 147460
  426.3 22.9 %copy-start.29 = (f32[192,64]{1,0:T(8,128)S(1)}, f32[192,64]{1,0:T(8,128)}, u32[]{:S(2)}) copy-start(f32[192,64]{1,0:T(8,128)} %get-tuple-element.366) | copy-start | bytes 147460
  426.3 22.9 %copy-start.38 = (f32[192,64]{1,0:T(8,128)S(1)}, f32[192,64]{1,0:T(8,128)}, u32[]{:S(2)}) copy-start(f32[192,64]{1,0:T(8,128)} %fusion.12) | copy-start | bytes 147460
  426.3 25.2 %copy-start.57 = (f32[192]{0:T(256)S(1)}, f32[192]{0:T(256)}, u32[]{:S(2)}) copy-start(f32[192]{0:T(256)} %param.39) | copy-start | bytes 2308
  426.3 56.1 %copy-start.43 = (f32[768]{0:T(1024)S(1)}, f32[768]{0:T(1024)}, u32[]{:S(2)}) copy-start(f32[768]{0:T(1024)} %param.29) | copy-start | bytes 9220
  443.8 40.6 %copy-start.53 = (f32[2,128]{1,0:T(2,128)S(1)}, f32[2,128]{1,0:T(2,128)}, u32[]{:S(2)}) copy-start(f32[2,128]{1,0:T(2,128)} %copy-done.52) | copy-start | bytes 3076
  443.8 40.6 %copy-start.47 = (f32[2,128]{1,0:T(2,128)S(1)}, f32[2,128]{1,0:T(2,128)}, u32[]{:S(2)}) copy-start(f32[2,128]{1,0:T(2,128)} %copy-done.46) | copy-start | bytes 3076
  443.8 42.8 %copy-start.20 = (bf16[2,128,192]{1,2,0:T(8,128)(2,1)S(1)}, bf16[2,128,192]{1,2,0:T(8,128)(2,1)}, u32[]{:S(2)}) copy-start(bf16[2,128,192]{1,2,0:T(8,128)(2,1)} %copy-done.19) | copy-start | bytes 294916
  443.8 43.9 %copy-start.56 = (f32[768]{0:T(1024)S(1)}, f32[768]{0:T(1024)}, u32[]{:S(2)}) copy-start(f32[768]{0:T(1024)} %param.30) | copy-start | bytes 9220
  449.1 117.0 %all-reduce.14.cloned.1.call-start = ((), (), s32[]{:S(2)}) async-start(), calls=%async_computation.2 | async-start | bytes 792576 | tf_op jit(solution)/shard_map/psum | solution.py:282
  486.6 321.5 %all-reduce.16.cloned.1.call-start = ((), (), s32[]{:S(2)}) async-start(), calls=%async_computation.3 | async-start | bytes 14155776 | tf_op jit(solution)/shard_map/psum | solution.py:282
  566.1 261.1 %copy-start.59 = (f32[768]{0:T(1024)S(1)}, f32[768]{0:T(1024)}, u32[]{:S(2)}) copy-start(f32[768]{0:T(1024)} %get-tuple-element.514) | copy-start | bytes 9220
  808.1 19.8 %copy-start.6 = (f32[768,768]{1,0:T(8,128)S(1)}, f32[768,768]{1,0:T(8,128)}, u32[]{:S(2)}) copy-start(f32[768,768]{1,0:T(8,128)} %get-tuple-element.515) | copy-start | bytes 7077892
  809.5 20.4 %copy-start.1 = (bf16[768,768]{1,0:T(8,128)(2,1)S(1)}, bf16[768,768]{1,0:T(8,128)(2,1)}, u32[]{:S(2)}) copy-start(bf16[768,768]{1,0:T(8,128)(2,1)} %param.46) | copy-start | bytes 3538948
  (26 other events, 194.4 us)
Sparse Core Ops, SparseCore 0:
  153.0 33.0 all-reduce.9
  197.1 32.5 all-reduce.11
  449.2 33.2 all-reduce.17
  489.3 76.7 all-reduce.13
  572.8 235.2 all-reduce.15
where the time goes:
time: 843 us; the launch traced here: 837 us
  waiting for transfers between devices  403 us (48%)
  matrix products  234 us (28%)
  blocking collectives  95.5 us (11%)
  local copies, waits for them, and re-layouts  42.7 us (5%)
  other arithmetic  38.1 us (5%)
  between operations  14.9 us (2%)
    psum x2, waiting for transfers between devices, shards(): lax.psum((grad_ln1_gain, grad_ln1_bias, grad_w_qkv, grad_b_qkv, grad_shif...  312 us
    dot_general x3, matrix products, ssm_local(): jnp.einsum('icn,jcn->ijc', rising * (ssm_c * input_gain)[None], growing,...  68.6 us
    all_gather x2, blocking collectives, prefix(): lax.all_gather(a.astype(kind), axis)  62.2 us
    dot_general x3, matrix products, advance(): jnp.einsum('ijc,sjc->sic', toeplitz, piece, precision=highest)  55.1 us
    dot_general x3, matrix products, advance(): jnp.einsum('icn,scn->sic', rising, ssm_c * state, precision=highest)  33.8 us
    all_gather x1, blocking collectives, prefix_2(): lax.all_gather(a.astype(kind), axis)  33.3 us
    unnamed x160, local copies, waits for them, and re-layouts  32.8 us
    psum x1, waiting for transfers between devices, shards(): lax.psum(attention_terms.astype(jnp.bfloat16), 'head').astype(jnp.float32)  31.7 us
  transfers between devices with their start and end apart: 7, of which 5 were waited for; matrix products, arithmetic and copies ran while one was open for 9% of the time, Pallas kernels for 0%

commit v1 on v0

v1 whole, which is shorter than its diff:
```python
import functools

import jax
import jax.numpy as jnp
from jax import lax
from jax.experimental import pallas as pl
from jax.experimental.pallas import tpu as pltpu
from jax.sharding import PartitionSpec as P

highest = lax.Precision.HIGHEST
norm_epsilon = 1e-05


f32 = jnp.float32
bf16 = jnp.bfloat16
LANES = 128
SUBS = 8


def shifted(shard, axis, by):
    peers = lax.axis_size(axis)
    return lax.ppermute(shard, axis, [(i, i + by) for i in range(peers) if 0 <= i + by < peers])


def swapped(shard, axis, mask):
    return lax.ppermute(shard, axis, [(i, i ^ mask) for i in range(lax.axis_size(axis))])


def pick(pair, index):
    return lax.dynamic_index_in_dim(pair, index, 0, False)


def head_sum(part, axis="head"):
    peers = lax.axis_size(axis)
    if peers & (peers - 1) or peers < 2 or part.shape[0] % 2:
        return lax.psum(part.astype(f32), axis)
    place = lax.axis_index(axis)
    low_bit = place % 2
    halves = part.reshape((2, part.shape[0] // 2) + part.shape[1:])
    total = pick(halves, low_bit).astype(f32) + swapped(pick(halves, 1 - low_bit), axis, 1).astype(f32)
    mask = 2
    while mask < peers:
        total = total + swapped(total.astype(bf16), axis, mask).astype(f32)
        mask *= 2
    own = total.astype(bf16)
    other = swapped(own, axis, 1)
    first = jnp.where(low_bit == 0, own, other)
    second = jnp.where(low_bit == 0, other, own)
    return jnp.concatenate([first, second], axis=0).astype(f32)


def halving_sum(block, axis, masks):
    place = lax.axis_index(axis)
    for mask in masks:
        bit = (place // mask) % 2
        halves = block.reshape((2, block.shape[0] // 2) + block.shape[1:])
        got = swapped(pick(halves, 1 - bit), axis, mask)
        block = (pick(halves, bit).astype(f32) + got.astype(f32)).astype(bf16)
    for mask in masks[::-1]:
        bit = (place // mask) % 2
        got = swapped(block, axis, mask)
        first = jnp.where(bit == 0, block, got)
        second = jnp.where(bit == 0, got, block)
        block = jnp.concatenate([first, second], axis=0)
    return block


def seq_sums(first, second, axis="seq"):
    peers = lax.axis_size(axis)
    masks = []
    while 2 ** len(masks) < peers:
        masks.append(2 ** len(masks))
    other = masks[1::-1] + masks[2:] if len(masks) > 1 else masks
    return halving_sum(first, axis, masks), halving_sum(second, axis, other)


def carried_state(ends, whole, axis, ahead):
    peers = lax.axis_size(axis)
    way = -1 if ahead else 1
    if peers % 2 or peers > 8:
        state = shifted(ends.astype(bf16), axis, way).astype(f32)
        power, step = whole, 1
        while step < peers:
            state = state + power * shifted(state.astype(bf16), axis, way * step).astype(f32)
            power, step = power * power, step * 2
        return state
    inner = lax.axis_index(axis) % 2
    is_near = inner == (0 if ahead else 1)
    mate = swapped(ends.astype(bf16), axis, 1).astype(f32)
    far, near = jnp.where(is_near, mate, ends), jnp.where(is_near, ends, mate)
    pair = (near + whole * far).astype(bf16)
    square = whole * whole
    power = jnp.ones_like(whole)
    state = jnp.zeros_like(ends)
    for step in range(2, peers, 2):
        state = state + power * shifted(pair, axis, way * step).astype(f32)
        power = power * square
    return jnp.where(is_near, mate + whole * state, state)


def layer_norm(rows_in, norm_gain, norm_bias):
    mean_val = jnp.mean(rows_in, axis=-1, keepdims=True)
    centred = rows_in - mean_val
    spread = jnp.mean(centred * centred, axis=-1, keepdims=True)
    return centred * lax.rsqrt(spread + norm_epsilon) * norm_gain + norm_bias


def smooth_gate(values_in):
    return jax.nn.gelu(values_in, approximate=True)


def shift_mix(extended, values, shift_taps, shift_skip):
    filters = jnp.concatenate([shift_taps[::-1], shift_skip[None]], axis=0)[:, None, :]
    shifted = lax.conv_general_dilated(
        extended,
        filters,
        (1,),
        "VALID",
        dimension_numbers=("NWC", "WIO", "NWC"),
        feature_group_count=extended.shape[2],
        precision=highest,
    )
    return shifted * values


def lane_tiles(width):
    return [slice(i, i + LANES) for i in range(0, width, LANES)]


def folded(product):
    states, lanes = product.shape
    return jnp.sum(product.reshape(states // SUBS, SUBS, lanes), axis=0)


def end_kernel(reverse, series_ref, decay_ref, end_ref):
    rows = series_ref.shape[0]
    blocks = rows // SUBS
    for lanes in lane_tiles(series_ref.shape[1]):
        decay = decay_ref[:, lanes]

        def one(lap, state, lanes=lanes, decay=decay):
            place = blocks - 1 - lap if reverse else lap
            tile = series_ref[pl.ds(pl.multiple_of(place * SUBS, SUBS), SUBS), lanes]
            for r in range(SUBS):
                r = SUBS - 1 - r if reverse else r
                state = decay * state + tile[r : r + 1, :]
            return state

        end_ref[:, lanes] = lax.fori_loop(0, blocks, one, jnp.zeros_like(decay))


def forward_kernel(series_ref, decay_ref, weight_ref, start_ref, out_ref, part_ref):
    rows = series_ref.shape[0]
    blocks = rows // SUBS
    for lanes in lane_tiles(series_ref.shape[1]):
        decay = decay_ref[:, lanes]
        weight = weight_ref[:, lanes]

        def one(lap, state, lanes=lanes, decay=decay, weight=weight):
            tile = series_ref[pl.ds(pl.multiple_of(lap * SUBS, SUBS), SUBS), lanes]
            base = pl.multiple_of(lap * SUBS * SUBS, SUBS)
            for r in range(SUBS):
                state = decay * state + tile[r : r + 1, :]
                part_ref[pl.ds(base + r * SUBS, SUBS), :] = folded(weight * state)
            return state

        lax.fori_loop(0, blocks, one, start_ref[:, lanes])
        total = part_ref[pl.ds(0, rows, stride=SUBS), :]
        for r in range(1, SUBS):
            total = total + part_ref[pl.ds(r, rows, stride=SUBS), :]
        out_ref[:, lanes] = total


def backward_kernel(
    series_ref, grad_ref, decay_ref, weight_ref, start_ref, end_ref,
    out_ref, gain_ref, power_ref, part_ref, past_ref,
):
    rows = series_ref.shape[0]
    blocks = rows // SUBS
    states = decay_ref.shape[0]
    for lanes in lane_tiles(series_ref.shape[1]):
        decay = decay_ref[:, lanes]
        weight = weight_ref[:, lanes]

        def rise(lap, state, lanes=lanes, decay=decay):
            tile = series_ref[pl.ds(pl.multiple_of(lap * SUBS, SUBS), SUBS), lanes]
            base = pl.multiple_of(lap * SUBS * states, SUBS)
            for r in range(SUBS):
                past_ref[pl.ds(base + r * states, states), :] = state
                state = decay * state + tile[r : r + 1, :]
            return state

        lax.fori_loop(0, blocks, rise, start_ref[:, lanes])

        def fall(lap, carry, lanes=lanes, decay=decay, weight=weight):
            adjoint, gain, power = carry
            place = blocks - 1 - lap
            at = pl.ds(pl.multiple_of(place * SUBS, SUBS), SUBS)
            tile, grads = series_ref[at, lanes], grad_ref[at, lanes]
            base = pl.multiple_of(place * SUBS * SUBS, SUBS)
            far = pl.multiple_of(place * SUBS * states, SUBS)
            for r in range(SUBS - 1, -1, -1):
                adjoint = decay * adjoint + grads[r : r + 1, :]
                part_ref[pl.ds(base + r * SUBS, SUBS), :] = folded(weight * adjoint)
                gain = gain + adjoint * tile[r : r + 1, :]
                power = power + adjoint * past_ref[pl.ds(far + r * states, states), :]
            return adjoint, gain, power

        zero = jnp.zeros_like(decay)
        _, gain, power = lax.fori_loop(0, blocks, fall, (end_ref[:, lanes], zero, zero))
        gain_ref[:, lanes] = gain
        power_ref[:, lanes] = power
        total = part_ref[pl.ds(0, rows, stride=SUBS), :]
        for r in range(1, SUBS):
            total = total + part_ref[pl.ds(r, rows, stride=SUBS), :]
        out_ref[:, lanes] = total


def cost(flops, *arrays):
    size = sum(a.size * a.dtype.itemsize for a in arrays)
    return pl.CostEstimate(flops=flops, bytes_accessed=size, transcendentals=0)


def ssm_end(series, decay, reverse):
    rows, width = series.shape
    return pl.pallas_call(
        functools.partial(end_kernel, reverse),
        out_shape=jax.ShapeDtypeStruct(decay.shape, f32),
        compiler_params=pltpu.CompilerParams(vmem_limit_bytes=16 << 20),
        cost_estimate=cost(2 * rows * decay.size, series, decay),
    )(series, decay)


def ssm_forward(series, decay, weight, start):
    rows, width = series.shape
    return pl.pallas_call(
        forward_kernel,
        out_shape=jax.ShapeDtypeStruct(series.shape, f32),
        scratch_shapes=[pltpu.VMEM((rows * SUBS, LANES), f32)],
        compiler_params=pltpu.CompilerParams(vmem_limit_bytes=16 << 20),
        cost_estimate=cost(4 * rows * decay.size, series, decay, weight, start),
    )(series, decay, weight, start)


def ssm_backward(series, grads, decay, weight, start, end):
    rows, width = series.shape
    states = decay.shape[0]
    return pl.pallas_call(
        backward_kernel,
        out_shape=(
            jax.ShapeDtypeStruct(series.shape, f32),
            jax.ShapeDtypeStruct(decay.shape, f32),
            jax.ShapeDtypeStruct(decay.shape, f32),
        ),
        scratch_shapes=[
            pltpu.VMEM((rows * SUBS, LANES), f32),
            pltpu.VMEM((rows * states, LANES), f32),
        ],
        compiler_params=pltpu.CompilerParams(vmem_limit_bytes=24 << 20),
        cost_estimate=cost(10 * rows * decay.size, series, grads, decay, weight, start, end),
    )(series, grads, decay, weight, start, end)


def packed(array):
    return jnp.concatenate([array[s] for s in range(array.shape[0])], axis=-1)


def unpacked(array, slots):
    return jnp.stack(jnp.split(array, slots, axis=-1))


def shards(
    inputs,
    cotangent,
    lengths,
    ln1_gain,
    ln1_bias,
    query_key_value_weight,
    b_qkv,
    shift_taps,
    shift_skip,
    ssm_a,
    ssm_b,
    ssm_c,
    ssm_skip,
    ssm_step,
    output_weight,
    b_out,
    ln2_gain,
    ln2_bias,
    up_weight,
    up_bias,
    down_weight,
    b_down,
):
    slot_count, row_count, width_all = inputs.shape
    tap_count, chan_count = shift_taps.shape
    state_count = ssm_a.shape[1]
    places = lax.axis_index("seq") * row_count + jnp.arange(row_count, dtype=jnp.int32)
    valid_rows = (places[None, :] < lengths[:, None]).astype(jnp.float32)[:, :, None]
    residual_in = inputs.astype(jnp.float32)

    def repeated(array):
        return jnp.concatenate([array] * slot_count, axis=-1)

    rate = (ssm_step[:, None] * ssm_a).T
    decay = jnp.exp(-rate)
    gain_root = jnp.sqrt(-jnp.expm1(-2.0 * rate))
    in_weight = gain_root * ssm_b.T
    out_weight = ssm_c.T
    decay_wide = repeated(decay)
    whole_wide = repeated(jnp.exp(-rate * row_count))
    weight_wide = repeated(out_weight * in_weight)
    skip_wide = repeated(ssm_skip)

    normed_one, undo_one = jax.vjp(layer_norm, residual_in, ln1_gain, ln1_bias)
    first_activation = normed_one.astype(jnp.bfloat16)
    projected = (
        jnp.einsum(
            "vbg,tgi->tvbi",
            first_activation,
            query_key_value_weight,
            preferred_element_type=jnp.float32,
        )
        + b_qkv[:, None, None, :]
    )
    queries = projected[0]
    keys_low = projected[1].astype(jnp.bfloat16)
    values = projected[2]
    edge_rows = shifted(keys_low[:, row_count - tap_count :, :], "seq", 1)
    extended = jnp.concatenate([edge_rows, keys_low], axis=1).astype(jnp.float32)
    mixed_u, shift_undo = jax.vjp(shift_mix, extended, values, shift_taps, shift_skip)
    series = packed(mixed_u)
    end_local = ssm_end(series, decay_wide, False)
    start_state = carried_state(end_local, whole_wide, "seq", False)
    ssm_out = unpacked(
        ssm_forward(series, decay_wide, weight_wide, start_state) + skip_wide * series, slot_count
    )
    gated_mixture = (queries * ssm_out).astype(jnp.bfloat16)
    attention_terms = jnp.einsum(
        "upm,mq->upq", gated_mixture, output_weight, preferred_element_type=jnp.float32
    )
    attended = head_sum(attention_terms.astype(jnp.bfloat16)) + b_out
    middle = residual_in + attended
    normed_two, undo_two = jax.vjp(layer_norm, middle, ln2_gain, ln2_bias)
    second_activation = normed_two.astype(jnp.bfloat16)
    up_projected = (
        jnp.einsum("pwu,uj->pwj", second_activation, up_weight, preferred_element_type=jnp.float32)
        + up_bias
    )
    hidden_full, gelu_undo = jax.vjp(smooth_gate, up_projected)
    hidden_activations = hidden_full.astype(jnp.bfloat16)
    down_projection_terms = jnp.einsum(
        "jiq,qx->jix", hidden_activations, down_weight, preferred_element_type=jnp.float32
    )
    feed_out = head_sum(down_projection_terms.astype(jnp.bfloat16)) + b_down
    layer_out = valid_rows * (middle + feed_out)
    grad_out = cotangent * valid_rows
    grad_b_down = jnp.sum(grad_out, axis=(0, 1))
    output_lower_gradient = grad_out.astype(jnp.bfloat16)
    grad_w_down = jnp.einsum(
        "iqe,iqy->ey", hidden_activations, output_lower_gradient, preferred_element_type=jnp.float32
    )
    grad_hidden = jnp.einsum(
        "apo,io->api", output_lower_gradient, down_weight, preferred_element_type=jnp.float32
    )
    up_gradient = gelu_undo(grad_hidden)[0].astype(jnp.bfloat16)
    grad_b_up = jnp.sum(up_gradient.astype(jnp.float32), axis=(0, 1))
    up_weight_gradient = jnp.einsum(
        "bar,bak->rk", second_activation, up_gradient, preferred_element_type=jnp.float32
    )
    second_activation_terms = jnp.einsum(
        "hxe,ge->hxg", up_gradient, up_weight, preferred_element_type=jnp.float32
    )
    grad_act_two = head_sum(second_activation_terms.astype(jnp.bfloat16))
    grad_mid_norm, grad_ln2_gain, grad_ln2_bias = undo_two(grad_act_two)
    grad_middle = grad_out + grad_mid_norm
    sum_up, sum_down = seq_sums(up_weight_gradient.astype(bf16), grad_w_down.astype(bf16))
    grad_b_out = jnp.sum(grad_middle, axis=(0, 1))
    middle_lower_gradient = grad_middle.astype(jnp.bfloat16)
    grad_w_out = jnp.einsum(
        "hxq,hxe->qe", gated_mixture, middle_lower_gradient, preferred_element_type=jnp.float32
    )
    gated_gradient = jnp.einsum(
        "ihq,zq->ihz", middle_lower_gradient, output_weight, preferred_element_type=jnp.float32
    )
    grad_queries = gated_gradient * ssm_out
    grad_ssm = packed(gated_gradient * queries)
    front_local = ssm_end(grad_ssm, decay_wide, True)
    end_adjoint = carried_state(front_local, whole_wide, "seq", True)
    grad_series, gain_sum, power_sum = ssm_backward(
        series, grad_ssm, decay_wide, weight_wide, start_state, end_adjoint
    )
    grad_mixed_u = unpacked(grad_series + skip_wide * grad_ssm, slot_count)
    gain_sum = jnp.sum(gain_sum.reshape(state_count, slot_count, chan_count), axis=1)
    power_sum = jnp.sum(power_sum.reshape(state_count, slot_count, chan_count), axis=1)
    grad_ssm_c = in_weight * gain_sum
    grad_in_weight = out_weight * gain_sum
    grad_ssm_b = grad_in_weight * gain_root
    grad_rate = (
        grad_in_weight * ssm_b.T * jnp.exp(-2.0 * rate) / gain_root
        - decay * out_weight * in_weight * power_sum
    )
    grad_ssm_a = grad_rate * ssm_step
    grad_ssm_step = jnp.sum(grad_rate * ssm_a.T, axis=0)
    grad_ssm_skip = jnp.sum(
        jnp.sum(grad_ssm * series, axis=0).reshape(slot_count, chan_count), axis=0
    )
    grad_ext, grad_values, grad_shift_taps, grad_shift_skip = shift_undo(grad_mixed_u)
    received = shifted(grad_ext[:, :tap_count, :].astype(jnp.bfloat16), "seq", -1).astype(
        jnp.float32
    )
    grad_keys = grad_ext[:, tap_count:, :] + jnp.pad(
        received, ((0, 0), (row_count - tap_count, 0), (0, 0))
    )
    projected_gradient = jnp.stack([grad_queries, grad_keys, grad_values]).astype(jnp.bfloat16)
    grad_b_qkv = jnp.sum(projected_gradient.astype(jnp.float32), axis=(1, 2))
    grad_w_qkv = jnp.einsum(
        "quf,gquv->gvf", first_activation, projected_gradient, preferred_element_type=jnp.float32
    )
    act_one_terms = jnp.einsum(
        "znpu,zru->npr",
        projected_gradient,
        query_key_value_weight,
        preferred_element_type=jnp.float32,
    )
    grad_act_one = head_sum(act_one_terms.astype(jnp.bfloat16))
    grad_in_norm, grad_ln1_gain, grad_ln1_bias = undo_one(grad_act_one)
    grad_inputs = grad_middle + grad_in_norm

    small = [
        grad_ln1_gain,
        grad_ln1_bias,
        grad_b_qkv,
        grad_shift_taps,
        grad_shift_skip,
        grad_ssm_a,
        grad_ssm_b,
        grad_ssm_c,
        grad_ssm_skip,
        grad_ssm_step,
        grad_b_out,
        grad_ln2_gain,
        grad_ln2_bias,
        grad_b_up,
        grad_b_down,
    ]
    flat = jnp.concatenate([a.reshape(-1) for a in small])
    pieces = [grad_w_qkv.reshape(3 * chan_count, width_all), grad_w_out]
    rows_big = 4 * chan_count
    unit = 2 * lax.axis_size("seq") * SUBS
    rows_all = -(-(rows_big * width_all + flat.size) // (width_all * unit)) * unit
    flat = jnp.pad(flat, (0, (rows_all - rows_big) * width_all - flat.size))
    pieces.append(flat.reshape(rows_all - rows_big, width_all))
    whole_buffer = jnp.concatenate(pieces, axis=0).astype(bf16)
    half = rows_all // 2
    summed = jnp.concatenate(seq_sums(whole_buffer[:half], whole_buffer[half:]), axis=0)
    sum_qkv = jnp.transpose(summed[: 3 * chan_count].reshape(3, chan_count, width_all), (0, 2, 1))
    sum_out = summed[3 * chan_count : rows_big]
    flat = summed[rows_big:].reshape(-1).astype(f32)
    sums, offset = [], 0
    for a in small:
        sums.append(flat[offset : offset + a.size].reshape(a.shape))
        offset += a.size
    return (
        layer_out,
        grad_inputs,
        sums[0],
        sums[1],
        sum_qkv.astype(f32),
        sums[2],
        sums[3],
        sums[4],
        sums[5].T,
        sums[6].T,
        sums[7].T,
        sums[8],
        sums[9],
        sum_out.astype(f32),
        sums[10],
        sums[11],
        sums[12],
        sum_up.astype(f32),
        sums[13],
        sum_down.astype(f32),
        sums[14],
    )


def solution(mesh):
    in_specs = (
        P(None, "seq", None),
        P(None, "seq", None),
        P(),
        P(),
        P(),
        P(None, None, "head"),
        P(None, "head"),
        P(None, "head"),
        P("head"),
        P("head", None),
        P("head", None),
        P("head", None),
        P("head"),
        P("head"),
        P("head", None),
        P(),
        P(),
        P(),
        P(None, "head"),
        P("head"),
        P("head", None),
        P(),
    )
    out_specs = (
        P(None, "seq", None),
        P(None, "seq", None),
        P(),
        P(),
        P(None, None, "head"),
        P(None, "head"),
        P(None, "head"),
        P("head"),
        P("head", None),
        P("head", None),
        P("head", None),
        P("head"),
        P("head"),
        P("head", None),
        P(),
        P(),
        P(),
        P(None, "head"),
        P("head"),
        P("head", None),
        P(),
    )
    return jax.shard_map(shards, mesh=mesh, in_specs=in_specs, out_specs=out_specs, check_vma=False)
```

time: 843 us -> 241 us (0.29)
  waiting for transfers between devices: 403 us -> 77.6 us
  matrix products: 234 us -> 24.8 us
  blocking collectives: 95.5 us -> 0 us
  starting transfers between devices: 7.31 us -> 61.5 us
  between operations: 14.9 us -> 2.15 us
  local copies, waits for them, and re-layouts: 42.7 us -> 30.5 us
  Pallas kernels: 0 us -> 9.11 us
    psum x5 -> x0, waiting for transfers between devices: 403 us -> none  [the longest x2 312 us: shards(): lax.psum((grad_ln1_gain, grad_ln1_bias, grad_w_qkv, grad_b_qkv, grad_shif...]
    dot_general x14 -> x1, matrix products: 202 us -> 1.52 us  [shards(): jnp.einsum('quf,gquv->gvf', first_activation, projected_gradient, preferr...]
    all_gather x3 -> x0, blocking collectives: 95.5 us -> none  [the longest x2 62.2 us: prefix(): lax.all_gather(a.astype(kind), axis)]
    ppermute x2 -> x46, waiting for transfers between devices: 0.01 us -> 77.6 us  [the longest x38 74.1 us: swapped(): lax.ppermute(shard, axis, [(i, i ^ mask) for i in range(lax.axis_size(axi...]
    ppermute x2 -> x46, starting transfers between devices: 6.92 us -> 61.5 us  [the longest x38 40.4 us: swapped(): lax.ppermute(shard, axis, [(i, i ^ mask) for i in range(lax.axis_size(axi...]
    unnamed x160 -> x104, local copies, waits for them, and re-layouts: 32.8 us -> 2.81 us
    convert_element_type x0 -> x29, other arithmetic: none -> 9.9 us  [the longest x12 2.86 us: halving_sum(): block = (pick(halves, bit).astype(f32) + got.astype(f32)).astype(bf16)]
    pallas_call x0 -> x4, Pallas kernels: none -> 9.11 us  [the longest x1 4.98 us: ssm_backward(): pl.pallas_call(backward_kernel, out_shape=(jax.ShapeDtypeStruct(series.sh...]
  transfers between devices with their start and end apart: 7 -> 46, of which waited for: 5 -> 23; matrix products, arithmetic and copies ran while one was open for 9% -> 30% of each run, Pallas kernels for 0% -> 3%
where the time goes in v1:
time: 241 us; the launch traced here: 239 us
  waiting for transfers between devices  77.6 us (32%)
  starting transfers between devices  61.5 us (26%)
  other arithmetic  33.8 us (14%)
  local copies, waits for them, and re-layouts  30.5 us (13%)
  matrix products  24.8 us (10%)
  Pallas kernels  9.11 us (4%)
    ppermute x38, waiting for transfers between devices, swapped(): lax.ppermute(shard, axis, [(i, i ^ mask) for i in range(lax.axis_size(axi...  74.1 us
    ppermute x38, starting transfers between devices, swapped(): lax.ppermute(shard, axis, [(i, i ^ mask) for i in range(lax.axis_size(axi...  40.4 us
    ppermute x8, starting transfers between devices, shifted(): lax.ppermute(shard, axis, [(i, i + by) for i in range(peers) if 0 <= i +...  21.1 us
    conv_general_dilated x3, matrix products, shift_mix(): lax.conv_general_dilated(extended, filters, (1,), 'VALID', dimension_numb...  11.8 us
    concatenate x1, local copies, waits for them, and re-layouts, shards(): flat = jnp.concatenate([a.reshape(-1) for a in small])  9.16 us
    slice x9, local copies, waits for them, and re-layouts, shards(): sums.append(flat[offset:offset + a.size].reshape(a.shape))  8.28 us
    pallas_call x1, Pallas kernels, ssm_backward(): pl.pallas_call(backward_kernel, out_shape=(jax.ShapeDtypeStruct(series.sh...  4.98 us
  transfers between devices with their start and end apart: 46, of which 23 were waited for; matrix products, arithmetic and copies ran while one was open for 30% of the time, Pallas kernels for 3%

profile of v1, /device:TPU:0, one launch (start us, length us, event | category | flops | bytes accessed | tf_op | source)
XLA Modules:
  0.0 239.5 jit_solution(10961312449601700694)
XLA Ops:
  3.3 1.9 fusion
  5.3 4.9 %collective-permute-start = (bf16[2,64,192]{2,1,0:T(8,128)(2,1)S(1)}, bf16[2,64,192]{2,1,0:T(8,128)(2,1)S(1)}, u32[]{:S(2)}, u32[]{:S(2)}) collective-permute-start(bf16[2,64,192]{2,1,0:T(8,128)(2,1)S(1)} %slice.154), channel_id=1, source_target_pairs={{0,4},{4,8},{8,12},{12,16},{16,20},{20,24},{24,28},{1,5},{5,9},{9,... | collective-permute-start | bytes 147464 | tf_op jit(solution)/shard_map/ppermute | solution.py:22
  12.1 3.1 %fusion.76 = f32[2,128,192]{2,0,1:T(2,128)S(1)} fusion(f32[65,1,192]{2,1,0:T(1,128)S(1)} %broadcast_in_dim.15, bf16[2,192,192]{2,1,0:T(8,128)(2,1)S(1)} %pad_maximum_fusion.17), kind=kOutput, calls=%fused_computation.210 | convolution fusion | flops 38338560 | bytes 393984 | tf_op jit(solution)/shard_map/jvp()/conv_general_dilated | solution.py:114
  17.1 2.4 %collective-permute-start.1 = (bf16[64,384]{1,0:T(8,128)(2,1)S(1)}, bf16[64,384]{1,0:T(8,128)(2,1)S(1)}, u32[]{:S(2)}, u32[]{:S(2)}) collective-permute-start(bf16[64,384]{1,0:T(8,128)(2,1)S(1)} %convert_element_type.364), channel_id=1, source_target_pairs={{0,4},{4,0},{8,12},{12,8},{16,20},{20,16},{24,28},{28,24},{1,5},{5... | collective-permute-start | bytes 147464 | tf_op jit(solution)/shard_map/ppermute | solution.py:26
  19.6 2.0 collective-permute-done.1
  21.7 6.9 %collective-permute-start.4 = (bf16[64,384]{1,0:T(8,128)(2,1)S(1)}, bf16[64,384]{1,0:T(8,128)(2,1)S(1)}, u32[]{:S(2)}, u32[]{:S(2)}) collective-permute-start(bf16[64,384]{1,0:T(8,128)(2,1)S(1)} %fusion.79), channel_id=1, source_target_pairs={{0,24},{4,28},{1,25},{5,29},{2,26},{6,30},{3,27},{7,31}} | collective-permute-start | bytes 147464 | tf_op jit(solution)/shard_map/ppermute | solution.py:22
  29.9 2.5 %collective-permute-start.2 = (bf16[64,384]{1,0:T(8,128)(2,1)S(1)}, bf16[64,384]{1,0:T(8,128)(2,1)S(1)}, u32[]{:S(2)}, u32[]{:S(2)}) collective-permute-start(bf16[64,384]{1,0:T(8,128)(2,1)S(1)} %fusion.79), channel_id=1, source_target_pairs={{0,8},{4,12},{8,16},{12,20},{16,24},{20,28},{1,9},{5,13},{9,17},{1... | collective-permute-start | bytes 147464 | tf_op jit(solution)/shard_map/ppermute | solution.py:22
  32.5 1.6 collective-permute-done.2
  34.2 2.1 shard_map.374
  39.2 1.6 collective-permute-start.6
  40.7 5.6 %collective-permute-done.6 = bf16[1,128,768]{2,1,0:T(8,128)(2,1)} collective-permute-done((bf16[1,128,768]{2,1,0:T(8,128)(2,1)S(1)}, bf16[1,128,768]{2,1,0:T(8,128)(2,1)}, u32[]{:S(2)}, u32[]{:S(2)}) %collective-permute-start.6) | collective-permute-done | bytes 196640 | tf_op jit(solution)/shard_map/ppermute | solution.py:26
  55.3 2.4 %collective-permute-start.40 = (bf16[384,768]{1,0:T(8,128)(2,1)S(1)}, bf16[384,768]{1,0:T(8,128)(2,1)S(1)}, u32[]{:S(2)}, u32[]{:S(2)}) collective-permute-start(bf16[384,768]{1,0:T(8,128)(2,1)S(1)} %dynamic-slice_bitcast_fusion), channel_id=1, source_target_pairs={{0,8},{4,12},{8,0},{12,4},{16,24},{20,28},{24,16},{28,20},{1,9},{5... | collective-permute-start | bytes 1769480 | tf_op jit(solution)/shard_map/ppermute | solution.py:26
  58.5 1.6 collective-permute-start.12
  60.7 5.7 %collective-permute-done.12 = bf16[1,128,768]{2,1,0:T(8,128)(2,1)S(1)} collective-permute-done((bf16[1,128,768]{2,1,0:T(8,128)(2,1)S(1)}, bf16[1,128,768]{2,1,0:T(8,128)(2,1)S(1)}, u32[]{:S(2)}, u32[]{:S(2)}) %collective-permute-start.12) | collective-permute-done | bytes 196640 | tf_op jit(solution)/shard_map/ppermute | solution.py:26
  66.6 2.6 %collective-permute-done.9 = bf16[1,128,768]{2,1,0:T(8,128)(2,1)S(1)} collective-permute-done((bf16[1,128,768]{2,1,0:T(8,128)(2,1)S(1)}, bf16[1,128,768]{2,1,0:T(8,128)(2,1)S(1)}, u32[]{:S(2)}, u32[]{:S(2)}) %collective-permute-start.9) | collective-permute-done | bytes 196640 | tf_op jit(solution)/shard_map/ppermute | solution.py:26
  73.3 2.0 fusion.104
  75.4 1.9 fusion.69
  80.8 1.9 collective-permute-done.14
  87.6 2.6 %collective-permute-start.35 = (bf16[192,768]{1,0:T(8,128)(2,1)}, bf16[192,768]{1,0:T(8,128)(2,1)}, u32[]{:S(2)}, u32[]{:S(2)}) collective-permute-start(bf16[192,768]{1,0:T(8,128)(2,1)} %dynamic-slice_bitcast_fusion.5), channel_id=1, source_target_pairs={{0,8},{4,12},{8,0},{12,4},{16,24},{20,28},{24,16},{28,20},{1,9},{5... | collective-permute-start | bytes 884744 | tf_op jit(solution)/shard_map/ppermute | solution.py:26
  92.5 5.0 %shard_map.376 = (f32[128,384]{1,0:T(8,128)S(1)}, f32[64,384]{1,0:T(8,128)S(1)}, f32[64,384]{1,0:T(8,128)S(1)}) custom-call(f32[128,384]{1,0:T(8,128)S(1)} %pad_maximum_fusion.18.series_ref, f32[128,384]{1,0:T(8,128)S(1)} %get-tuple-element.42.series_ref.grad_ref, f32[64,384]{1,0:T(8,128)S(1)} %pad_maximum_fusion.22.decay_ref, ...), custom_call_target="tpu_custom_call" | custom-call | flops 31457280 | bytes 786432 | tf_op jit(solution)/shard_map/pallas_call | solution.py:248
  98.8 6.7 %fusion.61 = bf16[65,1,192]{2,1,0:T(2,128)(2,1)} fusion(f32[2,128,192]{2,1,0:T(8,128)S(1)} %get-tuple-element.92, bf16[2,192,192]{2,1,0:T(8,128)(2,1)S(1)} %copy-done.25), kind=kOutput, calls=%fused_computation.151 | convolution fusion | flops 38338560 | bytes 369024 | tf_op jit(solution)/shard_map/transpose(jvp())/conv_general_dilated | solution.py:114
  105.5 2.0 fusion.63
  116.5 1.7 fusion.1
  119.8 1.5 bitcast_convert_fusion.2
  122.5 4.2 %collective-permute-start.42 = (bf16[96,768]{1,0:T(8,128)(2,1)S(1)}, bf16[96,768]{1,0:T(8,128)(2,1)S(1)}, u32[]{:S(2)}, u32[]{:S(2)}) collective-permute-start(bf16[96,768]{1,0:T(8,128)(2,1)S(1)} %dynamic-slice_bitcast_fusion.8), channel_id=1, source_target_pairs={{0,16},{4,20},{8,24},{12,28},{16,0},{20,4},{24,8},{28,12},{1,17},{... | collective-permute-start | bytes 442376 | tf_op jit(solution)/shard_map/ppermute | solution.py:26
  127.9 1.6 collective-permute-start.20
  129.4 8.2 %collective-permute-done.42 = bf16[96,768]{1,0:T(8,128)(2,1)S(1)} collective-permute-done((bf16[96,768]{1,0:T(8,128)(2,1)S(1)}, bf16[96,768]{1,0:T(8,128)(2,1)S(1)}, u32[]{:S(2)}, u32[]{:S(2)}) %collective-permute-start.42) | collective-permute-done | bytes 147488 | tf_op jit(solution)/shard_map/ppermute | solution.py:26
  137.8 2.8 %collective-permute-done.36 = bf16[96,768]{1,0:T(8,128)(2,1)S(1)} collective-permute-done((bf16[96,768]{1,0:T(8,128)(2,1)S(1)}, bf16[96,768]{1,0:T(8,128)(2,1)S(1)}, u32[]{:S(2)}, u32[]{:S(2)}) %collective-permute-start.36) | collective-permute-done | bytes 147488 | tf_op jit(solution)/shard_map/ppermute | solution.py:26
  141.0 7.5 %collective-permute-done.43 = bf16[96,768]{1,0:T(8,128)(2,1)S(1)} collective-permute-done((bf16[96,768]{1,0:T(8,128)(2,1)S(1)}, bf16[96,768]{1,0:T(8,128)(2,1)S(1)}, u32[]{:S(2)}, u32[]{:S(2)}) %collective-permute-start.43) | collective-permute-done | bytes 147488 | tf_op jit(solution)/shard_map/ppermute | solution.py:26
  149.2 3.5 %collective-permute-start.44 = (bf16[192,768]{1,0:T(8,128)(2,1)}, bf16[192,768]{1,0:T(8,128)(2,1)}, u32[]{:S(2)}, u32[]{:S(2)}) collective-permute-start(bf16[192,768]{1,0:T(8,128)(2,1)} %pad_maximum_fusion.14), channel_id=1, source_target_pairs={{0,4},{4,0},{8,12},{12,8},{16,20},{20,16},{24,28},{28,24},{1,5},{5... | collective-permute-start | bytes 884744 | tf_op jit(solution)/shard_map/ppermute | solution.py:26
  153.5 2.5 %collective-permute-start.38 = (bf16[192,768]{1,0:T(8,128)(2,1)}, bf16[192,768]{1,0:T(8,128)(2,1)}, u32[]{:S(2)}, u32[]{:S(2)}) collective-permute-start(bf16[192,768]{1,0:T(8,128)(2,1)} %pad_maximum_fusion.13), channel_id=1, source_target_pairs={{0,8},{4,12},{8,0},{12,4},{16,24},{20,28},{24,16},{28,20},{1,9},{5... | collective-permute-start | bytes 884744 | tf_op jit(solution)/shard_map/ppermute | solution.py:26
  158.6 9.2 %concatenate.94 = bf16[55680]{0:T(1024)(128)(2,1)S(1)} concatenate(bf16[768]{0:T(1024)(128)(2,1)} %get-tuple-element.29, bf16[768]{0:T(1024)(128)(2,1)} %reduce_sum.265, bf16[576]{0:T(1024)(128)(2,1)} %reshape.305, bf16[12288]{0:T(1024)(128)(2,1)S(1)} %reshape.306, bf16[192]{0:T(256)(128)(2,1)} %fusion.95, bf16[12288]{0:T(1024)(128)(2,1)S(1)} %reshape.309, ...), dimensions={0} | concatenate | bytes 222720 | tf_op jit(solution)/shard_map/concatenate | solution.py:448
  168.5 1.8 reshape.313
  171.8 1.8 collective-permute-start.22
  177.5 2.0 collective-permute-start.39
  179.5 3.4 %collective-permute-done.28 = bf16[224,768]{1,0:T(8,128)(2,1)S(1)} collective-permute-done((bf16[224,768]{1,0:T(8,128)(2,1)S(1)}, bf16[224,768]{1,0:T(8,128)(2,1)S(1)}, u32[]{:S(2)}, u32[]{:S(2)}) %collective-permute-start.28) | collective-permute-done | bytes 344096 | tf_op jit(solution)/shard_map/ppermute | solution.py:26
  183.2 1.9 collective-permute-start.23
  185.0 12.5 %collective-permute-done.29 = bf16[112,768]{1,0:T(8,128)(2,1)S(1)} collective-permute-done((bf16[112,768]{1,0:T(8,128)(2,1)S(1)}, bf16[112,768]{1,0:T(8,128)(2,1)S(1)}, u32[]{:S(2)}, u32[]{:S(2)}) %collective-permute-start.29) | collective-permute-done | bytes 172064 | tf_op jit(solution)/shard_map/ppermute | solution.py:26
  197.6 2.3 collective-permute-start.30
  200.7 6.6 %collective-permute-done.30 = bf16[56,768]{1,0:T(8,128)(2,1)S(1)} collective-permute-done((bf16[56,768]{1,0:T(8,128)(2,1)S(1)}, bf16[56,768]{1,0:T(8,128)(2,1)S(1)}, u32[]{:S(2)}, u32[]{:S(2)}) %collective-permute-start.30) | collective-permute-done | bytes 86048 | tf_op jit(solution)/shard_map/ppermute | solution.py:26
  207.4 1.7 collective-permute-done.24
  210.4 3.1 %collective-permute-done.31 = bf16[56,768]{1,0:T(8,128)(2,1)S(1)} collective-permute-done((bf16[56,768]{1,0:T(8,128)(2,1)S(1)}, bf16[56,768]{1,0:T(8,128)(2,1)S(1)}, u32[]{:S(2)}, u32[]{:S(2)}) %collective-permute-start.31) | collective-permute-done | bytes 86048 | tf_op jit(solution)/shard_map/ppermute | solution.py:26
  213.7 1.8 collective-permute-done.25
  217.2 1.6 maximum_convert_fusion
  218.8 1.6 maximum_convert_fusion.1
  223.4 5.0 %collective-permute-done.27 = bf16[224,768]{1,0:T(8,128)(2,1)S(1)} collective-permute-done((bf16[224,768]{1,0:T(8,128)(2,1)S(1)}, bf16[224,768]{1,0:T(8,128)(2,1)S(1)}, u32[]{:S(2)}, u32[]{:S(2)}) %collective-permute-start.27) | collective-permute-done | bytes 344096 | tf_op jit(solution)/shard_map/ppermute | solution.py:26
  232.2 1.5 slice.143
  233.7 1.5 slice.141
  (318 shorter events, 75.8 us)
Async XLA Ops:
  0.7 49.4 %copy-start = (bf16[768,768]{1,0:T(8,128)(2,1)S(1)}, bf16[768,768]{1,0:T(8,128)(2,1)}, u32[]{:S(2)}) copy-start(bf16[768,768]{1,0:T(8,128)(2,1)} %param.42) | copy-start | bytes 3538948
  5.2 31.4 %copy-start.6 = (f32[3,2,128,192]{3,2,1,0:T(8,128)}, f32[3,2,128,192]{3,2,1,0:T(8,128)S(1)}, u32[]{:S(2)}) copy-start(f32[3,2,128,192]{3,2,1,0:T(8,128)S(1)} %fusion) | copy-start | bytes 1769476
  5.3 6.8 %collective-permute-start = (bf16[2,64,192]{2,1,0:T(8,128)(2,1)S(1)}, bf16[2,64,192]{2,1,0:T(8,128)(2,1)S(1)}, u32[]{:S(2)}, u32[]{:S(2)}) collective-permute-start(bf16[2,64,192]{2,1,0:T(8,128)(2,1)S(1)} %slice.154), channel_id=1, source_target_pairs={{0,4},{4,8},{8,12},{12,16},{16,20},{20,24},{24,28},{1,5},{5,9},{9,... | collective-permute-start | bytes 147464 | tf_op jit(solution)/shard_map/ppermute | solution.py:22
  17.1 4.5 %collective-permute-start.1 = (bf16[64,384]{1,0:T(8,128)(2,1)S(1)}, bf16[64,384]{1,0:T(8,128)(2,1)S(1)}, u32[]{:S(2)}, u32[]{:S(2)}) collective-permute-start(bf16[64,384]{1,0:T(8,128)(2,1)S(1)} %convert_element_type.364), channel_id=1, source_target_pairs={{0,4},{4,0},{8,12},{12,8},{16,20},{20,16},{24,28},{28,24},{1,5},{5... | collective-permute-start | bytes 147464 | tf_op jit(solution)/shard_map/ppermute | solution.py:26
  21.7 10.8 %collective-permute-start.4 = (bf16[64,384]{1,0:T(8,128)(2,1)S(1)}, bf16[64,384]{1,0:T(8,128)(2,1)S(1)}, u32[]{:S(2)}, u32[]{:S(2)}) collective-permute-start(bf16[64,384]{1,0:T(8,128)(2,1)S(1)} %fusion.79), channel_id=1, source_target_pairs={{0,24},{4,28},{1,25},{5,29},{2,26},{6,30},{3,27},{7,31}} | collective-permute-start | bytes 147464 | tf_op jit(solution)/shard_map/ppermute | solution.py:22
  28.6 3.9 %collective-permute-start.3 = (bf16[64,384]{1,0:T(8,128)(2,1)S(1)}, bf16[64,384]{1,0:T(8,128)(2,1)S(1)}, u32[]{:S(2)}, u32[]{:S(2)}) collective-permute-start(bf16[64,384]{1,0:T(8,128)(2,1)S(1)} %fusion.79), channel_id=1, source_target_pairs={{0,16},{4,20},{8,24},{12,28},{1,17},{5,21},{9,25},{13,29},{2,18},{... | collective-permute-start | bytes 147464 | tf_op jit(solution)/shard_map/ppermute | solution.py:22
  29.9 4.2 %collective-permute-start.2 = (bf16[64,384]{1,0:T(8,128)(2,1)S(1)}, bf16[64,384]{1,0:T(8,128)(2,1)S(1)}, u32[]{:S(2)}, u32[]{:S(2)}) collective-permute-start(bf16[64,384]{1,0:T(8,128)(2,1)S(1)} %fusion.79), channel_id=1, source_target_pairs={{0,8},{4,12},{8,16},{12,20},{16,24},{20,28},{1,9},{5,13},{9,17},{1... | collective-permute-start | bytes 147464 | tf_op jit(solution)/shard_map/ppermute | solution.py:22
  37.6 1.5 collective-permute-start.5
  39.2 7.1 %collective-permute-start.6 = (bf16[1,128,768]{2,1,0:T(8,128)(2,1)S(1)}, bf16[1,128,768]{2,1,0:T(8,128)(2,1)}, u32[]{:S(2)}, u32[]{:S(2)}) collective-permute-start(bf16[1,128,768]{2,1,0:T(8,128)(2,1)S(1)} %fusion.44), channel_id=1, source_target_pairs={{0,2},{1,3},{2,0},{3,1},{4,6},{5,7},{6,4},{7,5},{8,10},{9,11},{10,... | collective-permute-start | bytes 589832 | tf_op jit(solution)/shard_map/ppermute | solution.py:26
  47.3 1.5 collective-permute-start.7
  54.6 5.5 %collective-permute-start.8 = (bf16[1,128,768]{2,1,0:T(8,128)(2,1)S(1)}, bf16[1,128,768]{2,1,0:T(8,128)(2,1)S(1)}, u32[]{:S(2)}, u32[]{:S(2)}) collective-permute-start(bf16[1,128,768]{2,1,0:T(8,128)(2,1)S(1)} %constant_dynamic-slice_fusion.2), channel_id=1, source_target_pairs={{0,1},{1,0},{2,3},{3,2},{4,5},{5,4},{6,7},{7,6},{8,9},{9,8},{10,11... | collective-permute-start | bytes 589832 | tf_op jit(solution)/shard_map/ppermute | solution.py:26
  54.9 3.6 %collective-permute-start.11 = (bf16[1,128,768]{2,1,0:T(8,128)(2,1)S(1)}, bf16[1,128,768]{2,1,0:T(8,128)(2,1)S(1)}, u32[]{:S(2)}, u32[]{:S(2)}) collective-permute-start(bf16[1,128,768]{2,1,0:T(8,128)(2,1)S(1)} %constant_dynamic-slice_fusion.1), channel_id=1, source_target_pairs={{0,1},{1,0},{2,3},{3,2},{4,5},{5,4},{6,7},{7,6},{8,9},{9,8},{10,11... | collective-permute-start | bytes 589832 | tf_op jit(solution)/shard_map/ppermute | solution.py:26
  55.3 16.0 %collective-permute-start.40 = (bf16[384,768]{1,0:T(8,128)(2,1)S(1)}, bf16[384,768]{1,0:T(8,128)(2,1)S(1)}, u32[]{:S(2)}, u32[]{:S(2)}) collective-permute-start(bf16[384,768]{1,0:T(8,128)(2,1)S(1)} %dynamic-slice_bitcast_fusion), channel_id=1, source_target_pairs={{0,8},{4,12},{8,0},{12,4},{16,24},{20,28},{24,16},{28,20},{1,9},{5... | collective-permute-start | bytes 1769480 | tf_op jit(solution)/shard_map/ppermute | solution.py:26
  57.8 22.8 %collective-permute-start.34 = (bf16[384,768]{1,0:T(8,128)(2,1)S(1)}, bf16[384,768]{1,0:T(8,128)(2,1)S(1)}, u32[]{:S(2)}, u32[]{:S(2)}) collective-permute-start(bf16[384,768]{1,0:T(8,128)(2,1)S(1)} %dynamic-slice_bitcast_fusion.1), channel_id=1, source_target_pairs={{0,4},{4,0},{8,12},{12,8},{16,20},{20,16},{24,28},{28,24},{1,5},{5... | collective-permute-start | bytes 1769480 | tf_op jit(solution)/shard_map/ppermute | solution.py:26
  58.5 7.9 %collective-permute-start.12 = (bf16[1,128,768]{2,1,0:T(8,128)(2,1)S(1)}, bf16[1,128,768]{2,1,0:T(8,128)(2,1)S(1)}, u32[]{:S(2)}, u32[]{:S(2)}) collective-permute-start(bf16[1,128,768]{2,1,0:T(8,128)(2,1)S(1)} %fusion.46), channel_id=1, source_target_pairs={{0,2},{1,3},{2,0},{3,1},{4,6},{5,7},{6,4},{7,5},{8,10},{9,11},{10,... | collective-permute-start | bytes 589832 | tf_op jit(solution)/shard_map/ppermute | solution.py:26
  60.1 9.1 %collective-permute-start.9 = (bf16[1,128,768]{2,1,0:T(8,128)(2,1)S(1)}, bf16[1,128,768]{2,1,0:T(8,128)(2,1)S(1)}, u32[]{:S(2)}, u32[]{:S(2)}) collective-permute-start(bf16[1,128,768]{2,1,0:T(8,128)(2,1)S(1)} %fusion.45), channel_id=1, source_target_pairs={{0,2},{1,3},{2,0},{3,1},{4,6},{5,7},{6,4},{7,5},{8,10},{9,11},{10,... | collective-permute-start | bytes 589832 | tf_op jit(solution)/shard_map/ppermute | solution.py:26
  66.5 2.9 %collective-permute-start.13 = (bf16[1,128,768]{2,1,0:T(8,128)(2,1)S(1)}, bf16[1,128,768]{2,1,0:T(8,128)(2,1)S(1)}, u32[]{:S(2)}, u32[]{:S(2)}) collective-permute-start(bf16[1,128,768]{2,1,0:T(8,128)(2,1)S(1)} %add_convert_fusion.2), channel_id=1, source_target_pairs={{0,1},{1,0},{2,3},{3,2},{4,5},{5,4},{6,7},{7,6},{8,9},{9,8},{10,11... | collective-permute-start | bytes 589832 | tf_op jit(solution)/shard_map/ppermute | solution.py:26
  69.3 4.0 %collective-permute-start.10 = (bf16[1,128,768]{2,1,0:T(8,128)(2,1)S(1)}, bf16[1,128,768]{2,1,0:T(8,128)(2,1)S(1)}, u32[]{:S(2)}, u32[]{:S(2)}) collective-permute-start(bf16[1,128,768]{2,1,0:T(8,128)(2,1)S(1)} %add_convert_fusion.3), channel_id=1, source_target_pairs={{0,1},{1,0},{2,3},{3,2},{4,5},{5,4},{6,7},{7,6},{8,9},{9,8},{10,11... | collective-permute-start | bytes 589832 | tf_op jit(solution)/shard_map/ppermute | solution.py:26
  72.3 49.0 %collective-permute-start.41 = (bf16[192,768]{1,0:T(8,128)(2,1)}, bf16[192,768]{1,0:T(8,128)(2,1)}, u32[]{:S(2)}, u32[]{:S(2)}) collective-permute-start(bf16[192,768]{1,0:T(8,128)(2,1)} %dynamic-slice_bitcast_fusion.4), channel_id=1, source_target_pairs={{0,4},{4,0},{8,12},{12,8},{16,20},{20,16},{24,28},{28,24},{1,5},{5... | collective-permute-start | bytes 884744 | tf_op jit(solution)/shard_map/ppermute | solution.py:26
  78.5 4.2 %collective-permute-start.14 = (bf16[64,384]{1,0:T(8,128)(2,1)S(1)}, bf16[64,384]{1,0:T(8,128)(2,1)S(1)}, u32[]{:S(2)}, u32[]{:S(2)}) collective-permute-start(bf16[64,384]{1,0:T(8,128)(2,1)S(1)} %convert_element_type.397), channel_id=1, source_target_pairs={{0,4},{4,0},{8,12},{12,8},{16,20},{20,16},{24,28},{28,24},{1,5},{5... | collective-permute-start | bytes 147464 | tf_op jit(solution)/shard_map/ppermute | solution.py:26
  82.7 8.7 %collective-permute-start.17 = (bf16[64,384]{1,0:T(8,128)(2,1)S(1)}, bf16[64,384]{1,0:T(8,128)(2,1)S(1)}, u32[]{:S(2)}, u32[]{:S(2)}) collective-permute-start(bf16[64,384]{1,0:T(8,128)(2,1)S(1)} %fusion.83), channel_id=1, source_target_pairs={{24,0},{28,4},{25,1},{29,5},{26,2},{30,6},{27,3},{31,7}} | collective-permute-start | bytes 147464 | tf_op jit(solution)/shard_map/ppermute | solution.py:22
  84.2 8.1 %collective-permute-start.16 = (bf16[64,384]{1,0:T(8,128)(2,1)S(1)}, bf16[64,384]{1,0:T(8,128)(2,1)S(1)}, u32[]{:S(2)}, u32[]{:S(2)}) collective-permute-start(bf16[64,384]{1,0:T(8,128)(2,1)S(1)} %fusion.83), channel_id=1, source_target_pairs={{16,0},{20,4},{24,8},{28,12},{17,1},{21,5},{25,9},{29,13},{18,2},{... | collective-permute-start | bytes 147464 | tf_op jit(solution)/shard_map/ppermute | solution.py:22
  85.5 6.9 %collective-permute-start.15 = (bf16[64,384]{1,0:T(8,128)(2,1)S(1)}, bf16[64,384]{1,0:T(8,128)(2,1)S(1)}, u32[]{:S(2)}, u32[]{:S(2)}) collective-permute-start(bf16[64,384]{1,0:T(8,128)(2,1)S(1)} %fusion.83), channel_id=1, source_target_pairs={{8,0},{12,4},{16,8},{20,12},{24,16},{28,20},{9,1},{13,5},{17,9},{2... | collective-permute-start | bytes 147464 | tf_op jit(solution)/shard_map/ppermute | solution.py:22
  87.6 39.0 %collective-permute-start.35 = (bf16[192,768]{1,0:T(8,128)(2,1)}, bf16[192,768]{1,0:T(8,128)(2,1)}, u32[]{:S(2)}, u32[]{:S(2)}) collective-permute-start(bf16[192,768]{1,0:T(8,128)(2,1)} %dynamic-slice_bitcast_fusion.5), channel_id=1, source_target_pairs={{0,8},{4,12},{8,0},{12,4},{16,24},{20,28},{24,16},{28,20},{1,9},{5... | collective-permute-start | bytes 884744 | tf_op jit(solution)/shard_map/ppermute | solution.py:26
  108.2 7.3 %collective-permute-start.18 = (bf16[2,64,192]{2,1,0:T(8,128)(2,1)}, bf16[2,64,192]{2,1,0:T(8,128)(2,1)}, u32[]{:S(2)}, u32[]{:S(2)}) collective-permute-start(bf16[2,64,192]{2,1,0:T(8,128)(2,1)} %copy.131), channel_id=1, source_target_pairs={{4,0},{8,4},{12,8},{16,12},{20,16},{24,20},{28,24},{5,1},{9,5},{13... | collective-permute-start | bytes 147464 | tf_op jit(solution)/shard_map/ppermute | solution.py:22
  119.8 8.1 %collective-permute-start.19 = (bf16[1,128,768]{2,1,0:T(8,128)(2,1)}, bf16[1,128,768]{2,1,0:T(8,128)(2,1)S(1)}, u32[]{:S(2)}, u32[]{:S(2)}) collective-permute-start(bf16[1,128,768]{2,1,0:T(8,128)(2,1)} %constant_dynamic-slice_fusion), channel_id=1, source_target_pairs={{0,1},{1,0},{2,3},{3,2},{4,5},{5,4},{6,7},{7,6},{8,9},{9,8},{10,11... | collective-permute-start | bytes 589832 | tf_op jit(solution)/shard_map/ppermute | solution.py:26
  122.5 15.2 %collective-permute-start.42 = (bf16[96,768]{1,0:T(8,128)(2,1)S(1)}, bf16[96,768]{1,0:T(8,128)(2,1)S(1)}, u32[]{:S(2)}, u32[]{:S(2)}) collective-permute-start(bf16[96,768]{1,0:T(8,128)(2,1)S(1)} %dynamic-slice_bitcast_fusion.8), channel_id=1, source_target_pairs={{0,16},{4,20},{8,24},{12,28},{16,0},{20,4},{24,8},{28,12},{1,17},{... | collective-permute-start | bytes 442376 | tf_op jit(solution)/shard_map/ppermute | solution.py:26
  127.7 12.9 %collective-permute-start.36 = (bf16[96,768]{1,0:T(8,128)(2,1)S(1)}, bf16[96,768]{1,0:T(8,128)(2,1)S(1)}, u32[]{:S(2)}, u32[]{:S(2)}) collective-permute-start(bf16[96,768]{1,0:T(8,128)(2,1)S(1)} %dynamic-slice_bitcast_fusion.9), channel_id=1, source_target_pairs={{0,16},{4,20},{8,24},{12,28},{16,0},{20,4},{24,8},{28,12},{1,17},{... | collective-permute-start | bytes 442376 | tf_op jit(solution)/shard_map/ppermute | solution.py:26
  127.9 12.9 %collective-permute-start.20 = (bf16[1,128,768]{2,1,0:T(8,128)(2,1)S(1)}, bf16[1,128,768]{2,1,0:T(8,128)(2,1)S(1)}, u32[]{:S(2)}, u32[]{:S(2)}) collective-permute-start(bf16[1,128,768]{2,1,0:T(8,128)(2,1)S(1)} %fusion.47), channel_id=1, source_target_pairs={{0,2},{1,3},{2,0},{3,1},{4,6},{5,7},{6,4},{7,5},{8,10},{9,11},{10,... | collective-permute-start | bytes 589832 | tf_op jit(solution)/shard_map/ppermute | solution.py:26
  137.7 10.8 %collective-permute-start.43 = (bf16[96,768]{1,0:T(8,128)(2,1)S(1)}, bf16[96,768]{1,0:T(8,128)(2,1)S(1)}, u32[]{:S(2)}, u32[]{:S(2)}) collective-permute-start(bf16[96,768]{1,0:T(8,128)(2,1)S(1)} %fusion.52), channel_id=1, source_target_pairs={{0,16},{4,20},{8,24},{12,28},{16,0},{20,4},{24,8},{28,12},{1,17},{... | collective-permute-start | bytes 442376 | tf_op jit(solution)/shard_map/ppermute | solution.py:26
  140.7 12.1 %collective-permute-start.37 = (bf16[96,768]{1,0:T(8,128)(2,1)S(1)}, bf16[96,768]{1,0:T(8,128)(2,1)S(1)}, u32[]{:S(2)}, u32[]{:S(2)}) collective-permute-start(bf16[96,768]{1,0:T(8,128)(2,1)S(1)} %fusion.53), channel_id=1, source_target_pairs={{0,16},{4,20},{8,24},{12,28},{16,0},{20,4},{24,8},{28,12},{1,17},{... | collective-permute-start | bytes 442376 | tf_op jit(solution)/shard_map/ppermute | solution.py:26
  140.9 15.1 %collective-permute-start.21 = (bf16[1,128,768]{2,1,0:T(8,128)(2,1)S(1)}, bf16[1,128,768]{2,1,0:T(8,128)(2,1)S(1)}, u32[]{:S(2)}, u32[]{:S(2)}) collective-permute-start(bf16[1,128,768]{2,1,0:T(8,128)(2,1)S(1)} %add_convert_fusion.1), channel_id=1, source_target_pairs={{0,1},{1,0},{2,3},{3,2},{4,5},{5,4},{6,7},{7,6},{8,9},{9,8},{10,11... | collective-permute-start | bytes 589832 | tf_op jit(solution)/shard_map/ppermute | solution.py:26
  149.2 25.6 %collective-permute-start.44 = (bf16[192,768]{1,0:T(8,128)(2,1)}, bf16[192,768]{1,0:T(8,128)(2,1)}, u32[]{:S(2)}, u32[]{:S(2)}) collective-permute-start(bf16[192,768]{1,0:T(8,128)(2,1)} %pad_maximum_fusion.14), channel_id=1, source_target_pairs={{0,4},{4,0},{8,12},{12,8},{16,20},{20,16},{24,28},{28,24},{1,5},{5... | collective-permute-start | bytes 884744 | tf_op jit(solution)/shard_map/ppermute | solution.py:26
  153.5 22.8 %collective-permute-start.38 = (bf16[192,768]{1,0:T(8,128)(2,1)}, bf16[192,768]{1,0:T(8,128)(2,1)}, u32[]{:S(2)}, u32[]{:S(2)}) collective-permute-start(bf16[192,768]{1,0:T(8,128)(2,1)} %pad_maximum_fusion.13), channel_id=1, source_target_pairs={{0,8},{4,12},{8,0},{12,4},{16,24},{20,28},{24,16},{28,20},{1,9},{5... | collective-permute-start | bytes 884744 | tf_op jit(solution)/shard_map/ppermute | solution.py:26
  171.8 11.1 %collective-permute-start.28 = (bf16[224,768]{1,0:T(8,128)(2,1)S(1)}, bf16[224,768]{1,0:T(8,128)(2,1)S(1)}, u32[]{:S(2)}, u32[]{:S(2)}) collective-permute-start(bf16[224,768]{1,0:T(8,128)(2,1)S(1)} %dynamic-slice_bitcast_fusion.2), channel_id=1, source_target_pairs={{0,4},{4,0},{8,12},{12,8},{16,20},{20,16},{24,28},{28,24},{1,5},{5... | collective-permute-start | bytes 1032200 | tf_op jit(solution)/shard_map/ppermute | solution.py:26
  171.8 11.2 %collective-permute-start.22 = (bf16[224,768]{1,0:T(8,128)(2,1)S(1)}, bf16[224,768]{1,0:T(8,128)(2,1)S(1)}, u32[]{:S(2)}, u32[]{:S(2)}) collective-permute-start(bf16[224,768]{1,0:T(8,128)(2,1)S(1)} %dynamic-slice_bitcast_fusion.3), channel_id=1, source_target_pairs={{0,8},{4,12},{8,0},{12,4},{16,24},{20,28},{24,16},{28,20},{1,9},{5... | collective-permute-start | bytes 1032200 | tf_op jit(solution)/shard_map/ppermute | solution.py:26
  175.9 40.8 %collective-permute-start.45 = (bf16[384,768]{1,0:T(8,128)(2,1)S(1)}, bf16[384,768]{1,0:T(8,128)(2,1)S(1)}, u32[]{:S(2)}, u32[]{:S(2)}) collective-permute-start(bf16[384,768]{1,0:T(8,128)(2,1)S(1)} %pad_maximum_fusion.5), channel_id=1, source_target_pairs={{0,8},{4,12},{8,0},{12,4},{16,24},{20,28},{24,16},{28,20},{1,9},{5... | collective-permute-start | bytes 1769480 | tf_op jit(solution)/shard_map/ppermute | solution.py:26
  177.5 39.5 %collective-permute-start.39 = (bf16[384,768]{1,0:T(8,128)(2,1)S(1)}, bf16[384,768]{1,0:T(8,128)(2,1)S(1)}, u32[]{:S(2)}, u32[]{:S(2)}) collective-permute-start(bf16[384,768]{1,0:T(8,128)(2,1)S(1)} %pad_maximum_fusion.4), channel_id=1, source_target_pairs={{0,4},{4,0},{8,12},{12,8},{16,20},{20,16},{24,28},{28,24},{1,5},{5... | collective-permute-start | bytes 1769480 | tf_op jit(solution)/shard_map/ppermute | solution.py:26
  182.9 14.6 %collective-permute-start.29 = (bf16[112,768]{1,0:T(8,128)(2,1)S(1)}, bf16[112,768]{1,0:T(8,128)(2,1)S(1)}, u32[]{:S(2)}, u32[]{:S(2)}) collective-permute-start(bf16[112,768]{1,0:T(8,128)(2,1)S(1)} %dynamic-slice_bitcast_fusion.6), channel_id=1, source_target_pairs={{0,8},{4,12},{8,0},{12,4},{16,24},{20,28},{24,16},{28,20},{1,9},{5... | collective-permute-start | bytes 516104 | tf_op jit(solution)/shard_map/ppermute | solution.py:26
  183.2 16.7 %collective-permute-start.23 = (bf16[112,768]{1,0:T(8,128)(2,1)S(1)}, bf16[112,768]{1,0:T(8,128)(2,1)S(1)}, u32[]{:S(2)}, u32[]{:S(2)}) collective-permute-start(bf16[112,768]{1,0:T(8,128)(2,1)S(1)} %dynamic-slice_bitcast_fusion.7), channel_id=1, source_target_pairs={{0,4},{4,0},{8,12},{12,8},{16,20},{20,16},{24,28},{28,24},{1,5},{5... | collective-permute-start | bytes 516104 | tf_op jit(solution)/shard_map/ppermute | solution.py:26
  197.6 9.7 %collective-permute-start.30 = (bf16[56,768]{1,0:T(8,128)(2,1)S(1)}, bf16[56,768]{1,0:T(8,128)(2,1)S(1)}, u32[]{:S(2)}, u32[]{:S(2)}) collective-permute-start(bf16[56,768]{1,0:T(8,128)(2,1)S(1)} %dynamic-slice_bitcast_fusion.10), channel_id=1, source_target_pairs={{0,16},{4,20},{8,24},{12,28},{16,0},{20,4},{24,8},{28,12},{1,17},{... | collective-permute-start | bytes 258056 | tf_op jit(solution)/shard_map/ppermute | solution.py:26
  200.0 9.1 %collective-permute-start.24 = (bf16[56,768]{1,0:T(8,128)(2,1)S(1)}, bf16[56,768]{1,0:T(8,128)(2,1)S(1)}, u32[]{:S(2)}, u32[]{:S(2)}) collective-permute-start(bf16[56,768]{1,0:T(8,128)(2,1)S(1)} %dynamic-slice_bitcast_fusion.11), channel_id=1, source_target_pairs={{0,16},{4,20},{8,24},{12,28},{16,0},{20,4},{24,8},{28,12},{1,17},{... | collective-permute-start | bytes 258056 | tf_op jit(solution)/shard_map/ppermute | solution.py:26
  207.3 6.2 %collective-permute-start.31 = (bf16[56,768]{1,0:T(8,128)(2,1)S(1)}, bf16[56,768]{1,0:T(8,128)(2,1)S(1)}, u32[]{:S(2)}, u32[]{:S(2)}) collective-permute-start(bf16[56,768]{1,0:T(8,128)(2,1)S(1)} %fusion.67), channel_id=1, source_target_pairs={{0,16},{4,20},{8,24},{12,28},{16,0},{20,4},{24,8},{28,12},{1,17},{... | collective-permute-start | bytes 258056 | tf_op jit(solution)/shard_map/ppermute | solution.py:26
  209.1 6.4 %collective-permute-start.25 = (bf16[56,768]{1,0:T(8,128)(2,1)S(1)}, bf16[56,768]{1,0:T(8,128)(2,1)S(1)}, u32[]{:S(2)}, u32[]{:S(2)}) collective-permute-start(bf16[56,768]{1,0:T(8,128)(2,1)S(1)} %fusion.68), channel_id=1, source_target_pairs={{0,16},{4,20},{8,24},{12,28},{16,0},{20,4},{24,8},{28,12},{1,17},{... | collective-permute-start | bytes 258056 | tf_op jit(solution)/shard_map/ppermute | solution.py:26
  213.6 7.8 %collective-permute-start.32 = (bf16[112,768]{1,0:T(8,128)(2,1)S(1)}, bf16[112,768]{1,0:T(8,128)(2,1)S(1)}, u32[]{:S(2)}, u32[]{:S(2)}) collective-permute-start(bf16[112,768]{1,0:T(8,128)(2,1)S(1)} %pad_maximum_fusion.21), channel_id=1, source_target_pairs={{0,8},{4,12},{8,0},{12,4},{16,24},{20,28},{24,16},{28,20},{1,9},{5... | collective-permute-start | bytes 516104 | tf_op jit(solution)/shard_map/ppermute | solution.py:26
  215.5 5.5 %collective-permute-start.26 = (bf16[112,768]{1,0:T(8,128)(2,1)S(1)}, bf16[112,768]{1,0:T(8,128)(2,1)S(1)}, u32[]{:S(2)}, u32[]{:S(2)}) collective-permute-start(bf16[112,768]{1,0:T(8,128)(2,1)S(1)} %pad_maximum_fusion.20), channel_id=1, source_target_pairs={{0,4},{4,0},{8,12},{12,8},{16,20},{20,16},{24,28},{28,24},{1,5},{5... | collective-permute-start | bytes 516104 | tf_op jit(solution)/shard_map/ppermute | solution.py:26
  221.1 7.3 %collective-permute-start.27 = (bf16[224,768]{1,0:T(8,128)(2,1)S(1)}, bf16[224,768]{1,0:T(8,128)(2,1)S(1)}, u32[]{:S(2)}, u32[]{:S(2)}) collective-permute-start(bf16[224,768]{1,0:T(8,128)(2,1)S(1)} %pad_maximum_fusion.10), channel_id=1, source_target_pairs={{0,8},{4,12},{8,0},{12,4},{16,24},{20,28},{24,16},{28,20},{1,9},{5... | collective-permute-start | bytes 1032200 | tf_op jit(solution)/shard_map/ppermute | solution.py:26
  222.2 15.7 %collective-permute-start.33 = (bf16[224,768]{1,0:T(8,128)(2,1)}, bf16[224,768]{1,0:T(8,128)(2,1)S(1)}, u32[]{:S(2)}, u32[]{:S(2)}) collective-permute-start(bf16[224,768]{1,0:T(8,128)(2,1)} %pad_maximum_fusion.11), channel_id=1, source_target_pairs={{0,4},{4,0},{8,12},{12,8},{16,20},{20,16},{24,28},{28,24},{1,5},{5... | collective-permute-start | bytes 1032200 | tf_op jit(solution)/shard_map/ppermute | solution.py:26
  (49 other events, 205.9 us)

commit v2 on v0

v2 whole, which is shorter than its diff:
```python
import functools

import jax
import jax.numpy as jnp
from jax import lax
from jax.experimental import pallas as pl
from jax.experimental.pallas import tpu as pltpu
from jax.sharding import PartitionSpec as P

norm_epsilon = 1e-05
f32 = jnp.float32
bf16 = jnp.bfloat16
LANES = 128
FLOPS_PER_US = 0.5e9
SUBS = 8


def shifted(shard, axis, by):
    peers = lax.axis_size(axis)
    return lax.ppermute(shard, axis, [(i, i + by) for i in range(peers) if 0 <= i + by < peers])


def swapped(shard, axis, mask):
    return lax.ppermute(shard, axis, [(i, i ^ mask) for i in range(lax.axis_size(axis))])


class Steps:
    def __init__(self, steps):
        self.steps, self.value, self.ended = steps, None, False
        self.step()

    def step(self):
        try:
            if not self.ended:
                next(self.steps)
        except StopIteration as end:
            self.value, self.ended = end.value, True

    def result(self):
        while not self.ended:
            self.step()
        return self.value


def stepped(work):
    return lambda *args: Steps(work(*args))


@stepped
def halving_steps(call, groups, orders, spot, axis):
    keeps, sends = [g[0] for g in groups], [g[1] for g in groups]
    count = len(orders[0])
    for stage in range(count):
        gots = [swapped(send, axis, order[stage]) for send, order in zip(sends, orders)]
        yield
        operands = [a for pair in zip(keeps, gots) for a in pair]
        if stage + 1 < count:
            after = tuple(order[stage + 1] for order in orders)
            shapes = [like((k.shape[0] // 2, k.shape[1]), bf16) for k in keeps for _ in range(2)]
            parts = call(
                functools.partial(halve_kernel, after), shapes, [spot, *operands], limit=8, scalars=1
            )
            keeps, sends = parts[0::2], parts[1::2]
        else:
            owns = call(add_kernel, [like(k.shape, bf16) for k in keeps], operands, limit=8)
    for stage in range(count - 1, -1, -1):
        gots = [swapped(own, axis, order[stage]) for own, order in zip(owns, orders)]
        operands = [a for pair in zip(owns, gots) for a in pair]
        if stage:
            yield
            shapes = [like((2 * own.shape[0], own.shape[1]), bf16) for own in owns]
            owns = call(
                functools.partial(double_kernel, tuple(order[stage] for order in orders)),
                shapes, [spot, *operands], limit=8, scalars=1,
            )
    return operands


@stepped
def head_steps(call, keep, send, axis="head"):
    got = swapped(send, axis, 1)
    mask = 2
    while True:
        yield
        total, low = call(
            join_kernel, [like(keep.shape), like(keep.shape, bf16)], [keep, got], limit=8
        )
        if mask >= lax.axis_size(axis):
            return low, swapped(low, axis, 1)
        keep, got = total, swapped(low, axis, mask)
        mask *= 2


@stepped
def carry_steps(call, total, low, whole, spot, axis, ahead):
    carry = jnp.zeros_like(total)
    mask = 1
    while True:
        got = swapped(low, axis, mask)
        if 2 * mask >= lax.axis_size(axis):
            return carry, got
        yield
        total, low, carry = call(
            functools.partial(merge_kernel, mask, ahead),
            [like(total.shape), like(total.shape, bf16), like(total.shape)],
            [spot, whole, total, got, carry],
            limit=8,
            scalars=1,
        )
        mask *= 2


@stepped
def sum_steps(call, rows, axis):
    mask = 1
    while mask < lax.axis_size(axis):
        got = swapped(rows, axis, mask)
        yield
        (rows,) = call(plain_add_kernel, [like(rows.shape)], [rows, got], limit=4)
        mask *= 2
    return rows


def lane_tiles(width):
    return [slice(i, i + LANES) for i in range(0, width, LANES)]


def folded(product):
    states, lanes = product.shape
    return jnp.sum(product.reshape(states // SUBS, SUBS, lanes), axis=0)


def rows_at(start, size):
    return pl.ds(pl.multiple_of(start, SUBS), size)


def centred_rows(rows):
    centred = rows - jnp.mean(rows, axis=-1, keepdims=True)
    spread = jnp.mean(centred * centred, axis=-1, keepdims=True)
    return centred, lax.rsqrt(spread + norm_epsilon)


def row(vector_ref):
    return vector_ref[...].reshape(1, vector_ref.shape[0])


def wide(array, slots):
    return jnp.concatenate([array] * slots, axis=-1)


def slot_of(array, slot, width):
    return array[:, slot * width : (slot + 1) * width]


def contract(left, right, left_dim, right_dim):
    return lax.dot_general(
        left, right, (((left_dim,), (right_dim,)), ((), ())), preferred_element_type=f32
    )


def run_scan(series_ref, decay_ref, out_ref, reverse):
    blocks = series_ref.shape[0] // SUBS
    for lanes in lane_tiles(series_ref.shape[1]):
        decay = decay_ref[:, lanes]

        def one(lap, state, lanes=lanes, decay=decay):
            place = blocks - 1 - lap if reverse else lap
            tile = series_ref[rows_at(place * SUBS, SUBS), lanes]
            for r in range(SUBS):
                r = SUBS - 1 - r if reverse else r
                state = decay * state + tile[r : r + 1, :]
            return state

        out_ref[:, lanes] = lax.fori_loop(0, blocks, one, jnp.zeros_like(decay))


def part_total(part_ref, rows):
    total = part_ref[pl.ds(0, rows, stride=SUBS), :]
    for r in range(1, SUBS):
        total = total + part_ref[pl.ds(r, rows, stride=SUBS), :]
    return total


def power_of(whole, exponent, mask):
    power, bit = jnp.ones_like(whole), 1
    while bit < mask:
        power = jnp.where((exponent // bit) % 2 == 1, power * whole, power)
        whole = whole * whole
        bit *= 2
    return power, whole


def merged(mask, ahead, place, whole, got, carry):
    inner = place % mask
    far = (place // mask) % 2
    if ahead:
        inner, far = mask - 1 - inner, 1 - far
    power, step = power_of(whole, inner, mask)
    return jnp.where(far == 1, carry + power * got, carry), far, step


def merge_kernel(mask, ahead, spot_ref, whole_ref, total_ref, got_ref, carry_ref, sum_ref, low_ref, out_ref):
    got = got_ref[...].astype(f32)
    total = total_ref[...]
    out_ref[...], far, step = merged(
        mask, ahead, spot_ref[0], whole_ref[...], got, carry_ref[...]
    )
    total = jnp.where(far == 1, step * got + total, step * total + got)
    sum_ref[...] = total
    low_ref[...] = total.astype(bf16)


def bit_of(spot, mask):
    return (spot[0] // mask) % 2


def halve_kernel(after, spot_ref, *refs):
    ins, outs = refs[: 2 * len(after)], refs[2 * len(after) :]
    for k, mask in enumerate(after):
        total = ins[2 * k][...].astype(f32) + ins[2 * k + 1][...].astype(f32)
        half = total.shape[0] // 2
        put_halves(bit_of(spot_ref, mask), total[:half], total[half:], outs[2 * k], outs[2 * k + 1])


def plain_add_kernel(own_ref, got_ref, out_ref):
    out_ref[...] = own_ref[...] + got_ref[...]


def add_kernel(*refs):
    count = len(refs) // 3
    for k, out_ref in enumerate(refs[2 * count :]):
        total = refs[2 * k][...].astype(f32) + refs[2 * k + 1][...].astype(f32)
        out_ref[...] = total.astype(bf16)


def double_kernel(masks, spot_ref, *refs):
    for k, mask in enumerate(masks):
        out_ref = refs[2 * len(masks) + k]
        half = out_ref.shape[0] // 2
        first, second = halves_of(bit_of(spot_ref, mask), refs[2 * k], refs[2 * k + 1])
        out_ref[0:half, :] = first.astype(bf16)
        out_ref[half:, :] = second.astype(bf16)


def join_kernel(keep_ref, got_ref, total_ref, low_ref):
    total = keep_ref[...].astype(f32) + got_ref[...].astype(f32)
    total_ref[...] = total
    low_ref[...] = total.astype(bf16)


def ordered(bit, own, other):
    return jnp.where(bit == 0, own, other), jnp.where(bit == 0, other, own)


def halves_of(bit, own_ref, other_ref):
    return ordered(bit, own_ref[...].astype(f32), other_ref[...].astype(f32))


def put_halves(bit, first, second, keep_ref, send_ref):
    keep, send = ordered(bit, first, second)
    keep_ref[...] = keep.astype(bf16)
    send_ref[...] = send.astype(bf16)


def project_kernel(
    spot_ref, x_hbm, gain_hbm, bias_hbm, w_hbm, wb_hbm, act_ref, q_ref, k_ref, v_ref,
    x_ref, gain_ref, bias_ref, w_ref, wb_ref, sems,
):
    pairs = ((x_hbm, x_ref), (gain_hbm, gain_ref), (bias_hbm, bias_ref), (w_hbm, w_ref), (wb_hbm, wb_ref))
    copies = [pltpu.make_async_copy(a, b, sems.at[i]) for i, (a, b) in enumerate(pairs)]
    for copy in copies:
        copy.start()
    for copy in copies:
        copy.wait()
    slots, rows, _ = x_ref.shape
    gain, bias = row(gain_ref), row(bias_ref)
    kept = [[], [], []]
    for s in range(slots):
        centred, root = centred_rows(x_ref[s].astype(f32))
        act = (centred * root * gain + bias).astype(bf16)
        act_ref[s * rows : (s + 1) * rows, :] = act
        for j in range(3):
            kept[j].append(contract(act, w_ref[j], 1, 1) + wb_ref[j : j + 1, :])
    q_ref[...] = jnp.concatenate(kept[0], axis=-1)
    k_ref[...] = jnp.concatenate(kept[1], axis=-1).astype(bf16)
    v_ref[...] = jnp.concatenate(kept[2], axis=-1)


def masked_kernel(spot_ref, lengths_ref, cotangent_ref, low_ref, sum_ref):
    slots, rows, model = cotangent_ref.shape
    spot = spot_ref[0] * rows + lax.broadcasted_iota(jnp.int32, (rows, model), 0)
    total = 0.0
    for s in range(slots):
        grads = jnp.where(spot < lengths_ref[s], cotangent_ref[s], 0.0)
        low_ref[s * rows : (s + 1) * rows, :] = grads.astype(bf16)
        total = total + jnp.sum(grads, axis=0, keepdims=True)
    sum_ref[...] = total


def mix_kernel(
    edge_ref, k_ref, v_ref, taps_ref, skip_ref, decay_ref,
    shifted_ref, u_ref, end_ref, low_ref, ext_ref, wide_ref,
):
    taps, width = edge_ref.shape
    rows = k_ref.shape[0]
    slots = width // taps_ref.shape[1]
    ext_ref[0:taps, :] = edge_ref[...].astype(f32)
    ext_ref[taps : taps + rows, :] = k_ref[...].astype(f32)
    wide_ref[0:taps, :] = wide(taps_ref[...], slots)
    wide_ref[taps : taps + 1, :] = wide(row(skip_ref), slots)
    for lanes in lane_tiles(width):
        total = wide_ref[taps : taps + 1, lanes] * ext_ref[taps : taps + rows, lanes]
        for r in range(SUBS):
            if r:
                block = ext_ref[SUBS - r : taps + rows - r, lanes]
            else:
                block = ext_ref[0 : taps + rows - SUBS, lanes]
            for q in range(taps // SUBS):
                i = SUBS * q + (r if r else SUBS)
                start = taps - SUBS - SUBS * q
                total = total + wide_ref[i - 1 : i, lanes] * block[start : start + rows, :]
        shifted_ref[:, lanes] = total
        u_ref[:, lanes] = total * v_ref[:, lanes]
    run_scan(u_ref, decay_ref, end_ref, False)
    low_ref[...] = end_ref[...].astype(bf16)


def attend_kernel(
    mask, spot_ref, u_ref, decay_ref, weight_ref, whole_ref, got_ref, carry_ref, skip_ref,
    q_ref, w_ref, ssm_ref, gated_ref, start_ref, keep_ref, send_ref, part_ref,
):
    rows, width = u_ref.shape
    chans = w_ref.shape[0]
    slots = width // chans
    blocks = rows // SUBS
    skip = wide(row(skip_ref), slots)
    start_ref[...], _, _ = merged(
        mask, False, spot_ref[0], whole_ref[...], got_ref[...].astype(f32), carry_ref[...]
    )
    for lanes in lane_tiles(width):
        decay = decay_ref[:, lanes]
        weight = weight_ref[:, lanes]

        def one(lap, state, lanes=lanes, decay=decay, weight=weight):
            tile = u_ref[rows_at(lap * SUBS, SUBS), lanes]
            for r in range(SUBS):
                state = decay * state + tile[r : r + 1, :]
                part_ref[rows_at(lap * SUBS * SUBS + r * SUBS, SUBS), :] = folded(weight * state)
            return state

        lax.fori_loop(0, blocks, one, start_ref[:, lanes])
        ssm_ref[:, lanes] = part_total(part_ref, rows) + skip[:, lanes] * u_ref[:, lanes]
    mixture = q_ref[...] * ssm_ref[...]
    terms = []
    for s in range(slots):
        gated = slot_of(mixture, s, chans).astype(bf16)
        gated_ref[s * rows : (s + 1) * rows, :] = gated
        terms.append(contract(gated, w_ref[...], 1, 0))
    half = slots // 2
    put_halves(
        spot_ref[1],
        jnp.concatenate(terms[:half], axis=0),
        jnp.concatenate(terms[half:], axis=0),
        keep_ref,
        send_ref,
    )


def gelu_parts(x):
    root = 0.7978845608028654
    square = x * x
    bend = jnp.tanh(root * (x + 0.044715 * (square * x)))
    value = 0.5 * x * (1.0 + bend)
    slope = 0.5 * (1.0 + bend) + 0.5 * x * (1.0 - bend * bend) * root * (1.0 + 0.134145 * square)
    return value, slope


def feed_kernel(
    mask_one, mask_two, spot_ref, own_ref, other_ref, x_ref, b_out_ref, gain_ref, bias_ref, up_ref, up_bias_ref, down_ref,
    gout_ref, mid_ref, keep_ref, send_ref, out_keep_ref, out_send_ref,
    bias_sum_ref, w_up_ref, w_up_send_ref, w_down_ref, w_down_send_ref, act_ref, hidden_ref, grad_ref,
):
    bias_sum = 0.0
    backs, outs = [], []
    rows = own_ref.shape[0]
    for half, attended in enumerate(halves_of(spot_ref[1], own_ref, other_ref)):
        at = slice(half * rows, (half + 1) * rows)
        middle = x_ref[at, :].astype(f32) + attended + row(b_out_ref)
        mid_ref[at, :] = middle
        centred, root = centred_rows(middle)
        act = (centred * root * row(gain_ref) + row(bias_ref)).astype(bf16)
        act_ref[at, :] = act
        value, slope = gelu_parts(contract(act, up_ref[...], 1, 0) + row(up_bias_ref))
        hidden = value.astype(bf16)
        hidden_ref[at, :] = hidden
        grads = (contract(gout_ref[at, :], down_ref[...], 1, 1) * slope).astype(bf16)
        grad_ref[at, :] = grads
        bias_sum = bias_sum + jnp.sum(grads.astype(f32), axis=0, keepdims=True)
        backs.append(contract(grads, up_ref[...], 1, 1))
        outs.append(contract(hidden, down_ref[...], 1, 0))
    bias_sum_ref[...] = bias_sum
    put_halves(spot_ref[1], backs[0], backs[1], keep_ref, send_ref)
    put_halves(spot_ref[1], outs[0], outs[1], out_keep_ref, out_send_ref)
    sums = contract(act_ref[...], grad_ref[...], 0, 0)
    half = sums.shape[0] // 2
    put_halves(bit_of(spot_ref, mask_one), sums[:half], sums[half:], w_up_ref, w_up_send_ref)
    sums = contract(hidden_ref[...], gout_ref[...], 0, 0)
    half = sums.shape[0] // 2
    put_halves(bit_of(spot_ref, mask_two), sums[:half], sums[half:], w_down_ref, w_down_send_ref)


def result_kernel(spot_ref, lengths_ref, own_ref, other_ref, mid_ref, b_down_ref, out_ref):
    slots, rows, model = out_ref.shape
    halves = halves_of(spot_ref[1], own_ref, other_ref)
    per = slots // 2
    spot = spot_ref[0] * rows + lax.broadcasted_iota(jnp.int32, (rows, model), 0)
    for s in range(slots):
        half = halves[s // per]
        feed = half[(s % per) * rows : (s % per + 1) * rows, :] + row(b_down_ref)
        total = mid_ref[s * rows : (s + 1) * rows, :] + feed
        out_ref[s] = jnp.where(spot < lengths_ref[s], total, 0.0)


def norm_grad(grad, hat, root, gain):
    scaled = grad * gain
    inner = jnp.mean(scaled * hat, axis=-1, keepdims=True)
    return root * (scaled - jnp.mean(scaled, axis=-1, keepdims=True) - hat * inner)


def entry_kernel(spot_ref, own_ref, other_ref, x_ref, gain_ref, gmid_ref, out_ref, rows_ref):
    rows = own_ref.shape[0]
    gain_rows = bias_rows = 0.0
    for half, grad in enumerate(halves_of(spot_ref[1], own_ref, other_ref)):
        at = slice(half * rows, (half + 1) * rows)
        centred, root = centred_rows(x_ref[at, :].astype(f32))
        hat = centred * root
        out_ref[at, :] = gmid_ref[at, :] + norm_grad(grad, hat, root, row(gain_ref))
        gain_rows = gain_rows + jnp.sum(grad * hat, axis=0, keepdims=True)
        bias_rows = bias_rows + jnp.sum(grad, axis=0, keepdims=True)
    rows_ref[...] = jnp.concatenate(
        [gain_rows, bias_rows, jnp.zeros((SUBS - 2, gain_rows.shape[1]), f32)], axis=0
    )


def middle_kernel(
    spot_ref, lengths_ref, own_ref, other_ref, mid_ref, cotangent_ref, gain_ref, w_ref, ssm_ref, q_ref, decay_ref,
    gmid_ref, low_ref, gq_ref, gs_ref, front_ref, front_low_ref, rows_ref,
):
    rows, width = ssm_ref.shape
    chans = w_ref.shape[0]
    gain = row(gain_ref)
    gain_rows = bias_rows = mid_rows = 0.0
    kept = []
    half = own_ref.shape[0]
    first, second = halves_of(spot_ref[1], own_ref, other_ref)
    for s in range(width // chans):
        at = slice(s * rows, (s + 1) * rows)
        inside = slice(s * rows % half, s * rows % half + rows)
        grad = (first if s * rows < half else second)[inside, :]
        centred, root = centred_rows(mid_ref[at, :])
        hat = centred * root
        spot = spot_ref[0] * rows + lax.broadcasted_iota(jnp.int32, hat.shape, 0)
        held = jnp.where(spot < lengths_ref[s], cotangent_ref[s], 0.0)
        grad_mid = held + norm_grad(grad, hat, root, gain)
        gmid_ref[at, :] = grad_mid
        low = grad_mid.astype(bf16)
        low_ref[at, :] = low
        gain_rows = gain_rows + jnp.sum(grad * hat, axis=0, keepdims=True)
        bias_rows = bias_rows + jnp.sum(grad, axis=0, keepdims=True)
        mid_rows = mid_rows + jnp.sum(grad_mid, axis=0, keepdims=True)
        kept.append(contract(low, w_ref[...], 1, 1))
    gated = jnp.concatenate(kept, axis=-1)
    gq_ref[...] = (gated * ssm_ref[...]).astype(bf16)
    gs_ref[...] = gated * q_ref[...]
    rows_ref[...] = jnp.zeros_like(rows_ref)
    rows_ref[0:1, :] = gain_rows
    rows_ref[1:2, :] = bias_rows
    rows_ref[2:3, :] = mid_rows
    run_scan(gs_ref, decay_ref, front_ref, True)
    front_low_ref[...] = front_ref[...].astype(bf16)


def local_kernel(
    u_ref, gs_ref, decay_ref, weight_ref, start_ref,
    out_ref, gain_ref, power_ref, reach_ref, part_ref, past_ref,
):
    rows = u_ref.shape[0]
    blocks = rows // SUBS
    states = decay_ref.shape[0]
    for lanes in lane_tiles(u_ref.shape[1]):
        decay = decay_ref[:, lanes]
        weight = weight_ref[:, lanes]

        def rise(lap, carry, lanes=lanes, decay=decay):
            state, reach = carry
            tile = u_ref[rows_at(lap * SUBS, SUBS), lanes]
            for r in range(SUBS):
                past_ref[rows_at(lap * SUBS * states + r * states, states), :] = state
                reach = decay * (reach + state)
                state = decay * state + tile[r : r + 1, :]
            return state, reach

        zero = jnp.zeros_like(decay)
        _, reach = lax.fori_loop(0, blocks, rise, (start_ref[:, lanes], zero))
        reach_ref[:, lanes] = reach

        def fall(lap, carry, lanes=lanes, decay=decay, weight=weight):
            adjoint, gain, power = carry
            place = blocks - 1 - lap
            tile = u_ref[rows_at(place * SUBS, SUBS), lanes]
            grads = gs_ref[rows_at(place * SUBS, SUBS), lanes]
            for r in range(SUBS - 1, -1, -1):
                adjoint = decay * adjoint + grads[r : r + 1, :]
                part_ref[rows_at(place * SUBS * SUBS + r * SUBS, SUBS), :] = folded(weight * adjoint)
                gain = gain + adjoint * tile[r : r + 1, :]
                power = power + adjoint * past_ref[
                    rows_at(place * SUBS * states + r * states, states), :
                ]
            return adjoint, gain, power

        _, gain, power = lax.fori_loop(0, blocks, fall, (zero, zero, zero))
        gain_ref[:, lanes] = gain
        power_ref[:, lanes] = power
        out_ref[:, lanes] = part_total(part_ref, rows)


def unmix_kernel(
    mask, spot_ref, gloc_ref, gs_ref, u_ref, decay_ref, weight_ref, whole_ref, got_ref, carry_ref, gain_ref, power_ref, reach_ref,
    end_ref, v_ref, shifted_ref, edge_ref, k_ref, taps_ref, shift_skip_ref, ssm_skip_ref,
    in_ref, out_ref, root_ref, slope_ref, fall_ref, a_ref, step_ref,
    gk_ref, halo_ref, gv_ref, small_ref, misc_ref,
    part_ref, ext_ref, pad_ref, wide_ref, sums_ref, tap_ref, behind_ref,
):
    rows, width = u_ref.shape
    blocks = rows // SUBS
    taps, chans = taps_ref.shape
    states = decay_ref.shape[0]
    slots = width // chans
    skip = wide(row(ssm_skip_ref), slots)
    behind_ref[...], _, _ = merged(
        mask, True, spot_ref[0], whole_ref[...], got_ref[...].astype(f32), carry_ref[...]
    )
    ext_ref[0:taps, :] = edge_ref[...].astype(f32)
    ext_ref[taps : taps + rows, :] = k_ref[...].astype(f32)
    pad_ref[0:taps, :] = jnp.zeros((taps, width), f32)
    pad_ref[taps + rows : 2 * taps + rows, :] = jnp.zeros((taps, width), f32)
    wide_ref[0:taps, :] = wide(taps_ref[...], slots)
    wide_ref[taps : taps + 1, :] = wide(row(shift_skip_ref), slots)
    for lanes in lane_tiles(width):
        decay = decay_ref[:, lanes]
        weight = weight_ref[:, lanes]

        def one(lap, state, decay=decay, weight=weight):
            place = blocks - 1 - lap
            for r in range(SUBS - 1, -1, -1):
                state = decay * state
                part_ref[rows_at(place * SUBS * SUBS + r * SUBS, SUBS), :] = folded(weight * state)
            return state

        lax.fori_loop(0, blocks, one, behind_ref[:, lanes])
        grad_u = (
            gloc_ref[:, lanes] + part_total(part_ref, rows) + skip[:, lanes] * gs_ref[:, lanes]
        )
        gv_ref[:, lanes] = (grad_u * shifted_ref[:, lanes]).astype(bf16)
        pad_ref[taps : taps + rows, lanes] = grad_u * v_ref[:, lanes]
        total = wide_ref[taps : taps + 1, lanes] * pad_ref[taps : taps + rows, lanes]
        borrowed = jnp.zeros((taps, LANES), f32)
        for r in range(SUBS):
            block = pad_ref[r : 2 * taps + rows - SUBS + r, lanes]
            for q in range(taps // SUBS + 1):
                i = SUBS * q + r
                if i < 1 or i > taps:
                    continue
                tap = wide_ref[i - 1 : i, lanes]
                start = taps + SUBS * q
                if start + rows <= block.shape[0]:
                    total = total + tap * block[start : start + rows, :]
                else:
                    live = block.shape[0] - start
                    total = total + tap * jnp.concatenate(
                        [block[start:, :], jnp.zeros((rows - live, LANES), f32)], axis=0
                    )
                borrowed = borrowed + tap * block[SUBS * q : SUBS * q + taps, :]
        gk_ref[:, lanes] = total
        halo_ref[:, lanes] = borrowed.astype(bf16)
        grad_shifted = pad_ref[taps : taps + rows, lanes]
        for r in range(SUBS):
            block = ext_ref[r : taps + rows - SUBS + r, lanes] if r else ext_ref[:, lanes]
            for q in range(taps // SUBS + 1):
                start = SUBS * q
                i = taps - start - r
                if i < 0:
                    continue
                product = grad_shifted * block[start : start + rows, :]
                sums_ref[SUBS * i : SUBS * (i + 1), :] = folded(product)
        tap_ref[0 : taps + 1, lanes] = part_total(sums_ref, taps + 1)
    gain = gain_ref[...] + behind_ref[...] * decay_ref[...] * end_ref[...]
    power = power_ref[...] + behind_ref[...] * reach_ref[...]

    def slots_total(array):
        total = slot_of(array, 0, chans)
        for s in range(1, slots):
            total = total + slot_of(array, s, chans)
        return total

    gain, power = slots_total(gain), slots_total(power)
    grad_in = out_ref[...] * gain
    grad_rate = grad_in * slope_ref[...] - fall_ref[...] * power
    tap_sums = slots_total(tap_ref[0 : taps + 1, :])
    small_ref[...] = jnp.concatenate(
        [
            tap_sums[1 : taps + 1, :],
            grad_rate * row(step_ref),
            grad_in * root_ref[...],
            in_ref[...] * gain,
        ],
        axis=-1,
    )
    misc_ref[...] = jnp.zeros_like(misc_ref)
    skip_sums = slots_total(jnp.sum(gs_ref[...] * u_ref[...], axis=0, keepdims=True))
    step_sums = jnp.sum(grad_rate * a_ref[...], axis=0, keepdims=True)
    misc_ref[0:1, :] = jnp.concatenate(
        [tap_sums[0:1, :], skip_sums, step_sums, jnp.zeros_like(skip_sums)], axis=-1
    )


def weights_kernel(gq_ref, act_ref, gated_ref, low_ref, out_ref):
    rows, width = gq_ref.shape
    chans = gated_ref.shape[1]
    query = 0.0
    for s in range(width // chans):
        grads = slot_of(gq_ref[...].astype(f32), s, chans).astype(bf16)
        query = query + contract(grads, act_ref[s * rows : (s + 1) * rows, :], 0, 0)
    out_ref[0:chans, :] = query.astype(bf16)
    out_ref[chans : 2 * chans, :] = contract(gated_ref[...], low_ref[...], 0, 0).astype(bf16)


def last_kernel(
    mask_one, mask_two, spot_ref, gq_ref, gk_ref, received_ref, gv_ref, act_ref, w_ref, early_ref, small_ref, misc_ref,
    rows_ref, up_ref, down_ref, keep_ref, send_ref, one_ref, one_send_ref, two_ref,
    two_send_ref, all_ref,
):
    rows, width = gk_ref.shape
    taps = received_ref.shape[0]
    chans = w_ref.shape[1]
    slots = width // chans
    grad_k = jnp.concatenate(
        [
            gk_ref[0 : rows - taps, :],
            gk_ref[rows - taps : rows, :] + received_ref[...].astype(f32),
        ],
        axis=0,
    ).astype(bf16)
    parts = [gq_ref[...].astype(f32), grad_k.astype(f32), gv_ref[...].astype(f32)]
    sums = [0.0, 0.0, 0.0]
    terms, biases = [], []
    for s in range(slots):
        act = act_ref[s * rows : (s + 1) * rows, :]
        term = 0.0
        for j in range(3):
            grads = slot_of(parts[j], s, chans).astype(bf16)
            term = term + contract(grads, w_ref[j], 1, 0)
            if j:
                sums[j] = sums[j] + contract(grads, act, 0, 0)
        terms.append(term)
    half = slots // 2
    put_halves(
        spot_ref[1],
        jnp.concatenate(terms[:half], axis=0),
        jnp.concatenate(terms[half:], axis=0),
        keep_ref,
        send_ref,
    )
    for j in range(3):
        total = jnp.sum(parts[j], axis=0, keepdims=True)
        bias = slot_of(total, 0, chans)
        for s in range(1, slots):
            bias = bias + slot_of(total, s, chans)
        biases.append(bias)
    place = 0

    def put(block):
        nonlocal place
        all_ref[place : place + block.shape[0], :] = block.astype(f32)
        place += block.shape[0]

    put(early_ref[...])
    put(sums[1])
    put(sums[2])
    put(small_ref[...])
    put(
        jnp.concatenate(
            [
                misc_ref[0:1, :],
                jnp.concatenate(biases + [jnp.zeros_like(biases[0])], axis=-1),
                rows_ref[0:3, :],
                up_ref[...],
                down_ref[...],
                jnp.zeros((2 * SUBS - 7, misc_ref.shape[1]), f32),
            ],
            axis=0,
        )
    )
    put(jnp.zeros((all_ref.shape[0] - place, misc_ref.shape[1]), f32))
    count = all_ref.shape[0] // 4
    quarters = [all_ref[k * count : (k + 1) * count, :] for k in range(4)]
    put_halves(bit_of(spot_ref, mask_one), quarters[0], quarters[1], one_ref, one_send_ref)
    put_halves(bit_of(spot_ref, mask_two), quarters[2], quarters[3], two_ref, two_send_ref)


def widen_kernel(mask_one, mask_two, spot_ref, up_ref, up_got_ref, down_ref, down_got_ref, one_ref, two_ref):
    for mask, own_ref, got_ref, out_ref in (
        (mask_one, up_ref, up_got_ref, one_ref),
        (mask_two, down_ref, down_got_ref, two_ref),
    ):
        half = own_ref.shape[0]
        first, second = halves_of(bit_of(spot_ref, mask), own_ref, got_ref)
        out_ref[0:half, :] = first
        out_ref[half:, :] = second


def spread_kernel(
    chans, taps, mask_one, mask_two, spot_ref, one_ref, one_got_ref, two_ref, two_got_ref,
    qkv_ref, bias_ref, tap_ref, shift_skip_ref, a_ref, b_ref, c_ref, ssm_skip_ref, step_ref, out_ref,
    gain_ref, norm_bias_ref, out_bias_ref, up_ref, down_ref, all_ref,
):
    quarter = one_ref.shape[0]
    pieces = halves_of(bit_of(spot_ref, mask_one), one_ref, one_got_ref)
    pieces += halves_of(bit_of(spot_ref, mask_two), two_ref, two_got_ref)
    for place, piece in enumerate(pieces):
        all_ref[place * quarter : (place + 1) * quarter, :] = piece
    for j, place in enumerate((0, 2, 3)):
        qkv_ref[j] = all_ref[place * chans : (place + 1) * chans, :]
    out_ref[...] = all_ref[chans : 2 * chans, :]
    base = 4 * chans
    small = all_ref[base : base + taps, :]
    for slot, ref in enumerate((tap_ref, a_ref, b_ref, c_ref)):
        ref[...] = slot_of(small, slot, chans)
    base = base + taps
    misc = all_ref[base : base + SUBS, :]
    for slot, ref in enumerate((shift_skip_ref, ssm_skip_ref, step_ref)):
        ref[...] = slot_of(misc[0:1, :], slot, chans).reshape(chans)
    bias_ref[...] = jnp.concatenate([slot_of(misc[1:2, :], j, chans) for j in range(3)], axis=0)
    for place, ref in enumerate((gain_ref, norm_bias_ref, out_bias_ref, up_ref, down_ref)):
        ref[...] = misc[2 + place : 3 + place, :].reshape(misc.shape[1])


def ordered_calls():
    held = [jnp.zeros((SUBS, LANES), f32)]

    def call(kernel, outs, args, scratch=(), us=0.5, limit=24, scalars=0, place=pltpu.VMEM):
        inputs = len(args)

        def body(*refs):
            given, rest = refs[:inputs], refs[inputs + 1 :]
            rest[len(outs)][...] = refs[inputs][...]
            kernel(*given, *rest[: len(outs)], *rest[len(outs) + 1 :])

        size = sum(a.size * a.dtype.itemsize for a in list(args) + list(outs))
        specs = [pl.BlockSpec(memory_space=pltpu.SMEM)] * scalars
        specs += [pl.BlockSpec(memory_space=place)] * (inputs - scalars)
        specs += [pl.BlockSpec(memory_space=pltpu.VMEM)]
        results = pl.pallas_call(
            body,
            in_specs=specs,
            out_shape=tuple(outs) + (like((SUBS, LANES)),),
            scratch_shapes=list(scratch),
            compiler_params=pltpu.CompilerParams(vmem_limit_bytes=limit << 20),
            cost_estimate=pl.CostEstimate(
                flops=int(us * FLOPS_PER_US), bytes_accessed=0, transcendentals=0
            ),
        )(*args, held[0])
        held[0] = results[-1]
        return results[:-1]

    return call


def like(shape, dtype=f32):
    return jax.ShapeDtypeStruct(shape, dtype)


def shards(
    inputs,
    cotangent,
    lengths,
    ln1_gain,
    ln1_bias,
    query_key_value_weight,
    b_qkv,
    shift_taps,
    shift_skip,
    ssm_a,
    ssm_b,
    ssm_c,
    ssm_skip,
    ssm_step,
    output_weight,
    b_out,
    ln2_gain,
    ln2_bias,
    up_weight,
    up_bias,
    down_weight,
    b_down,
):
    slots, rows, model = inputs.shape
    taps, chans = shift_taps.shape
    states = ssm_a.shape[1]
    width = slots * chans
    tokens = slots * rows
    spot = jnp.stack([lax.axis_index("seq"), lax.axis_index("head") % 2]).astype(jnp.int32)
    peers = lax.axis_size("seq")
    last_mask = peers // 2
    half_tokens = tokens // 2
    half_like = like((half_tokens, model), bf16)
    projections = jnp.swapaxes(query_key_value_weight, 1, 2)
    flat_inputs = inputs.reshape(tokens, model)
    hidden_count = up_bias.shape[0]
    masks = [2**k for k in range(peers.bit_length() - 1)]
    orders = (masks, masks[1::-1] + masks[2:])
    ends = tuple(order[0] for order in orders)
    call = ordered_calls()

    rate = (ssm_step[:, None] * ssm_a).T
    decay = jnp.exp(-rate)
    gain_root = jnp.sqrt(-jnp.expm1(-2.0 * rate))
    turned_b, turned_c = ssm_b.T, ssm_c.T
    in_weight = gain_root * turned_b
    decay_wide = wide(decay, slots)
    whole_wide = wide(jnp.exp(-rate * rows), slots)
    weight_wide = wide(turned_c * in_weight, slots)
    slope = turned_b * jnp.exp(-2.0 * rate) / gain_root
    fall = decay * turned_c * in_weight

    act_one, queries, keys, values = call(
        project_kernel,
        [like((tokens, model), bf16), like((rows, width)), like((rows, width), bf16), like((rows, width))],
        [spot] + [
            pltpu.with_memory_space_constraint(a, pltpu.HBM)
            for a in (inputs, ln1_gain, ln1_bias, projections, b_qkv)
        ],
        [
            pltpu.VMEM(inputs.shape, inputs.dtype),
            pltpu.VMEM(ln1_gain.shape, f32),
            pltpu.VMEM(ln1_bias.shape, f32),
            pltpu.VMEM(projections.shape, projections.dtype),
            pltpu.VMEM(b_qkv.shape, f32),
            pltpu.SemaphoreType.DMA((5,)),
        ],
        us=2.0,
        scalars=1,
        place=pltpu.HBM,
        limit=24,
    )
    edge = shifted(keys[rows - taps :, :], "seq", 1)
    shifted_keys, series, end_local, end_low = call(
        mix_kernel,
        [like((rows, width)), like((rows, width)), like((states, width)), like((states, width), bf16)],
        [edge, keys, values, shift_taps, shift_skip, decay_wide],
        [pltpu.VMEM((taps + rows, width), f32), pltpu.VMEM((taps + SUBS, width), f32)],
        us=2.9,
    )
    steps = carry_steps(call, end_local, end_low, whole_wide, spot, "seq", False)
    low_out, grad_b_down = call(
        masked_kernel,
        [like((tokens, model), bf16), like((1, model))],
        [spot, lengths, cotangent],
        us=0.8,
        scalars=2,
    )
    carry, got = steps.result()
    ssm_out, gated, start_state, keep, send = call(
        functools.partial(attend_kernel, last_mask),
        [like((rows, width)), like((tokens, chans), bf16), like((states, width)), half_like, half_like],
        [
            spot, series, decay_wide, weight_wide, whole_wide, got, carry, ssm_skip, queries,
            output_weight,
        ],
        [pltpu.VMEM((rows * SUBS, LANES), f32)],
        us=2.9,
        scalars=1,
    )
    own, other = head_steps(call, keep, send).result()
    middle, keep, send, out_keep, out_send, grad_b_up, up_keep, up_send, down_keep, down_send = call(
        functools.partial(feed_kernel, *ends),
        [
            like((tokens, model)),
            half_like,
            half_like,
            half_like,
            half_like,
            like((1, hidden_count)),
            like((model // 2, hidden_count), bf16),
            like((model // 2, hidden_count), bf16),
            like((hidden_count // 2, model), bf16),
            like((hidden_count // 2, model), bf16),
        ],
        [
            spot, own, other, flat_inputs, b_out, ln2_gain, ln2_bias, up_weight, up_bias, down_weight,
            low_out,
        ],
        [
            pltpu.VMEM((tokens, model), bf16),
            pltpu.VMEM((tokens, hidden_count), bf16),
            pltpu.VMEM((tokens, hidden_count), bf16),
        ],
        us=5.0,
        scalars=1,
        limit=32,
    )
    feed_sums = halving_steps(
        call, [(up_keep, up_send), (down_keep, down_send)], orders, spot, "seq"
    )
    steps = head_steps(call, keep, send)
    own, other = steps.result()
    grad_middle, low_middle, grad_queries, grad_ssm, front_local, front_low, norm_rows = call(
        middle_kernel,
        [
            like((tokens, model)),
            like((tokens, model), bf16),
            like((rows, width), bf16),
            like((rows, width)),
            like((states, width)),
            like((states, width), bf16),
            like((SUBS, model)),
        ],
        [
            spot, lengths, own, other, middle, cotangent, ln2_gain, output_weight, ssm_out, queries,
            decay_wide,
        ],
        us=2.5,
        scalars=2,
    )
    steps = carry_steps(call, front_local, front_low, whole_wide, spot, "seq", True)
    (early,) = call(
        weights_kernel,
        [like((2 * chans, model), bf16)],
        [grad_queries, act_one, gated, low_middle],
        us=0.5,
    )
    feed_sums.step()
    steps.step()
    carry, got = steps.result()
    grad_local, gain_local, power_local, reach = call(
        local_kernel,
        [like((rows, width)), like((states, width)), like((states, width)), like((states, width))],
        [series, grad_ssm, decay_wide, weight_wide, start_state],
        [pltpu.VMEM((rows * SUBS, LANES), f32), pltpu.VMEM((rows * states, LANES), f32)],
        us=5.8,
    )
    feed_sums.step()
    grad_keys, halo, grad_values, small, misc = call(
        functools.partial(unmix_kernel, last_mask),
        [
            like((rows, width)),
            like((taps, width), bf16),
            like((rows, width), bf16),
            like((states, 4 * chans)),
            like((SUBS, 4 * chans)),
        ],
        [
            spot, grad_local, grad_ssm, series, decay_wide, weight_wide, whole_wide, got, carry,
            gain_local, power_local, reach, end_local, values, shifted_keys, edge, keys, shift_taps,
            shift_skip, ssm_skip, in_weight, turned_c, gain_root, slope, fall, ssm_a.T, ssm_step,
        ],
        [
            pltpu.VMEM((rows * SUBS, LANES), f32),
            pltpu.VMEM((taps + rows, width), f32),
            pltpu.VMEM((2 * taps + rows, width), f32),
            pltpu.VMEM((taps + SUBS, width), f32),
            pltpu.VMEM(((taps + 1) * SUBS, LANES), f32),
            pltpu.VMEM((taps + SUBS, width), f32),
            pltpu.VMEM((states, width), f32),
        ],
        us=6.0,
        scalars=1,
    )
    received = shifted(halo, "seq", -1)
    feed_sums.step()
    unit = 2 * peers * SUBS
    last_rows = -(-(4 * chans + states + 2 * SUBS) // unit) * unit
    quarter = like((last_rows // 4, model), bf16)
    keep, send, one, one_send, two, two_send = call(
        functools.partial(last_kernel, *ends),
        [half_like, half_like, quarter, quarter, quarter, quarter],
        [
            spot, grad_queries, grad_keys, received, grad_values, act_one, projections, early, small,
            misc, norm_rows, grad_b_up, grad_b_down,
        ],
        [pltpu.VMEM((last_rows, model), f32)],
        us=1.5,
        scalars=1,
    )
    back = head_steps(call, keep, send)
    last_sums = halving_steps(call, [(one, one_send), (two, two_send)], orders, spot, "seq")
    back.step()
    feed_sums.step()
    own, other = back.result()
    last_sums.step()
    grad_inputs, ln1_rows = call(
        entry_kernel,
        [like((tokens, model)), like((SUBS, model))],
        [spot, own, other, flat_inputs, ln1_gain, grad_middle],
        scalars=1,
        us=2.0,
    )
    ln1 = sum_steps(call, ln1_rows, "seq")
    feed_joined = feed_sums.result()
    last_sums.step()
    feed = head_steps(call, out_keep, out_send)
    ln1.step()
    last_sums.step()
    feed.step()
    ln1.step()
    last_sums.step()
    sum_up, sum_down = call(
        functools.partial(widen_kernel, *ends),
        [like((model, hidden_count)), like((hidden_count, model))],
        [spot, *feed_joined],
        scalars=1,
        us=2.5,
    )
    own, other = feed.result()
    last_sums.step()
    (layer_out,) = call(
        result_kernel,
        [like(inputs.shape)],
        [spot, lengths, own, other, middle, b_down],
        scalars=2,
        us=1.5,
    )
    ln1_rows = ln1.result()
    joined = last_sums.result()
    spread = call(
        functools.partial(spread_kernel, chans, taps, *ends),
        [
            like((3, chans, model)),
            like((3, chans)),
            like((taps, chans)),
            like((chans,)),
            like((states, chans)),
            like((states, chans)),
            like((states, chans)),
            like((chans,)),
            like((chans,)),
            like((chans, model)),
            like((model,)),
            like((model,)),
            like((model,)),
            like(up_bias.shape),
            like((model,)),
        ],
        [spot, *joined],
        [pltpu.VMEM((last_rows, model), f32)],
        scalars=1,
        us=2.0,
    )
    (
        sum_qkv, sum_b_qkv, sum_taps, sum_shift_skip, sum_a, sum_b, sum_c, sum_ssm_skip, sum_step,
        sum_out, sum_ln2_gain, sum_ln2_bias, sum_b_out, sum_b_up, sum_b_down,
    ) = spread
    return (
        layer_out,
        grad_inputs.reshape(inputs.shape),
        ln1_rows[0],
        ln1_rows[1],
        jnp.swapaxes(sum_qkv, 1, 2),
        sum_b_qkv,
        sum_taps,
        sum_shift_skip,
        sum_a.T,
        sum_b.T,
        sum_c.T,
        sum_ssm_skip,
        sum_step,
        sum_out,
        sum_b_out,
        sum_ln2_gain,
        sum_ln2_bias,
        sum_up,
        sum_b_up,
        sum_down,
        sum_b_down,
    )


def solution(mesh):
    in_specs = (
        P(None, "seq", None),
        P(None, "seq", None),
        P(),
        P(),
        P(),
        P(None, None, "head"),
        P(None, "head"),
        P(None, "head"),
        P("head"),
        P("head", None),
        P("head", None),
        P("head", None),
        P("head"),
        P("head"),
        P("head", None),
        P(),
        P(),
        P(),
        P(None, "head"),
        P("head"),
        P("head", None),
        P(),
    )
    out_specs = (
        P(None, "seq", None),
        P(None, "seq", None),
        P(),
        P(),
        P(None, None, "head"),
        P(None, "head"),
        P(None, "head"),
        P("head"),
        P("head", None),
        P("head", None),
        P("head", None),
        P("head"),
        P("head"),
        P("head", None),
        P(),
        P(),
        P(),
        P(None, "head"),
        P("head"),
        P("head", None),
        P(),
    )
    return jax.shard_map(shards, mesh=mesh, in_specs=in_specs, out_specs=out_specs, check_vma=False)
```

time: 843 us -> 188 us (0.22)
  waiting for transfers between devices: 403 us -> 79.4 us
  matrix products: 234 us -> 0 us
  blocking collectives: 95.5 us -> 0 us
  Pallas kernels: 0 us -> 51.7 us
  starting transfers between devices: 7.31 us -> 54.7 us
  local copies, waits for them, and re-layouts: 42.7 us -> 0.74 us
  other arithmetic: 38.1 us -> 0.45 us
  between operations: 14.9 us -> 1.38 us
    psum x5 -> x0, waiting for transfers between devices: 403 us -> none  [the longest x2 312 us: shards(): lax.psum((grad_ln1_gain, grad_ln1_bias, grad_w_qkv, grad_b_qkv, grad_shif...]
    dot_general x25 -> x0, matrix products: 222 us -> none  [the longest x3 68.6 us: ssm_local(): jnp.einsum('icn,jcn->ijc', rising * (ssm_c * input_gain)[None], growing,...]
    all_gather x3 -> x0, blocking collectives: 95.5 us -> none  [the longest x2 62.2 us: prefix(): lax.all_gather(a.astype(kind), axis)]
    ppermute x2 -> x47, waiting for transfers between devices: 0.01 us -> 79.4 us  [the longest x45 76.4 us: swapped(): lax.ppermute(shard, axis, [(i, i ^ mask) for i in range(lax.axis_size(axi...]
    pallas_call x0 -> x39, Pallas kernels: none -> 51.7 us  [call(): pl.pallas_call(body, in_specs=specs, out_shape=tuple(outs) + (like((SUBS,...]
    ppermute x2 -> x47, starting transfers between devices: 6.92 us -> 54.7 us  [the longest x45 48.5 us: swapped(): lax.ppermute(shard, axis, [(i, i ^ mask) for i in range(lax.axis_size(axi...]
    unnamed x160 -> x40, local copies, waits for them, and re-layouts: 32.8 us -> 0.11 us
    reduce_sum x13 -> x0, other arithmetic: 19.3 us -> none  [the longest x4 8.11 us: layer_norm(): return centred * lax.rsqrt(spread + norm_epsilon) * norm_gain + norm_bias]
  transfers between devices with their start and end apart: 7 -> 47, of which waited for: 5 -> 30; matrix products, arithmetic and copies ran while one was open for 9% -> 1% of each run, Pallas kernels for 0% -> 17%
where the time goes in v2:
time: 188 us
  waiting for transfers between devices  79.4 us (42%)
  starting transfers between devices  54.7 us (29%)
  Pallas kernels  51.7 us (28%)
    ppermute x45, waiting for transfers between devices, swapped(): lax.ppermute(shard, axis, [(i, i ^ mask) for i in range(lax.axis_size(axi...  76.4 us
    pallas_call x39, Pallas kernels, call(): pl.pallas_call(body, in_specs=specs, out_shape=tuple(outs) + (like((SUBS,...  51.7 us
    ppermute x45, starting transfers between devices, swapped(): lax.ppermute(shard, axis, [(i, i ^ mask) for i in range(lax.axis_size(axi...  48.5 us
    ppermute x2, starting transfers between devices, shifted(): lax.ppermute(shard, axis, [(i, i + by) for i in range(peers) if 0 <= i +...  6.17 us
  transfers between devices with their start and end apart: 47, of which 30 were waited for; matrix products, arithmetic and copies ran while one was open for 1% of the time, Pallas kernels for 17%

profile of v2, /device:TPU:0, one launch (start us, length us, event | category | flops | bytes accessed | tf_op | source)
XLA Modules:
  0.0 188.3 jit_solution(11528425752415489107)
XLA Ops:
  0.8 2.9 %shard_map.373 = (bf16[256,768]{1,0:T(8,128)(2,1)S(1)}, f32[128,384]{1,0:T(8,128)S(1)}, bf16[128,384]{1,0:T(8,128)(2,1)S(1)}, f32[128,384]{1,0:T(8,128)S(1)}, f32[8,128]{1,0:T(8,128)S(1)}) custom-call(s32[2]{0:T(128)S(1)} %pad_add_fusion.refs_0_, bf16[2,128,768]{2,1,0:T(8,128)(2,1)} %refs_1_.4, f32[768]{0:T(1024)} %refs_4_.5, f32[768]{0:T(1024)} %refs_3_.2, ...), custom_call_target="tpu_custom_call" | custom-call | flops 1000000000 | tf_op jit(solution)/shard_map/pallas_call | solution.py:763
  3.7 4.9 %collective-permute-start = (bf16[64,384]{1,0:T(8,128)(2,1)S(1)}, bf16[64,384]{1,0:T(8,128)(2,1)S(1)}, u32[]{:S(2)}, u32[]{:S(2)}) collective-permute-start(bf16[64,384]{1,0:T(8,128)(2,1)S(1)} %slice.9), channel_id=1, source_target_pairs={{0,4},{4,8},{8,12},{12,16},{16,20},{20,24},{24,28},{1,5},{5,9},{9,... | collective-permute-start | bytes 147464 | tf_op jit(solution)/shard_map/ppermute | solution.py:20
  8.9 1.5 collective-permute-done.refs_0_.refs_15_
  10.3 2.8 %shard_map.374 = (f32[128,384]{1,0:T(8,128)S(1)}, f32[128,384]{1,0:T(8,128)S(1)}, f32[64,384]{1,0:T(8,128)S(1)}, bf16[64,384]{1,0:T(8,128)(2,1)S(1)}, f32[8,128]{1,0:T(8,128)S(1)}) custom-call(bf16[64,384]{1,0:T(8,128)(2,1)S(1)} %collective-permute-done.refs_0_.refs_15_, bf16[128,384]{1,0:T(8,128)(2,1)S(1)} %get-tuple-element.180.refs_1_.refs_16_, ...), custom_call_target="tpu_custom_call" | custom-call | flops 1450000000 | tf_op jit(solution)/shard_map/pallas_call | solution.py:763
  13.2 2.4 %collective-permute-start.1 = (bf16[64,384]{1,0:T(8,128)(2,1)S(1)}, bf16[64,384]{1,0:T(8,128)(2,1)S(1)}, u32[]{:S(2)}, u32[]{:S(2)}) collective-permute-start(bf16[64,384]{1,0:T(8,128)(2,1)S(1)} %get-tuple-element.185), channel_id=1, source_target_pairs={{0,4},{4,0},{8,12},{12,8},{16,20},{20,16},{24,28},{28,24},{1,5},{5... | collective-permute-start | bytes 147464 | tf_op jit(solution)/shard_map/ppermute | solution.py:24
  18.2 3.0 %collective-permute-start.2 = (bf16[64,384]{1,0:T(8,128)(2,1)S(1)}, bf16[64,384]{1,0:T(8,128)(2,1)S(1)}, u32[]{:S(2)}, u32[]{:S(2)}) collective-permute-start(bf16[64,384]{1,0:T(8,128)(2,1)S(1)} %get-tuple-element.189), channel_id=1, source_target_pairs={{0,8},{4,12},{8,0},{12,4},{16,24},{20,28},{24,16},{28,20},{1,9},{5... | collective-permute-start | bytes 147464 | tf_op jit(solution)/shard_map/ppermute | solution.py:24
  21.3 2.1 %collective-permute-done.2.refs_3_ = bf16[64,384]{1,0:T(8,128)(2,1)S(1)} collective-permute-done((bf16[64,384]{1,0:T(8,128)(2,1)S(1)}, bf16[64,384]{1,0:T(8,128)(2,1)S(1)}, u32[]{:S(2)}, u32[]{:S(2)}) %collective-permute-start.2) | collective-permute-done | bytes 49184 | tf_op jit(solution)/shard_map/ppermute | solution.py:24
  24.6 3.0 %collective-permute-start.3 = (bf16[64,384]{1,0:T(8,128)(2,1)S(1)}, bf16[64,384]{1,0:T(8,128)(2,1)S(1)}, u32[]{:S(2)}, u32[]{:S(2)}) collective-permute-start(bf16[64,384]{1,0:T(8,128)(2,1)S(1)} %get-tuple-element.192), channel_id=1, source_target_pairs={{0,16},{4,20},{8,24},{12,28},{16,0},{20,4},{24,8},{28,12},{1,17},{... | collective-permute-start | bytes 147464 | tf_op jit(solution)/shard_map/ppermute | solution.py:24
  27.7 2.0 %collective-permute-done.3.refs_5_ = bf16[64,384]{1,0:T(8,128)(2,1)S(1)} collective-permute-done((bf16[64,384]{1,0:T(8,128)(2,1)S(1)}, bf16[64,384]{1,0:T(8,128)(2,1)S(1)}, u32[]{:S(2)}, u32[]{:S(2)}) %collective-permute-start.3) | collective-permute-done | bytes 49184 | tf_op jit(solution)/shard_map/ppermute | solution.py:24
  29.7 3.0 %shard_map.378 = (f32[128,384]{1,0:T(8,128)S(1)}, bf16[256,192]{1,0:T(8,128)(2,1)S(1)}, f32[64,384]{1,0:T(8,128)S(1)}, bf16[128,768]{1,0:T(8,128)(2,1)S(1)}, bf1...) custom-call(s32[2]{0:T(128)S(1)} %pad_add_fusion.refs_0_, f32[128,384]{1,0:T(8,128)S(1)} %get-tuple-element.183.refs_1_.refs_0_.refs_3_, ...), custom_call_target="tpu_custom_call" | custom-call | flops 1450000000 | tf_op jit(solution)/shard_map/pallas_call | solution.py:763
  34.4 1.6 collective-permute-start.5
  35.9 5.5 %collective-permute-done.5.refs_1_ = bf16[128,768]{1,0:T(8,128)(2,1)S(1)} collective-permute-done((bf16[128,768]{1,0:T(8,128)(2,1)S(1)}, bf16[128,768]{1,0:T(8,128)(2,1)S(1)}, u32[]{:S(2)}, u32[]{:S(2)}) %collective-permute-start.5) | collective-permute-done | bytes 196640 | tf_op jit(solution)/shard_map/ppermute | solution.py:24
  42.2 1.4 collective-permute-done.6.refs_2_
  43.7 3.7 %shard_map.381 = (f32[256,768]{1,0:T(8,128)S(1)}, bf16[128,768]{1,0:T(8,128)(2,1)S(1)}, bf16[128,768]{1,0:T(8,128)(2,1)S(1)}, bf16[128,768]{1,0:T(8,128)(2,1)S(1...) custom-call(s32[2]{0:T(128)S(1)} %pad_add_fusion.refs_0_, ...), custom_call_target="tpu_custom_call" | custom-call | flops 2500000000 | tf_op jit(solution)/shard_map/pallas_call | solution.py:763
  48.5 1.6 collective-permute-start.13
  50.1 1.6 collective-permute-start.9
  51.7 5.1 %collective-permute-done.9.refs_1_ = bf16[128,768]{1,0:T(8,128)(2,1)S(1)} collective-permute-done((bf16[128,768]{1,0:T(8,128)(2,1)S(1)}, bf16[128,768]{1,0:T(8,128)(2,1)S(1)}, u32[]{:S(2)}, u32[]{:S(2)}) %collective-permute-start.9) | collective-permute-done | bytes 196640 | tf_op jit(solution)/shard_map/ppermute | solution.py:24
  57.6 1.4 collective-permute-done.10.refs_3_
  59.1 2.5 %shard_map.384 = (f32[256,768]{1,0:T(8,128)S(1)}, bf16[256,768]{1,0:T(8,128)(2,1)S(1)}, bf16[128,384]{1,0:T(8,128)(2,1)S(1)}, f32[128,384]{1,0:T(8,128)S(1)}, f3...) custom-call(s32[2]{0:T(128)S(1)} %pad_add_fusion.refs_0_, ...), custom_call_target="tpu_custom_call" | custom-call | flops 1250000000 | tf_op jit(solution)/shard_map/pallas_call | solution.py:763
  61.6 1.5 collective-permute-start.11
  72.2 3.0 %collective-permute-start.15 = (bf16[64,384]{1,0:T(8,128)(2,1)S(1)}, bf16[64,384]{1,0:T(8,128)(2,1)S(1)}, u32[]{:S(2)}, u32[]{:S(2)}) collective-permute-start(bf16[64,384]{1,0:T(8,128)(2,1)S(1)} %get-tuple-element.238), channel_id=1, source_target_pairs={{0,16},{4,20},{8,24},{12,28},{16,0},{20,4},{24,8},{28,12},{1,17},{... | collective-permute-start | bytes 147464 | tf_op jit(solution)/shard_map/ppermute | solution.py:24
  75.2 5.8 %shard_map.389 = (f32[128,384]{1,0:T(8,128)S(1)}, f32[64,384]{1,0:T(8,128)S(1)}, f32[64,384]{1,0:T(8,128)S(1)}, f32[64,384]{1,0:T(8,128)S(1)}, f32[8,128]{1,0:T(8,128)S(1)}) custom-call(f32[128,384]{1,0:T(8,128)S(1)} %get-tuple-element.183.refs_1_.refs_0_.refs_3_, f32[128,384]{1,0:T(8,128)S(1)} %get-tuple-element.218.refs_1_.refs_2_, ...), custom_call_target="tpu_custom_call" | custom-call | flops 2900000000 | tf_op jit(solution)/shard_map/pallas_call | solution.py:763
  81.8 2.9 %collective-permute-start.20 = (bf16[96,768]{1,0:T(8,128)(2,1)S(1)}, bf16[96,768]{1,0:T(8,128)(2,1)S(1)}, u32[]{:S(2)}, u32[]{:S(2)}) collective-permute-start(bf16[96,768]{1,0:T(8,128)(2,1)S(1)} %get-tuple-element.262), channel_id=1, source_target_pairs={{0,16},{4,20},{8,24},{12,28},{16,0},{20,4},{24,8},{28,12},{1,17},{... | collective-permute-start | bytes 442376 | tf_op jit(solution)/shard_map/ppermute | solution.py:24
  84.7 6.3 %shard_map.391 = (f32[128,384]{1,0:T(8,128)S(1)}, bf16[64,384]{1,0:T(8,128)(2,1)S(1)}, bf16[128,384]{1,0:T(8,128)(2,1)S(1)}, f32[64,768]{1,0:T(8,128)S(1)}, f32[8,768]{1,0:T(8,128)S(1)}, /*index=5*/f32[8,128]{1,0:T(8,128)S(1)}) custom-call(s32[2]{0:T(128)S(1)} %pad_add_fusion.refs_0_, f32[128,384]{1,0:T(8,128)S(1)} %get-tuple-element.237.refs_1_, ...), custom_call_target="tpu_custom_call" | custom-call | flops 3000000000 | tf_op jit(solution)/shard_map/pallas_call | solution.py:763
  92.7 2.8 %collective-permute-done.20.refs_3_ = bf16[96,768]{1,0:T(8,128)(2,1)S(1)} collective-permute-done((bf16[96,768]{1,0:T(8,128)(2,1)S(1)}, bf16[96,768]{1,0:T(8,128)(2,1)S(1)}, u32[]{:S(2)}, u32[]{:S(2)}) %collective-permute-start.20) | collective-permute-done | bytes 147488 | tf_op jit(solution)/shard_map/ppermute | solution.py:24
  95.6 1.5 collective-permute-done.18.refs_3_
  97.0 1.5 shard_map.393
  100.1 1.6 collective-permute-start.24
  102.2 2.4 %collective-permute-start.26 = (bf16[96,768]{1,0:T(8,128)(2,1)S(1)}, bf16[96,768]{1,0:T(8,128)(2,1)S(1)}, u32[]{:S(2)}, u32[]{:S(2)}) collective-permute-start(bf16[96,768]{1,0:T(8,128)(2,1)S(1)} %get-tuple-element.275.refs_3_), channel_id=1, source_target_pairs={{0,16},{4,20},{8,24},{12,28},{16,0},{20,4},{24,8},{28,12},{1,17},{... | collective-permute-start | bytes 442376 | tf_op jit(solution)/shard_map/ppermute | solution.py:24
  104.6 2.3 %collective-permute-start.21 = (bf16[224,768]{1,0:T(8,128)(2,1)S(1)}, bf16[224,768]{1,0:T(8,128)(2,1)S(1)}, u32[]{:S(2)}, u32[]{:S(2)}) collective-permute-start(bf16[224,768]{1,0:T(8,128)(2,1)S(1)} %get-tuple-element.266), channel_id=1, source_target_pairs={{0,4},{4,0},{8,12},{12,8},{16,20},{20,16},{24,28},{28,24},{1,5},{5... | collective-permute-start | bytes 1032200 | tf_op jit(solution)/shard_map/ppermute | solution.py:24
  107.4 7.7 %collective-permute-done.25.refs_2_ = bf16[96,768]{1,0:T(8,128)(2,1)S(1)} collective-permute-done((bf16[96,768]{1,0:T(8,128)(2,1)S(1)}, bf16[96,768]{1,0:T(8,128)(2,1)S(1)}, u32[]{:S(2)}, u32[]{:S(2)}) %collective-permute-start.25) | collective-permute-done | bytes 147488 | tf_op jit(solution)/shard_map/ppermute | solution.py:24
  115.1 2.6 %collective-permute-done.26.refs_4_ = bf16[96,768]{1,0:T(8,128)(2,1)S(1)} collective-permute-done((bf16[96,768]{1,0:T(8,128)(2,1)S(1)}, bf16[96,768]{1,0:T(8,128)(2,1)S(1)}, u32[]{:S(2)}, u32[]{:S(2)}) %collective-permute-start.26) | collective-permute-done | bytes 147488 | tf_op jit(solution)/shard_map/ppermute | solution.py:24
  118.5 2.3 %collective-permute-start.30 = (bf16[192,768]{1,0:T(8,128)(2,1)S(1)}, bf16[192,768]{1,0:T(8,128)(2,1)S(1)}, u32[]{:S(2)}, u32[]{:S(2)}) collective-permute-start(bf16[192,768]{1,0:T(8,128)(2,1)S(1)} %get-tuple-element.284.refs_3_), channel_id=1, source_target_pairs={{0,4},{4,0},{8,12},{12,8},{16,20},{20,16},{24,28},{28,24},{1,5},{5... | collective-permute-start | bytes 884744 | tf_op jit(solution)/shard_map/ppermute | solution.py:24
  123.4 2.1 %shard_map.398 = (f32[256,768]{1,0:T(8,128)}, f32[8,768]{1,0:T(8,128)S(1)}, f32[8,128]{1,0:T(8,128)S(1)}) custom-call(s32[2]{0:T(128)S(1)} %pad_add_fusion.refs_0_, bf16[128,768]{1,0:T(8,128)(2,1)S(1)} %get-tuple-element.285.refs_1_, bf16[128,768]{1,0:T(8,128)(2,1)S(1)} %collective-permute-done.31.refs_2_, bf16[256,768]{1,0:T(8,128)(2,1)S(1)} %bitcast.38, ...), custom_call_target="tpu_custom_call" | custom-call | flops 1000000000 | tf_op jit(solution)/shard_map/pallas_call | solution.py:763
  125.6 2.4 %collective-permute-done.29.refs_2_ = bf16[192,768]{1,0:T(8,128)(2,1)S(1)} collective-permute-done((bf16[192,768]{1,0:T(8,128)(2,1)S(1)}, bf16[192,768]{1,0:T(8,128)(2,1)S(1)}, u32[]{:S(2)}, u32[]{:S(2)}) %collective-permute-start.29) | collective-permute-done | bytes 294944 | tf_op jit(solution)/shard_map/ppermute | solution.py:24
  128.9 1.8 collective-permute-start.36
  130.7 1.7 collective-permute-start.37
  133.0 15.4 %collective-permute-done.27.refs_2_ = bf16[112,768]{1,0:T(8,128)(2,1)S(1)} collective-permute-done((bf16[112,768]{1,0:T(8,128)(2,1)S(1)}, bf16[112,768]{1,0:T(8,128)(2,1)S(1)}, u32[]{:S(2)}, u32[]{:S(2)}) %collective-permute-start.27) | collective-permute-done | bytes 172064 | tf_op jit(solution)/shard_map/ppermute | solution.py:24
  149.8 2.5 %collective-permute-done.34.refs_1_ = f32[8,768]{1,0:T(8,128)S(1)} collective-permute-done((f32[8,768]{1,0:T(8,128)S(1)}, f32[8,768]{1,0:T(8,128)S(1)}, u32[]{:S(2)}, u32[]{:S(2)}) %collective-permute-start.34) | collective-permute-done | bytes 24608 | tf_op jit(solution)/shard_map/ppermute | solution.py:24
  152.7 4.0 %collective-permute-done.32.refs_1_ = bf16[56,768]{1,0:T(8,128)(2,1)S(1)} collective-permute-done((bf16[56,768]{1,0:T(8,128)(2,1)S(1)}, bf16[56,768]{1,0:T(8,128)(2,1)S(1)}, u32[]{:S(2)}, u32[]{:S(2)}) %collective-permute-start.32) | collective-permute-done | bytes 86048 | tf_op jit(solution)/shard_map/ppermute | solution.py:24
  156.7 1.8 collective-permute-done.33.refs_3_
  158.7 2.9 %collective-permute-start.39 = (bf16[56,768]{1,0:T(8,128)(2,1)S(1)}, bf16[56,768]{1,0:T(8,128)(2,1)S(1)}, u32[]{:S(2)}, u32[]{:S(2)}) collective-permute-start(bf16[56,768]{1,0:T(8,128)(2,1)S(1)} %get-tuple-element.303.refs_3_), channel_id=1, source_target_pairs={{0,16},{4,20},{8,24},{12,28},{16,0},{20,4},{24,8},{28,12},{1,17},{... | collective-permute-start | bytes 258056 | tf_op jit(solution)/shard_map/ppermute | solution.py:24
  162.2 4.7 %collective-permute-done.40.refs_1_ = f32[8,768]{1,0:T(8,128)S(1)} collective-permute-done((f32[8,768]{1,0:T(8,128)S(1)}, f32[8,768]{1,0:T(8,128)S(1)}, u32[]{:S(2)}, u32[]{:S(2)}) %collective-permute-start.40) | collective-permute-done | bytes 24608 | tf_op jit(solution)/shard_map/ppermute | solution.py:24
  169.0 3.0 %shard_map.406 = (f32[768,768]{1,0:T(8,128)}, f32[768,768]{1,0:T(8,128)}, f32[8,128]{1,0:T(8,128)S(1)}) custom-call(s32[2]{0:T(128)S(1)} %pad_add_fusion.refs_0_, bf16[384,768]{1,0:T(8,128)(2,1)S(1)} %get-tuple-element.300.refs_1_, bf16[384,768]{1,0:T(8,128)(2,1)S(1)} %collective-permute-done.36.refs_2_, bf16[384,768]{1,0:T(8,128)(2,1)S(1)} %get-tuple-element.301.refs_3_, ...), custom_call_target="tpu_custom_call" | custom-call | flops 1250000000 | tf_op jit(solution)/shard_map/pallas_call | solution.py:763
  175.2 1.7 collective-permute-start.46
  177.5 1.6 shard_map.409
  179.2 5.9 %collective-permute-done.44.refs_1_ = f32[8,768]{1,0:T(8,128)S(1)} collective-permute-done((f32[8,768]{1,0:T(8,128)S(1)}, f32[8,768]{1,0:T(8,128)S(1)}, u32[]{:S(2)}, u32[]{:S(2)}) %collective-permute-start.44) | collective-permute-done | bytes 24608 | tf_op jit(solution)/shard_map/ppermute | solution.py:24
  185.8 2.2 %shard_map.411 = (f32[3,192,768]{2,1,0:T(8,128)}, f32[3,192]{1,0:T(4,128)}, f32[64,192]{1,0:T(8,128)}, f32[192]{0:T(256)}, f32[64,192]{1,0:T(8,128)}, /*index=5*...) custom-call(s32[2]{0:T(128)S(1)} %pad_add_fusion.refs_0_, ...), custom_call_target="tpu_custom_call" | custom-call | flops 1000000000 | tf_op jit(solution)/shard_map/pallas_call | solution.py:763
  (136 shorter events, 36.9 us)
Async XLA Ops:
  3.7 6.6 %collective-permute-start = (bf16[64,384]{1,0:T(8,128)(2,1)S(1)}, bf16[64,384]{1,0:T(8,128)(2,1)S(1)}, u32[]{:S(2)}, u32[]{:S(2)}) collective-permute-start(bf16[64,384]{1,0:T(8,128)(2,1)S(1)} %slice.9), channel_id=1, source_target_pairs={{0,4},{4,8},{8,12},{12,16},{16,20},{20,24},{24,28},{1,5},{5,9},{9,... | collective-permute-start | bytes 147464 | tf_op jit(solution)/shard_map/ppermute | solution.py:20
  13.2 4.5 %collective-permute-start.1 = (bf16[64,384]{1,0:T(8,128)(2,1)S(1)}, bf16[64,384]{1,0:T(8,128)(2,1)S(1)}, u32[]{:S(2)}, u32[]{:S(2)}) collective-permute-start(bf16[64,384]{1,0:T(8,128)(2,1)S(1)} %get-tuple-element.185), channel_id=1, source_target_pairs={{0,4},{4,0},{8,12},{12,8},{16,20},{20,16},{24,28},{28,24},{1,5},{5... | collective-permute-start | bytes 147464 | tf_op jit(solution)/shard_map/ppermute | solution.py:24
  18.2 5.1 %collective-permute-start.2 = (bf16[64,384]{1,0:T(8,128)(2,1)S(1)}, bf16[64,384]{1,0:T(8,128)(2,1)S(1)}, u32[]{:S(2)}, u32[]{:S(2)}) collective-permute-start(bf16[64,384]{1,0:T(8,128)(2,1)S(1)} %get-tuple-element.189), channel_id=1, source_target_pairs={{0,8},{4,12},{8,0},{12,4},{16,24},{20,28},{24,16},{28,20},{1,9},{5... | collective-permute-start | bytes 147464 | tf_op jit(solution)/shard_map/ppermute | solution.py:24
  24.6 5.1 %collective-permute-start.3 = (bf16[64,384]{1,0:T(8,128)(2,1)S(1)}, bf16[64,384]{1,0:T(8,128)(2,1)S(1)}, u32[]{:S(2)}, u32[]{:S(2)}) collective-permute-start(bf16[64,384]{1,0:T(8,128)(2,1)S(1)} %get-tuple-element.192), channel_id=1, source_target_pairs={{0,16},{4,20},{8,24},{12,28},{16,0},{20,4},{24,8},{28,12},{1,17},{... | collective-permute-start | bytes 147464 | tf_op jit(solution)/shard_map/ppermute | solution.py:24
  32.8 1.5 collective-permute-start.4
  34.4 7.0 %collective-permute-start.5 = (bf16[128,768]{1,0:T(8,128)(2,1)S(1)}, bf16[128,768]{1,0:T(8,128)(2,1)S(1)}, u32[]{:S(2)}, u32[]{:S(2)}) collective-permute-start(bf16[128,768]{1,0:T(8,128)(2,1)S(1)} %get-tuple-element.200), channel_id=1, source_target_pairs={{0,2},{1,3},{2,0},{3,1},{4,6},{5,7},{6,4},{7,5},{8,10},{9,11},{10,... | collective-permute-start | bytes 589832 | tf_op jit(solution)/shard_map/ppermute | solution.py:24
  42.2 1.4 collective-permute-start.6
  47.3 2.7 %collective-permute-start.8 = (bf16[128,768]{1,0:T(8,128)(2,1)S(1)}, bf16[128,768]{1,0:T(8,128)(2,1)S(1)}, u32[]{:S(2)}, u32[]{:S(2)}) collective-permute-start(bf16[128,768]{1,0:T(8,128)(2,1)S(1)} %get-tuple-element.208), channel_id=1, source_target_pairs={{0,1},{1,0},{2,3},{3,2},{4,5},{5,4},{6,7},{7,6},{8,9},{9,8},{10,11... | collective-permute-start | bytes 589832 | tf_op jit(solution)/shard_map/ppermute | solution.py:24
  47.5 16.0 %collective-permute-start.12 = (bf16[384,768]{1,0:T(8,128)(2,1)S(1)}, bf16[384,768]{1,0:T(8,128)(2,1)S(1)}, u32[]{:S(2)}, u32[]{:S(2)}) collective-permute-start(bf16[384,768]{1,0:T(8,128)(2,1)S(1)} %get-tuple-element.223), channel_id=1, source_target_pairs={{0,4},{4,0},{8,12},{12,8},{16,20},{20,16},{24,28},{28,24},{1,5},{5... | collective-permute-start | bytes 1769480 | tf_op jit(solution)/shard_map/ppermute | solution.py:24
  48.5 15.3 %collective-permute-start.13 = (bf16[384,768]{1,0:T(8,128)(2,1)S(1)}, bf16[384,768]{1,0:T(8,128)(2,1)S(1)}, u32[]{:S(2)}, u32[]{:S(2)}) collective-permute-start(bf16[384,768]{1,0:T(8,128)(2,1)S(1)} %get-tuple-element.225), channel_id=1, source_target_pairs={{0,8},{4,12},{8,0},{12,4},{16,24},{20,28},{24,16},{28,20},{1,9},{5... | collective-permute-start | bytes 1769480 | tf_op jit(solution)/shard_map/ppermute | solution.py:24
  50.1 6.7 %collective-permute-start.9 = (bf16[128,768]{1,0:T(8,128)(2,1)S(1)}, bf16[128,768]{1,0:T(8,128)(2,1)S(1)}, u32[]{:S(2)}, u32[]{:S(2)}) collective-permute-start(bf16[128,768]{1,0:T(8,128)(2,1)S(1)} %get-tuple-element.211), channel_id=1, source_target_pairs={{0,2},{1,3},{2,0},{3,1},{4,6},{5,7},{6,4},{7,5},{8,10},{9,11},{10,... | collective-permute-start | bytes 589832 | tf_op jit(solution)/shard_map/ppermute | solution.py:24
  57.6 1.4 collective-permute-start.10
  61.6 4.2 %collective-permute-start.11 = (bf16[64,384]{1,0:T(8,128)(2,1)S(1)}, bf16[64,384]{1,0:T(8,128)(2,1)S(1)}, u32[]{:S(2)}, u32[]{:S(2)}) collective-permute-start(bf16[64,384]{1,0:T(8,128)(2,1)S(1)} %get-tuple-element.221), channel_id=1, source_target_pairs={{0,4},{4,0},{8,12},{12,8},{16,20},{20,16},{24,28},{28,24},{1,5},{5... | collective-permute-start | bytes 147464 | tf_op jit(solution)/shard_map/ppermute | solution.py:24
  66.3 4.7 %collective-permute-start.14 = (bf16[64,384]{1,0:T(8,128)(2,1)S(1)}, bf16[64,384]{1,0:T(8,128)(2,1)S(1)}, u32[]{:S(2)}, u32[]{:S(2)}) collective-permute-start(bf16[64,384]{1,0:T(8,128)(2,1)S(1)} %get-tuple-element.233), channel_id=1, source_target_pairs={{0,8},{4,12},{8,0},{12,4},{16,24},{20,28},{24,16},{28,20},{1,9},{5... | collective-permute-start | bytes 147464 | tf_op jit(solution)/shard_map/ppermute | solution.py:24
  67.4 13.6 %collective-permute-start.16 = (bf16[192,768]{1,0:T(8,128)(2,1)S(1)}, bf16[192,768]{1,0:T(8,128)(2,1)S(1)}, u32[]{:S(2)}, u32[]{:S(2)}) collective-permute-start(bf16[192,768]{1,0:T(8,128)(2,1)S(1)} %get-tuple-element.245), channel_id=1, source_target_pairs={{0,8},{4,12},{8,0},{12,4},{16,24},{20,28},{24,16},{28,20},{1,9},{5... | collective-permute-start | bytes 884744 | tf_op jit(solution)/shard_map/ppermute | solution.py:24
  68.4 12.6 %collective-permute-start.17 = (bf16[192,768]{1,0:T(8,128)(2,1)S(1)}, bf16[192,768]{1,0:T(8,128)(2,1)S(1)}, u32[]{:S(2)}, u32[]{:S(2)}) collective-permute-start(bf16[192,768]{1,0:T(8,128)(2,1)S(1)} %get-tuple-element.247), channel_id=1, source_target_pairs={{0,4},{4,0},{8,12},{12,8},{16,20},{20,16},{24,28},{28,24},{1,5},{5... | collective-permute-start | bytes 884744 | tf_op jit(solution)/shard_map/ppermute | solution.py:24
  72.2 12.5 %collective-permute-start.15 = (bf16[64,384]{1,0:T(8,128)(2,1)S(1)}, bf16[64,384]{1,0:T(8,128)(2,1)S(1)}, u32[]{:S(2)}, u32[]{:S(2)}) collective-permute-start(bf16[64,384]{1,0:T(8,128)(2,1)S(1)} %get-tuple-element.238), channel_id=1, source_target_pairs={{0,16},{4,20},{8,24},{12,28},{16,0},{20,4},{24,8},{28,12},{1,17},{... | collective-permute-start | bytes 147464 | tf_op jit(solution)/shard_map/ppermute | solution.py:24
  81.8 10.9 %collective-permute-start.19 = (bf16[96,768]{1,0:T(8,128)(2,1)S(1)}, bf16[96,768]{1,0:T(8,128)(2,1)S(1)}, u32[]{:S(2)}, u32[]{:S(2)}) collective-permute-start(bf16[96,768]{1,0:T(8,128)(2,1)S(1)} %get-tuple-element.260), channel_id=1, source_target_pairs={{0,16},{4,20},{8,24},{12,28},{16,0},{20,4},{24,8},{28,12},{1,17},{... | collective-permute-start | bytes 442376 | tf_op jit(solution)/shard_map/ppermute | solution.py:24
  81.8 13.6 %collective-permute-start.20 = (bf16[96,768]{1,0:T(8,128)(2,1)S(1)}, bf16[96,768]{1,0:T(8,128)(2,1)S(1)}, u32[]{:S(2)}, u32[]{:S(2)}) collective-permute-start(bf16[96,768]{1,0:T(8,128)(2,1)S(1)} %get-tuple-element.262), channel_id=1, source_target_pairs={{0,16},{4,20},{8,24},{12,28},{16,0},{20,4},{24,8},{28,12},{1,17},{... | collective-permute-start | bytes 442376 | tf_op jit(solution)/shard_map/ppermute | solution.py:24
  91.0 6.0 %collective-permute-start.18 = (bf16[64,384]{1,0:T(8,128)(2,1)S(1)}, bf16[64,384]{1,0:T(8,128)(2,1)S(1)}, u32[]{:S(2)}, u32[]{:S(2)}) collective-permute-start(bf16[64,384]{1,0:T(8,128)(2,1)S(1)} %get-tuple-element.251), channel_id=1, source_target_pairs={{4,0},{8,4},{12,8},{16,12},{20,16},{24,20},{28,24},{5,1},{9,5},{13... | collective-permute-start | bytes 147464 | tf_op jit(solution)/shard_map/ppermute | solution.py:20
  98.5 1.5 collective-permute-start.23
  100.1 23.3 %copy-start.14 = (f32[768]{0:T(1024)S(1)}, f32[768]{0:T(1024)}, u32[]{:S(2)}) copy-start(f32[768]{0:T(1024)} %refs_4_.5) | copy-start | bytes 9220
  100.1 20.8 %collective-permute-start.24 = (bf16[128,768]{1,0:T(8,128)(2,1)S(1)}, bf16[128,768]{1,0:T(8,128)(2,1)S(1)}, u32[]{:S(2)}, u32[]{:S(2)}) collective-permute-start(bf16[128,768]{1,0:T(8,128)(2,1)S(1)} %get-tuple-element.273), channel_id=1, source_target_pairs={{0,2},{1,3},{2,0},{3,1},{4,6},{5,7},{6,4},{7,5},{8,10},{9,11},{10,... | collective-permute-start | bytes 589832 | tf_op jit(solution)/shard_map/ppermute | solution.py:24
  101.7 13.5 %collective-permute-start.25 = (bf16[96,768]{1,0:T(8,128)(2,1)S(1)}, bf16[96,768]{1,0:T(8,128)(2,1)S(1)}, u32[]{:S(2)}, u32[]{:S(2)}) collective-permute-start(bf16[96,768]{1,0:T(8,128)(2,1)S(1)} %get-tuple-element.274.refs_1_), channel_id=1, source_target_pairs={{0,16},{4,20},{8,24},{12,28},{16,0},{20,4},{24,8},{28,12},{1,17},{... | collective-permute-start | bytes 442376 | tf_op jit(solution)/shard_map/ppermute | solution.py:24
  102.2 15.6 %collective-permute-start.26 = (bf16[96,768]{1,0:T(8,128)(2,1)S(1)}, bf16[96,768]{1,0:T(8,128)(2,1)S(1)}, u32[]{:S(2)}, u32[]{:S(2)}) collective-permute-start(bf16[96,768]{1,0:T(8,128)(2,1)S(1)} %get-tuple-element.275.refs_3_), channel_id=1, source_target_pairs={{0,16},{4,20},{8,24},{12,28},{16,0},{20,4},{24,8},{28,12},{1,17},{... | collective-permute-start | bytes 442376 | tf_op jit(solution)/shard_map/ppermute | solution.py:24
  104.6 17.1 %collective-permute-start.21 = (bf16[224,768]{1,0:T(8,128)(2,1)S(1)}, bf16[224,768]{1,0:T(8,128)(2,1)S(1)}, u32[]{:S(2)}, u32[]{:S(2)}) collective-permute-start(bf16[224,768]{1,0:T(8,128)(2,1)S(1)} %get-tuple-element.266), channel_id=1, source_target_pairs={{0,4},{4,0},{8,12},{12,8},{16,20},{20,16},{24,28},{28,24},{1,5},{5... | collective-permute-start | bytes 1032200 | tf_op jit(solution)/shard_map/ppermute | solution.py:24
  106.9 15.7 %collective-permute-start.22 = (bf16[224,768]{1,0:T(8,128)(2,1)S(1)}, bf16[224,768]{1,0:T(8,128)(2,1)S(1)}, u32[]{:S(2)}, u32[]{:S(2)}) collective-permute-start(bf16[224,768]{1,0:T(8,128)(2,1)S(1)} %get-tuple-element.268), channel_id=1, source_target_pairs={{0,8},{4,12},{8,0},{12,4},{16,24},{20,28},{24,16},{28,20},{1,9},{5... | collective-permute-start | bytes 1032200 | tf_op jit(solution)/shard_map/ppermute | solution.py:24
  118.5 9.5 %collective-permute-start.29 = (bf16[192,768]{1,0:T(8,128)(2,1)S(1)}, bf16[192,768]{1,0:T(8,128)(2,1)S(1)}, u32[]{:S(2)}, u32[]{:S(2)}) collective-permute-start(bf16[192,768]{1,0:T(8,128)(2,1)S(1)} %get-tuple-element.283.refs_1_), channel_id=1, source_target_pairs={{0,8},{4,12},{8,0},{12,4},{16,24},{20,28},{24,16},{28,20},{1,9},{5... | collective-permute-start | bytes 884744 | tf_op jit(solution)/shard_map/ppermute | solution.py:24
  118.5 9.5 %collective-permute-start.30 = (bf16[192,768]{1,0:T(8,128)(2,1)S(1)}, bf16[192,768]{1,0:T(8,128)(2,1)S(1)}, u32[]{:S(2)}, u32[]{:S(2)}) collective-permute-start(bf16[192,768]{1,0:T(8,128)(2,1)S(1)} %get-tuple-element.284.refs_3_), channel_id=1, source_target_pairs={{0,4},{4,0},{8,12},{12,8},{16,20},{20,16},{24,28},{28,24},{1,5},{5... | collective-permute-start | bytes 884744 | tf_op jit(solution)/shard_map/ppermute | solution.py:24
  121.7 1.7 collective-permute-start.31
  128.9 40.1 %collective-permute-start.36 = (bf16[384,768]{1,0:T(8,128)(2,1)S(1)}, bf16[384,768]{1,0:T(8,128)(2,1)S(1)}, u32[]{:S(2)}, u32[]{:S(2)}) collective-permute-start(bf16[384,768]{1,0:T(8,128)(2,1)S(1)} %get-tuple-element.300.refs_1_), channel_id=1, source_target_pairs={{0,4},{4,0},{8,12},{12,8},{16,20},{20,16},{24,28},{28,24},{1,5},{5... | collective-permute-start | bytes 1769480 | tf_op jit(solution)/shard_map/ppermute | solution.py:24
  130.7 38.3 %collective-permute-start.37 = (bf16[384,768]{1,0:T(8,128)(2,1)S(1)}, bf16[384,768]{1,0:T(8,128)(2,1)S(1)}, u32[]{:S(2)}, u32[]{:S(2)}) collective-permute-start(bf16[384,768]{1,0:T(8,128)(2,1)S(1)} %get-tuple-element.301.refs_3_), channel_id=1, source_target_pairs={{0,8},{4,12},{8,0},{12,4},{16,24},{20,28},{24,16},{28,20},{1,9},{5... | collective-permute-start | bytes 1769480 | tf_op jit(solution)/shard_map/ppermute | solution.py:24
  132.4 16.1 %collective-permute-start.27 = (bf16[112,768]{1,0:T(8,128)(2,1)S(1)}, bf16[112,768]{1,0:T(8,128)(2,1)S(1)}, u32[]{:S(2)}, u32[]{:S(2)}) collective-permute-start(bf16[112,768]{1,0:T(8,128)(2,1)S(1)} %get-tuple-element.280), channel_id=1, source_target_pairs={{0,8},{4,12},{8,0},{12,4},{16,24},{20,28},{24,16},{28,20},{1,9},{5... | collective-permute-start | bytes 516104 | tf_op jit(solution)/shard_map/ppermute | solution.py:24
  132.7 16.3 %collective-permute-start.28 = (bf16[112,768]{1,0:T(8,128)(2,1)S(1)}, bf16[112,768]{1,0:T(8,128)(2,1)S(1)}, u32[]{:S(2)}, u32[]{:S(2)}) collective-permute-start(bf16[112,768]{1,0:T(8,128)(2,1)S(1)} %get-tuple-element.282), channel_id=1, source_target_pairs={{0,4},{4,0},{8,12},{12,8},{16,20},{20,16},{24,28},{28,24},{1,5},{5... | collective-permute-start | bytes 516104 | tf_op jit(solution)/shard_map/ppermute | solution.py:24
  133.0 28.6 %collective-permute-start.7 = (bf16[128,768]{1,0:T(8,128)(2,1)S(1)}, bf16[128,768]{1,0:T(8,128)(2,1)S(1)}, u32[]{:S(2)}, u32[]{:S(2)}) collective-permute-start(bf16[128,768]{1,0:T(8,128)(2,1)S(1)} %get-tuple-element.206), channel_id=1, source_target_pairs={{0,1},{1,0},{2,3},{3,2},{4,5},{5,4},{6,7},{7,6},{8,9},{9,8},{10,11... | collective-permute-start | bytes 589832 | tf_op jit(solution)/shard_map/ppermute | solution.py:24
  148.4 3.8 %collective-permute-start.34 = (f32[8,768]{1,0:T(8,128)S(1)}, f32[8,768]{1,0:T(8,128)S(1)}, u32[]{:S(2)}, u32[]{:S(2)}) collective-permute-start(f32[8,768]{1,0:T(8,128)S(1)} %get-tuple-element.294.refs_0_), channel_id=1, source_target_pairs={{0,4},{4,0},{8,12},{12,8},{16,20},{20,16},{24,28},{28,24},{1,5},{5... | collective-permute-start | bytes 73736 | tf_op jit(solution)/shard_map/ppermute | solution.py:24
  149.7 7.0 %collective-permute-start.32 = (bf16[56,768]{1,0:T(8,128)(2,1)S(1)}, bf16[56,768]{1,0:T(8,128)(2,1)S(1)}, u32[]{:S(2)}, u32[]{:S(2)}) collective-permute-start(bf16[56,768]{1,0:T(8,128)(2,1)S(1)} %get-tuple-element.291), channel_id=1, source_target_pairs={{0,16},{4,20},{8,24},{12,28},{16,0},{20,4},{24,8},{28,12},{1,17},{... | collective-permute-start | bytes 258056 | tf_op jit(solution)/shard_map/ppermute | solution.py:24
  152.3 6.3 %collective-permute-start.33 = (bf16[56,768]{1,0:T(8,128)(2,1)S(1)}, bf16[56,768]{1,0:T(8,128)(2,1)S(1)}, u32[]{:S(2)}, u32[]{:S(2)}) collective-permute-start(bf16[56,768]{1,0:T(8,128)(2,1)S(1)} %get-tuple-element.293), channel_id=1, source_target_pairs={{0,16},{4,20},{8,24},{12,28},{16,0},{20,4},{24,8},{28,12},{1,17},{... | collective-permute-start | bytes 258056 | tf_op jit(solution)/shard_map/ppermute | solution.py:24
  158.6 8.8 %collective-permute-start.38 = (bf16[56,768]{1,0:T(8,128)(2,1)S(1)}, bf16[56,768]{1,0:T(8,128)(2,1)S(1)}, u32[]{:S(2)}, u32[]{:S(2)}) collective-permute-start(bf16[56,768]{1,0:T(8,128)(2,1)S(1)} %get-tuple-element.302.refs_1_), channel_id=1, source_target_pairs={{0,16},{4,20},{8,24},{12,28},{16,0},{20,4},{24,8},{28,12},{1,17},{... | collective-permute-start | bytes 258056 | tf_op jit(solution)/shard_map/ppermute | solution.py:24
  158.7 8.8 %collective-permute-start.39 = (bf16[56,768]{1,0:T(8,128)(2,1)S(1)}, bf16[56,768]{1,0:T(8,128)(2,1)S(1)}, u32[]{:S(2)}, u32[]{:S(2)}) collective-permute-start(bf16[56,768]{1,0:T(8,128)(2,1)S(1)} %get-tuple-element.303.refs_3_), channel_id=1, source_target_pairs={{0,16},{4,20},{8,24},{12,28},{16,0},{20,4},{24,8},{28,12},{1,17},{... | collective-permute-start | bytes 258056 | tf_op jit(solution)/shard_map/ppermute | solution.py:24
  161.6 5.3 %collective-permute-start.40 = (f32[8,768]{1,0:T(8,128)S(1)}, f32[8,768]{1,0:T(8,128)S(1)}, u32[]{:S(2)}, u32[]{:S(2)}) collective-permute-start(f32[8,768]{1,0:T(8,128)S(1)} %get-tuple-element.304.refs_0_), channel_id=1, source_target_pairs={{0,8},{4,12},{8,0},{12,4},{16,24},{20,28},{24,16},{28,20},{1,9},{5... | collective-permute-start | bytes 73736 | tf_op jit(solution)/shard_map/ppermute | solution.py:24
  166.9 5.7 %collective-permute-start.35 = (bf16[128,768]{1,0:T(8,128)(2,1)S(1)}, bf16[128,768]{1,0:T(8,128)(2,1)S(1)}, u32[]{:S(2)}, u32[]{:S(2)}) collective-permute-start(bf16[128,768]{1,0:T(8,128)(2,1)S(1)} %get-tuple-element.299), channel_id=1, source_target_pairs={{0,2},{1,3},{2,0},{3,1},{4,6},{5,7},{6,4},{7,5},{8,10},{9,11},{10,... | collective-permute-start | bytes 589832 | tf_op jit(solution)/shard_map/ppermute | solution.py:24
  168.1 5.5 %collective-permute-start.42 = (bf16[112,768]{1,0:T(8,128)(2,1)S(1)}, bf16[112,768]{1,0:T(8,128)(2,1)S(1)}, u32[]{:S(2)}, u32[]{:S(2)}) collective-permute-start(bf16[112,768]{1,0:T(8,128)(2,1)S(1)} %get-tuple-element.310.refs_1_), channel_id=1, source_target_pairs={{0,8},{4,12},{8,0},{12,4},{16,24},{20,28},{24,16},{28,20},{1,9},{5... | collective-permute-start | bytes 516104 | tf_op jit(solution)/shard_map/ppermute | solution.py:24
  168.2 5.5 %collective-permute-start.43 = (bf16[112,768]{1,0:T(8,128)(2,1)S(1)}, bf16[112,768]{1,0:T(8,128)(2,1)S(1)}, u32[]{:S(2)}, u32[]{:S(2)}) collective-permute-start(bf16[112,768]{1,0:T(8,128)(2,1)S(1)} %get-tuple-element.311.refs_3_), channel_id=1, source_target_pairs={{0,4},{4,0},{8,12},{12,8},{16,20},{20,16},{24,28},{28,24},{1,5},{5... | collective-permute-start | bytes 516104 | tf_op jit(solution)/shard_map/ppermute | solution.py:24
  173.4 4.2 %collective-permute-start.41 = (bf16[128,768]{1,0:T(8,128)(2,1)S(1)}, bf16[128,768]{1,0:T(8,128)(2,1)S(1)}, u32[]{:S(2)}, u32[]{:S(2)}) collective-permute-start(bf16[128,768]{1,0:T(8,128)(2,1)S(1)} %get-tuple-element.309.refs_2_), channel_id=1, source_target_pairs={{0,1},{1,0},{2,3},{3,2},{4,5},{5,4},{6,7},{7,6},{8,9},{9,8},{10,11... | collective-permute-start | bytes 589832 | tf_op jit(solution)/shard_map/ppermute | solution.py:24
  174.4 11.3 %collective-permute-start.45 = (bf16[224,768]{1,0:T(8,128)(2,1)S(1)}, bf16[224,768]{1,0:T(8,128)(2,1)S(1)}, u32[]{:S(2)}, u32[]{:S(2)}) collective-permute-start(bf16[224,768]{1,0:T(8,128)(2,1)S(1)} %get-tuple-element.319.refs_1_), channel_id=1, source_target_pairs={{0,4},{4,0},{8,12},{12,8},{16,20},{20,16},{24,28},{28,24},{1,5},{5... | collective-permute-start | bytes 1032200 | tf_op jit(solution)/shard_map/ppermute | solution.py:24
  175.2 10.7 %collective-permute-start.46 = (bf16[224,768]{1,0:T(8,128)(2,1)S(1)}, bf16[224,768]{1,0:T(8,128)(2,1)S(1)}, u32[]{:S(2)}, u32[]{:S(2)}) collective-permute-start(bf16[224,768]{1,0:T(8,128)(2,1)S(1)} %get-tuple-element.320.refs_3_), channel_id=1, source_target_pairs={{0,8},{4,12},{8,0},{12,4},{16,24},{20,28},{24,16},{28,20},{1,9},{5... | collective-permute-start | bytes 1032200 | tf_op jit(solution)/shard_map/ppermute | solution.py:24
  176.9 8.2 %collective-permute-start.44 = (f32[8,768]{1,0:T(8,128)S(1)}, f32[8,768]{1,0:T(8,128)S(1)}, u32[]{:S(2)}, u32[]{:S(2)}) collective-permute-start(f32[8,768]{1,0:T(8,128)S(1)} %get-tuple-element.316.refs_0_), channel_id=1, source_target_pairs={{0,16},{4,20},{8,24},{12,28},{16,0},{20,4},{24,8},{28,12},{1,17},{... | collective-permute-start | bytes 73736 | tf_op jit(solution)/shard_map/ppermute | solution.py:24
  (19 other events, 186.4 us)

commit v3 on v2

--- a/solution.py
+++ b/solution.py
@@ -11,6 +11,7 @@
 f32 = jnp.float32
 bf16 = jnp.bfloat16
 LANES = 128
+ORDER = "mmmmEMmmMmMmmMmLmLNMLLNLN"
 FLOPS_PER_US = 0.5e9
 SUBS = 8
 
@@ -24,74 +25,66 @@
     return lax.ppermute(shard, axis, [(i, i ^ mask) for i in range(lax.axis_size(axis))])
 
 
-class Steps:
-    def __init__(self, steps):
-        self.steps, self.value, self.ended = steps, None, False
-        self.step()
-
-    def step(self):
-        try:
-            if not self.ended:
-                next(self.steps)
-        except StopIteration as end:
-            self.value, self.ended = end.value, True
-
-    def result(self):
-        while not self.ended:
-            self.step()
-        return self.value
-
-
-def stepped(work):
-    return lambda *args: Steps(work(*args))
-
-
-@stepped
 def halving_steps(call, groups, orders, spot, axis):
     keeps, sends = [g[0] for g in groups], [g[1] for g in groups]
     count = len(orders[0])
+    joint = [k > 0 and len({order[k] for order in orders}) == 1 for k in range(count)]
+
+    def shapes(rows, stage):
+        rows = [sum(rows)] if joint[stage] else rows
+        return [like((r, keeps[0].shape[1]), bf16) for r in rows]
+
+    def trade(blocks, stage):
+        return [swapped(block, axis, order[stage]) for block, order in zip(blocks, orders)]
+
     for stage in range(count):
-        gots = [swapped(send, axis, order[stage]) for send, order in zip(sends, orders)]
+        gots = trade(sends, stage)
         yield
-        operands = [a for pair in zip(keeps, gots) for a in pair]
+        rows = [k.shape[0] for k in keeps]
         if stage + 1 < count:
-            after = tuple(order[stage + 1] for order in orders)
-            shapes = [like((k.shape[0] // 2, k.shape[1]), bf16) for k in keeps for _ in range(2)]
-            parts = call(
-                functools.partial(halve_kernel, after), shapes, [spot, *operands], limit=8, scalars=1
+            half = [r // 2 for r in rows]
+            masks = tuple(order[stage + 1] for order in orders)
+            results = call(
+                functools.partial(halve_kernel, masks),
+                [like((r, keeps[0].shape[1]), bf16) for r in half] + shapes(half, stage + 1),
+                [spot, *keeps, *gots], limit=8, scalars=1,
             )
-            keeps, sends = parts[0::2], parts[1::2]
+            keeps, sends = results[: len(half)], results[len(half) :]
         else:
-            owns = call(add_kernel, [like(k.shape, bf16) for k in keeps], operands, limit=8)
+            owns = call(
+                functools.partial(sum_kernel, len(keeps)), shapes(rows, stage), [*keeps, *gots], limit=8
+            )
     for stage in range(count - 1, -1, -1):
-        gots = [swapped(own, axis, order[stage]) for own, order in zip(owns, orders)]
-        operands = [a for pair in zip(owns, gots) for a in pair]
-        if stage:
-            yield
-            shapes = [like((2 * own.shape[0], own.shape[1]), bf16) for own in owns]
-            owns = call(
-                functools.partial(double_kernel, tuple(order[stage] for order in orders)),
-                shapes, [spot, *operands], limit=8, scalars=1,
-            )
-    return operands
-
-
-@stepped
+        gots = trade(owns, stage)
+        yield
+        if not stage:
+            return [a for pair in zip(owns, gots) for a in pair]
+        masks = tuple(order[stage] for order in orders)
+        owns = call(
+            functools.partial(double_kernel, joint[stage], masks),
+            shapes([2 * r for r in rows], stage - 1),
+            [spot, *owns, *gots], limit=8, scalars=1,
+        )
+        rows = [2 * r for r in rows]
+
+
 def head_steps(call, keep, send, axis="head"):
     got = swapped(send, axis, 1)
     mask = 2
     while True:
         yield
-        total, low = call(
+        if mask >= lax.axis_size(axis):
+            (low,) = call(
+                functools.partial(sum_kernel, 1), [like(keep.shape, bf16)], [keep, got], limit=8
+            )
+            return low, swapped(low, axis, 1)
+        keep, low = call(
             join_kernel, [like(keep.shape), like(keep.shape, bf16)], [keep, got], limit=8
         )
-        if mask >= lax.axis_size(axis):
-            return low, swapped(low, axis, 1)
-        keep, got = total, swapped(low, axis, mask)
+        got = swapped(low, axis, mask)
         mask *= 2
 
 
-@stepped
 def carry_steps(call, total, low, whole, spot, axis, ahead):
     carry = jnp.zeros_like(total)
     mask = 1
@@ -100,25 +93,35 @@
         if 2 * mask >= lax.axis_size(axis):
             return carry, got
         yield
-        total, low, carry = call(
+        more = 4 * mask < lax.axis_size(axis)
+        low, carry, *kept = call(
             functools.partial(merge_kernel, mask, ahead),
-            [like(total.shape), like(total.shape, bf16), like(total.shape)],
+            [like(total.shape, bf16), like(total.shape)] + [like(total.shape)] * more,
             [spot, whole, total, got, carry],
             limit=8,
             scalars=1,
         )
+        total = kept[0] if kept else total
         mask *= 2
 
 
-@stepped
 def sum_steps(call, rows, axis):
     mask = 1
-    while mask < lax.axis_size(axis):
+    while True:
         got = swapped(rows, axis, mask)
         yield
+        mask *= 2
+        if mask >= lax.axis_size(axis):
+            return rows, got
         (rows,) = call(plain_add_kernel, [like(rows.shape)], [rows, got], limit=4)
-        mask *= 2
-    return rows
+
+
+def ran(steps):
+    while True:
+        try:
+            next(steps)
+        except StopIteration as end:
+            return end.value
 
 
 def lane_tiles(width):
@@ -160,24 +163,27 @@
 
 def run_scan(series_ref, decay_ref, out_ref, reverse):
     blocks = series_ref.shape[0] // SUBS
-    for lanes in lane_tiles(series_ref.shape[1]):
-        decay = decay_ref[:, lanes]
-
-        def one(lap, state, lanes=lanes, decay=decay):
-            place = blocks - 1 - lap if reverse else lap
-            tile = series_ref[rows_at(place * SUBS, SUBS), lanes]
-            for r in range(SUBS):
-                r = SUBS - 1 - r if reverse else r
-                state = decay * state + tile[r : r + 1, :]
-            return state
-
-        out_ref[:, lanes] = lax.fori_loop(0, blocks, one, jnp.zeros_like(decay))
-
-
-def part_total(part_ref, rows):
-    total = part_ref[pl.ds(0, rows, stride=SUBS), :]
+    tiles = lane_tiles(series_ref.shape[1])
+    decays = [decay_ref[:, lanes] for lanes in tiles]
+
+    def one(lap, states):
+        place = blocks - 1 - lap if reverse else lap
+        at = rows_at(place * SUBS, SUBS)
+        blocks_in = [series_ref[at, lanes] for lanes in tiles]
+        for r in range(SUBS):
+            r = SUBS - 1 - r if reverse else r
+            states = [d * s + b[r : r + 1, :] for d, s, b in zip(decays, states, blocks_in)]
+        return states
+
+    states = lax.fori_loop(0, blocks, one, [jnp.zeros_like(d) for d in decays])
+    for lanes, state in zip(tiles, states):
+        out_ref[:, lanes] = state
+
+
+def part_total(part_ref, rows, base=0):
+    total = part_ref[pl.ds(base, rows, stride=SUBS), :]
     for r in range(1, SUBS):
-        total = total + part_ref[pl.ds(r, rows, stride=SUBS), :]
+        total = total + part_ref[pl.ds(base + r, rows, stride=SUBS), :]
     return total
 
 
@@ -199,14 +205,15 @@
     return jnp.where(far == 1, carry + power * got, carry), far, step
 
 
-def merge_kernel(mask, ahead, spot_ref, whole_ref, total_ref, got_ref, carry_ref, sum_ref, low_ref, out_ref):
+def merge_kernel(mask, ahead, spot_ref, whole_ref, total_ref, got_ref, carry_ref, low_ref, out_ref, *sums):
     got = got_ref[...].astype(f32)
     total = total_ref[...]
     out_ref[...], far, step = merged(
         mask, ahead, spot_ref[0], whole_ref[...], got, carry_ref[...]
     )
     total = jnp.where(far == 1, step * got + total, step * total + got)
-    sum_ref[...] = total
+    for sum_ref in sums:
+        sum_ref[...] = total
     low_ref[...] = total.astype(bf16)
 
 
@@ -214,32 +221,60 @@
     return (spot[0] // mask) % 2
 
 
-def halve_kernel(after, spot_ref, *refs):
-    ins, outs = refs[: 2 * len(after)], refs[2 * len(after) :]
-    for k, mask in enumerate(after):
-        total = ins[2 * k][...].astype(f32) + ins[2 * k + 1][...].astype(f32)
-        half = total.shape[0] // 2
-        put_halves(bit_of(spot_ref, mask), total[:half], total[half:], outs[2 * k], outs[2 * k + 1])
+def split_blocks(refs, rows):
+    if len(refs) == len(rows):
+        return [ref[...].astype(f32) for ref in refs]
+    whole, starts = refs[0][...].astype(f32), [sum(rows[:k]) for k in range(len(rows))]
+    return [whole[start : start + r] for start, r in zip(starts, rows)]
+
+
+def put_blocks(refs, blocks):
+    if len(refs) == len(blocks):
+        for ref, block in zip(refs, blocks):
+            ref[...] = block.astype(bf16)
+        return
+    start = 0
+    for block in blocks:
+        refs[0][start : start + block.shape[0], :] = block.astype(bf16)
+        start += block.shape[0]
+
+
+def halve_kernel(masks, spot_ref, *refs):
+    count = len(masks)
+    keeps = [ref[...].astype(f32) for ref in refs[:count]]
+    rows = [keep.shape[0] for keep in keeps]
+    ours = next(k for k in range(count, len(refs)) if refs[k].shape[0] == rows[0] // 2)
+    totals = [a + b for a, b in zip(keeps, split_blocks(refs[count:ours], rows))]
+    pairs = [
+        ordered(bit_of(spot_ref, mask), total[: r // 2], total[r // 2 :])
+        for mask, total, r in zip(masks, totals, rows)
+    ]
+    put_blocks(refs[ours : ours + count], [pair[0] for pair in pairs])
+    put_blocks(refs[ours + count :], [pair[1] for pair in pairs])
+
+
+def sum_kernel(count, *refs):
+    keeps = [ref[...].astype(f32) for ref in refs[:count]]
+    rows = [keep.shape[0] for keep in keeps]
+    ours = count + (count if refs[count].shape[0] == rows[0] else 1)
+    totals = [a + b for a, b in zip(keeps, split_blocks(refs[count:ours], rows))]
+    put_blocks(refs[ours:], totals)
 
 
 def plain_add_kernel(own_ref, got_ref, out_ref):
     out_ref[...] = own_ref[...] + got_ref[...]
 
 
-def add_kernel(*refs):
-    count = len(refs) // 3
-    for k, out_ref in enumerate(refs[2 * count :]):
-        total = refs[2 * k][...].astype(f32) + refs[2 * k + 1][...].astype(f32)
-        out_ref[...] = total.astype(bf16)
-
-
-def double_kernel(masks, spot_ref, *refs):
-    for k, mask in enumerate(masks):
-        out_ref = refs[2 * len(masks) + k]
-        half = out_ref.shape[0] // 2
-        first, second = halves_of(bit_of(spot_ref, mask), refs[2 * k], refs[2 * k + 1])
-        out_ref[0:half, :] = first.astype(bf16)
-        out_ref[half:, :] = second.astype(bf16)
+def double_kernel(joint_in, masks, spot_ref, *refs):
+    count = len(masks)
+    ins = 1 if joint_in else count
+    rows = [refs[0].shape[0] // count] * count if joint_in else [ref.shape[0] for ref in refs[:count]]
+    owns, gots = split_blocks(refs[:ins], rows), split_blocks(refs[ins : 2 * ins], rows)
+    blocks = [
+        jnp.concatenate(ordered(bit_of(spot_ref, mask), own, got), axis=0)
+        for mask, own, got in zip(masks, owns, gots)
+    ]
+    put_blocks(refs[2 * ins :], blocks)
 
 
 def join_kernel(keep_ref, got_ref, total_ref, low_ref):
@@ -270,20 +305,24 @@
     copies = [pltpu.make_async_copy(a, b, sems.at[i]) for i, (a, b) in enumerate(pairs)]
     for copy in copies:
         copy.start()
-    for copy in copies:
+    for copy in copies[:3]:
         copy.wait()
     slots, rows, _ = x_ref.shape
     gain, bias = row(gain_ref), row(bias_ref)
-    kept = [[], [], []]
+    acts = []
     for s in range(slots):
         centred, root = centred_rows(x_ref[s].astype(f32))
-        act = (centred * root * gain + bias).astype(bf16)
-        act_ref[s * rows : (s + 1) * rows, :] = act
-        for j in range(3):
-            kept[j].append(contract(act, w_ref[j], 1, 1) + wb_ref[j : j + 1, :])
-    q_ref[...] = jnp.concatenate(kept[0], axis=-1)
-    k_ref[...] = jnp.concatenate(kept[1], axis=-1).astype(bf16)
-    v_ref[...] = jnp.concatenate(kept[2], axis=-1)
+        acts.append((centred * root * gain + bias).astype(bf16))
+        act_ref[s * rows : (s + 1) * rows, :] = acts[s]
+    for copy in copies[3:]:
+        copy.wait()
+    kept = [
+        jnp.concatenate([contract(a, w_ref[j], 1, 1) + wb_ref[j : j + 1, :] for a in acts], axis=-1)
+        for j in range(3)
+    ]
+    q_ref[...] = kept[0]
+    k_ref[...] = kept[1].astype(bf16)
+    v_ref[...] = kept[2]
 
 
 def masked_kernel(spot_ref, lengths_ref, cotangent_ref, low_ref, sum_ref):
@@ -409,36 +448,36 @@
     put_halves(bit_of(spot_ref, mask_two), sums[:half], sums[half:], w_down_ref, w_down_send_ref)
 
 
-def result_kernel(spot_ref, lengths_ref, own_ref, other_ref, mid_ref, b_down_ref, out_ref):
-    slots, rows, model = out_ref.shape
-    halves = halves_of(spot_ref[1], own_ref, other_ref)
-    per = slots // 2
-    spot = spot_ref[0] * rows + lax.broadcasted_iota(jnp.int32, (rows, model), 0)
-    for s in range(slots):
-        half = halves[s // per]
-        feed = half[(s % per) * rows : (s % per + 1) * rows, :] + row(b_down_ref)
-        total = mid_ref[s * rows : (s + 1) * rows, :] + feed
-        out_ref[s] = jnp.where(spot < lengths_ref[s], total, 0.0)
-
-
 def norm_grad(grad, hat, root, gain):
     scaled = grad * gain
     inner = jnp.mean(scaled * hat, axis=-1, keepdims=True)
     return root * (scaled - jnp.mean(scaled, axis=-1, keepdims=True) - hat * inner)
 
 
-def entry_kernel(spot_ref, own_ref, other_ref, x_ref, gain_ref, gmid_ref, out_ref, rows_ref):
-    rows = own_ref.shape[0]
+def entry_kernel(
+    spot_ref, lengths_ref, own_ref, other_ref, x_ref, gain_ref, gmid_ref, mid_ref, b_down_ref,
+    out_ref, rows_ref, layer_ref,
+):
+    slots, rows, model = layer_ref.shape
+    half = own_ref.shape[0] // 2
+    first, second = halves_of(spot_ref[1], own_ref, other_ref)
     gain_rows = bias_rows = 0.0
-    for half, grad in enumerate(halves_of(spot_ref[1], own_ref, other_ref)):
-        at = slice(half * rows, (half + 1) * rows)
+    spot = spot_ref[0] * rows + lax.broadcasted_iota(jnp.int32, (rows, model), 0)
+    for s in range(slots):
+        at = slice(s * rows, (s + 1) * rows)
+        held = first if s * rows < half else second
+        inside = s * rows % half
+        grad = held[inside : inside + rows]
+        feed = held[half + inside : half + inside + rows]
         centred, root = centred_rows(x_ref[at, :].astype(f32))
         hat = centred * root
         out_ref[at, :] = gmid_ref[at, :] + norm_grad(grad, hat, root, row(gain_ref))
         gain_rows = gain_rows + jnp.sum(grad * hat, axis=0, keepdims=True)
         bias_rows = bias_rows + jnp.sum(grad, axis=0, keepdims=True)
+        total = mid_ref[at, :] + feed + row(b_down_ref)
+        layer_ref[s] = jnp.where(spot < lengths_ref[s], total, 0.0)
     rows_ref[...] = jnp.concatenate(
-        [gain_rows, bias_rows, jnp.zeros((SUBS - 2, gain_rows.shape[1]), f32)], axis=0
+        [gain_rows, bias_rows, jnp.zeros((SUBS - 2, model), f32)], axis=0
     )
 
 
@@ -546,20 +585,23 @@
     pad_ref[taps + rows : 2 * taps + rows, :] = jnp.zeros((taps, width), f32)
     wide_ref[0:taps, :] = wide(taps_ref[...], slots)
     wide_ref[taps : taps + 1, :] = wide(row(shift_skip_ref), slots)
-    for lanes in lane_tiles(width):
-        decay = decay_ref[:, lanes]
-        weight = weight_ref[:, lanes]
-
-        def one(lap, state, decay=decay, weight=weight):
-            place = blocks - 1 - lap
-            for r in range(SUBS - 1, -1, -1):
-                state = decay * state
-                part_ref[rows_at(place * SUBS * SUBS + r * SUBS, SUBS), :] = folded(weight * state)
-            return state
-
-        lax.fori_loop(0, blocks, one, behind_ref[:, lanes])
+    tiles = lane_tiles(width)
+    decays = [decay_ref[:, lanes] for lanes in tiles]
+
+    def one(lap, carried):
+        place = blocks - 1 - lap
+        for r in range(SUBS - 1, -1, -1):
+            carried = [d * c for d, c in zip(decays, carried)]
+            for k, c in enumerate(carried):
+                part_ref[rows_at((k * rows + place * SUBS + r) * SUBS, SUBS), :] = folded(c)
+        return carried
+
+    lax.fori_loop(
+        0, blocks, one, [weight_ref[:, lanes] * behind_ref[:, lanes] for lanes in tiles]
+    )
+    for k, lanes in enumerate(tiles):
         grad_u = (
-            gloc_ref[:, lanes] + part_total(part_ref, rows) + skip[:, lanes] * gs_ref[:, lanes]
+            gloc_ref[:, lanes] + part_total(part_ref, rows, k * rows * SUBS) + skip[:, lanes] * gs_ref[:, lanes]
         )
         gv_ref[:, lanes] = (grad_u * shifted_ref[:, lanes]).astype(bf16)
         pad_ref[taps : taps + rows, lanes] = grad_u * v_ref[:, lanes]
@@ -572,15 +614,15 @@
                 if i < 1 or i > taps:
                     continue
                 tap = wide_ref[i - 1 : i, lanes]
+                live = min(rows, -(-(rows - i) // SUBS) * SUBS)
                 start = taps + SUBS * q
-                if start + rows <= block.shape[0]:
-                    total = total + tap * block[start : start + rows, :]
-                else:
-                    live = block.shape[0] - start
-                    total = total + tap * jnp.concatenate(
-                        [block[start:, :], jnp.zeros((rows - live, LANES), f32)], axis=0
-                    )
-                borrowed = borrowed + tap * block[SUBS * q : SUBS * q + taps, :]
+                live = min(live, block.shape[0] - start)
+                fresh = total[:live] + tap * block[start : start + live, :]
+                total = fresh if live == rows else jnp.concatenate([fresh, total[live:]], axis=0)
+                idle = (taps - i) // SUBS * SUBS
+                start = SUBS * q + idle
+                fresh = borrowed[idle:] + tap * block[start : start + taps - idle, :]
+                borrowed = fresh if not idle else jnp.concatenate([borrowed[:idle], fresh], axis=0)
         gk_ref[:, lanes] = total
         halo_ref[:, lanes] = borrowed.astype(bf16)
         grad_shifted = pad_ref[taps : taps + rows, lanes]
@@ -636,7 +678,7 @@
 
 
 def last_kernel(
-    mask_one, mask_two, spot_ref, gq_ref, gk_ref, received_ref, gv_ref, act_ref, w_ref, early_ref, small_ref, misc_ref,
+    mask_one, mask_two, spot_ref, out_keep_ref, out_send_ref, gq_ref, gk_ref, received_ref, gv_ref, act_ref, w_ref, early_ref, small_ref, misc_ref,
     rows_ref, up_ref, down_ref, keep_ref, send_ref, one_ref, one_send_ref, two_ref,
     two_send_ref, all_ref,
 ):
@@ -664,13 +706,16 @@
                 sums[j] = sums[j] + contract(grads, act, 0, 0)
         terms.append(term)
     half = slots // 2
+    count = out_keep_ref.shape[0]
     put_halves(
         spot_ref[1],
         jnp.concatenate(terms[:half], axis=0),
         jnp.concatenate(terms[half:], axis=0),
-        keep_ref,
-        send_ref,
-    )
+        keep_ref.at[0:count, :],
+        send_ref.at[0:count, :],
+    )
+    keep_ref[count:, :] = out_keep_ref[...]
+    send_ref[count:, :] = out_send_ref[...]
     for j in range(3):
         total = jnp.sum(parts[j], axis=0, keepdims=True)
         bias = slot_of(total, 0, chans)
@@ -720,10 +765,13 @@
 
 
 def spread_kernel(
-    chans, taps, mask_one, mask_two, spot_ref, one_ref, one_got_ref, two_ref, two_got_ref,
+    chans, taps, mask_one, mask_two, spot_ref, ln1_ref, ln1_got_ref, one_ref, one_got_ref, two_ref, two_got_ref,
     qkv_ref, bias_ref, tap_ref, shift_skip_ref, a_ref, b_ref, c_ref, ssm_skip_ref, step_ref, out_ref,
-    gain_ref, norm_bias_ref, out_bias_ref, up_ref, down_ref, all_ref,
+    gain_ref, norm_bias_ref, out_bias_ref, up_ref, down_ref, entry_gain_ref, entry_bias_ref, all_ref,
 ):
+    entry = ln1_ref[...] + ln1_got_ref[...]
+    entry_gain_ref[...] = entry[0:1, :].reshape(entry.shape[1])
+    entry_bias_ref[...] = entry[1:2, :].reshape(entry.shape[1])
     quarter = one_ref.shape[0]
     pieces = halves_of(bit_of(spot_ref, mask_one), one_ref, one_got_ref)
     pieces += halves_of(bit_of(spot_ref, mask_two), two_ref, two_got_ref)
@@ -862,6 +910,7 @@
         us=2.9,
     )
     steps = carry_steps(call, end_local, end_low, whole_wide, spot, "seq", False)
+    next(steps)
     low_out, grad_b_down = call(
         masked_kernel,
         [like((tokens, model), bf16), like((1, model))],
@@ -869,7 +918,7 @@
         us=0.8,
         scalars=2,
     )
-    carry, got = steps.result()
+    carry, got = ran(steps)
     ssm_out, gated, start_state, keep, send = call(
         functools.partial(attend_kernel, last_mask),
         [like((rows, width)), like((tokens, chans), bf16), like((states, width)), half_like, half_like],
@@ -881,8 +930,8 @@
         us=2.9,
         scalars=1,
     )
-    own, other = head_steps(call, keep, send).result()
-    middle, keep, send, out_keep, out_send, grad_b_up, up_keep, up_send, down_keep, down_send = call(
+    own, other = ran(head_steps(call, keep, send))
+    middle, back_keep, back_send, out_keep, out_send, grad_b_up, up_keep, up_send, down_keep, down_send = call(
         functools.partial(feed_kernel, *ends),
         [
             like((tokens, model)),
@@ -909,129 +958,153 @@
         scalars=1,
         limit=32,
     )
-    feed_sums = halving_steps(
-        call, [(up_keep, up_send), (down_keep, down_send)], orders, spot, "seq"
-    )
-    steps = head_steps(call, keep, send)
-    own, other = steps.result()
-    grad_middle, low_middle, grad_queries, grad_ssm, front_local, front_low, norm_rows = call(
-        middle_kernel,
-        [
-            like((tokens, model)),
-            like((tokens, model), bf16),
-            like((rows, width), bf16),
-            like((rows, width)),
-            like((states, width)),
-            like((states, width), bf16),
-            like((SUBS, model)),
-        ],
-        [
-            spot, lengths, own, other, middle, cotangent, ln2_gain, output_weight, ssm_out, queries,
-            decay_wide,
-        ],
-        us=2.5,
-        scalars=2,
-    )
-    steps = carry_steps(call, front_local, front_low, whole_wide, spot, "seq", True)
-    (early,) = call(
-        weights_kernel,
-        [like((2 * chans, model), bf16)],
-        [grad_queries, act_one, gated, low_middle],
-        us=0.5,
-    )
-    feed_sums.step()
-    steps.step()
-    carry, got = steps.result()
-    grad_local, gain_local, power_local, reach = call(
-        local_kernel,
-        [like((rows, width)), like((states, width)), like((states, width)), like((states, width))],
-        [series, grad_ssm, decay_wide, weight_wide, start_state],
-        [pltpu.VMEM((rows * SUBS, LANES), f32), pltpu.VMEM((rows * states, LANES), f32)],
-        us=5.8,
-    )
-    feed_sums.step()
-    grad_keys, halo, grad_values, small, misc = call(
-        functools.partial(unmix_kernel, last_mask),
-        [
-            like((rows, width)),
-            like((taps, width), bf16),
-            like((rows, width), bf16),
-            like((states, 4 * chans)),
-            like((SUBS, 4 * chans)),
-        ],
-        [
-            spot, grad_local, grad_ssm, series, decay_wide, weight_wide, whole_wide, got, carry,
-            gain_local, power_local, reach, end_local, values, shifted_keys, edge, keys, shift_taps,
-            shift_skip, ssm_skip, in_weight, turned_c, gain_root, slope, fall, ssm_a.T, ssm_step,
-        ],
-        [
-            pltpu.VMEM((rows * SUBS, LANES), f32),
-            pltpu.VMEM((taps + rows, width), f32),
-            pltpu.VMEM((2 * taps + rows, width), f32),
-            pltpu.VMEM((taps + SUBS, width), f32),
-            pltpu.VMEM(((taps + 1) * SUBS, LANES), f32),
-            pltpu.VMEM((taps + SUBS, width), f32),
-            pltpu.VMEM((states, width), f32),
-        ],
-        us=6.0,
-        scalars=1,
-    )
-    received = shifted(halo, "seq", -1)
-    feed_sums.step()
-    unit = 2 * peers * SUBS
-    last_rows = -(-(4 * chans + states + 2 * SUBS) // unit) * unit
-    quarter = like((last_rows // 4, model), bf16)
-    keep, send, one, one_send, two, two_send = call(
-        functools.partial(last_kernel, *ends),
-        [half_like, half_like, quarter, quarter, quarter, quarter],
-        [
-            spot, grad_queries, grad_keys, received, grad_values, act_one, projections, early, small,
-            misc, norm_rows, grad_b_up, grad_b_down,
-        ],
-        [pltpu.VMEM((last_rows, model), f32)],
-        us=1.5,
-        scalars=1,
-    )
-    back = head_steps(call, keep, send)
-    last_sums = halving_steps(call, [(one, one_send), (two, two_send)], orders, spot, "seq")
-    back.step()
-    feed_sums.step()
-    own, other = back.result()
-    last_sums.step()
-    grad_inputs, ln1_rows = call(
-        entry_kernel,
-        [like((tokens, model)), like((SUBS, model))],
-        [spot, own, other, flat_inputs, ln1_gain, grad_middle],
-        scalars=1,
-        us=2.0,
-    )
-    ln1 = sum_steps(call, ln1_rows, "seq")
-    feed_joined = feed_sums.result()
-    last_sums.step()
-    feed = head_steps(call, out_keep, out_send)
-    ln1.step()
-    last_sums.step()
-    feed.step()
-    ln1.step()
-    last_sums.step()
-    sum_up, sum_down = call(
-        functools.partial(widen_kernel, *ends),
-        [like((model, hidden_count)), like((hidden_count, model))],
-        [spot, *feed_joined],
-        scalars=1,
-        us=2.5,
-    )
-    own, other = feed.result()
-    last_sums.step()
-    (layer_out,) = call(
-        result_kernel,
-        [like(inputs.shape)],
-        [spot, lengths, own, other, middle, b_down],
-        scalars=2,
-        us=1.5,
-    )
-    ln1_rows = ln1.result()
-    joined = last_sums.result()
+    low_middle = early = last_parts = entry_parts = grad_inputs = layer_out = None
+    sum_up = sum_down = last_rows = grad_queries = None
+
+    def feed_work():
+        nonlocal sum_up, sum_down
+        feed_joined = yield from halving_steps(
+            call, [(up_keep, up_send), (down_keep, down_send)], orders, spot, "seq"
+        )
+        sum_up, sum_down = call(
+            functools.partial(widen_kernel, *ends),
+            [like((model, hidden_count)), like((hidden_count, model))],
+            [spot, *feed_joined],
+            scalars=1,
+            us=2.5,
+        )
+
+    def early_work():
+        nonlocal early
+        while low_middle is None:
+            yield
+        (early,) = call(
+            weights_kernel,
+            [like((2 * chans, model), bf16)],
+            [grad_queries, act_one, gated, low_middle],
+            us=0.5,
+        )
+
+    def last_work():
+        while last_parts is None:
+            yield
+        one, one_send, two, two_send = last_parts
+        return (
+            yield from halving_steps(call, [(one, one_send), (two, two_send)], orders, spot, "seq")
+        )
+
+    def entry_work():
+        while entry_parts is None:
+            yield
+        return (yield from sum_steps(call, entry_parts, "seq"))
+
+    def main_work():
+        nonlocal low_middle, grad_queries, last_parts, entry_parts, grad_inputs, layer_out, last_rows
+        own, other = yield from head_steps(call, back_keep, back_send)
+        grad_middle, low_middle, grad_queries, grad_ssm, front_local, front_low, norm_rows = call(
+            middle_kernel,
+            [
+                like((tokens, model)),
+                like((tokens, model), bf16),
+                like((rows, width), bf16),
+                like((rows, width)),
+                like((states, width)),
+                like((states, width), bf16),
+                like((SUBS, model)),
+            ],
+            [
+                spot, lengths, own, other, middle, cotangent, ln2_gain, output_weight, ssm_out, queries,
+                decay_wide,
+            ],
+            us=2.5,
+            scalars=2,
+        )
+        yield
+        steps = carry_steps(call, front_local, front_low, whole_wide, spot, "seq", True)
+        carry, got = yield from steps
+        grad_local, gain_local, power_local, reach = call(
+            local_kernel,
+            [like((rows, width)), like((states, width)), like((states, width)), like((states, width))],
+            [series, grad_ssm, decay_wide, weight_wide, start_state],
+            [pltpu.VMEM((rows * SUBS, LANES), f32), pltpu.VMEM((rows * states, LANES), f32)],
+            us=5.8,
+        )
+        yield
+        grad_keys, halo, grad_values, small, misc = call(
+            functools.partial(unmix_kernel, last_mask),
+            [
+                like((rows, width)),
+                like((taps, width), bf16),
+                like((rows, width), bf16),
+                like((states, 4 * chans)),
+                like((SUBS, 4 * chans)),
+            ],
+            [
+                spot, grad_local, grad_ssm, series, decay_wide, weight_wide, whole_wide, got, carry,
+                gain_local, power_local, reach, end_local, values, shifted_keys, edge, keys, shift_taps,
+                shift_skip, ssm_skip, in_weight, turned_c, gain_root, slope, fall, ssm_a.T, ssm_step,
+            ],
+            [
+                pltpu.VMEM((width * rows * SUBS // LANES, LANES), f32),
+                pltpu.VMEM((taps + rows, width), f32),
+                pltpu.VMEM((2 * taps + rows, width), f32),
+                pltpu.VMEM((taps + SUBS, width), f32),
+                pltpu.VMEM(((taps + 1) * SUBS, LANES), f32),
+                pltpu.VMEM((taps + SUBS, width), f32),
+                pltpu.VMEM((states, width), f32),
+            ],
+            us=6.0,
+            scalars=1,
+        )
+        received = shifted(halo, "seq", -1)
+        yield
+        while early is None:
+            step("E")
+        unit = 2 * peers * SUBS
+        last_rows = -(-(4 * chans + states + 2 * SUBS) // unit) * unit
+        quarter = like((last_rows // 4, model), bf16)
+        keep, send, one, one_send, two, two_send = call(
+            functools.partial(last_kernel, *ends),
+            [like((tokens, model), bf16)] * 2 + [quarter, quarter, quarter, quarter],
+            [
+                spot, out_keep, out_send, grad_queries, grad_keys, received, grad_values, act_one, projections, early, small,
+                misc, norm_rows, grad_b_up, grad_b_down,
+            ],
+            [pltpu.VMEM((last_rows, model), f32)],
+            us=1.5,
+            scalars=1,
+        )
+        last_parts = (one, one_send, two, two_send)
+        step("L")
+        own, other = yield from head_steps(call, keep, send)
+        yield
+        grad_inputs, rows_sum, layer_out = call(
+            entry_kernel,
+            [like((tokens, model)), like((SUBS, model)), like(inputs.shape)],
+            [spot, lengths, own, other, flat_inputs, ln1_gain, grad_middle, middle, b_down],
+            scalars=2,
+            us=3.0,
+        )
+        entry_parts = rows_sum
+        step("N")
+
+    works = {"m": main_work(), "M": feed_work(), "E": early_work(), "L": last_work(), "N": entry_work()}
+    ended = {}
+
+    def step(name):
+        if name not in ended:
+            try:
+                next(works[name])
+            except StopIteration as end:
+                ended[name] = end.value
+
+    step("M")
+    for name in ORDER:
+        step(name)
+    for name in "mMLN":
+        while name not in ended:
+            step(name)
+    joined, ln1_parts = ended["L"], ended["N"]
     spread = call(
         functools.partial(spread_kernel, chans, taps, *ends),
         [
@@ -1050,8 +1123,10 @@
             like((model,)),
             like(up_bias.shape),
             like((model,)),
+            like((model,)),
+            like((model,)),
         ],
-        [spot, *joined],
+        [spot, *ln1_parts, *joined],
         [pltpu.VMEM((last_rows, model), f32)],
         scalars=1,
         us=2.0,
@@ -1059,12 +1134,13 @@
     (
         sum_qkv, sum_b_qkv, sum_taps, sum_shift_skip, sum_a, sum_b, sum_c, sum_ssm_skip, sum_step,
         sum_out, sum_ln2_gain, sum_ln2_bias, sum_b_out, sum_b_up, sum_b_down,
+        sum_ln1_gain, sum_ln1_bias,
     ) = spread
     return (
         layer_out,
         grad_inputs.reshape(inputs.shape),
-        ln1_rows[0],
-        ln1_rows[1],
+        sum_ln1_gain,
+        sum_ln1_bias,
         jnp.swapaxes(sum_qkv, 1, 2),
         sum_b_qkv,
         sum_taps,

time: 188 us -> 168 us (0.89)
  Pallas kernels: 51.7 us -> 44.5 us
  waiting for transfers between devices: 79.4 us -> 72.7 us
  starting transfers between devices: 54.7 us -> 48.2 us
    pallas_call x39 -> x35, Pallas kernels: 51.7 us -> 44.5 us  [call(): pl.pallas_call(body, in_specs=specs, out_shape=tuple(outs) + (like((SUBS,...]
    ppermute x45 -> x38, starting transfers between devices: 48.5 us -> 41.8 us  [swapped(): lax.ppermute(shard, axis, [(i, i ^ mask) for i in range(lax.axis_size(axi...]
    ppermute x45 -> x38, waiting for transfers between devices: 76.4 us -> 71.3 us  [swapped(): lax.ppermute(shard, axis, [(i, i ^ mask) for i in range(lax.axis_size(axi...]
  transfers between devices with their start and end apart: 47 -> 40, of which waited for: 30 -> 25; matrix products, arithmetic and copies ran while one was open for 1% -> 0% of each run, Pallas kernels for 17% -> 16%
where the time goes in v3:
time: 168 us
  waiting for transfers between devices  72.7 us (43%)
  starting transfers between devices  48.2 us (29%)
  Pallas kernels  44.5 us (26%)
    ppermute x38, waiting for transfers between devices, swapped(): lax.ppermute(shard, axis, [(i, i ^ mask) for i in range(lax.axis_size(axi...  71.3 us
    pallas_call x35, Pallas kernels, call(): pl.pallas_call(body, in_specs=specs, out_shape=tuple(outs) + (like((SUBS,...  44.5 us
    ppermute x38, starting transfers between devices, swapped(): lax.ppermute(shard, axis, [(i, i ^ mask) for i in range(lax.axis_size(axi...  41.8 us
    ppermute x2, starting transfers between devices, shifted(): lax.ppermute(shard, axis, [(i, i + by) for i in range(peers) if 0 <= i +...  6.39 us
  transfers between devices with their start and end apart: 40, of which 25 were waited for; matrix products, arithmetic and copies ran while one was open for 0% of the time, Pallas kernels for 16%

profile of v3, /device:TPU:0, one launch (start us, length us, event | category | flops | bytes accessed | tf_op | source)
XLA Modules:
  0.0 167.5 jit_solution(16262234442515990489)
XLA Ops:
  0.8 2.7 %shard_map.373 = (bf16[256,768]{1,0:T(8,128)(2,1)S(1)}, f32[128,384]{1,0:T(8,128)S(1)}, bf16[128,384]{1,0:T(8,128)(2,1)S(1)}, f32[128,384]{1,0:T(8,128)S(1)}, f32[8,128]{1,0:T(8,128)S(1)}) custom-call(s32[2]{0:T(128)S(1)} %pad_add_fusion.refs_0_, bf16[2,128,768]{2,1,0:T(8,128)(2,1)} %refs_1_.4, f32[768]{0:T(1024)} %refs_5_.7, f32[768]{0:T(1024)} %refs_3_.2, ...), custom_call_target="tpu_custom_call" | custom-call | flops 1000000000 | tf_op jit(solution)/shard_map/pallas_call | solution.py:811
  3.5 4.9 %collective-permute-start = (bf16[64,384]{1,0:T(8,128)(2,1)S(1)}, bf16[64,384]{1,0:T(8,128)(2,1)S(1)}, u32[]{:S(2)}, u32[]{:S(2)}) collective-permute-start(bf16[64,384]{1,0:T(8,128)(2,1)S(1)} %slice.3), channel_id=1, source_target_pairs={{0,4},{4,8},{8,12},{12,16},{16,20},{20,24},{24,28},{1,5},{5,9},{9,... | collective-permute-start | bytes 147464 | tf_op jit(solution)/shard_map/ppermute | solution.py:21
  8.6 1.5 collective-permute-done.refs_0_.refs_15_
  10.1 2.8 %shard_map.374 = (f32[128,384]{1,0:T(8,128)S(1)}, f32[128,384]{1,0:T(8,128)S(1)}, f32[64,384]{1,0:T(8,128)S(1)}, bf16[64,384]{1,0:T(8,128)(2,1)S(1)}, f32[8,128]{1,0:T(8,128)S(1)}) custom-call(bf16[64,384]{1,0:T(8,128)(2,1)S(1)} %collective-permute-done.refs_0_.refs_15_, bf16[128,384]{1,0:T(8,128)(2,1)S(1)} %get-tuple-element.170.refs_1_.refs_16_, ...), custom_call_target="tpu_custom_call" | custom-call | flops 1450000000 | tf_op jit(solution)/shard_map/pallas_call | solution.py:811
  12.9 2.4 %collective-permute-start.1 = (bf16[64,384]{1,0:T(8,128)(2,1)S(1)}, bf16[64,384]{1,0:T(8,128)(2,1)S(1)}, u32[]{:S(2)}, u32[]{:S(2)}) collective-permute-start(bf16[64,384]{1,0:T(8,128)(2,1)S(1)} %get-tuple-element.175), channel_id=1, source_target_pairs={{0,4},{4,0},{8,12},{12,8},{16,20},{20,16},{24,28},{28,24},{1,5},{5... | collective-permute-start | bytes 147464 | tf_op jit(solution)/shard_map/ppermute | solution.py:25
  16.1 1.3 collective-permute-done.1.refs_3_
  18.0 3.1 %collective-permute-start.2 = (bf16[64,384]{1,0:T(8,128)(2,1)S(1)}, bf16[64,384]{1,0:T(8,128)(2,1)S(1)}, u32[]{:S(2)}, u32[]{:S(2)}) collective-permute-start(bf16[64,384]{1,0:T(8,128)(2,1)S(1)} %get-tuple-element.179), channel_id=1, source_target_pairs={{0,8},{4,12},{8,0},{12,4},{16,24},{20,28},{24,16},{28,20},{1,9},{5... | collective-permute-start | bytes 147464 | tf_op jit(solution)/shard_map/ppermute | solution.py:25
  21.1 2.1 %collective-permute-done.2.refs_3_ = bf16[64,384]{1,0:T(8,128)(2,1)S(1)} collective-permute-done((bf16[64,384]{1,0:T(8,128)(2,1)S(1)}, bf16[64,384]{1,0:T(8,128)(2,1)S(1)}, u32[]{:S(2)}, u32[]{:S(2)}) %collective-permute-start.2) | collective-permute-done | bytes 49184 | tf_op jit(solution)/shard_map/ppermute | solution.py:25
  23.7 3.5 %collective-permute-start.3 = (bf16[64,384]{1,0:T(8,128)(2,1)S(1)}, bf16[64,384]{1,0:T(8,128)(2,1)S(1)}, u32[]{:S(2)}, u32[]{:S(2)}) collective-permute-start(bf16[64,384]{1,0:T(8,128)(2,1)S(1)} %get-tuple-element.182), channel_id=1, source_target_pairs={{0,16},{4,20},{8,24},{12,28},{16,0},{20,4},{24,8},{28,12},{1,17},{... | collective-permute-start | bytes 147464 | tf_op jit(solution)/shard_map/ppermute | solution.py:25
  27.3 2.0 %collective-permute-done.3.refs_5_ = bf16[64,384]{1,0:T(8,128)(2,1)S(1)} collective-permute-done((bf16[64,384]{1,0:T(8,128)(2,1)S(1)}, bf16[64,384]{1,0:T(8,128)(2,1)S(1)}, u32[]{:S(2)}, u32[]{:S(2)}) %collective-permute-start.3) | collective-permute-done | bytes 49184 | tf_op jit(solution)/shard_map/ppermute | solution.py:25
  29.3 3.0 %shard_map.378 = (f32[128,384]{1,0:T(8,128)S(1)}, bf16[256,192]{1,0:T(8,128)(2,1)S(1)}, f32[64,384]{1,0:T(8,128)S(1)}, bf16[128,768]{1,0:T(8,128)(2,1)S(1)}, bf1...) custom-call(s32[2]{0:T(128)S(1)} %pad_add_fusion.refs_0_, f32[128,384]{1,0:T(8,128)S(1)} %get-tuple-element.173.refs_1_.refs_0_.refs_3_, ...), custom_call_target="tpu_custom_call" | custom-call | flops 1450000000 | tf_op jit(solution)/shard_map/pallas_call | solution.py:811
  32.5 1.4 collective-permute-done.4.refs_1_
  34.0 1.6 collective-permute-start.5
  35.6 5.4 %collective-permute-done.5.refs_1_ = bf16[128,768]{1,0:T(8,128)(2,1)S(1)} collective-permute-done((bf16[128,768]{1,0:T(8,128)(2,1)S(1)}, bf16[128,768]{1,0:T(8,128)(2,1)S(1)}, u32[]{:S(2)}, u32[]{:S(2)}) %collective-permute-start.5) | collective-permute-done | bytes 196640 | tf_op jit(solution)/shard_map/ppermute | solution.py:25
  41.2 1.4 collective-permute-done.6.refs_2_
  42.6 3.7 %shard_map.381 = (f32[256,768]{1,0:T(8,128)S(1)}, bf16[128,768]{1,0:T(8,128)(2,1)S(1)}, bf16[128,768]{1,0:T(8,128)(2,1)S(1)}, bf16[128,768]{1,0:T(8,128)(2,1)S(1...) custom-call(s32[2]{0:T(128)S(1)} %pad_add_fusion.refs_0_, ...), custom_call_target="tpu_custom_call" | custom-call | flops 2500000000 | tf_op jit(solution)/shard_map/pallas_call | solution.py:811
  47.2 1.4 collective-permute-start.12
  48.7 1.5 collective-permute-start.8
  50.2 5.2 %collective-permute-done.8.refs_1_ = bf16[128,768]{1,0:T(8,128)(2,1)S(1)} collective-permute-done((bf16[128,768]{1,0:T(8,128)(2,1)S(1)}, bf16[128,768]{1,0:T(8,128)(2,1)S(1)}, u32[]{:S(2)}, u32[]{:S(2)}) %collective-permute-start.8) | collective-permute-done | bytes 196640 | tf_op jit(solution)/shard_map/ppermute | solution.py:25
  55.5 1.4 collective-permute-done.9.refs_3_
  56.9 2.4 %shard_map.384 = (f32[256,768]{1,0:T(8,128)S(1)}, bf16[256,768]{1,0:T(8,128)(2,1)S(1)}, bf16[128,384]{1,0:T(8,128)(2,1)S(1)}, f32[128,384]{1,0:T(8,128)S(1)}, f3...) custom-call(s32[2]{0:T(128)S(1)} %pad_add_fusion.refs_0_, ...), custom_call_target="tpu_custom_call" | custom-call | flops 1250000000 | tf_op jit(solution)/shard_map/pallas_call | solution.py:811
  59.3 1.5 collective-permute-start.10
  64.1 1.5 collective-permute-start.13
  66.2 1.4 collective-permute-start.16
  69.3 3.2 %collective-permute-start.14 = (bf16[64,384]{1,0:T(8,128)(2,1)S(1)}, bf16[64,384]{1,0:T(8,128)(2,1)S(1)}, u32[]{:S(2)}, u32[]{:S(2)}) collective-permute-start(bf16[64,384]{1,0:T(8,128)(2,1)S(1)} %get-tuple-element.228), channel_id=1, source_target_pairs={{0,16},{4,20},{8,24},{12,28},{16,0},{20,4},{24,8},{28,12},{1,17},{... | collective-permute-start | bytes 147464 | tf_op jit(solution)/shard_map/ppermute | solution.py:25
  72.4 5.8 %shard_map.389 = (f32[128,384]{1,0:T(8,128)S(1)}, f32[64,384]{1,0:T(8,128)S(1)}, f32[64,384]{1,0:T(8,128)S(1)}, f32[64,384]{1,0:T(8,128)S(1)}, f32[8,128]{1,0:T(8,128)S(1)}) custom-call(f32[128,384]{1,0:T(8,128)S(1)} %get-tuple-element.173.refs_1_.refs_0_.refs_3_, f32[128,384]{1,0:T(8,128)S(1)} %get-tuple-element.208.refs_1_.refs_2_, ...), custom_call_target="tpu_custom_call" | custom-call | flops 2900000000 | tf_op jit(solution)/shard_map/pallas_call | solution.py:811
  79.0 5.0 %shard_map.391 = (f32[128,384]{1,0:T(8,128)S(1)}, bf16[64,384]{1,0:T(8,128)(2,1)S(1)}, bf16[128,384]{1,0:T(8,128)(2,1)S(1)}, f32[64,768]{1,0:T(8,128)S(1)}, f32[8,768]{1,0:T(8,128)S(1)}, /*index=5*/f32[8,128]{1,0:T(8,128)S(1)}) custom-call(s32[2]{0:T(128)S(1)} %pad_add_fusion.refs_0_, f32[128,384]{1,0:T(8,128)S(1)} %get-tuple-element.227.refs_1_, ...), custom_call_target="tpu_custom_call" | custom-call | flops 3000000000 | tf_op jit(solution)/shard_map/pallas_call | solution.py:811
  84.0 1.5 collective-permute-start.17
  85.6 7.4 %collective-permute-done.18.refs_2_ = bf16[192,768]{1,0:T(8,128)(2,1)S(1)} collective-permute-done((bf16[192,768]{1,0:T(8,128)(2,1)S(1)}, bf16[192,768]{1,0:T(8,128)(2,1)S(1)}, u32[]{:S(2)}, u32[]{:S(2)}) %collective-permute-start.18) | collective-permute-done | bytes 294944 | tf_op jit(solution)/shard_map/ppermute | solution.py:25
  93.0 1.5 shard_map.393
  94.6 1.7 %collective-permute-done.19.refs_1_ = bf16[256,768]{1,0:T(8,128)(2,1)S(1)} collective-permute-done((bf16[256,768]{1,0:T(8,128)(2,1)S(1)}, bf16[256,768]{1,0:T(8,128)(2,1)S(1)}, u32[]{:S(2)}, u32[]{:S(2)}) %collective-permute-start.19) | collective-permute-done | bytes 393248 | tf_op jit(solution)/shard_map/ppermute | solution.py:25
  96.5 1.6 collective-permute-start.20
  98.1 2.2 %collective-permute-start.23 = (bf16[224,768]{1,0:T(8,128)(2,1)S(1)}, bf16[224,768]{1,0:T(8,128)(2,1)S(1)}, u32[]{:S(2)}, u32[]{:S(2)}) collective-permute-start(bf16[224,768]{1,0:T(8,128)(2,1)S(1)} %get-tuple-element.266), channel_id=1, source_target_pairs={{0,4},{4,0},{8,12},{12,8},{16,20},{20,16},{24,28},{28,24},{1,5},{5... | collective-permute-start | bytes 1032200 | tf_op jit(solution)/shard_map/ppermute | solution.py:25
  100.7 11.8 %collective-permute-done.21.refs_2_ = bf16[192,768]{1,0:T(8,128)(2,1)S(1)} collective-permute-done((bf16[192,768]{1,0:T(8,128)(2,1)S(1)}, bf16[192,768]{1,0:T(8,128)(2,1)S(1)}, u32[]{:S(2)}, u32[]{:S(2)}) %collective-permute-start.21) | collective-permute-done | bytes 294944 | tf_op jit(solution)/shard_map/ppermute | solution.py:25
  113.4 2.4 %collective-permute-done.24.refs_4_ = bf16[224,768]{1,0:T(8,128)(2,1)S(1)} collective-permute-done((bf16[224,768]{1,0:T(8,128)(2,1)S(1)}, bf16[224,768]{1,0:T(8,128)(2,1)S(1)}, u32[]{:S(2)}, u32[]{:S(2)}) %collective-permute-start.24) | collective-permute-done | bytes 344096 | tf_op jit(solution)/shard_map/ppermute | solution.py:25
  117.3 1.6 collective-permute-start.30
  118.8 1.8 %collective-permute-start.31 = (bf16[192,768]{1,0:T(8,128)(2,1)S(1)}, bf16[192,768]{1,0:T(8,128)(2,1)S(1)}, u32[]{:S(2)}, u32[]{:S(2)}) collective-permute-start(bf16[192,768]{1,0:T(8,128)(2,1)S(1)} %get-tuple-element.284.refs_2_), channel_id=1, source_target_pairs={{0,4},{4,0},{8,12},{12,8},{16,20},{20,16},{24,28},{28,24},{1,5},{5... | collective-permute-start | bytes 884744 | tf_op jit(solution)/shard_map/ppermute | solution.py:25
  120.7 2.4 %shard_map.398 = (f32[256,768]{1,0:T(8,128)}, f32[8,768]{1,0:T(8,128)S(1)}, f32[2,128,768]{2,1,0:T(8,128)}, f32[8,128]{1,0:T(8,128)S(1)}) custom-call(s32[2]{0:T(128)S(1)} %pad_add_fusion.refs_0_, s32[2]{0:T(128)S(1)} %copy-done.18, bf16[256,768]{1,0:T(8,128)(2,1)S(1)} %get-tuple-element.262.refs_2_, bf16[256,768]{1,0:T(8,128)(2,1)S(1)} %collective-permute-done.22.refs_3_, ...), custom_call_target="tpu_custom_call" | custom-call | flops 1500000000 | tf_op jit(solution)/shard_map/pallas_call | solution.py:811
  124.4 3.1 %collective-permute-start.29 = (bf16[112,768]{1,0:T(8,128)(2,1)S(1)}, bf16[112,768]{1,0:T(8,128)(2,1)S(1)}, u32[]{:S(2)}, u32[]{:S(2)}) collective-permute-start(bf16[112,768]{1,0:T(8,128)(2,1)S(1)} %get-tuple-element.282), channel_id=1, source_target_pairs={{0,16},{4,20},{8,24},{12,28},{16,0},{20,4},{24,8},{28,12},{1,17},{... | collective-permute-start | bytes 516104 | tf_op jit(solution)/shard_map/ppermute | solution.py:25
  127.6 3.8 %collective-permute-done.25.refs_1_ = f32[8,768]{1,0:T(8,128)S(1)} collective-permute-done((f32[8,768]{1,0:T(8,128)S(1)}, f32[8,768]{1,0:T(8,128)S(1)}, u32[]{:S(2)}, u32[]{:S(2)}) %collective-permute-start.25) | collective-permute-done | bytes 24608 | tf_op jit(solution)/shard_map/ppermute | solution.py:25
  132.3 4.2 %collective-permute-done.29.refs_2_ = bf16[112,768]{1,0:T(8,128)(2,1)S(1)} collective-permute-done((bf16[112,768]{1,0:T(8,128)(2,1)S(1)}, bf16[112,768]{1,0:T(8,128)(2,1)S(1)}, u32[]{:S(2)}, u32[]{:S(2)}) %collective-permute-start.29) | collective-permute-done | bytes 172064 | tf_op jit(solution)/shard_map/ppermute | solution.py:25
  136.7 2.3 %collective-permute-start.39 = (bf16[384,768]{1,0:T(8,128)(2,1)S(1)}, bf16[384,768]{1,0:T(8,128)(2,1)S(1)}, u32[]{:S(2)}, u32[]{:S(2)}) collective-permute-start(bf16[384,768]{1,0:T(8,128)(2,1)S(1)} %get-tuple-element.297.refs_3_), channel_id=1, source_target_pairs={{0,8},{4,12},{8,0},{12,4},{16,24},{20,28},{24,16},{28,20},{1,9},{5... | collective-permute-start | bytes 1769480 | tf_op jit(solution)/shard_map/ppermute | solution.py:25
  139.0 5.3 %collective-permute-done.32.refs_2_ = bf16[112,768]{1,0:T(8,128)(2,1)S(1)} collective-permute-done((bf16[112,768]{1,0:T(8,128)(2,1)S(1)}, bf16[112,768]{1,0:T(8,128)(2,1)S(1)}, u32[]{:S(2)}, u32[]{:S(2)}) %collective-permute-start.32) | collective-permute-done | bytes 172064 | tf_op jit(solution)/shard_map/ppermute | solution.py:25
  145.2 1.9 %collective-permute-start.28 = (f32[8,768]{1,0:T(8,128)S(1)}, f32[8,768]{1,0:T(8,128)S(1)}, u32[]{:S(2)}, u32[]{:S(2)}) collective-permute-start(f32[8,768]{1,0:T(8,128)S(1)} %get-tuple-element.279.refs_0_), channel_id=1, source_target_pairs={{0,8},{4,12},{8,0},{12,4},{16,24},{20,28},{24,16},{28,20},{1,9},{5... | collective-permute-start | bytes 73736 | tf_op jit(solution)/shard_map/ppermute | solution.py:25
  147.1 8.8 %collective-permute-done.28.refs_1_ = f32[8,768]{1,0:T(8,128)S(1)} collective-permute-done((f32[8,768]{1,0:T(8,128)S(1)}, f32[8,768]{1,0:T(8,128)S(1)}, u32[]{:S(2)}, u32[]{:S(2)}) %collective-permute-start.28) | collective-permute-done | bytes 24608 | tf_op jit(solution)/shard_map/ppermute | solution.py:25
  157.9 1.5 collective-permute-start.33
  159.5 3.0 %shard_map.406 = (f32[768,768]{1,0:T(8,128)}, f32[768,768]{1,0:T(8,128)}, f32[8,128]{1,0:T(8,128)S(1)}) custom-call(s32[2]{0:T(128)S(1)} %pad_add_fusion.refs_0_, bf16[384,768]{1,0:T(8,128)(2,1)S(1)} %get-tuple-element.296.refs_1_, bf16[384,768]{1,0:T(8,128)(2,1)S(1)} %collective-permute-done.38.refs_2_, bf16[384,768]{1,0:T(8,128)(2,1)S(1)} %get-tuple-element.297.refs_3_, ...), custom_call_target="tpu_custom_call" | custom-call | flops 1250000000 | tf_op jit(solution)/shard_map/pallas_call | solution.py:811
  165.1 2.2 %shard_map.407 = (f32[3,192,768]{2,1,0:T(8,128)}, f32[3,192]{1,0:T(4,128)}, f32[64,192]{1,0:T(8,128)}, f32[192]{0:T(256)}, f32[64,192]{1,0:T(8,128)}, /*index=5*...) custom-call(s32[2]{0:T(128)S(1)} %pad_add_fusion.refs_0_, ...), custom_call_target="tpu_custom_call" | custom-call | flops 1000000000 | tf_op jit(solution)/shard_map/pallas_call | solution.py:811
  (117 shorter events, 21.0 us)
Async XLA Ops:
  3.5 6.6 %collective-permute-start = (bf16[64,384]{1,0:T(8,128)(2,1)S(1)}, bf16[64,384]{1,0:T(8,128)(2,1)S(1)}, u32[]{:S(2)}, u32[]{:S(2)}) collective-permute-start(bf16[64,384]{1,0:T(8,128)(2,1)S(1)} %slice.3), channel_id=1, source_target_pairs={{0,4},{4,8},{8,12},{12,16},{16,20},{20,24},{24,28},{1,5},{5,9},{9,... | collective-permute-start | bytes 147464 | tf_op jit(solution)/shard_map/ppermute | solution.py:21
  12.9 4.5 %collective-permute-start.1 = (bf16[64,384]{1,0:T(8,128)(2,1)S(1)}, bf16[64,384]{1,0:T(8,128)(2,1)S(1)}, u32[]{:S(2)}, u32[]{:S(2)}) collective-permute-start(bf16[64,384]{1,0:T(8,128)(2,1)S(1)} %get-tuple-element.175), channel_id=1, source_target_pairs={{0,4},{4,0},{8,12},{12,8},{16,20},{20,16},{24,28},{28,24},{1,5},{5... | collective-permute-start | bytes 147464 | tf_op jit(solution)/shard_map/ppermute | solution.py:25
  15.4 13.9 %copy-start.8 = (bf16[192,768]{1,0:T(8,128)(2,1)S(1)}, bf16[192,768]{1,0:T(8,128)(2,1)}, u32[]{:S(2)}) copy-start(bf16[192,768]{1,0:T(8,128)(2,1)} %refs_7_.5) | copy-start | bytes 884740
  15.4 13.9 %copy-start.17 = (f32[192]{0:T(256)S(1)}, f32[192]{0:T(256)}, u32[]{:S(2)}) copy-start(f32[192]{0:T(256)} %refs_19_.1) | copy-start | bytes 2308
  18.0 5.1 %collective-permute-start.2 = (bf16[64,384]{1,0:T(8,128)(2,1)S(1)}, bf16[64,384]{1,0:T(8,128)(2,1)S(1)}, u32[]{:S(2)}, u32[]{:S(2)}) collective-permute-start(bf16[64,384]{1,0:T(8,128)(2,1)S(1)} %get-tuple-element.179), channel_id=1, source_target_pairs={{0,8},{4,12},{8,0},{12,4},{16,24},{20,28},{24,16},{28,20},{1,9},{5... | collective-permute-start | bytes 147464 | tf_op jit(solution)/shard_map/ppermute | solution.py:25
  23.7 5.6 %collective-permute-start.3 = (bf16[64,384]{1,0:T(8,128)(2,1)S(1)}, bf16[64,384]{1,0:T(8,128)(2,1)S(1)}, u32[]{:S(2)}, u32[]{:S(2)}) collective-permute-start(bf16[64,384]{1,0:T(8,128)(2,1)S(1)} %get-tuple-element.182), channel_id=1, source_target_pairs={{0,16},{4,20},{8,24},{12,28},{16,0},{20,4},{24,8},{28,12},{1,17},{... | collective-permute-start | bytes 147464 | tf_op jit(solution)/shard_map/ppermute | solution.py:25
  29.3 13.3 %copy-start.5 = (bf16[768,768]{1,0:T(8,128)(2,1)S(1)}, bf16[768,768]{1,0:T(8,128)(2,1)}, u32[]{:S(2)}) copy-start(bf16[768,768]{1,0:T(8,128)(2,1)} %refs_9_.3) | copy-start | bytes 3538948
  32.4 10.2 %copy-start.4 = (bf16[768,768]{1,0:T(8,128)(2,1)S(1)}, bf16[768,768]{1,0:T(8,128)(2,1)}, u32[]{:S(2)}) copy-start(bf16[768,768]{1,0:T(8,128)(2,1)} %refs_7_.4) | copy-start | bytes 3538948
  32.4 10.2 %copy-start.7 = (bf16[2,128,768]{2,1,0:T(8,128)(2,1)S(1)}, bf16[2,128,768]{2,1,0:T(8,128)(2,1)}, u32[]{:S(2)}) copy-start(bf16[2,128,768]{2,1,0:T(8,128)(2,1)} %refs_1_.4) | copy-start | bytes 1179652
  32.4 1.5 collective-permute-start.4
  34.0 7.0 %collective-permute-start.5 = (bf16[128,768]{1,0:T(8,128)(2,1)S(1)}, bf16[128,768]{1,0:T(8,128)(2,1)S(1)}, u32[]{:S(2)}, u32[]{:S(2)}) collective-permute-start(bf16[128,768]{1,0:T(8,128)(2,1)S(1)} %get-tuple-element.190), channel_id=1, source_target_pairs={{0,2},{1,3},{2,0},{3,1},{4,6},{5,7},{6,4},{7,5},{8,10},{9,11},{10,... | collective-permute-start | bytes 589832 | tf_op jit(solution)/shard_map/ppermute | solution.py:25
  41.1 1.5 collective-permute-start.6
  46.3 2.3 %collective-permute-start.7 = (bf16[128,768]{1,0:T(8,128)(2,1)S(1)}, bf16[128,768]{1,0:T(8,128)(2,1)S(1)}, u32[]{:S(2)}, u32[]{:S(2)}) collective-permute-start(bf16[128,768]{1,0:T(8,128)(2,1)S(1)} %get-tuple-element.198), channel_id=1, source_target_pairs={{0,1},{1,0},{2,3},{3,2},{4,5},{5,4},{6,7},{7,6},{8,9},{9,8},{10,11... | collective-permute-start | bytes 589832 | tf_op jit(solution)/shard_map/ppermute | solution.py:25
  46.5 15.6 %collective-permute-start.11 = (bf16[384,768]{1,0:T(8,128)(2,1)S(1)}, bf16[384,768]{1,0:T(8,128)(2,1)S(1)}, u32[]{:S(2)}, u32[]{:S(2)}) collective-permute-start(bf16[384,768]{1,0:T(8,128)(2,1)S(1)} %get-tuple-element.214), channel_id=1, source_target_pairs={{0,4},{4,0},{8,12},{12,8},{16,20},{20,16},{24,28},{28,24},{1,5},{5... | collective-permute-start | bytes 1769480 | tf_op jit(solution)/shard_map/ppermute | solution.py:25
  47.2 15.3 %collective-permute-start.12 = (bf16[384,768]{1,0:T(8,128)(2,1)S(1)}, bf16[384,768]{1,0:T(8,128)(2,1)S(1)}, u32[]{:S(2)}, u32[]{:S(2)}) collective-permute-start(bf16[384,768]{1,0:T(8,128)(2,1)S(1)} %get-tuple-element.215), channel_id=1, source_target_pairs={{0,8},{4,12},{8,0},{12,4},{16,24},{20,28},{24,16},{28,20},{1,9},{5... | collective-permute-start | bytes 1769480 | tf_op jit(solution)/shard_map/ppermute | solution.py:25
  48.7 6.7 %collective-permute-start.8 = (bf16[128,768]{1,0:T(8,128)(2,1)S(1)}, bf16[128,768]{1,0:T(8,128)(2,1)S(1)}, u32[]{:S(2)}, u32[]{:S(2)}) collective-permute-start(bf16[128,768]{1,0:T(8,128)(2,1)S(1)} %get-tuple-element.201), channel_id=1, source_target_pairs={{0,2},{1,3},{2,0},{3,1},{4,6},{5,7},{6,4},{7,5},{8,10},{9,11},{10,... | collective-permute-start | bytes 589832 | tf_op jit(solution)/shard_map/ppermute | solution.py:25
  55.4 1.5 collective-permute-start.9
  59.3 4.2 %collective-permute-start.10 = (bf16[64,384]{1,0:T(8,128)(2,1)S(1)}, bf16[64,384]{1,0:T(8,128)(2,1)S(1)}, u32[]{:S(2)}, u32[]{:S(2)}) collective-permute-start(bf16[64,384]{1,0:T(8,128)(2,1)S(1)} %get-tuple-element.211), channel_id=1, source_target_pairs={{0,4},{4,0},{8,12},{12,8},{16,20},{20,16},{24,28},{28,24},{1,5},{5... | collective-permute-start | bytes 147464 | tf_op jit(solution)/shard_map/ppermute | solution.py:25
  64.1 4.6 %collective-permute-start.13 = (bf16[64,384]{1,0:T(8,128)(2,1)S(1)}, bf16[64,384]{1,0:T(8,128)(2,1)S(1)}, u32[]{:S(2)}, u32[]{:S(2)}) collective-permute-start(bf16[64,384]{1,0:T(8,128)(2,1)S(1)} %get-tuple-element.223), channel_id=1, source_target_pairs={{0,8},{4,12},{8,0},{12,4},{16,24},{20,28},{24,16},{28,20},{1,9},{5... | collective-permute-start | bytes 147464 | tf_op jit(solution)/shard_map/ppermute | solution.py:25
  65.5 12.6 %collective-permute-start.15 = (bf16[192,768]{1,0:T(8,128)(2,1)S(1)}, bf16[192,768]{1,0:T(8,128)(2,1)S(1)}, u32[]{:S(2)}, u32[]{:S(2)}) collective-permute-start(bf16[192,768]{1,0:T(8,128)(2,1)S(1)} %get-tuple-element.236), channel_id=1, source_target_pairs={{0,8},{4,12},{8,0},{12,4},{16,24},{20,28},{24,16},{28,20},{1,9},{5... | collective-permute-start | bytes 884744 | tf_op jit(solution)/shard_map/ppermute | solution.py:25
  66.2 12.0 %collective-permute-start.16 = (bf16[192,768]{1,0:T(8,128)(2,1)S(1)}, bf16[192,768]{1,0:T(8,128)(2,1)S(1)}, u32[]{:S(2)}, u32[]{:S(2)}) collective-permute-start(bf16[192,768]{1,0:T(8,128)(2,1)S(1)} %get-tuple-element.237), channel_id=1, source_target_pairs={{0,4},{4,0},{8,12},{12,8},{16,20},{20,16},{24,28},{28,24},{1,5},{5... | collective-permute-start | bytes 884744 | tf_op jit(solution)/shard_map/ppermute | solution.py:25
  69.3 9.8 %collective-permute-start.14 = (bf16[64,384]{1,0:T(8,128)(2,1)S(1)}, bf16[64,384]{1,0:T(8,128)(2,1)S(1)}, u32[]{:S(2)}, u32[]{:S(2)}) collective-permute-start(bf16[64,384]{1,0:T(8,128)(2,1)S(1)} %get-tuple-element.228), channel_id=1, source_target_pairs={{0,16},{4,20},{8,24},{12,28},{16,0},{20,4},{24,8},{28,12},{1,17},{... | collective-permute-start | bytes 147464 | tf_op jit(solution)/shard_map/ppermute | solution.py:25
  78.9 14.0 %collective-permute-start.18 = (bf16[192,768]{1,0:T(8,128)(2,1)S(1)}, bf16[192,768]{1,0:T(8,128)(2,1)S(1)}, u32[]{:S(2)}, u32[]{:S(2)}) collective-permute-start(bf16[192,768]{1,0:T(8,128)(2,1)S(1)} %get-tuple-element.251), channel_id=1, source_target_pairs={{0,16},{4,20},{8,24},{12,28},{16,0},{20,4},{24,8},{28,12},{1,17},{... | collective-permute-start | bytes 884744 | tf_op jit(solution)/shard_map/ppermute | solution.py:25
  79.0 14.0 %copy-start = (bf16[3,768,192]{1,2,0:T(8,128)(2,1)S(1)}, bf16[3,768,192]{1,2,0:T(8,128)(2,1)}, u32[]{:S(2)}) copy-start(bf16[3,768,192]{1,2,0:T(8,128)(2,1)} %param.27) | copy-start | bytes 2654212
  84.0 9.0 %collective-permute-start.17 = (bf16[64,384]{1,0:T(8,128)(2,1)S(1)}, bf16[64,384]{1,0:T(8,128)(2,1)S(1)}, u32[]{:S(2)}, u32[]{:S(2)}) collective-permute-start(bf16[64,384]{1,0:T(8,128)(2,1)S(1)} %get-tuple-element.241), channel_id=1, source_target_pairs={{4,0},{8,4},{12,8},{16,12},{20,16},{24,20},{28,24},{5,1},{9,5},{13... | collective-permute-start | bytes 147464 | tf_op jit(solution)/shard_map/ppermute | solution.py:21
  94.6 1.8 %collective-permute-start.19 = (bf16[256,768]{1,0:T(8,128)(2,1)S(1)}, bf16[256,768]{1,0:T(8,128)(2,1)S(1)}, u32[]{:S(2)}, u32[]{:S(2)}) collective-permute-start(bf16[256,768]{1,0:T(8,128)(2,1)S(1)} %get-tuple-element.255), channel_id=1, source_target_pairs={{0,1},{1,0},{2,3},{3,2},{4,5},{5,4},{6,7},{7,6},{8,9},{9,8},{10,11... | collective-permute-start | bytes 1179656 | tf_op jit(solution)/shard_map/ppermute | solution.py:25
  96.5 24.2 %copy-start.14 = (f32[768]{0:T(1024)S(1)}, f32[768]{0:T(1024)}, u32[]{:S(2)}) copy-start(f32[768]{0:T(1024)} %refs_5_.7) | copy-start | bytes 9220
  96.5 24.2 %copy-start.15 = (f32[768]{0:T(1024)S(1)}, f32[768]{0:T(1024)}, u32[]{:S(2)}) copy-start(f32[768]{0:T(1024)} %refs_8_.3) | copy-start | bytes 9220
  96.5 16.7 %collective-permute-start.20 = (bf16[256,768]{1,0:T(8,128)(2,1)S(1)}, bf16[256,768]{1,0:T(8,128)(2,1)S(1)}, u32[]{:S(2)}, u32[]{:S(2)}) collective-permute-start(bf16[256,768]{1,0:T(8,128)(2,1)S(1)} %get-tuple-element.258), channel_id=1, source_target_pairs={{0,2},{1,3},{2,0},{3,1},{4,6},{5,7},{6,4},{7,5},{8,10},{9,11},{10,... | collective-permute-start | bytes 1179656 | tf_op jit(solution)/shard_map/ppermute | solution.py:25
  98.1 14.4 %collective-permute-start.21 = (bf16[192,768]{1,0:T(8,128)(2,1)S(1)}, bf16[192,768]{1,0:T(8,128)(2,1)S(1)}, u32[]{:S(2)}, u32[]{:S(2)}) collective-permute-start(bf16[192,768]{1,0:T(8,128)(2,1)S(1)} %get-tuple-element.259.refs_1_), channel_id=1, source_target_pairs={{0,16},{4,20},{8,24},{12,28},{16,0},{20,4},{24,8},{28,12},{1,17},{... | collective-permute-start | bytes 884744 | tf_op jit(solution)/shard_map/ppermute | solution.py:25
  98.1 15.3 %collective-permute-start.23 = (bf16[224,768]{1,0:T(8,128)(2,1)S(1)}, bf16[224,768]{1,0:T(8,128)(2,1)S(1)}, u32[]{:S(2)}, u32[]{:S(2)}) collective-permute-start(bf16[224,768]{1,0:T(8,128)(2,1)S(1)} %get-tuple-element.266), channel_id=1, source_target_pairs={{0,4},{4,0},{8,12},{12,8},{16,20},{20,16},{24,28},{28,24},{1,5},{5... | collective-permute-start | bytes 1032200 | tf_op jit(solution)/shard_map/ppermute | solution.py:25
  100.3 15.5 %collective-permute-start.24 = (bf16[224,768]{1,0:T(8,128)(2,1)S(1)}, bf16[224,768]{1,0:T(8,128)(2,1)S(1)}, u32[]{:S(2)}, u32[]{:S(2)}) collective-permute-start(bf16[224,768]{1,0:T(8,128)(2,1)S(1)} %get-tuple-element.267), channel_id=1, source_target_pairs={{0,8},{4,12},{8,0},{12,4},{16,24},{20,28},{24,16},{28,20},{1,9},{5... | collective-permute-start | bytes 1032200 | tf_op jit(solution)/shard_map/ppermute | solution.py:25
  113.3 7.4 %collective-permute-start.22 = (bf16[256,768]{1,0:T(8,128)(2,1)S(1)}, bf16[256,768]{1,0:T(8,128)(2,1)S(1)}, u32[]{:S(2)}, u32[]{:S(2)}) collective-permute-start(bf16[256,768]{1,0:T(8,128)(2,1)S(1)} %get-tuple-element.262.refs_2_), channel_id=1, source_target_pairs={{0,1},{1,0},{2,3},{3,2},{4,5},{5,4},{6,7},{7,6},{8,9},{9,8},{10,11... | collective-permute-start | bytes 1179656 | tf_op jit(solution)/shard_map/ppermute | solution.py:25
  116.5 7.2 %collective-permute-start.26 = (bf16[112,768]{1,0:T(8,128)(2,1)S(1)}, bf16[112,768]{1,0:T(8,128)(2,1)S(1)}, u32[]{:S(2)}, u32[]{:S(2)}) collective-permute-start(bf16[112,768]{1,0:T(8,128)(2,1)S(1)} %get-tuple-element.275), channel_id=1, source_target_pairs={{0,8},{4,12},{8,0},{12,4},{16,24},{20,28},{24,16},{28,20},{1,9},{5... | collective-permute-start | bytes 516104 | tf_op jit(solution)/shard_map/ppermute | solution.py:25
  116.6 7.2 %collective-permute-start.27 = (bf16[112,768]{1,0:T(8,128)(2,1)S(1)}, bf16[112,768]{1,0:T(8,128)(2,1)S(1)}, u32[]{:S(2)}, u32[]{:S(2)}) collective-permute-start(bf16[112,768]{1,0:T(8,128)(2,1)S(1)} %get-tuple-element.276), channel_id=1, source_target_pairs={{0,4},{4,0},{8,12},{12,8},{16,20},{20,16},{24,28},{28,24},{1,5},{5... | collective-permute-start | bytes 516104 | tf_op jit(solution)/shard_map/ppermute | solution.py:25
  117.3 14.1 %collective-permute-start.30 = (bf16[192,768]{1,0:T(8,128)(2,1)S(1)}, bf16[192,768]{1,0:T(8,128)(2,1)S(1)}, u32[]{:S(2)}, u32[]{:S(2)}) collective-permute-start(bf16[192,768]{1,0:T(8,128)(2,1)S(1)} %get-tuple-element.283.refs_1_), channel_id=1, source_target_pairs={{0,8},{4,12},{8,0},{12,4},{16,24},{20,28},{24,16},{28,20},{1,9},{5... | collective-permute-start | bytes 884744 | tf_op jit(solution)/shard_map/ppermute | solution.py:25
  118.8 12.6 %collective-permute-start.31 = (bf16[192,768]{1,0:T(8,128)(2,1)S(1)}, bf16[192,768]{1,0:T(8,128)(2,1)S(1)}, u32[]{:S(2)}, u32[]{:S(2)}) collective-permute-start(bf16[192,768]{1,0:T(8,128)(2,1)S(1)} %get-tuple-element.284.refs_2_), channel_id=1, source_target_pairs={{0,4},{4,0},{8,12},{12,8},{16,20},{20,16},{24,28},{28,24},{1,5},{5... | collective-permute-start | bytes 884744 | tf_op jit(solution)/shard_map/ppermute | solution.py:25
  124.4 12.0 %collective-permute-start.29 = (bf16[112,768]{1,0:T(8,128)(2,1)S(1)}, bf16[112,768]{1,0:T(8,128)(2,1)S(1)}, u32[]{:S(2)}, u32[]{:S(2)}) collective-permute-start(bf16[112,768]{1,0:T(8,128)(2,1)S(1)} %get-tuple-element.282), channel_id=1, source_target_pairs={{0,16},{4,20},{8,24},{12,28},{16,0},{20,4},{24,8},{28,12},{1,17},{... | collective-permute-start | bytes 516104 | tf_op jit(solution)/shard_map/ppermute | solution.py:25
  127.6 3.8 %collective-permute-start.25 = (f32[8,768]{1,0:T(8,128)S(1)}, f32[8,768]{1,0:T(8,128)S(1)}, u32[]{:S(2)}, u32[]{:S(2)}) collective-permute-start(f32[8,768]{1,0:T(8,128)S(1)} %get-tuple-element.272.refs_0_), channel_id=1, source_target_pairs={{0,4},{4,0},{8,12},{12,8},{16,20},{20,16},{24,28},{28,24},{1,5},{5... | collective-permute-start | bytes 73736 | tf_op jit(solution)/shard_map/ppermute | solution.py:25
  136.5 7.8 %collective-permute-start.32 = (bf16[112,768]{1,0:T(8,128)(2,1)S(1)}, bf16[112,768]{1,0:T(8,128)(2,1)S(1)}, u32[]{:S(2)}, u32[]{:S(2)}) collective-permute-start(bf16[112,768]{1,0:T(8,128)(2,1)S(1)} %get-tuple-element.287.refs_1_), channel_id=1, source_target_pairs={{0,16},{4,20},{8,24},{12,28},{16,0},{20,4},{24,8},{28,12},{1,17},{... | collective-permute-start | bytes 516104 | tf_op jit(solution)/shard_map/ppermute | solution.py:25
  136.6 22.8 %collective-permute-start.38 = (bf16[384,768]{1,0:T(8,128)(2,1)S(1)}, bf16[384,768]{1,0:T(8,128)(2,1)S(1)}, u32[]{:S(2)}, u32[]{:S(2)}) collective-permute-start(bf16[384,768]{1,0:T(8,128)(2,1)S(1)} %get-tuple-element.296.refs_1_), channel_id=1, source_target_pairs={{0,4},{4,0},{8,12},{12,8},{16,20},{20,16},{24,28},{28,24},{1,5},{5... | collective-permute-start | bytes 1769480 | tf_op jit(solution)/shard_map/ppermute | solution.py:25
  136.7 22.8 %collective-permute-start.39 = (bf16[384,768]{1,0:T(8,128)(2,1)S(1)}, bf16[384,768]{1,0:T(8,128)(2,1)S(1)}, u32[]{:S(2)}, u32[]{:S(2)}) collective-permute-start(bf16[384,768]{1,0:T(8,128)(2,1)S(1)} %get-tuple-element.297.refs_3_), channel_id=1, source_target_pairs={{0,8},{4,12},{8,0},{12,4},{16,24},{20,28},{24,16},{28,20},{1,9},{5... | collective-permute-start | bytes 1769480 | tf_op jit(solution)/shard_map/ppermute | solution.py:25
  145.0 10.9 %collective-permute-start.34 = (bf16[112,768]{1,0:T(8,128)(2,1)S(1)}, bf16[112,768]{1,0:T(8,128)(2,1)S(1)}, u32[]{:S(2)}, u32[]{:S(2)}) collective-permute-start(bf16[112,768]{1,0:T(8,128)(2,1)S(1)} %get-tuple-element.291.refs_1_), channel_id=1, source_target_pairs={{0,8},{4,12},{8,0},{12,4},{16,24},{20,28},{24,16},{28,20},{1,9},{5... | collective-permute-start | bytes 516104 | tf_op jit(solution)/shard_map/ppermute | solution.py:25
  145.1 10.8 %collective-permute-start.35 = (bf16[112,768]{1,0:T(8,128)(2,1)S(1)}, bf16[112,768]{1,0:T(8,128)(2,1)S(1)}, u32[]{:S(2)}, u32[]{:S(2)}) collective-permute-start(bf16[112,768]{1,0:T(8,128)(2,1)S(1)} %get-tuple-element.292.refs_2_), channel_id=1, source_target_pairs={{0,4},{4,0},{8,12},{12,8},{16,20},{20,16},{24,28},{28,24},{1,5},{5... | collective-permute-start | bytes 516104 | tf_op jit(solution)/shard_map/ppermute | solution.py:25
  145.2 10.7 %collective-permute-start.28 = (f32[8,768]{1,0:T(8,128)S(1)}, f32[8,768]{1,0:T(8,128)S(1)}, u32[]{:S(2)}, u32[]{:S(2)}) collective-permute-start(f32[8,768]{1,0:T(8,128)S(1)} %get-tuple-element.279.refs_0_), channel_id=1, source_target_pairs={{0,8},{4,12},{8,0},{12,4},{16,24},{20,28},{24,16},{28,20},{1,9},{5... | collective-permute-start | bytes 73736 | tf_op jit(solution)/shard_map/ppermute | solution.py:25
  156.6 7.3 %collective-permute-start.36 = (bf16[224,768]{1,0:T(8,128)(2,1)S(1)}, bf16[224,768]{1,0:T(8,128)(2,1)S(1)}, u32[]{:S(2)}, u32[]{:S(2)}) collective-permute-start(bf16[224,768]{1,0:T(8,128)(2,1)S(1)} %get-tuple-element.294.refs_3_), channel_id=1, source_target_pairs={{0,4},{4,0},{8,12},{12,8},{16,20},{20,16},{24,28},{28,24},{1,5},{5... | collective-permute-start | bytes 1032200 | tf_op jit(solution)/shard_map/ppermute | solution.py:25
  157.6 7.5 %collective-permute-start.37 = (bf16[224,768]{1,0:T(8,128)(2,1)S(1)}, bf16[224,768]{1,0:T(8,128)(2,1)S(1)}, u32[]{:S(2)}, u32[]{:S(2)}) collective-permute-start(bf16[224,768]{1,0:T(8,128)(2,1)S(1)} %get-tuple-element.295.refs_5_), channel_id=1, source_target_pairs={{0,8},{4,12},{8,0},{12,4},{16,24},{20,28},{24,16},{28,20},{1,9},{5... | collective-permute-start | bytes 1032200 | tf_op jit(solution)/shard_map/ppermute | solution.py:25
  157.9 5.0 %collective-permute-start.33 = (f32[8,768]{1,0:T(8,128)S(1)}, f32[8,768]{1,0:T(8,128)S(1)}, u32[]{:S(2)}, u32[]{:S(2)}) collective-permute-start(f32[8,768]{1,0:T(8,128)S(1)} %get-tuple-element.290.refs_1_), channel_id=1, source_target_pairs={{0,16},{4,20},{8,24},{12,28},{16,0},{20,4},{24,8},{28,12},{1,17},{... | collective-permute-start | bytes 73736 | tf_op jit(solution)/shard_map/ppermute | solution.py:25
  (12 other events, 100.7 us)

commit v4 on v3

--- a/solution.py
+++ b/solution.py
@@ -11,8 +11,8 @@
 f32 = jnp.float32
 bf16 = jnp.bfloat16
 LANES = 128
-ORDER = "mmmmEMmmMmMmmMmLmLNMLLNLN"
-FLOPS_PER_US = 0.5e9
+ORDER = "mmmmEmMmMmMmmMmLmLNMLLNLN"
+FLOPS_PER_US = 0.54e9
 SUBS = 8
 
 
@@ -105,15 +105,45 @@
         mask *= 2
 
 
-def sum_steps(call, rows, axis):
-    mask = 1
+def plain_head_total(keep, send, axis="head"):
+    total = keep.astype(f32) + swapped(send, axis, 1).astype(f32)
+    mask = 2
+    while mask < lax.axis_size(axis):
+        total = total + swapped(total.astype(bf16), axis, mask).astype(f32)
+        mask *= 2
+    low = total.astype(bf16)
+    return low, swapped(low, axis, 1)
+
+
+def plain_carry(total, low, whole, place, axis):
+    carry = jnp.zeros_like(total)
+    mask, step = 1, whole
     while True:
+        got = swapped(low, axis, mask)
+        if 2 * mask >= lax.axis_size(axis):
+            return carry, got
+        far = (place & mask) > 0
+        power, bit, base = jnp.ones_like(whole), 1, whole
+        while bit < mask:
+            power = jnp.where((place & bit) > 0, power * base, power)
+            base = base * base
+            bit *= 2
+        got = got.astype(f32)
+        carry = carry + jnp.where(far, power, 0.0) * got
+        total = jnp.where(far, step, 1.0) * got + jnp.where(far, 1.0, step) * total
+        low = total.astype(bf16)
+        step = step * step
+        mask *= 2
+
+
+def sum_steps(call, rows, masks, axis):
+    for mask in masks[:-1]:
         got = swapped(rows, axis, mask)
         yield
-        mask *= 2
-        if mask >= lax.axis_size(axis):
-            return rows, got
         (rows,) = call(plain_add_kernel, [like(rows.shape)], [rows, got], limit=4)
+    got = swapped(rows, axis, masks[-1])
+    yield
+    return rows, got
 
 
 def ran(steps):
@@ -519,52 +549,54 @@
     front_low_ref[...] = front_ref[...].astype(bf16)
 
 
-def local_kernel(
-    u_ref, gs_ref, decay_ref, weight_ref, start_ref,
-    out_ref, gain_ref, power_ref, reach_ref, part_ref, past_ref,
-):
-    rows = u_ref.shape[0]
-    blocks = rows // SUBS
-    states = decay_ref.shape[0]
+def reach_kernel(u_ref, decay_ref, reach_ref):
+    blocks = u_ref.shape[0] // SUBS
     for lanes in lane_tiles(u_ref.shape[1]):
         decay = decay_ref[:, lanes]
-        weight = weight_ref[:, lanes]
 
         def rise(lap, carry, lanes=lanes, decay=decay):
             state, reach = carry
             tile = u_ref[rows_at(lap * SUBS, SUBS), lanes]
             for r in range(SUBS):
-                past_ref[rows_at(lap * SUBS * states + r * states, states), :] = state
                 reach = decay * (reach + state)
                 state = decay * state + tile[r : r + 1, :]
             return state, reach
 
         zero = jnp.zeros_like(decay)
-        _, reach = lax.fori_loop(0, blocks, rise, (start_ref[:, lanes], zero))
-        reach_ref[:, lanes] = reach
+        reach_ref[:, lanes] = lax.fori_loop(0, blocks, rise, (zero, zero))[1]
+
+
+def local_kernel(
+    u_ref, gs_ref, decay_ref, weight_ref, start_ref, out_ref, gain_ref, power_ref, part_ref
+):
+    rows = u_ref.shape[0]
+    blocks = rows // SUBS
+    for lanes in lane_tiles(u_ref.shape[1]):
+        decay = decay_ref[:, lanes]
+        weight = weight_ref[:, lanes]
 
         def fall(lap, carry, lanes=lanes, decay=decay, weight=weight):
-            adjoint, gain, power = carry
+            adjoint, slope, gain, power = carry
             place = blocks - 1 - lap
             tile = u_ref[rows_at(place * SUBS, SUBS), lanes]
             grads = gs_ref[rows_at(place * SUBS, SUBS), lanes]
             for r in range(SUBS - 1, -1, -1):
+                slope = decay * slope + adjoint
                 adjoint = decay * adjoint + grads[r : r + 1, :]
                 part_ref[rows_at(place * SUBS * SUBS + r * SUBS, SUBS), :] = folded(weight * adjoint)
                 gain = gain + adjoint * tile[r : r + 1, :]
-                power = power + adjoint * past_ref[
-                    rows_at(place * SUBS * states + r * states, states), :
-                ]
-            return adjoint, gain, power
-
-        _, gain, power = lax.fori_loop(0, blocks, fall, (zero, zero, zero))
+                power = power + slope * tile[r : r + 1, :]
+            return adjoint, slope, gain, power
+
+        zero = jnp.zeros_like(decay)
+        adjoint, slope, gain, power = lax.fori_loop(0, blocks, fall, (zero, zero, zero, zero))
         gain_ref[:, lanes] = gain
-        power_ref[:, lanes] = power
+        power_ref[:, lanes] = power + start_ref[:, lanes] * (decay * slope + adjoint)
         out_ref[:, lanes] = part_total(part_ref, rows)
 
 
 def unmix_kernel(
-    mask, spot_ref, gloc_ref, gs_ref, u_ref, decay_ref, weight_ref, whole_ref, got_ref, carry_ref, gain_ref, power_ref, reach_ref,
+    mask, spot_ref, gloc_ref, gs_ref, u_ref, decay_ref, weight_ref, whole_ref, got_ref, carry_ref, gain_ref, power_ref, reach_ref, start_ref,
     end_ref, v_ref, shifted_ref, edge_ref, k_ref, taps_ref, shift_skip_ref, ssm_skip_ref,
     in_ref, out_ref, root_ref, slope_ref, fall_ref, a_ref, step_ref,
     gk_ref, halo_ref, gv_ref, small_ref, misc_ref,
@@ -637,7 +669,8 @@
                 sums_ref[SUBS * i : SUBS * (i + 1), :] = folded(product)
         tap_ref[0 : taps + 1, lanes] = part_total(sums_ref, taps + 1)
     gain = gain_ref[...] + behind_ref[...] * decay_ref[...] * end_ref[...]
-    power = power_ref[...] + behind_ref[...] * reach_ref[...]
+    reach = reach_ref[...] + rows * whole_ref[...] * start_ref[...]
+    power = power_ref[...] + behind_ref[...] * reach
 
     def slots_total(array):
         total = slot_of(array, 0, chans)
@@ -909,8 +942,6 @@
         [pltpu.VMEM((taps + rows, width), f32), pltpu.VMEM((taps + SUBS, width), f32)],
         us=2.9,
     )
-    steps = carry_steps(call, end_local, end_low, whole_wide, spot, "seq", False)
-    next(steps)
     low_out, grad_b_down = call(
         masked_kernel,
         [like((tokens, model), bf16), like((1, model))],
@@ -918,7 +949,7 @@
         us=0.8,
         scalars=2,
     )
-    carry, got = ran(steps)
+    carry, got = plain_carry(end_local, end_low, whole_wide, spot[:1].reshape(1, 1), "seq")
     ssm_out, gated, start_state, keep, send = call(
         functools.partial(attend_kernel, last_mask),
         [like((rows, width)), like((tokens, chans), bf16), like((states, width)), half_like, half_like],
@@ -930,7 +961,7 @@
         us=2.9,
         scalars=1,
     )
-    own, other = ran(head_steps(call, keep, send))
+    own, other = plain_head_total(keep, send)
     middle, back_keep, back_send, out_keep, out_send, grad_b_up, up_keep, up_send, down_keep, down_send = call(
         functools.partial(feed_kernel, *ends),
         [
@@ -996,11 +1027,19 @@
     def entry_work():
         while entry_parts is None:
             yield
-        return (yield from sum_steps(call, entry_parts, "seq"))
+        return (yield from sum_steps(call, entry_parts, masks[:1] + masks[:0:-1], "seq"))
 
     def main_work():
         nonlocal low_middle, grad_queries, last_parts, entry_parts, grad_inputs, layer_out, last_rows
-        own, other = yield from head_steps(call, back_keep, back_send)
+        joins = head_steps(call, back_keep, back_send)
+        next(joins)
+        yield
+        next(joins)
+        (reach,) = call(
+            reach_kernel, [like((states, width))], [series, decay_wide], us=2.0
+        )
+        yield
+        own, other = ran(joins)
         grad_middle, low_middle, grad_queries, grad_ssm, front_local, front_low, norm_rows = call(
             middle_kernel,
             [
@@ -1016,18 +1055,18 @@
                 spot, lengths, own, other, middle, cotangent, ln2_gain, output_weight, ssm_out, queries,
                 decay_wide,
             ],
-            us=2.5,
+            us=3.00,
             scalars=2,
         )
         yield
         steps = carry_steps(call, front_local, front_low, whole_wide, spot, "seq", True)
         carry, got = yield from steps
-        grad_local, gain_local, power_local, reach = call(
+        grad_local, gain_local, power_local = call(
             local_kernel,
-            [like((rows, width)), like((states, width)), like((states, width)), like((states, width))],
+            [like((rows, width)), like((states, width)), like((states, width))],
             [series, grad_ssm, decay_wide, weight_wide, start_state],
-            [pltpu.VMEM((rows * SUBS, LANES), f32), pltpu.VMEM((rows * states, LANES), f32)],
-            us=5.8,
+            [pltpu.VMEM((rows * SUBS, LANES), f32)],
+            us=4.8,
         )
         yield
         grad_keys, halo, grad_values, small, misc = call(
@@ -1041,7 +1080,7 @@
             ],
             [
                 spot, grad_local, grad_ssm, series, decay_wide, weight_wide, whole_wide, got, carry,
-                gain_local, power_local, reach, end_local, values, shifted_keys, edge, keys, shift_taps,
+                gain_local, power_local, reach, start_state, end_local, values, shifted_keys, edge, keys, shift_taps,
                 shift_skip, ssm_skip, in_weight, turned_c, gain_root, slope, fall, ssm_a.T, ssm_step,
             ],
             [
@@ -1071,7 +1110,7 @@
                 misc, norm_rows, grad_b_up, grad_b_down,
             ],
             [pltpu.VMEM((last_rows, model), f32)],
-            us=1.5,
+            us=0.45,
             scalars=1,
         )
         last_parts = (one, one_send, two, two_send)
@@ -1083,7 +1122,7 @@
             [like((tokens, model)), like((SUBS, model)), like(inputs.shape)],
             [spot, lengths, own, other, flat_inputs, ln1_gain, grad_middle, middle, b_down],
             scalars=2,
-            us=3.0,
+            us=0.90,
         )
         entry_parts = rows_sum
         step("N")

time: 168 us -> 166 us (0.988)
  waiting for transfers between devices: 72.7 us -> 66.8 us
  starting transfers between devices: 48.2 us -> 52.7 us
    ppermute x38, waiting for transfers between devices: 71.3 us -> 65.3 us  [swapped(): lax.ppermute(shard, axis, [(i, i ^ mask) for i in range(lax.axis_size(axi...]
    ppermute x38, starting transfers between devices: 41.8 us -> 46.5 us  [swapped(): lax.ppermute(shard, axis, [(i, i ^ mask) for i in range(lax.axis_size(axi...]
    pallas_call x35 -> x32, Pallas kernels: 44.5 us -> 43.9 us  [call(): pl.pallas_call(body, in_specs=specs, out_shape=tuple(outs) + (like((SUBS,...]
  transfers between devices with their start and end apart: 40 -> 40, of which waited for: 25 -> 23; matrix products, arithmetic and copies ran while one was open for 0% -> 0% of each run, Pallas kernels for 16% -> 17%
where the time goes in v4:
time: 166 us
  waiting for transfers between devices  66.8 us (40%)
  starting transfers between devices  52.7 us (32%)
  Pallas kernels  43.9 us (26%)
    ppermute x38, waiting for transfers between devices, swapped(): lax.ppermute(shard, axis, [(i, i ^ mask) for i in range(lax.axis_size(axi...  65.3 us
    ppermute x38, starting transfers between devices, swapped(): lax.ppermute(shard, axis, [(i, i ^ mask) for i in range(lax.axis_size(axi...  46.5 us
    pallas_call x32, Pallas kernels, call(): pl.pallas_call(body, in_specs=specs, out_shape=tuple(outs) + (like((SUBS,...  43.9 us
    ppermute x2, starting transfers between devices, shifted(): lax.ppermute(shard, axis, [(i, i + by) for i in range(peers) if 0 <= i +...  6.16 us
  transfers between devices with their start and end apart: 40, of which 23 were waited for; matrix products, arithmetic and copies ran while one was open for 0% of the time, Pallas kernels for 17%

profile of v4, /device:TPU:0, one launch (start us, length us, event | category | flops | bytes accessed | tf_op | source)
XLA Modules:
  0.0 165.6 jit_solution(12099213451546115459)
XLA Ops:
  0.8 2.7 %shard_map.373 = (bf16[256,768]{1,0:T(8,128)(2,1)S(1)}, f32[128,384]{1,0:T(8,128)S(1)}, bf16[128,384]{1,0:T(8,128)(2,1)S(1)}, f32[128,384]{1,0:T(8,128)S(1)}, f32[8,128]{1,0:T(8,128)S(1)}) custom-call(s32[2]{0:T(128)S(1)} %pad_add_fusion.refs_0_, bf16[2,128,768]{2,1,0:T(8,128)(2,1)} %refs_1_.4, f32[768]{0:T(1024)} %refs_5_.7, f32[768]{0:T(1024)} %refs_3_.2, ...), custom_call_target="tpu_custom_call" | custom-call | flops 1080000000 | tf_op jit(solution)/shard_map/pallas_call | solution.py:844
  3.5 4.9 %collective-permute-start = (bf16[64,384]{1,0:T(8,128)(2,1)S(1)}, bf16[64,384]{1,0:T(8,128)(2,1)S(1)}, u32[]{:S(2)}, u32[]{:S(2)}) collective-permute-start(bf16[64,384]{1,0:T(8,128)(2,1)S(1)} %slice.3), channel_id=1, source_target_pairs={{0,4},{4,8},{8,12},{12,16},{16,20},{20,24},{24,28},{1,5},{5,9},{9,... | collective-permute-start | bytes 147464 | tf_op jit(solution)/shard_map/ppermute | solution.py:21
  8.6 1.5 collective-permute-done.refs_0_.refs_16_
  10.1 2.6 %shard_map.374 = (f32[128,384]{1,0:T(8,128)S(1)}, f32[128,384]{1,0:T(8,128)S(1)}, f32[64,384]{1,0:T(8,128)S(1)}, bf16[64,384]{1,0:T(8,128)(2,1)S(1)}, f32[8,128]{1,0:T(8,128)S(1)}) custom-call(bf16[64,384]{1,0:T(8,128)(2,1)S(1)} %collective-permute-done.refs_0_.refs_16_, bf16[128,384]{1,0:T(8,128)(2,1)S(1)} %get-tuple-element.159.refs_1_.refs_17_, ...), custom_call_target="tpu_custom_call" | custom-call | flops 1566000000 | tf_op jit(solution)/shard_map/pallas_call | solution.py:844
  12.7 2.4 %collective-permute-start.1 = (bf16[64,384]{1,0:T(8,128)(2,1)S(1)}, bf16[64,384]{1,0:T(8,128)(2,1)S(1)}, u32[]{:S(2)}, u32[]{:S(2)}) collective-permute-start(bf16[64,384]{1,0:T(8,128)(2,1)S(1)} %get-tuple-element.163), channel_id=1, source_target_pairs={{0,4},{4,0},{8,12},{12,8},{16,20},{20,16},{24,28},{28,24},{1,5},{5... | collective-permute-start | bytes 147464 | tf_op jit(solution)/shard_map/ppermute | solution.py:25
  15.2 2.0 %collective-permute-done.1 = bf16[64,384]{1,0:T(8,128)(2,1)S(1)} collective-permute-done((bf16[64,384]{1,0:T(8,128)(2,1)S(1)}, bf16[64,384]{1,0:T(8,128)(2,1)S(1)}, u32[]{:S(2)}, u32[]{:S(2)}) %collective-permute-start.1) | collective-permute-done | bytes 49184 | tf_op jit(solution)/shard_map/ppermute | solution.py:25
  17.3 3.1 %collective-permute-start.2 = (bf16[64,384]{1,0:T(8,128)(2,1)S(1)}, bf16[64,384]{1,0:T(8,128)(2,1)S(1)}, u32[]{:S(2)}, u32[]{:S(2)}) collective-permute-start(bf16[64,384]{1,0:T(8,128)(2,1)S(1)} %fusion.6), channel_id=1, source_target_pairs={{0,8},{4,12},{8,0},{12,4},{16,24},{20,28},{24,16},{28,20},{1,9},{5... | collective-permute-start | bytes 147464 | tf_op jit(solution)/shard_map/ppermute | solution.py:25
  20.4 2.0 %collective-permute-done.2 = bf16[64,384]{1,0:T(8,128)(2,1)S(1)} collective-permute-done((bf16[64,384]{1,0:T(8,128)(2,1)S(1)}, bf16[64,384]{1,0:T(8,128)(2,1)S(1)}, u32[]{:S(2)}, u32[]{:S(2)}) %collective-permute-start.2) | collective-permute-done | bytes 49184 | tf_op jit(solution)/shard_map/ppermute | solution.py:25
  22.6 3.2 %collective-permute-start.3 = (bf16[64,384]{1,0:T(8,128)(2,1)S(1)}, bf16[64,384]{1,0:T(8,128)(2,1)S(1)}, u32[]{:S(2)}, u32[]{:S(2)}) collective-permute-start(bf16[64,384]{1,0:T(8,128)(2,1)S(1)} %get-tuple-element.301), channel_id=1, source_target_pairs={{0,16},{4,20},{8,24},{12,28},{16,0},{20,4},{24,8},{28,12},{1,17},{... | collective-permute-start | bytes 147464 | tf_op jit(solution)/shard_map/ppermute | solution.py:25
  26.5 1.3 collective-permute-done.3.refs_5_
  27.9 3.1 %shard_map.376 = (f32[128,384]{1,0:T(8,128)S(1)}, bf16[256,192]{1,0:T(8,128)(2,1)S(1)}, f32[64,384]{1,0:T(8,128)S(1)}, bf16[128,768]{1,0:T(8,128)(2,1)S(1)}, bf1...) custom-call(s32[2]{0:T(128)S(1)} %pad_add_fusion.refs_0_, f32[128,384]{1,0:T(8,128)S(1)} %get-tuple-element.162.refs_1_.refs_0_.refs_3_, ...), custom_call_target="tpu_custom_call" | custom-call | flops 1566000000 | tf_op jit(solution)/shard_map/pallas_call | solution.py:844
  31.0 1.4 collective-permute-done.4
  32.5 1.5 collective-permute-start.5
  34.1 5.5 %collective-permute-done.5 = bf16[128,768]{1,0:T(8,128)(2,1)S(1)} collective-permute-done((bf16[128,768]{1,0:T(8,128)(2,1)S(1)}, bf16[128,768]{1,0:T(8,128)(2,1)S(1)}, u32[]{:S(2)}, u32[]{:S(2)}) %collective-permute-start.5) | collective-permute-done | bytes 196640 | tf_op jit(solution)/shard_map/ppermute | solution.py:25
  39.7 1.4 collective-permute-done.6.refs_2_
  41.2 3.7 %shard_map.377 = (f32[256,768]{1,0:T(8,128)S(1)}, bf16[128,768]{1,0:T(8,128)(2,1)S(1)}, bf16[128,768]{1,0:T(8,128)(2,1)S(1)}, bf16[128,768]{1,0:T(8,128)(2,1)S(1...) custom-call(s32[2]{0:T(128)S(1)} %pad_add_fusion.refs_0_, ...), custom_call_target="tpu_custom_call" | custom-call | flops 2700000000 | tf_op jit(solution)/shard_map/pallas_call | solution.py:844
  46.4 1.5 collective-permute-start.8
  48.8 1.6 collective-permute-start.13
  50.4 1.7 %shard_map.379 = (f32[64,384]{1,0:T(8,128)S(1)}, f32[8,128]{1,0:T(8,128)S(1)}) custom-call(f32[128,384]{1,0:T(8,128)S(1)} %get-tuple-element.162.refs_1_.refs_0_.refs_3_, f32[64,384]{1,0:T(8,128)S(1)} %pad_maximum_fusion.refs_5_.refs_2_.refs_1_.refs_10_.refs_4_, f32[8,128]{1,0:T(8,128)S(1)} %get-tuple-element.179.refs_2_), custom_call_target="tpu_custom_call" | custom-call | flops 1080000000 | tf_op jit(solution)/shard_map/pallas_call | solution.py:844
  52.1 1.4 collective-permute-done.8.refs_1_
  53.6 1.4 collective-permute-done.9.refs_3_
  55.0 2.4 %shard_map.381 = (f32[256,768]{1,0:T(8,128)S(1)}, bf16[256,768]{1,0:T(8,128)(2,1)S(1)}, bf16[128,384]{1,0:T(8,128)(2,1)S(1)}, f32[128,384]{1,0:T(8,128)S(1)}, f3...) custom-call(s32[2]{0:T(128)S(1)} %pad_add_fusion.refs_0_, ...), custom_call_target="tpu_custom_call" | custom-call | flops 1620000000 | tf_op jit(solution)/shard_map/pallas_call | solution.py:844
  58.8 5.3 %collective-permute-done.10.refs_3_ = bf16[64,384]{1,0:T(8,128)(2,1)S(1)} collective-permute-done((bf16[64,384]{1,0:T(8,128)(2,1)S(1)}, bf16[64,384]{1,0:T(8,128)(2,1)S(1)}, u32[]{:S(2)}, u32[]{:S(2)}) %collective-permute-start.10) | collective-permute-done | bytes 49184 | tf_op jit(solution)/shard_map/ppermute | solution.py:25
  64.7 1.9 %collective-permute-start.11 = (bf16[64,384]{1,0:T(8,128)(2,1)S(1)}, bf16[64,384]{1,0:T(8,128)(2,1)S(1)}, u32[]{:S(2)}, u32[]{:S(2)}) collective-permute-start(bf16[64,384]{1,0:T(8,128)(2,1)S(1)} %get-tuple-element.196), channel_id=1, source_target_pairs={{0,8},{4,12},{8,0},{12,4},{16,24},{20,28},{24,16},{28,20},{1,9},{5... | collective-permute-start | bytes 147464 | tf_op jit(solution)/shard_map/ppermute | solution.py:25
  69.5 3.0 %collective-permute-start.14 = (bf16[64,384]{1,0:T(8,128)(2,1)S(1)}, bf16[64,384]{1,0:T(8,128)(2,1)S(1)}, u32[]{:S(2)}, u32[]{:S(2)}) collective-permute-start(bf16[64,384]{1,0:T(8,128)(2,1)S(1)} %get-tuple-element.206), channel_id=1, source_target_pairs={{0,16},{4,20},{8,24},{12,28},{16,0},{20,4},{24,8},{28,12},{1,17},{... | collective-permute-start | bytes 147464 | tf_op jit(solution)/shard_map/ppermute | solution.py:25
  72.5 4.8 %shard_map.386 = (f32[128,384]{1,0:T(8,128)S(1)}, f32[64,384]{1,0:T(8,128)S(1)}, f32[64,384]{1,0:T(8,128)S(1)}, f32[8,128]{1,0:T(8,128)S(1)}) custom-call(f32[128,384]{1,0:T(8,128)S(1)} %get-tuple-element.162.refs_1_.refs_0_.refs_3_, f32[128,384]{1,0:T(8,128)S(1)} %get-tuple-element.186.refs_1_.refs_2_, ...), custom_call_target="tpu_custom_call" | custom-call | flops 2592000000 | tf_op jit(solution)/shard_map/pallas_call | solution.py:844
  78.0 1.6 collective-permute-start.18
  79.7 5.1 %shard_map.388 = (f32[128,384]{1,0:T(8,128)S(1)}, bf16[64,384]{1,0:T(8,128)(2,1)S(1)}, bf16[128,384]{1,0:T(8,128)(2,1)S(1)}, f32[64,768]{1,0:T(8,128)S(1)}, f32[8,768]{1,0:T(8,128)S(1)}, /*index=5*/f32[8,128]{1,0:T(8,128)S(1)}) custom-call(s32[2]{0:T(128)S(1)} %pad_add_fusion.refs_0_, f32[128,384]{1,0:T(8,128)S(1)} %get-tuple-element.205.refs_1_, ...), custom_call_target="tpu_custom_call" | custom-call | flops 3240000000 | tf_op jit(solution)/shard_map/pallas_call | solution.py:844
  86.1 6.4 %collective-permute-done.18.refs_2_ = bf16[192,768]{1,0:T(8,128)(2,1)S(1)} collective-permute-done((bf16[192,768]{1,0:T(8,128)(2,1)S(1)}, bf16[192,768]{1,0:T(8,128)(2,1)S(1)}, u32[]{:S(2)}, u32[]{:S(2)}) %collective-permute-start.18) | collective-permute-done | bytes 294944 | tf_op jit(solution)/shard_map/ppermute | solution.py:25
  92.6 1.5 shard_map.390
  94.2 1.7 %collective-permute-done.19.refs_1_ = bf16[256,768]{1,0:T(8,128)(2,1)S(1)} collective-permute-done((bf16[256,768]{1,0:T(8,128)(2,1)S(1)}, bf16[256,768]{1,0:T(8,128)(2,1)S(1)}, u32[]{:S(2)}, u32[]{:S(2)}) %collective-permute-start.19) | collective-permute-done | bytes 393248 | tf_op jit(solution)/shard_map/ppermute | solution.py:25
  96.6 1.4 collective-permute-start.23
  99.3 12.4 %collective-permute-done.21.refs_2_ = bf16[192,768]{1,0:T(8,128)(2,1)S(1)} collective-permute-done((bf16[192,768]{1,0:T(8,128)(2,1)S(1)}, bf16[192,768]{1,0:T(8,128)(2,1)S(1)}, u32[]{:S(2)}, u32[]{:S(2)}) %collective-permute-start.21) | collective-permute-done | bytes 294944 | tf_op jit(solution)/shard_map/ppermute | solution.py:25
  115.4 1.9 %collective-permute-start.30 = (bf16[192,768]{1,0:T(8,128)(2,1)S(1)}, bf16[192,768]{1,0:T(8,128)(2,1)S(1)}, u32[]{:S(2)}, u32[]{:S(2)}) collective-permute-start(bf16[192,768]{1,0:T(8,128)(2,1)S(1)} %get-tuple-element.261.refs_1_), channel_id=1, source_target_pairs={{0,8},{4,12},{8,0},{12,4},{16,24},{20,28},{24,16},{28,20},{1,9},{5... | collective-permute-start | bytes 884744 | tf_op jit(solution)/shard_map/ppermute | solution.py:25
  118.6 2.4 %shard_map.395 = (f32[256,768]{1,0:T(8,128)}, f32[8,768]{1,0:T(8,128)S(1)}, f32[2,128,768]{2,1,0:T(8,128)}, f32[8,128]{1,0:T(8,128)S(1)}) custom-call(s32[2]{0:T(128)S(1)} %pad_add_fusion.refs_0_, s32[2]{0:T(128)S(1)} %copy-done.7, bf16[256,768]{1,0:T(8,128)(2,1)S(1)} %get-tuple-element.240.refs_2_, bf16[256,768]{1,0:T(8,128)(2,1)S(1)} %collective-permute-done.22.refs_3_, ...), custom_call_target="tpu_custom_call" | custom-call | flops 486000000 | tf_op jit(solution)/shard_map/pallas_call | solution.py:844
  122.5 3.9 %collective-permute-start.29 = (bf16[112,768]{1,0:T(8,128)(2,1)S(1)}, bf16[112,768]{1,0:T(8,128)(2,1)S(1)}, u32[]{:S(2)}, u32[]{:S(2)}) collective-permute-start(bf16[112,768]{1,0:T(8,128)(2,1)S(1)} %get-tuple-element.260), channel_id=1, source_target_pairs={{0,16},{4,20},{8,24},{12,28},{16,0},{20,4},{24,8},{28,12},{1,17},{... | collective-permute-start | bytes 516104 | tf_op jit(solution)/shard_map/ppermute | solution.py:25
  126.5 3.7 %collective-permute-done.25.refs_1_ = f32[8,768]{1,0:T(8,128)S(1)} collective-permute-done((f32[8,768]{1,0:T(8,128)S(1)}, f32[8,768]{1,0:T(8,128)S(1)}, u32[]{:S(2)}, u32[]{:S(2)}) %collective-permute-start.25) | collective-permute-done | bytes 24608 | tf_op jit(solution)/shard_map/ppermute | solution.py:25
  131.1 3.7 %collective-permute-done.29.refs_2_ = bf16[112,768]{1,0:T(8,128)(2,1)S(1)} collective-permute-done((bf16[112,768]{1,0:T(8,128)(2,1)S(1)}, bf16[112,768]{1,0:T(8,128)(2,1)S(1)}, u32[]{:S(2)}, u32[]{:S(2)}) %collective-permute-start.29) | collective-permute-done | bytes 172064 | tf_op jit(solution)/shard_map/ppermute | solution.py:25
  135.0 5.0 %collective-permute-start.39 = (bf16[384,768]{1,0:T(8,128)(2,1)S(1)}, bf16[384,768]{1,0:T(8,128)(2,1)S(1)}, u32[]{:S(2)}, u32[]{:S(2)}) collective-permute-start(bf16[384,768]{1,0:T(8,128)(2,1)S(1)} %get-tuple-element.275.refs_3_), channel_id=1, source_target_pairs={{0,8},{4,12},{8,0},{12,4},{16,24},{20,28},{24,16},{28,20},{1,9},{5... | collective-permute-start | bytes 1769480 | tf_op jit(solution)/shard_map/ppermute | solution.py:25
  140.0 2.8 %collective-permute-done.32.refs_2_ = bf16[112,768]{1,0:T(8,128)(2,1)S(1)} collective-permute-done((bf16[112,768]{1,0:T(8,128)(2,1)S(1)}, bf16[112,768]{1,0:T(8,128)(2,1)S(1)}, u32[]{:S(2)}, u32[]{:S(2)}) %collective-permute-start.32) | collective-permute-done | bytes 172064 | tf_op jit(solution)/shard_map/ppermute | solution.py:25
  143.6 2.5 %collective-permute-start.35 = (bf16[112,768]{1,0:T(8,128)(2,1)S(1)}, bf16[112,768]{1,0:T(8,128)(2,1)S(1)}, u32[]{:S(2)}, u32[]{:S(2)}) collective-permute-start(bf16[112,768]{1,0:T(8,128)(2,1)S(1)} %get-tuple-element.270.refs_2_), channel_id=1, source_target_pairs={{0,4},{4,0},{8,12},{12,8},{16,20},{20,16},{24,28},{28,24},{1,5},{5... | collective-permute-start | bytes 516104 | tf_op jit(solution)/shard_map/ppermute | solution.py:25
  146.0 1.4 collective-permute-start.28
  147.4 3.4 %collective-permute-done.28.refs_1_ = f32[8,768]{1,0:T(8,128)S(1)} collective-permute-done((f32[8,768]{1,0:T(8,128)S(1)}, f32[8,768]{1,0:T(8,128)S(1)}, u32[]{:S(2)}, u32[]{:S(2)}) %collective-permute-start.28) | collective-permute-done | bytes 24608 | tf_op jit(solution)/shard_map/ppermute | solution.py:25
  150.9 3.4 %collective-permute-done.34.refs_3_ = bf16[112,768]{1,0:T(8,128)(2,1)S(1)} collective-permute-done((bf16[112,768]{1,0:T(8,128)(2,1)S(1)}, bf16[112,768]{1,0:T(8,128)(2,1)S(1)}, u32[]{:S(2)}, u32[]{:S(2)}) %collective-permute-start.34) | collective-permute-done | bytes 172064 | tf_op jit(solution)/shard_map/ppermute | solution.py:25
  156.2 1.5 collective-permute-start.33
  157.7 3.0 %shard_map.403 = (f32[768,768]{1,0:T(8,128)}, f32[768,768]{1,0:T(8,128)}, f32[8,128]{1,0:T(8,128)S(1)}) custom-call(s32[2]{0:T(128)S(1)} %pad_add_fusion.refs_0_, bf16[384,768]{1,0:T(8,128)(2,1)S(1)} %get-tuple-element.274.refs_1_, bf16[384,768]{1,0:T(8,128)(2,1)S(1)} %collective-permute-done.38.refs_2_, bf16[384,768]{1,0:T(8,128)(2,1)S(1)} %get-tuple-element.275.refs_3_, ...), custom_call_target="tpu_custom_call" | custom-call | flops 1350000000 | tf_op jit(solution)/shard_map/pallas_call | solution.py:844
  160.8 2.5 %collective-permute-done.33.refs_2_ = f32[8,768]{1,0:T(8,128)S(1)} collective-permute-done((f32[8,768]{1,0:T(8,128)S(1)}, f32[8,768]{1,0:T(8,128)S(1)}, u32[]{:S(2)}, u32[]{:S(2)}) %collective-permute-start.33) | collective-permute-done | bytes 24608 | tf_op jit(solution)/shard_map/ppermute | solution.py:25
  163.2 2.2 %shard_map.404 = (f32[3,192,768]{2,1,0:T(8,128)}, f32[3,192]{1,0:T(4,128)}, f32[64,192]{1,0:T(8,128)}, f32[192]{0:T(256)}, f32[64,192]{1,0:T(8,128)}, /*index=5*...) custom-call(s32[2]{0:T(128)S(1)} %pad_add_fusion.refs_0_, ...), custom_call_target="tpu_custom_call" | custom-call | flops 1080000000 | tf_op jit(solution)/shard_map/pallas_call | solution.py:844
  (117 shorter events, 23.3 us)
Async XLA Ops:
  3.5 6.6 %collective-permute-start = (bf16[64,384]{1,0:T(8,128)(2,1)S(1)}, bf16[64,384]{1,0:T(8,128)(2,1)S(1)}, u32[]{:S(2)}, u32[]{:S(2)}) collective-permute-start(bf16[64,384]{1,0:T(8,128)(2,1)S(1)} %slice.3), channel_id=1, source_target_pairs={{0,4},{4,8},{8,12},{12,16},{16,20},{20,24},{24,28},{1,5},{5,9},{9,... | collective-permute-start | bytes 147464 | tf_op jit(solution)/shard_map/ppermute | solution.py:21
  10.1 15.7 %copy-start.7 = (s32[2]{0:T(128)S(1)}, s32[2]{0:T(128)}, u32[]{:S(2)}) copy-start(s32[2]{0:T(128)} %refs_1_.7) | copy-start | bytes 28
  10.1 15.7 %copy-start.10 = (f32[2,128,768]{2,1,0:T(8,128)S(1)}, f32[2,128,768]{2,1,0:T(8,128)}, u32[]{:S(2)}) copy-start(f32[2,128,768]{2,1,0:T(8,128)} %refs_5_.6) | copy-start | bytes 2359300
  12.7 15.1 %copy-start.11 = (bf16[192,768]{1,0:T(8,128)(2,1)S(1)}, bf16[192,768]{1,0:T(8,128)(2,1)}, u32[]{:S(2)}) copy-start(bf16[192,768]{1,0:T(8,128)(2,1)} %refs_7_.5) | copy-start | bytes 884740
  12.7 15.1 %copy-start.18 = (f32[192]{0:T(256)S(1)}, f32[192]{0:T(256)}, u32[]{:S(2)}) copy-start(f32[192]{0:T(256)} %refs_20_.1) | copy-start | bytes 2308
  12.7 4.5 %collective-permute-start.1 = (bf16[64,384]{1,0:T(8,128)(2,1)S(1)}, bf16[64,384]{1,0:T(8,128)(2,1)S(1)}, u32[]{:S(2)}, u32[]{:S(2)}) collective-permute-start(bf16[64,384]{1,0:T(8,128)(2,1)S(1)} %get-tuple-element.163), channel_id=1, source_target_pairs={{0,4},{4,0},{8,12},{12,8},{16,20},{20,16},{24,28},{28,24},{1,5},{5... | collective-permute-start | bytes 147464 | tf_op jit(solution)/shard_map/ppermute | solution.py:25
  17.3 5.1 %collective-permute-start.2 = (bf16[64,384]{1,0:T(8,128)(2,1)S(1)}, bf16[64,384]{1,0:T(8,128)(2,1)S(1)}, u32[]{:S(2)}, u32[]{:S(2)}) collective-permute-start(bf16[64,384]{1,0:T(8,128)(2,1)S(1)} %fusion.6), channel_id=1, source_target_pairs={{0,8},{4,12},{8,0},{12,4},{16,24},{20,28},{24,16},{28,20},{1,9},{5... | collective-permute-start | bytes 147464 | tf_op jit(solution)/shard_map/ppermute | solution.py:25
  22.6 5.3 %collective-permute-start.3 = (bf16[64,384]{1,0:T(8,128)(2,1)S(1)}, bf16[64,384]{1,0:T(8,128)(2,1)S(1)}, u32[]{:S(2)}, u32[]{:S(2)}) collective-permute-start(bf16[64,384]{1,0:T(8,128)(2,1)S(1)} %get-tuple-element.301), channel_id=1, source_target_pairs={{0,16},{4,20},{8,24},{12,28},{16,0},{20,4},{24,8},{28,12},{1,17},{... | collective-permute-start | bytes 147464 | tf_op jit(solution)/shard_map/ppermute | solution.py:25
  27.8 13.3 %copy-start.1 = (bf16[2,128,768]{2,1,0:T(8,128)(2,1)S(1)}, bf16[2,128,768]{2,1,0:T(8,128)(2,1)}, u32[]{:S(2)}) copy-start(bf16[2,128,768]{2,1,0:T(8,128)(2,1)} %refs_1_.4) | copy-start | bytes 1179652
  27.8 13.3 %copy-start.8 = (bf16[768,768]{1,0:T(8,128)(2,1)S(1)}, bf16[768,768]{1,0:T(8,128)(2,1)}, u32[]{:S(2)}) copy-start(bf16[768,768]{1,0:T(8,128)(2,1)} %refs_7_.4) | copy-start | bytes 3538948
  27.8 13.3 %copy-start.9 = (bf16[768,768]{1,0:T(8,128)(2,1)S(1)}, bf16[768,768]{1,0:T(8,128)(2,1)}, u32[]{:S(2)}) copy-start(bf16[768,768]{1,0:T(8,128)(2,1)} %refs_9_.3) | copy-start | bytes 3538948
  27.9 13.3 %copy-start.13 = (f32[768]{0:T(1024)S(1)}, f32[768]{0:T(1024)}, u32[]{:S(2)}) copy-start(f32[768]{0:T(1024)} %refs_4_.3) | copy-start | bytes 9220
  31.0 1.5 collective-permute-start.4
  32.5 7.0 %collective-permute-start.5 = (bf16[128,768]{1,0:T(8,128)(2,1)S(1)}, bf16[128,768]{1,0:T(8,128)(2,1)S(1)}, u32[]{:S(2)}, u32[]{:S(2)}) collective-permute-start(bf16[128,768]{1,0:T(8,128)(2,1)S(1)} %fusion), channel_id=1, source_target_pairs={{0,2},{1,3},{2,0},{3,1},{4,6},{5,7},{6,4},{7,5},{8,10},{9,11},{10,... | collective-permute-start | bytes 589832 | tf_op jit(solution)/shard_map/ppermute | solution.py:25
  39.6 1.5 collective-permute-start.6
  44.9 1.5 collective-permute-start.7
  46.4 7.0 %collective-permute-start.8 = (bf16[128,768]{1,0:T(8,128)(2,1)S(1)}, bf16[128,768]{1,0:T(8,128)(2,1)S(1)}, u32[]{:S(2)}, u32[]{:S(2)}) collective-permute-start(bf16[128,768]{1,0:T(8,128)(2,1)S(1)} %get-tuple-element.178), channel_id=1, source_target_pairs={{0,2},{1,3},{2,0},{3,1},{4,6},{5,7},{6,4},{7,5},{8,10},{9,11},{10,... | collective-permute-start | bytes 589832 | tf_op jit(solution)/shard_map/ppermute | solution.py:25
  48.0 18.6 %collective-permute-start.12 = (bf16[384,768]{1,0:T(8,128)(2,1)S(1)}, bf16[384,768]{1,0:T(8,128)(2,1)S(1)}, u32[]{:S(2)}, u32[]{:S(2)}) collective-permute-start(bf16[384,768]{1,0:T(8,128)(2,1)S(1)} %get-tuple-element.200), channel_id=1, source_target_pairs={{0,4},{4,0},{8,12},{12,8},{16,20},{20,16},{24,28},{28,24},{1,5},{5... | collective-permute-start | bytes 1769480 | tf_op jit(solution)/shard_map/ppermute | solution.py:25
  48.8 17.8 %collective-permute-start.13 = (bf16[384,768]{1,0:T(8,128)(2,1)S(1)}, bf16[384,768]{1,0:T(8,128)(2,1)S(1)}, u32[]{:S(2)}, u32[]{:S(2)}) collective-permute-start(bf16[384,768]{1,0:T(8,128)(2,1)S(1)} %get-tuple-element.201), channel_id=1, source_target_pairs={{0,8},{4,12},{8,0},{12,4},{16,24},{20,28},{24,16},{28,20},{1,9},{5... | collective-permute-start | bytes 1769480 | tf_op jit(solution)/shard_map/ppermute | solution.py:25
  53.5 1.5 collective-permute-start.9
  57.4 6.7 %collective-permute-start.10 = (bf16[64,384]{1,0:T(8,128)(2,1)S(1)}, bf16[64,384]{1,0:T(8,128)(2,1)S(1)}, u32[]{:S(2)}, u32[]{:S(2)}) collective-permute-start(bf16[64,384]{1,0:T(8,128)(2,1)S(1)} %get-tuple-element.189), channel_id=1, source_target_pairs={{0,4},{4,0},{8,12},{12,8},{16,20},{20,16},{24,28},{28,24},{1,5},{5... | collective-permute-start | bytes 147464 | tf_op jit(solution)/shard_map/ppermute | solution.py:25
  64.7 4.2 %collective-permute-start.11 = (bf16[64,384]{1,0:T(8,128)(2,1)S(1)}, bf16[64,384]{1,0:T(8,128)(2,1)S(1)}, u32[]{:S(2)}, u32[]{:S(2)}) collective-permute-start(bf16[64,384]{1,0:T(8,128)(2,1)S(1)} %get-tuple-element.196), channel_id=1, source_target_pairs={{0,8},{4,12},{8,0},{12,4},{16,24},{20,28},{24,16},{28,20},{1,9},{5... | collective-permute-start | bytes 147464 | tf_op jit(solution)/shard_map/ppermute | solution.py:25
  67.5 9.7 %collective-permute-start.15 = (bf16[192,768]{1,0:T(8,128)(2,1)S(1)}, bf16[192,768]{1,0:T(8,128)(2,1)S(1)}, u32[]{:S(2)}, u32[]{:S(2)}) collective-permute-start(bf16[192,768]{1,0:T(8,128)(2,1)S(1)} %get-tuple-element.214), channel_id=1, source_target_pairs={{0,8},{4,12},{8,0},{12,4},{16,24},{20,28},{24,16},{28,20},{1,9},{5... | collective-permute-start | bytes 884744 | tf_op jit(solution)/shard_map/ppermute | solution.py:25
  67.8 9.5 %collective-permute-start.16 = (bf16[192,768]{1,0:T(8,128)(2,1)S(1)}, bf16[192,768]{1,0:T(8,128)(2,1)S(1)}, u32[]{:S(2)}, u32[]{:S(2)}) collective-permute-start(bf16[192,768]{1,0:T(8,128)(2,1)S(1)} %get-tuple-element.215), channel_id=1, source_target_pairs={{0,4},{4,0},{8,12},{12,8},{16,20},{20,16},{24,28},{28,24},{1,5},{5... | collective-permute-start | bytes 884744 | tf_op jit(solution)/shard_map/ppermute | solution.py:25
  69.5 10.2 %collective-permute-start.14 = (bf16[64,384]{1,0:T(8,128)(2,1)S(1)}, bf16[64,384]{1,0:T(8,128)(2,1)S(1)}, u32[]{:S(2)}, u32[]{:S(2)}) collective-permute-start(bf16[64,384]{1,0:T(8,128)(2,1)S(1)} %get-tuple-element.206), channel_id=1, source_target_pairs={{0,16},{4,20},{8,24},{12,28},{16,0},{20,4},{24,8},{28,12},{1,17},{... | collective-permute-start | bytes 147464 | tf_op jit(solution)/shard_map/ppermute | solution.py:25
  78.0 14.5 %collective-permute-start.18 = (bf16[192,768]{1,0:T(8,128)(2,1)S(1)}, bf16[192,768]{1,0:T(8,128)(2,1)S(1)}, u32[]{:S(2)}, u32[]{:S(2)}) collective-permute-start(bf16[192,768]{1,0:T(8,128)(2,1)S(1)} %get-tuple-element.229), channel_id=1, source_target_pairs={{0,16},{4,20},{8,24},{12,28},{16,0},{20,4},{24,8},{28,12},{1,17},{... | collective-permute-start | bytes 884744 | tf_op jit(solution)/shard_map/ppermute | solution.py:25
  84.8 7.8 %collective-permute-start.17 = (bf16[64,384]{1,0:T(8,128)(2,1)S(1)}, bf16[64,384]{1,0:T(8,128)(2,1)S(1)}, u32[]{:S(2)}, u32[]{:S(2)}) collective-permute-start(bf16[64,384]{1,0:T(8,128)(2,1)S(1)} %get-tuple-element.219), channel_id=1, source_target_pairs={{4,0},{8,4},{12,8},{16,12},{20,16},{24,20},{28,24},{5,1},{9,5},{13... | collective-permute-start | bytes 147464 | tf_op jit(solution)/shard_map/ppermute | solution.py:21
  94.1 1.8 %collective-permute-start.19 = (bf16[256,768]{1,0:T(8,128)(2,1)S(1)}, bf16[256,768]{1,0:T(8,128)(2,1)S(1)}, u32[]{:S(2)}, u32[]{:S(2)}) collective-permute-start(bf16[256,768]{1,0:T(8,128)(2,1)S(1)} %get-tuple-element.233), channel_id=1, source_target_pairs={{0,1},{1,0},{2,3},{3,2},{4,5},{5,4},{6,7},{7,6},{8,9},{9,8},{10,11... | collective-permute-start | bytes 1179656 | tf_op jit(solution)/shard_map/ppermute | solution.py:25
  96.0 16.4 %collective-permute-start.20 = (bf16[256,768]{1,0:T(8,128)(2,1)S(1)}, bf16[256,768]{1,0:T(8,128)(2,1)S(1)}, u32[]{:S(2)}, u32[]{:S(2)}) collective-permute-start(bf16[256,768]{1,0:T(8,128)(2,1)S(1)} %get-tuple-element.236), channel_id=1, source_target_pairs={{0,2},{1,3},{2,0},{3,1},{4,6},{5,7},{6,4},{7,5},{8,10},{9,11},{10,... | collective-permute-start | bytes 1179656 | tf_op jit(solution)/shard_map/ppermute | solution.py:25
  96.6 15.1 %collective-permute-start.21 = (bf16[192,768]{1,0:T(8,128)(2,1)S(1)}, bf16[192,768]{1,0:T(8,128)(2,1)S(1)}, u32[]{:S(2)}, u32[]{:S(2)}) collective-permute-start(bf16[192,768]{1,0:T(8,128)(2,1)S(1)} %get-tuple-element.237.refs_1_), channel_id=1, source_target_pairs={{0,16},{4,20},{8,24},{12,28},{16,0},{20,4},{24,8},{28,12},{1,17},{... | collective-permute-start | bytes 884744 | tf_op jit(solution)/shard_map/ppermute | solution.py:25
  96.6 15.9 %collective-permute-start.23 = (bf16[224,768]{1,0:T(8,128)(2,1)S(1)}, bf16[224,768]{1,0:T(8,128)(2,1)S(1)}, u32[]{:S(2)}, u32[]{:S(2)}) collective-permute-start(bf16[224,768]{1,0:T(8,128)(2,1)S(1)} %get-tuple-element.244), channel_id=1, source_target_pairs={{0,4},{4,0},{8,12},{12,8},{16,20},{20,16},{24,28},{28,24},{1,5},{5... | collective-permute-start | bytes 1032200 | tf_op jit(solution)/shard_map/ppermute | solution.py:25
  98.1 15.6 %collective-permute-start.24 = (bf16[224,768]{1,0:T(8,128)(2,1)S(1)}, bf16[224,768]{1,0:T(8,128)(2,1)S(1)}, u32[]{:S(2)}, u32[]{:S(2)}) collective-permute-start(bf16[224,768]{1,0:T(8,128)(2,1)S(1)} %get-tuple-element.245), channel_id=1, source_target_pairs={{0,8},{4,12},{8,0},{12,4},{16,24},{20,28},{24,16},{28,20},{1,9},{5... | collective-permute-start | bytes 1032200 | tf_op jit(solution)/shard_map/ppermute | solution.py:25
  112.5 6.1 %collective-permute-start.22 = (bf16[256,768]{1,0:T(8,128)(2,1)S(1)}, bf16[256,768]{1,0:T(8,128)(2,1)S(1)}, u32[]{:S(2)}, u32[]{:S(2)}) collective-permute-start(bf16[256,768]{1,0:T(8,128)(2,1)S(1)} %get-tuple-element.240.refs_2_), channel_id=1, source_target_pairs={{0,1},{1,0},{2,3},{3,2},{4,5},{5,4},{6,7},{7,6},{8,9},{9,8},{10,11... | collective-permute-start | bytes 1179656 | tf_op jit(solution)/shard_map/ppermute | solution.py:25
  114.4 7.4 %collective-permute-start.26 = (bf16[112,768]{1,0:T(8,128)(2,1)S(1)}, bf16[112,768]{1,0:T(8,128)(2,1)S(1)}, u32[]{:S(2)}, u32[]{:S(2)}) collective-permute-start(bf16[112,768]{1,0:T(8,128)(2,1)S(1)} %get-tuple-element.253), channel_id=1, source_target_pairs={{0,8},{4,12},{8,0},{12,4},{16,24},{20,28},{24,16},{28,20},{1,9},{5... | collective-permute-start | bytes 516104 | tf_op jit(solution)/shard_map/ppermute | solution.py:25
  114.5 7.3 %collective-permute-start.27 = (bf16[112,768]{1,0:T(8,128)(2,1)S(1)}, bf16[112,768]{1,0:T(8,128)(2,1)S(1)}, u32[]{:S(2)}, u32[]{:S(2)}) collective-permute-start(bf16[112,768]{1,0:T(8,128)(2,1)S(1)} %get-tuple-element.254), channel_id=1, source_target_pairs={{0,4},{4,0},{8,12},{12,8},{16,20},{20,16},{24,28},{28,24},{1,5},{5... | collective-permute-start | bytes 516104 | tf_op jit(solution)/shard_map/ppermute | solution.py:25
  115.4 14.8 %collective-permute-start.30 = (bf16[192,768]{1,0:T(8,128)(2,1)S(1)}, bf16[192,768]{1,0:T(8,128)(2,1)S(1)}, u32[]{:S(2)}, u32[]{:S(2)}) collective-permute-start(bf16[192,768]{1,0:T(8,128)(2,1)S(1)} %get-tuple-element.261.refs_1_), channel_id=1, source_target_pairs={{0,8},{4,12},{8,0},{12,4},{16,24},{20,28},{24,16},{28,20},{1,9},{5... | collective-permute-start | bytes 884744 | tf_op jit(solution)/shard_map/ppermute | solution.py:25
  117.4 12.8 %collective-permute-start.31 = (bf16[192,768]{1,0:T(8,128)(2,1)S(1)}, bf16[192,768]{1,0:T(8,128)(2,1)S(1)}, u32[]{:S(2)}, u32[]{:S(2)}) collective-permute-start(bf16[192,768]{1,0:T(8,128)(2,1)S(1)} %get-tuple-element.262.refs_2_), channel_id=1, source_target_pairs={{0,4},{4,0},{8,12},{12,8},{16,20},{20,16},{24,28},{28,24},{1,5},{5... | collective-permute-start | bytes 884744 | tf_op jit(solution)/shard_map/ppermute | solution.py:25
  122.5 12.3 %collective-permute-start.29 = (bf16[112,768]{1,0:T(8,128)(2,1)S(1)}, bf16[112,768]{1,0:T(8,128)(2,1)S(1)}, u32[]{:S(2)}, u32[]{:S(2)}) collective-permute-start(bf16[112,768]{1,0:T(8,128)(2,1)S(1)} %get-tuple-element.260), channel_id=1, source_target_pairs={{0,16},{4,20},{8,24},{12,28},{16,0},{20,4},{24,8},{28,12},{1,17},{... | collective-permute-start | bytes 516104 | tf_op jit(solution)/shard_map/ppermute | solution.py:25
  126.4 3.8 %collective-permute-start.25 = (f32[8,768]{1,0:T(8,128)S(1)}, f32[8,768]{1,0:T(8,128)S(1)}, u32[]{:S(2)}, u32[]{:S(2)}) collective-permute-start(f32[8,768]{1,0:T(8,128)S(1)} %get-tuple-element.250.refs_0_), channel_id=1, source_target_pairs={{0,4},{4,0},{8,12},{12,8},{16,20},{20,16},{24,28},{28,24},{1,5},{5... | collective-permute-start | bytes 73736 | tf_op jit(solution)/shard_map/ppermute | solution.py:25
  134.9 8.0 %collective-permute-start.32 = (bf16[112,768]{1,0:T(8,128)(2,1)S(1)}, bf16[112,768]{1,0:T(8,128)(2,1)S(1)}, u32[]{:S(2)}, u32[]{:S(2)}) collective-permute-start(bf16[112,768]{1,0:T(8,128)(2,1)S(1)} %get-tuple-element.265.refs_1_), channel_id=1, source_target_pairs={{0,16},{4,20},{8,24},{12,28},{16,0},{20,4},{24,8},{28,12},{1,17},{... | collective-permute-start | bytes 516104 | tf_op jit(solution)/shard_map/ppermute | solution.py:25
  134.9 22.8 %collective-permute-start.38 = (bf16[384,768]{1,0:T(8,128)(2,1)S(1)}, bf16[384,768]{1,0:T(8,128)(2,1)S(1)}, u32[]{:S(2)}, u32[]{:S(2)}) collective-permute-start(bf16[384,768]{1,0:T(8,128)(2,1)S(1)} %get-tuple-element.274.refs_1_), channel_id=1, source_target_pairs={{0,4},{4,0},{8,12},{12,8},{16,20},{20,16},{24,28},{28,24},{1,5},{5... | collective-permute-start | bytes 1769480 | tf_op jit(solution)/shard_map/ppermute | solution.py:25
  135.0 22.7 %collective-permute-start.39 = (bf16[384,768]{1,0:T(8,128)(2,1)S(1)}, bf16[384,768]{1,0:T(8,128)(2,1)S(1)}, u32[]{:S(2)}, u32[]{:S(2)}) collective-permute-start(bf16[384,768]{1,0:T(8,128)(2,1)S(1)} %get-tuple-element.275.refs_3_), channel_id=1, source_target_pairs={{0,8},{4,12},{8,0},{12,4},{16,24},{20,28},{24,16},{28,20},{1,9},{5... | collective-permute-start | bytes 1769480 | tf_op jit(solution)/shard_map/ppermute | solution.py:25
  143.5 10.8 %collective-permute-start.34 = (bf16[112,768]{1,0:T(8,128)(2,1)S(1)}, bf16[112,768]{1,0:T(8,128)(2,1)S(1)}, u32[]{:S(2)}, u32[]{:S(2)}) collective-permute-start(bf16[112,768]{1,0:T(8,128)(2,1)S(1)} %get-tuple-element.269.refs_1_), channel_id=1, source_target_pairs={{0,8},{4,12},{8,0},{12,4},{16,24},{20,28},{24,16},{28,20},{1,9},{5... | collective-permute-start | bytes 516104 | tf_op jit(solution)/shard_map/ppermute | solution.py:25
  143.6 10.7 %collective-permute-start.35 = (bf16[112,768]{1,0:T(8,128)(2,1)S(1)}, bf16[112,768]{1,0:T(8,128)(2,1)S(1)}, u32[]{:S(2)}, u32[]{:S(2)}) collective-permute-start(bf16[112,768]{1,0:T(8,128)(2,1)S(1)} %get-tuple-element.270.refs_2_), channel_id=1, source_target_pairs={{0,4},{4,0},{8,12},{12,8},{16,20},{20,16},{24,28},{28,24},{1,5},{5... | collective-permute-start | bytes 516104 | tf_op jit(solution)/shard_map/ppermute | solution.py:25
  146.0 4.8 %collective-permute-start.28 = (f32[8,768]{1,0:T(8,128)S(1)}, f32[8,768]{1,0:T(8,128)S(1)}, u32[]{:S(2)}, u32[]{:S(2)}) collective-permute-start(f32[8,768]{1,0:T(8,128)S(1)} %get-tuple-element.257.refs_0_), channel_id=1, source_target_pairs={{0,16},{4,20},{8,24},{12,28},{16,0},{20,4},{24,8},{28,12},{1,17},{... | collective-permute-start | bytes 73736 | tf_op jit(solution)/shard_map/ppermute | solution.py:25
  155.0 8.2 %collective-permute-start.36 = (bf16[224,768]{1,0:T(8,128)(2,1)S(1)}, bf16[224,768]{1,0:T(8,128)(2,1)S(1)}, u32[]{:S(2)}, u32[]{:S(2)}) collective-permute-start(bf16[224,768]{1,0:T(8,128)(2,1)S(1)} %get-tuple-element.272.refs_3_), channel_id=1, source_target_pairs={{0,4},{4,0},{8,12},{12,8},{16,20},{20,16},{24,28},{28,24},{1,5},{5... | collective-permute-start | bytes 1032200 | tf_op jit(solution)/shard_map/ppermute | solution.py:25
  155.7 7.5 %collective-permute-start.37 = (bf16[224,768]{1,0:T(8,128)(2,1)S(1)}, bf16[224,768]{1,0:T(8,128)(2,1)S(1)}, u32[]{:S(2)}, u32[]{:S(2)}) collective-permute-start(bf16[224,768]{1,0:T(8,128)(2,1)S(1)} %get-tuple-element.273.refs_5_), channel_id=1, source_target_pairs={{0,8},{4,12},{8,0},{12,4},{16,24},{20,28},{24,16},{28,20},{1,9},{5... | collective-permute-start | bytes 1032200 | tf_op jit(solution)/shard_map/ppermute | solution.py:25
  156.2 7.0 %collective-permute-start.33 = (f32[8,768]{1,0:T(8,128)S(1)}, f32[8,768]{1,0:T(8,128)S(1)}, u32[]{:S(2)}, u32[]{:S(2)}) collective-permute-start(f32[8,768]{1,0:T(8,128)S(1)} %get-tuple-element.268.refs_1_), channel_id=1, source_target_pairs={{0,8},{4,12},{8,0},{12,4},{16,24},{20,28},{24,16},{28,20},{1,9},{5... | collective-permute-start | bytes 73736 | tf_op jit(solution)/shard_map/ppermute | solution.py:25
  (12 other events, 115.8 us)

commit v5 on v4

--- a/solution.py
+++ b/solution.py
@@ -11,8 +11,8 @@
 f32 = jnp.float32
 bf16 = jnp.bfloat16
 LANES = 128
-ORDER = "mmmmEmMmMmMmmMmLmLNMLLNLN"
-FLOPS_PER_US = 0.54e9
+ORDER = "mmmmEmMmMmMmmMmLmLLMLLM"
+FLOPS_PER_US = 0.5e9
 SUBS = 8
 
 
@@ -25,47 +25,59 @@
     return lax.ppermute(shard, axis, [(i, i ^ mask) for i in range(lax.axis_size(axis))])
 
 
-def halving_steps(call, groups, orders, spot, axis):
+def halving_steps(call, groups, orders, spot, axis, extra=None):
     keeps, sends = [g[0] for g in groups], [g[1] for g in groups]
-    count = len(orders[0])
+    count, groups_count, model = len(orders[0]), len(groups), keeps[0].shape[1]
     joint = [k > 0 and len({order[k] for order in orders}) == 1 for k in range(count)]
+    rows = [k.shape[0] for k in keeps]
+    tail = 0
 
     def shapes(rows, stage):
-        rows = [sum(rows)] if joint[stage] else rows
-        return [like((r, keeps[0].shape[1]), bf16) for r in rows]
+        sizes = [sum(rows) + tail] if joint[stage] else [rows[0] + tail] + rows[1:]
+        return [like((size, model), bf16) for size in sizes]
 
     def trade(blocks, stage):
         return [swapped(block, axis, order[stage]) for block, order in zip(blocks, orders)]
+
+    def masks_at(stage):
+        return tuple(order[stage] for order in orders)
 
     for stage in range(count):
         gots = trade(sends, stage)
         yield
-        rows = [k.shape[0] for k in keeps]
         if stage + 1 < count:
             half = [r // 2 for r in rows]
-            masks = tuple(order[stage + 1] for order in orders)
+            held = []
+            if extra and stage + 2 == count:
+                held, tail = [extra()], SUBS
             results = call(
-                functools.partial(halve_kernel, masks),
-                [like((r, keeps[0].shape[1]), bf16) for r in half] + shapes(half, stage + 1),
-                [spot, *keeps, *gots], limit=8, scalars=1,
+                functools.partial(halve_kernel, masks_at(stage + 1), len(gots), len(held)),
+                [like((r, model), bf16) for r in half] + shapes(half, stage + 1),
+                [spot, *keeps, *gots, *held], limit=8, scalars=1,
             )
-            keeps, sends = results[: len(half)], results[len(half) :]
+            keeps, sends, rows = results[:groups_count], results[groups_count:], half
         else:
+            kept = tail
+            tail = 0
             owns = call(
-                functools.partial(sum_kernel, len(keeps)), shapes(rows, stage), [*keeps, *gots], limit=8
+                functools.partial(sum_kernel, groups_count, len(gots), kept),
+                shapes(rows, stage) + [like((SUBS, model))] * len(held),
+                [*keeps, *gots, *held], limit=8,
             )
+            owns, held = (owns[:-1], [owns[-1]]) if held else (owns, [])
     for stage in range(count - 1, -1, -1):
         gots = trade(owns, stage)
         yield
         if not stage:
             return [a for pair in zip(owns, gots) for a in pair]
-        masks = tuple(order[stage] for order in orders)
+        before = tail
+        tail = SUBS if held or tail else 0
+        double = [2 * r for r in rows]
         owns = call(
-            functools.partial(double_kernel, joint[stage], masks),
-            shapes([2 * r for r in rows], stage - 1),
-            [spot, *owns, *gots], limit=8, scalars=1,
-        )
-        rows = [2 * r for r in rows]
+            functools.partial(double_kernel, masks_at(stage), tuple(rows), len(gots), before, len(held)),
+            shapes(double, stage - 1), [spot, *owns, *gots, *held], limit=8, scalars=1,
+        )
+        rows, held = double, []
 
 
 def head_steps(call, keep, send, axis="head"):
@@ -75,7 +87,7 @@
         yield
         if mask >= lax.axis_size(axis):
             (low,) = call(
-                functools.partial(sum_kernel, 1), [like(keep.shape, bf16)], [keep, got], limit=8
+                functools.partial(sum_kernel, 1, 1, 0), [like(keep.shape, bf16)], [keep, got], limit=8
             )
             return low, swapped(low, axis, 1)
         keep, low = call(
@@ -136,16 +148,6 @@
         mask *= 2
 
 
-def sum_steps(call, rows, masks, axis):
-    for mask in masks[:-1]:
-        got = swapped(rows, axis, mask)
-        yield
-        (rows,) = call(plain_add_kernel, [like(rows.shape)], [rows, got], limit=4)
-    got = swapped(rows, axis, masks[-1])
-    yield
-    return rows, got
-
-
 def ran(steps):
     while True:
         try:
@@ -251,60 +253,63 @@
     return (spot[0] // mask) % 2
 
 
-def split_blocks(refs, rows):
-    if len(refs) == len(rows):
-        return [ref[...].astype(f32) for ref in refs]
-    whole, starts = refs[0][...].astype(f32), [sum(rows[:k]) for k in range(len(rows))]
-    return [whole[start : start + r] for start, r in zip(starts, rows)]
-
-
-def put_blocks(refs, blocks):
-    if len(refs) == len(blocks):
-        for ref, block in zip(refs, blocks):
-            ref[...] = block.astype(bf16)
-        return
-    start = 0
-    for block in blocks:
-        refs[0][start : start + block.shape[0], :] = block.astype(bf16)
-        start += block.shape[0]
-
-
-def halve_kernel(masks, spot_ref, *refs):
+def split_blocks(refs, rows, tail=0):
+    if len(refs) == 1:
+        sizes, whole = list(rows) + [tail], refs[0][...].astype(f32)
+        blocks = [whole[sum(sizes[:k]) : sum(sizes[: k + 1])] for k in range(len(rows))]
+        return blocks, whole[sum(rows) :] if tail else None
+    blocks = [ref[0:r, :].astype(f32) for ref, r in zip(refs, rows)]
+    return blocks, refs[0][rows[0] :, :].astype(f32) if tail else None
+
+
+def put_blocks(refs, blocks, riding=None):
+    blocks = list(blocks)
+    rider = [] if riding is None else [riding]
+    parts = [blocks + rider] if len(refs) == 1 else [blocks[:1] + rider] + [[b] for b in blocks[1:]]
+    for ref, pieces in zip(refs, parts):
+        start = 0
+        for piece in pieces:
+            ref[start : start + piece.shape[0], :] = piece.astype(bf16)
+            start += piece.shape[0]
+
+
+def halve_kernel(masks, got_count, held, spot_ref, *refs):
     count = len(masks)
     keeps = [ref[...].astype(f32) for ref in refs[:count]]
     rows = [keep.shape[0] for keep in keeps]
-    ours = next(k for k in range(count, len(refs)) if refs[k].shape[0] == rows[0] // 2)
-    totals = [a + b for a, b in zip(keeps, split_blocks(refs[count:ours], rows))]
+    ins = count + got_count
+    totals = [a + b for a, b in zip(keeps, split_blocks(refs[count:ins], rows)[0])]
     pairs = [
         ordered(bit_of(spot_ref, mask), total[: r // 2], total[r // 2 :])
         for mask, total, r in zip(masks, totals, rows)
     ]
-    put_blocks(refs[ours : ours + count], [pair[0] for pair in pairs])
-    put_blocks(refs[ours + count :], [pair[1] for pair in pairs])
-
-
-def sum_kernel(count, *refs):
+    outs = refs[ins + held :]
+    for ref, pair in zip(outs[:count], pairs):
+        ref[...] = pair[0].astype(bf16)
+    put_blocks(outs[count:], [pair[1] for pair in pairs], refs[ins][...] if held else None)
+
+
+def sum_kernel(count, got_count, tail, *refs):
     keeps = [ref[...].astype(f32) for ref in refs[:count]]
     rows = [keep.shape[0] for keep in keeps]
-    ours = count + (count if refs[count].shape[0] == rows[0] else 1)
-    totals = [a + b for a, b in zip(keeps, split_blocks(refs[count:ours], rows))]
-    put_blocks(refs[ours:], totals)
-
-
-def plain_add_kernel(own_ref, got_ref, out_ref):
-    out_ref[...] = own_ref[...] + got_ref[...]
-
-
-def double_kernel(joint_in, masks, spot_ref, *refs):
-    count = len(masks)
-    ins = 1 if joint_in else count
-    rows = [refs[0].shape[0] // count] * count if joint_in else [ref.shape[0] for ref in refs[:count]]
-    owns, gots = split_blocks(refs[:ins], rows), split_blocks(refs[ins : 2 * ins], rows)
+    ins = count + got_count
+    gots, riding = split_blocks(refs[count:ins], rows, tail)
+    outs = refs[ins + (1 if tail else 0) :]
+    if tail:
+        outs[-1][...] = refs[ins][...].astype(bf16).astype(f32) + riding
+        outs = outs[:-1]
+    put_blocks(outs, [a + b for a, b in zip(keeps, gots)])
+
+
+def double_kernel(masks, rows, ins, tail, held, spot_ref, *refs):
+    owns, mine = split_blocks(refs[:ins], rows, tail)
+    gots, theirs = split_blocks(refs[ins : 2 * ins], rows, tail)
+    riding = mine + theirs if tail else refs[2 * ins][...] if held else None
     blocks = [
         jnp.concatenate(ordered(bit_of(spot_ref, mask), own, got), axis=0)
         for mask, own, got in zip(masks, owns, gots)
     ]
-    put_blocks(refs[2 * ins :], blocks)
+    put_blocks(refs[2 * ins + held :], blocks, riding)
 
 
 def join_kernel(keep_ref, got_ref, total_ref, low_ref):
@@ -798,15 +803,15 @@
 
 
 def spread_kernel(
-    chans, taps, mask_one, mask_two, spot_ref, ln1_ref, ln1_got_ref, one_ref, one_got_ref, two_ref, two_got_ref,
+    chans, taps, mask_one, mask_two, spot_ref, one_ref, one_got_ref, two_ref, two_got_ref,
     qkv_ref, bias_ref, tap_ref, shift_skip_ref, a_ref, b_ref, c_ref, ssm_skip_ref, step_ref, out_ref,
     gain_ref, norm_bias_ref, out_bias_ref, up_ref, down_ref, entry_gain_ref, entry_bias_ref, all_ref,
 ):
-    entry = ln1_ref[...] + ln1_got_ref[...]
+    quarter = two_ref.shape[0]
+    entry = one_ref[quarter:, :].astype(f32) + one_got_ref[quarter:, :].astype(f32)
     entry_gain_ref[...] = entry[0:1, :].reshape(entry.shape[1])
     entry_bias_ref[...] = entry[1:2, :].reshape(entry.shape[1])
-    quarter = one_ref.shape[0]
-    pieces = halves_of(bit_of(spot_ref, mask_one), one_ref, one_got_ref)
+    pieces = halves_of(bit_of(spot_ref, mask_one), one_ref.at[0:quarter, :], one_got_ref.at[0:quarter, :])
     pieces += halves_of(bit_of(spot_ref, mask_two), two_ref, two_got_ref)
     for place, piece in enumerate(pieces):
         all_ref[place * quarter : (place + 1) * quarter, :] = piece
@@ -1020,14 +1025,17 @@
         while last_parts is None:
             yield
         one, one_send, two, two_send = last_parts
+
+        def extra():
+            while entry_parts is None:
+                step("m")
+            return entry_parts
+
         return (
-            yield from halving_steps(call, [(one, one_send), (two, two_send)], orders, spot, "seq")
-        )
-
-    def entry_work():
-        while entry_parts is None:
-            yield
-        return (yield from sum_steps(call, entry_parts, masks[:1] + masks[:0:-1], "seq"))
+            yield from halving_steps(
+                call, [(one, one_send), (two, two_send)], orders, spot, "seq", extra
+            )
+        )
 
     def main_work():
         nonlocal low_middle, grad_queries, last_parts, entry_parts, grad_inputs, layer_out, last_rows
@@ -1110,7 +1118,7 @@
                 misc, norm_rows, grad_b_up, grad_b_down,
             ],
             [pltpu.VMEM((last_rows, model), f32)],
-            us=0.45,
+            us=4.50,
             scalars=1,
         )
         last_parts = (one, one_send, two, two_send)
@@ -1122,12 +1130,11 @@
             [like((tokens, model)), like((SUBS, model)), like(inputs.shape)],
             [spot, lengths, own, other, flat_inputs, ln1_gain, grad_middle, middle, b_down],
             scalars=2,
-            us=0.90,
+            us=3.0,
         )
         entry_parts = rows_sum
-        step("N")
-
-    works = {"m": main_work(), "M": feed_work(), "E": early_work(), "L": last_work(), "N": entry_work()}
+
+    works = {"m": main_work(), "M": feed_work(), "E": early_work(), "L": last_work()}
     ended = {}
 
     def step(name):
@@ -1140,10 +1147,10 @@
     step("M")
     for name in ORDER:
         step(name)
-    for name in "mMLN":
+    for name in "mML":
         while name not in ended:
             step(name)
-    joined, ln1_parts = ended["L"], ended["N"]
+    joined = ended["L"]
     spread = call(
         functools.partial(spread_kernel, chans, taps, *ends),
         [
@@ -1165,7 +1172,7 @@
             like((model,)),
             like((model,)),
         ],
-        [spot, *ln1_parts, *joined],
+        [spot, *joined],
         [pltpu.VMEM((last_rows, model), f32)],
         scalars=1,
         us=2.0,

time: 166 us -> 167 us (level)
  waiting for transfers between devices: 66.8 us -> 70.4 us
  starting transfers between devices: 52.7 us -> 50.5 us
    ppermute x38 -> x35, waiting for transfers between devices: 65.3 us -> 68.9 us  [swapped(): lax.ppermute(shard, axis, [(i, i ^ mask) for i in range(lax.axis_size(axi...]
    ppermute x38 -> x35, starting transfers between devices: 46.5 us -> 44.3 us  [swapped(): lax.ppermute(shard, axis, [(i, i ^ mask) for i in range(lax.axis_size(axi...]
    pallas_call x32 -> x30, Pallas kernels: 43.9 us -> 43.9 us  [call(): pl.pallas_call(body, in_specs=specs, out_shape=tuple(outs) + (like((SUBS,...]
  transfers between devices with their start and end apart: 40 -> 37, of which waited for: 23 -> 22; matrix products, arithmetic and copies ran while one was open for 0% -> 0% of each run, Pallas kernels for 17% -> 17%
where the time goes in v5:
time: 167 us
  waiting for transfers between devices  70.4 us (42%)
  starting transfers between devices  50.5 us (30%)
  Pallas kernels  43.9 us (26%)
    ppermute x35, waiting for transfers between devices, swapped(): lax.ppermute(shard, axis, [(i, i ^ mask) for i in range(lax.axis_size(axi...  68.9 us
    ppermute x35, starting transfers between devices, swapped(): lax.ppermute(shard, axis, [(i, i ^ mask) for i in range(lax.axis_size(axi...  44.3 us
    pallas_call x30, Pallas kernels, call(): pl.pallas_call(body, in_specs=specs, out_shape=tuple(outs) + (like((SUBS,...  43.9 us
    ppermute x2, starting transfers between devices, shifted(): lax.ppermute(shard, axis, [(i, i + by) for i in range(peers) if 0 <= i +...  6.16 us
  transfers between devices with their start and end apart: 37, of which 22 were waited for; matrix products, arithmetic and copies ran while one was open for 0% of the time, Pallas kernels for 17%

profile of v5, /device:TPU:0, one launch (start us, length us, event | category | flops | bytes accessed | tf_op | source)
XLA Modules:
  0.0 167.0 jit_solution(8358774720942845296)
XLA Ops:
  0.8 2.7 %shard_map.373 = (bf16[256,768]{1,0:T(8,128)(2,1)S(1)}, f32[128,384]{1,0:T(8,128)S(1)}, bf16[128,384]{1,0:T(8,128)(2,1)S(1)}, f32[128,384]{1,0:T(8,128)S(1)}, f32[8,128]{1,0:T(8,128)S(1)}) custom-call(s32[2]{0:T(128)S(1)} %pad_add_fusion.refs_0_, bf16[2,128,768]{2,1,0:T(8,128)(2,1)} %refs_1_.4, f32[768]{0:T(1024)} %refs_5_.7, f32[768]{0:T(1024)} %refs_3_.2, ...), custom_call_target="tpu_custom_call" | custom-call | flops 1000000000 | tf_op jit(solution)/shard_map/pallas_call | solution.py:849
  3.5 4.9 %collective-permute-start = (bf16[64,384]{1,0:T(8,128)(2,1)S(1)}, bf16[64,384]{1,0:T(8,128)(2,1)S(1)}, u32[]{:S(2)}, u32[]{:S(2)}) collective-permute-start(bf16[64,384]{1,0:T(8,128)(2,1)S(1)} %slice.3), channel_id=1, source_target_pairs={{0,4},{4,8},{8,12},{12,16},{16,20},{20,24},{24,28},{1,5},{5,9},{9,... | collective-permute-start | bytes 147464 | tf_op jit(solution)/shard_map/ppermute | solution.py:21
  8.6 1.5 collective-permute-done.refs_0_.refs_16_
  10.1 2.6 %shard_map.374 = (f32[128,384]{1,0:T(8,128)S(1)}, f32[128,384]{1,0:T(8,128)S(1)}, f32[64,384]{1,0:T(8,128)S(1)}, bf16[64,384]{1,0:T(8,128)(2,1)S(1)}, f32[8,128]{1,0:T(8,128)S(1)}) custom-call(bf16[64,384]{1,0:T(8,128)(2,1)S(1)} %collective-permute-done.refs_0_.refs_16_, bf16[128,384]{1,0:T(8,128)(2,1)S(1)} %get-tuple-element.156.refs_1_.refs_17_, ...), custom_call_target="tpu_custom_call" | custom-call | flops 1450000000 | tf_op jit(solution)/shard_map/pallas_call | solution.py:849
  12.7 2.4 %collective-permute-start.1 = (bf16[64,384]{1,0:T(8,128)(2,1)S(1)}, bf16[64,384]{1,0:T(8,128)(2,1)S(1)}, u32[]{:S(2)}, u32[]{:S(2)}) collective-permute-start(bf16[64,384]{1,0:T(8,128)(2,1)S(1)} %get-tuple-element.160), channel_id=1, source_target_pairs={{0,4},{4,0},{8,12},{12,8},{16,20},{20,16},{24,28},{28,24},{1,5},{5... | collective-permute-start | bytes 147464 | tf_op jit(solution)/shard_map/ppermute | solution.py:25
  15.2 2.0 %collective-permute-done.1 = bf16[64,384]{1,0:T(8,128)(2,1)S(1)} collective-permute-done((bf16[64,384]{1,0:T(8,128)(2,1)S(1)}, bf16[64,384]{1,0:T(8,128)(2,1)S(1)}, u32[]{:S(2)}, u32[]{:S(2)}) %collective-permute-start.1) | collective-permute-done | bytes 49184 | tf_op jit(solution)/shard_map/ppermute | solution.py:25
  17.3 3.1 %collective-permute-start.2 = (bf16[64,384]{1,0:T(8,128)(2,1)S(1)}, bf16[64,384]{1,0:T(8,128)(2,1)S(1)}, u32[]{:S(2)}, u32[]{:S(2)}) collective-permute-start(bf16[64,384]{1,0:T(8,128)(2,1)S(1)} %fusion.6), channel_id=1, source_target_pairs={{0,8},{4,12},{8,0},{12,4},{16,24},{20,28},{24,16},{28,20},{1,9},{5... | collective-permute-start | bytes 147464 | tf_op jit(solution)/shard_map/ppermute | solution.py:25
  20.4 2.0 %collective-permute-done.2 = bf16[64,384]{1,0:T(8,128)(2,1)S(1)} collective-permute-done((bf16[64,384]{1,0:T(8,128)(2,1)S(1)}, bf16[64,384]{1,0:T(8,128)(2,1)S(1)}, u32[]{:S(2)}, u32[]{:S(2)}) %collective-permute-start.2) | collective-permute-done | bytes 49184 | tf_op jit(solution)/shard_map/ppermute | solution.py:25
  22.6 3.2 %collective-permute-start.3 = (bf16[64,384]{1,0:T(8,128)(2,1)S(1)}, bf16[64,384]{1,0:T(8,128)(2,1)S(1)}, u32[]{:S(2)}, u32[]{:S(2)}) collective-permute-start(bf16[64,384]{1,0:T(8,128)(2,1)S(1)} %get-tuple-element.295), channel_id=1, source_target_pairs={{0,16},{4,20},{8,24},{12,28},{16,0},{20,4},{24,8},{28,12},{1,17},{... | collective-permute-start | bytes 147464 | tf_op jit(solution)/shard_map/ppermute | solution.py:25
  26.5 1.3 collective-permute-done.3.refs_5_
  27.9 3.0 %shard_map.376 = (f32[128,384]{1,0:T(8,128)S(1)}, bf16[256,192]{1,0:T(8,128)(2,1)S(1)}, f32[64,384]{1,0:T(8,128)S(1)}, bf16[128,768]{1,0:T(8,128)(2,1)S(1)}, bf1...) custom-call(s32[2]{0:T(128)S(1)} %pad_add_fusion.refs_0_, f32[128,384]{1,0:T(8,128)S(1)} %get-tuple-element.159.refs_1_.refs_0_.refs_3_, ...), custom_call_target="tpu_custom_call" | custom-call | flops 1450000000 | tf_op jit(solution)/shard_map/pallas_call | solution.py:849
  31.0 1.4 collective-permute-done.4
  32.5 1.5 collective-permute-start.5
  34.1 5.5 %collective-permute-done.5 = bf16[128,768]{1,0:T(8,128)(2,1)S(1)} collective-permute-done((bf16[128,768]{1,0:T(8,128)(2,1)S(1)}, bf16[128,768]{1,0:T(8,128)(2,1)S(1)}, u32[]{:S(2)}, u32[]{:S(2)}) %collective-permute-start.5) | collective-permute-done | bytes 196640 | tf_op jit(solution)/shard_map/ppermute | solution.py:25
  39.7 1.4 collective-permute-done.6.refs_2_
  41.2 3.7 %shard_map.377 = (f32[256,768]{1,0:T(8,128)S(1)}, bf16[128,768]{1,0:T(8,128)(2,1)S(1)}, bf16[128,768]{1,0:T(8,128)(2,1)S(1)}, bf16[128,768]{1,0:T(8,128)(2,1)S(1...) custom-call(s32[2]{0:T(128)S(1)} %pad_add_fusion.refs_0_, ...), custom_call_target="tpu_custom_call" | custom-call | flops 2500000000 | tf_op jit(solution)/shard_map/pallas_call | solution.py:849
  45.0 1.3 collective-permute-done.7.refs_1_
  46.4 1.5 collective-permute-start.8
  48.8 1.6 collective-permute-start.13
  50.4 1.7 %shard_map.379 = (f32[64,384]{1,0:T(8,128)S(1)}, f32[8,128]{1,0:T(8,128)S(1)}) custom-call(f32[128,384]{1,0:T(8,128)S(1)} %get-tuple-element.159.refs_1_.refs_0_.refs_3_, f32[64,384]{1,0:T(8,128)S(1)} %pad_maximum_fusion.refs_5_.refs_2_.refs_1_.refs_10_.refs_4_, f32[8,128]{1,0:T(8,128)S(1)} %get-tuple-element.176.refs_2_), custom_call_target="tpu_custom_call" | custom-call | flops 1000000000 | tf_op jit(solution)/shard_map/pallas_call | solution.py:849
  52.1 1.4 collective-permute-done.8.refs_1_
  53.5 1.4 collective-permute-done.9.refs_3_
  55.0 2.5 %shard_map.381 = (f32[256,768]{1,0:T(8,128)S(1)}, bf16[256,768]{1,0:T(8,128)(2,1)S(1)}, bf16[128,384]{1,0:T(8,128)(2,1)S(1)}, f32[128,384]{1,0:T(8,128)S(1)}, f3...) custom-call(s32[2]{0:T(128)S(1)} %pad_add_fusion.refs_0_, ...), custom_call_target="tpu_custom_call" | custom-call | flops 1500000000 | tf_op jit(solution)/shard_map/pallas_call | solution.py:849
  58.8 5.3 %collective-permute-done.10.refs_3_ = bf16[64,384]{1,0:T(8,128)(2,1)S(1)} collective-permute-done((bf16[64,384]{1,0:T(8,128)(2,1)S(1)}, bf16[64,384]{1,0:T(8,128)(2,1)S(1)}, u32[]{:S(2)}, u32[]{:S(2)}) %collective-permute-start.10) | collective-permute-done | bytes 49184 | tf_op jit(solution)/shard_map/ppermute | solution.py:25
  64.7 1.9 %collective-permute-start.11 = (bf16[64,384]{1,0:T(8,128)(2,1)S(1)}, bf16[64,384]{1,0:T(8,128)(2,1)S(1)}, u32[]{:S(2)}, u32[]{:S(2)}) collective-permute-start(bf16[64,384]{1,0:T(8,128)(2,1)S(1)} %get-tuple-element.193), channel_id=1, source_target_pairs={{0,8},{4,12},{8,0},{12,4},{16,24},{20,28},{24,16},{28,20},{1,9},{5... | collective-permute-start | bytes 147464 | tf_op jit(solution)/shard_map/ppermute | solution.py:25
  69.5 3.0 %collective-permute-start.14 = (bf16[64,384]{1,0:T(8,128)(2,1)S(1)}, bf16[64,384]{1,0:T(8,128)(2,1)S(1)}, u32[]{:S(2)}, u32[]{:S(2)}) collective-permute-start(bf16[64,384]{1,0:T(8,128)(2,1)S(1)} %get-tuple-element.203), channel_id=1, source_target_pairs={{0,16},{4,20},{8,24},{12,28},{16,0},{20,4},{24,8},{28,12},{1,17},{... | collective-permute-start | bytes 147464 | tf_op jit(solution)/shard_map/ppermute | solution.py:25
  72.5 4.8 %shard_map.386 = (f32[128,384]{1,0:T(8,128)S(1)}, f32[64,384]{1,0:T(8,128)S(1)}, f32[64,384]{1,0:T(8,128)S(1)}, f32[8,128]{1,0:T(8,128)S(1)}) custom-call(f32[128,384]{1,0:T(8,128)S(1)} %get-tuple-element.159.refs_1_.refs_0_.refs_3_, f32[128,384]{1,0:T(8,128)S(1)} %get-tuple-element.183.refs_1_.refs_2_, ...), custom_call_target="tpu_custom_call" | custom-call | flops 2400000000 | tf_op jit(solution)/shard_map/pallas_call | solution.py:849
  78.0 1.6 collective-permute-start.18
  79.6 5.1 %shard_map.388 = (f32[128,384]{1,0:T(8,128)S(1)}, bf16[64,384]{1,0:T(8,128)(2,1)S(1)}, bf16[128,384]{1,0:T(8,128)(2,1)S(1)}, f32[64,768]{1,0:T(8,128)S(1)}, f32[8,768]{1,0:T(8,128)S(1)}, /*index=5*/f32[8,128]{1,0:T(8,128)S(1)}) custom-call(s32[2]{0:T(128)S(1)} %pad_add_fusion.refs_0_, f32[128,384]{1,0:T(8,128)S(1)} %get-tuple-element.202.refs_1_, ...), custom_call_target="tpu_custom_call" | custom-call | flops 3000000000 | tf_op jit(solution)/shard_map/pallas_call | solution.py:849
  84.8 1.3 collective-permute-start.17
  86.1 6.4 %collective-permute-done.18.refs_2_ = bf16[192,768]{1,0:T(8,128)(2,1)S(1)} collective-permute-done((bf16[192,768]{1,0:T(8,128)(2,1)S(1)}, bf16[192,768]{1,0:T(8,128)(2,1)S(1)}, u32[]{:S(2)}, u32[]{:S(2)}) %collective-permute-start.18) | collective-permute-done | bytes 294944 | tf_op jit(solution)/shard_map/ppermute | solution.py:25
  92.6 1.5 shard_map.390
  94.2 1.7 %collective-permute-done.19.refs_1_ = bf16[256,768]{1,0:T(8,128)(2,1)S(1)} collective-permute-done((bf16[256,768]{1,0:T(8,128)(2,1)S(1)}, bf16[256,768]{1,0:T(8,128)(2,1)S(1)}, u32[]{:S(2)}, u32[]{:S(2)}) %collective-permute-start.19) | collective-permute-done | bytes 393248 | tf_op jit(solution)/shard_map/ppermute | solution.py:25
  96.7 1.4 collective-permute-start.23
  99.3 12.4 %collective-permute-done.21.refs_2_ = bf16[192,768]{1,0:T(8,128)(2,1)S(1)} collective-permute-done((bf16[192,768]{1,0:T(8,128)(2,1)S(1)}, bf16[192,768]{1,0:T(8,128)(2,1)S(1)}, u32[]{:S(2)}, u32[]{:S(2)}) %collective-permute-start.21) | collective-permute-done | bytes 294944 | tf_op jit(solution)/shard_map/ppermute | solution.py:25
  115.4 1.9 %collective-permute-start.29 = (bf16[192,768]{1,0:T(8,128)(2,1)S(1)}, bf16[192,768]{1,0:T(8,128)(2,1)S(1)}, u32[]{:S(2)}, u32[]{:S(2)}) collective-permute-start(bf16[192,768]{1,0:T(8,128)(2,1)S(1)} %get-tuple-element.259.refs_1_), channel_id=1, source_target_pairs={{0,8},{4,12},{8,0},{12,4},{16,24},{20,28},{24,16},{28,20},{1,9},{5... | collective-permute-start | bytes 884744 | tf_op jit(solution)/shard_map/ppermute | solution.py:25
  118.6 2.4 %shard_map.395 = (f32[256,768]{1,0:T(8,128)}, f32[8,768]{1,0:T(8,128)S(1)}, f32[2,128,768]{2,1,0:T(8,128)}, f32[8,128]{1,0:T(8,128)S(1)}) custom-call(s32[2]{0:T(128)S(1)} %pad_add_fusion.refs_0_, s32[2]{0:T(128)S(1)} %copy-done.18, bf16[256,768]{1,0:T(8,128)(2,1)S(1)} %get-tuple-element.237.refs_2_, bf16[256,768]{1,0:T(8,128)(2,1)S(1)} %collective-permute-done.22.refs_3_, ...), custom_call_target="tpu_custom_call" | custom-call | flops 1500000000 | tf_op jit(solution)/shard_map/pallas_call | solution.py:849
  122.5 3.9 %collective-permute-start.27 = (bf16[120,768]{1,0:T(8,128)(2,1)S(1)}, bf16[120,768]{1,0:T(8,128)(2,1)S(1)}, u32[]{:S(2)}, u32[]{:S(2)}) collective-permute-start(bf16[120,768]{1,0:T(8,128)(2,1)S(1)} %get-tuple-element.255), channel_id=1, source_target_pairs={{0,16},{4,20},{8,24},{12,28},{16,0},{20,4},{24,8},{28,12},{1,17},{... | collective-permute-start | bytes 552968 | tf_op jit(solution)/shard_map/ppermute | solution.py:25
  126.4 9.1 %collective-permute-done.27.refs_2_ = bf16[120,768]{1,0:T(8,128)(2,1)S(1)} collective-permute-done((bf16[120,768]{1,0:T(8,128)(2,1)S(1)}, bf16[120,768]{1,0:T(8,128)(2,1)S(1)}, u32[]{:S(2)}, u32[]{:S(2)}) %collective-permute-start.27) | collective-permute-done | bytes 184352 | tf_op jit(solution)/shard_map/ppermute | solution.py:25
  136.6 4.9 %collective-permute-start.36 = (bf16[384,768]{1,0:T(8,128)(2,1)S(1)}, bf16[384,768]{1,0:T(8,128)(2,1)S(1)}, u32[]{:S(2)}, u32[]{:S(2)}) collective-permute-start(bf16[384,768]{1,0:T(8,128)(2,1)S(1)} %get-tuple-element.269.refs_3_), channel_id=1, source_target_pairs={{0,8},{4,12},{8,0},{12,4},{16,24},{20,28},{24,16},{28,20},{1,9},{5... | collective-permute-start | bytes 1769480 | tf_op jit(solution)/shard_map/ppermute | solution.py:25
  141.5 1.7 %collective-permute-done.28.refs_2_ = bf16[112,768]{1,0:T(8,128)(2,1)S(1)} collective-permute-done((bf16[112,768]{1,0:T(8,128)(2,1)S(1)}, bf16[112,768]{1,0:T(8,128)(2,1)S(1)}, u32[]{:S(2)}, u32[]{:S(2)}) %collective-permute-start.28) | collective-permute-done | bytes 172064 | tf_op jit(solution)/shard_map/ppermute | solution.py:25
  143.9 2.6 %collective-permute-start.32 = (bf16[112,768]{1,0:T(8,128)(2,1)S(1)}, bf16[112,768]{1,0:T(8,128)(2,1)S(1)}, u32[]{:S(2)}, u32[]{:S(2)}) collective-permute-start(bf16[112,768]{1,0:T(8,128)(2,1)S(1)} %get-tuple-element.264.refs_2_), channel_id=1, source_target_pairs={{0,4},{4,0},{8,12},{12,8},{16,20},{20,16},{24,28},{28,24},{1,5},{5... | collective-permute-start | bytes 516104 | tf_op jit(solution)/shard_map/ppermute | solution.py:25
  146.6 4.2 %collective-permute-done.32.refs_4_ = bf16[112,768]{1,0:T(8,128)(2,1)S(1)} collective-permute-done((bf16[112,768]{1,0:T(8,128)(2,1)S(1)}, bf16[112,768]{1,0:T(8,128)(2,1)S(1)}, u32[]{:S(2)}, u32[]{:S(2)}) %collective-permute-start.32) | collective-permute-done | bytes 172064 | tf_op jit(solution)/shard_map/ppermute | solution.py:25
  150.8 3.9 %collective-permute-done.31.refs_3_ = bf16[120,768]{1,0:T(8,128)(2,1)S(1)} collective-permute-done((bf16[120,768]{1,0:T(8,128)(2,1)S(1)}, bf16[120,768]{1,0:T(8,128)(2,1)S(1)}, u32[]{:S(2)}, u32[]{:S(2)}) %collective-permute-start.31) | collective-permute-done | bytes 184352 | tf_op jit(solution)/shard_map/ppermute | solution.py:25
  155.4 1.9 %collective-permute-start.33 = (bf16[232,768]{1,0:T(8,128)(2,1)S(1)}, bf16[232,768]{1,0:T(8,128)(2,1)S(1)}, u32[]{:S(2)}, u32[]{:S(2)}) collective-permute-start(bf16[232,768]{1,0:T(8,128)(2,1)S(1)} %get-tuple-element.266.refs_1_), channel_id=1, source_target_pairs={{0,4},{4,0},{8,12},{12,8},{16,20},{20,16},{24,28},{28,24},{1,5},{5... | collective-permute-start | bytes 1069064 | tf_op jit(solution)/shard_map/ppermute | solution.py:25
  157.4 3.0 %shard_map.401 = (f32[768,768]{1,0:T(8,128)}, f32[768,768]{1,0:T(8,128)}, f32[8,128]{1,0:T(8,128)S(1)}) custom-call(s32[2]{0:T(128)S(1)} %pad_add_fusion.refs_0_, bf16[384,768]{1,0:T(8,128)(2,1)S(1)} %get-tuple-element.268.refs_1_, bf16[384,768]{1,0:T(8,128)(2,1)S(1)} %collective-permute-done.35.refs_2_, bf16[384,768]{1,0:T(8,128)(2,1)S(1)} %get-tuple-element.269.refs_3_, ...), custom_call_target="tpu_custom_call" | custom-call | flops 1250000000 | tf_op jit(solution)/shard_map/pallas_call | solution.py:849
  160.4 4.2 %collective-permute-done.34.refs_4_ = bf16[224,768]{1,0:T(8,128)(2,1)S(1)} collective-permute-done((bf16[224,768]{1,0:T(8,128)(2,1)S(1)}, bf16[224,768]{1,0:T(8,128)(2,1)S(1)}, u32[]{:S(2)}, u32[]{:S(2)}) %collective-permute-start.34) | collective-permute-done | bytes 344096 | tf_op jit(solution)/shard_map/ppermute | solution.py:25
  164.6 2.2 %shard_map.402 = (f32[3,192,768]{2,1,0:T(8,128)}, f32[3,192]{1,0:T(4,128)}, f32[64,192]{1,0:T(8,128)}, f32[192]{0:T(256)}, f32[64,192]{1,0:T(8,128)}, /*index=5*...) custom-call(s32[2]{0:T(128)S(1)} %pad_add_fusion.refs_0_, ...), custom_call_target="tpu_custom_call" | custom-call | flops 1000000000 | tf_op jit(solution)/shard_map/pallas_call | solution.py:849
  (109 shorter events, 19.4 us)
Async XLA Ops:
  3.5 6.6 %collective-permute-start = (bf16[64,384]{1,0:T(8,128)(2,1)S(1)}, bf16[64,384]{1,0:T(8,128)(2,1)S(1)}, u32[]{:S(2)}, u32[]{:S(2)}) collective-permute-start(bf16[64,384]{1,0:T(8,128)(2,1)S(1)} %slice.3), channel_id=1, source_target_pairs={{0,4},{4,8},{8,12},{12,16},{16,20},{20,24},{24,28},{1,5},{5,9},{9,... | collective-permute-start | bytes 147464 | tf_op jit(solution)/shard_map/ppermute | solution.py:21
  10.1 15.7 %copy-start.6 = (f32[2,128,768]{2,1,0:T(8,128)S(1)}, f32[2,128,768]{2,1,0:T(8,128)}, u32[]{:S(2)}) copy-start(f32[2,128,768]{2,1,0:T(8,128)} %refs_5_.6) | copy-start | bytes 2359300
  10.1 15.7 %copy-start.18 = (s32[2]{0:T(128)S(1)}, s32[2]{0:T(128)}, u32[]{:S(2)}) copy-start(s32[2]{0:T(128)} %refs_1_.7) | copy-start | bytes 28
  12.7 15.1 %copy-start.8 = (bf16[192,768]{1,0:T(8,128)(2,1)S(1)}, bf16[192,768]{1,0:T(8,128)(2,1)}, u32[]{:S(2)}) copy-start(bf16[192,768]{1,0:T(8,128)(2,1)} %refs_7_.5) | copy-start | bytes 884740
  12.7 15.1 %copy-start.17 = (f32[192]{0:T(256)S(1)}, f32[192]{0:T(256)}, u32[]{:S(2)}) copy-start(f32[192]{0:T(256)} %refs_20_.1) | copy-start | bytes 2308
  12.7 4.5 %collective-permute-start.1 = (bf16[64,384]{1,0:T(8,128)(2,1)S(1)}, bf16[64,384]{1,0:T(8,128)(2,1)S(1)}, u32[]{:S(2)}, u32[]{:S(2)}) collective-permute-start(bf16[64,384]{1,0:T(8,128)(2,1)S(1)} %get-tuple-element.160), channel_id=1, source_target_pairs={{0,4},{4,0},{8,12},{12,8},{16,20},{20,16},{24,28},{28,24},{1,5},{5... | collective-permute-start | bytes 147464 | tf_op jit(solution)/shard_map/ppermute | solution.py:25
  17.3 5.1 %collective-permute-start.2 = (bf16[64,384]{1,0:T(8,128)(2,1)S(1)}, bf16[64,384]{1,0:T(8,128)(2,1)S(1)}, u32[]{:S(2)}, u32[]{:S(2)}) collective-permute-start(bf16[64,384]{1,0:T(8,128)(2,1)S(1)} %fusion.6), channel_id=1, source_target_pairs={{0,8},{4,12},{8,0},{12,4},{16,24},{20,28},{24,16},{28,20},{1,9},{5... | collective-permute-start | bytes 147464 | tf_op jit(solution)/shard_map/ppermute | solution.py:25
  22.6 5.2 %collective-permute-start.3 = (bf16[64,384]{1,0:T(8,128)(2,1)S(1)}, bf16[64,384]{1,0:T(8,128)(2,1)S(1)}, u32[]{:S(2)}, u32[]{:S(2)}) collective-permute-start(bf16[64,384]{1,0:T(8,128)(2,1)S(1)} %get-tuple-element.295), channel_id=1, source_target_pairs={{0,16},{4,20},{8,24},{12,28},{16,0},{20,4},{24,8},{28,12},{1,17},{... | collective-permute-start | bytes 147464 | tf_op jit(solution)/shard_map/ppermute | solution.py:25
  27.8 13.3 %copy-start.3 = (bf16[768,768]{1,0:T(8,128)(2,1)S(1)}, bf16[768,768]{1,0:T(8,128)(2,1)}, u32[]{:S(2)}) copy-start(bf16[768,768]{1,0:T(8,128)(2,1)} %refs_7_.4) | copy-start | bytes 3538948
  27.8 13.3 %copy-start.4 = (bf16[768,768]{1,0:T(8,128)(2,1)S(1)}, bf16[768,768]{1,0:T(8,128)(2,1)}, u32[]{:S(2)}) copy-start(bf16[768,768]{1,0:T(8,128)(2,1)} %refs_9_.3) | copy-start | bytes 3538948
  27.8 13.3 %copy-start.7 = (bf16[2,128,768]{2,1,0:T(8,128)(2,1)S(1)}, bf16[2,128,768]{2,1,0:T(8,128)(2,1)}, u32[]{:S(2)}) copy-start(bf16[2,128,768]{2,1,0:T(8,128)(2,1)} %refs_1_.4) | copy-start | bytes 1179652
  27.8 13.3 %copy-start.10 = (f32[768]{0:T(1024)S(1)}, f32[768]{0:T(1024)}, u32[]{:S(2)}) copy-start(f32[768]{0:T(1024)} %refs_4_.3) | copy-start | bytes 9220
  27.9 13.3 %copy-start.11 = (f32[768]{0:T(1024)S(1)}, f32[768]{0:T(1024)}, u32[]{:S(2)}) copy-start(f32[768]{0:T(1024)} %refs_6_.2) | copy-start | bytes 9220
  31.0 1.5 collective-permute-start.4
  32.5 7.0 %collective-permute-start.5 = (bf16[128,768]{1,0:T(8,128)(2,1)S(1)}, bf16[128,768]{1,0:T(8,128)(2,1)S(1)}, u32[]{:S(2)}, u32[]{:S(2)}) collective-permute-start(bf16[128,768]{1,0:T(8,128)(2,1)S(1)} %fusion), channel_id=1, source_target_pairs={{0,2},{1,3},{2,0},{3,1},{4,6},{5,7},{6,4},{7,5},{8,10},{9,11},{10,... | collective-permute-start | bytes 589832 | tf_op jit(solution)/shard_map/ppermute | solution.py:25
  39.6 1.5 collective-permute-start.6
  44.8 1.5 collective-permute-start.7
  46.4 7.0 %collective-permute-start.8 = (bf16[128,768]{1,0:T(8,128)(2,1)S(1)}, bf16[128,768]{1,0:T(8,128)(2,1)S(1)}, u32[]{:S(2)}, u32[]{:S(2)}) collective-permute-start(bf16[128,768]{1,0:T(8,128)(2,1)S(1)} %get-tuple-element.175), channel_id=1, source_target_pairs={{0,2},{1,3},{2,0},{3,1},{4,6},{5,7},{6,4},{7,5},{8,10},{9,11},{10,... | collective-permute-start | bytes 589832 | tf_op jit(solution)/shard_map/ppermute | solution.py:25
  48.0 18.6 %collective-permute-start.12 = (bf16[384,768]{1,0:T(8,128)(2,1)S(1)}, bf16[384,768]{1,0:T(8,128)(2,1)S(1)}, u32[]{:S(2)}, u32[]{:S(2)}) collective-permute-start(bf16[384,768]{1,0:T(8,128)(2,1)S(1)} %get-tuple-element.197), channel_id=1, source_target_pairs={{0,4},{4,0},{8,12},{12,8},{16,20},{20,16},{24,28},{28,24},{1,5},{5... | collective-permute-start | bytes 1769480 | tf_op jit(solution)/shard_map/ppermute | solution.py:25
  48.8 17.8 %collective-permute-start.13 = (bf16[384,768]{1,0:T(8,128)(2,1)S(1)}, bf16[384,768]{1,0:T(8,128)(2,1)S(1)}, u32[]{:S(2)}, u32[]{:S(2)}) collective-permute-start(bf16[384,768]{1,0:T(8,128)(2,1)S(1)} %get-tuple-element.198), channel_id=1, source_target_pairs={{0,8},{4,12},{8,0},{12,4},{16,24},{20,28},{24,16},{28,20},{1,9},{5... | collective-permute-start | bytes 1769480 | tf_op jit(solution)/shard_map/ppermute | solution.py:25
  53.5 1.5 collective-permute-start.9
  57.4 6.7 %collective-permute-start.10 = (bf16[64,384]{1,0:T(8,128)(2,1)S(1)}, bf16[64,384]{1,0:T(8,128)(2,1)S(1)}, u32[]{:S(2)}, u32[]{:S(2)}) collective-permute-start(bf16[64,384]{1,0:T(8,128)(2,1)S(1)} %get-tuple-element.186), channel_id=1, source_target_pairs={{0,4},{4,0},{8,12},{12,8},{16,20},{20,16},{24,28},{28,24},{1,5},{5... | collective-permute-start | bytes 147464 | tf_op jit(solution)/shard_map/ppermute | solution.py:25
  64.7 4.2 %collective-permute-start.11 = (bf16[64,384]{1,0:T(8,128)(2,1)S(1)}, bf16[64,384]{1,0:T(8,128)(2,1)S(1)}, u32[]{:S(2)}, u32[]{:S(2)}) collective-permute-start(bf16[64,384]{1,0:T(8,128)(2,1)S(1)} %get-tuple-element.193), channel_id=1, source_target_pairs={{0,8},{4,12},{8,0},{12,4},{16,24},{20,28},{24,16},{28,20},{1,9},{5... | collective-permute-start | bytes 147464 | tf_op jit(solution)/shard_map/ppermute | solution.py:25
  67.5 9.7 %collective-permute-start.15 = (bf16[192,768]{1,0:T(8,128)(2,1)S(1)}, bf16[192,768]{1,0:T(8,128)(2,1)S(1)}, u32[]{:S(2)}, u32[]{:S(2)}) collective-permute-start(bf16[192,768]{1,0:T(8,128)(2,1)S(1)} %get-tuple-element.211), channel_id=1, source_target_pairs={{0,8},{4,12},{8,0},{12,4},{16,24},{20,28},{24,16},{28,20},{1,9},{5... | collective-permute-start | bytes 884744 | tf_op jit(solution)/shard_map/ppermute | solution.py:25
  67.8 9.5 %collective-permute-start.16 = (bf16[192,768]{1,0:T(8,128)(2,1)S(1)}, bf16[192,768]{1,0:T(8,128)(2,1)S(1)}, u32[]{:S(2)}, u32[]{:S(2)}) collective-permute-start(bf16[192,768]{1,0:T(8,128)(2,1)S(1)} %get-tuple-element.212), channel_id=1, source_target_pairs={{0,4},{4,0},{8,12},{12,8},{16,20},{20,16},{24,28},{28,24},{1,5},{5... | collective-permute-start | bytes 884744 | tf_op jit(solution)/shard_map/ppermute | solution.py:25
  69.5 10.2 %collective-permute-start.14 = (bf16[64,384]{1,0:T(8,128)(2,1)S(1)}, bf16[64,384]{1,0:T(8,128)(2,1)S(1)}, u32[]{:S(2)}, u32[]{:S(2)}) collective-permute-start(bf16[64,384]{1,0:T(8,128)(2,1)S(1)} %get-tuple-element.203), channel_id=1, source_target_pairs={{0,16},{4,20},{8,24},{12,28},{16,0},{20,4},{24,8},{28,12},{1,17},{... | collective-permute-start | bytes 147464 | tf_op jit(solution)/shard_map/ppermute | solution.py:25
  78.0 14.5 %collective-permute-start.18 = (bf16[192,768]{1,0:T(8,128)(2,1)S(1)}, bf16[192,768]{1,0:T(8,128)(2,1)S(1)}, u32[]{:S(2)}, u32[]{:S(2)}) collective-permute-start(bf16[192,768]{1,0:T(8,128)(2,1)S(1)} %get-tuple-element.226), channel_id=1, source_target_pairs={{0,16},{4,20},{8,24},{12,28},{16,0},{20,4},{24,8},{28,12},{1,17},{... | collective-permute-start | bytes 884744 | tf_op jit(solution)/shard_map/ppermute | solution.py:25
  84.8 7.8 %collective-permute-start.17 = (bf16[64,384]{1,0:T(8,128)(2,1)S(1)}, bf16[64,384]{1,0:T(8,128)(2,1)S(1)}, u32[]{:S(2)}, u32[]{:S(2)}) collective-permute-start(bf16[64,384]{1,0:T(8,128)(2,1)S(1)} %get-tuple-element.216), channel_id=1, source_target_pairs={{4,0},{8,4},{12,8},{16,12},{20,16},{24,20},{28,24},{5,1},{9,5},{13... | collective-permute-start | bytes 147464 | tf_op jit(solution)/shard_map/ppermute | solution.py:21
  94.1 1.8 %collective-permute-start.19 = (bf16[256,768]{1,0:T(8,128)(2,1)S(1)}, bf16[256,768]{1,0:T(8,128)(2,1)S(1)}, u32[]{:S(2)}, u32[]{:S(2)}) collective-permute-start(bf16[256,768]{1,0:T(8,128)(2,1)S(1)} %get-tuple-element.230), channel_id=1, source_target_pairs={{0,1},{1,0},{2,3},{3,2},{4,5},{5,4},{6,7},{7,6},{8,9},{9,8},{10,11... | collective-permute-start | bytes 1179656 | tf_op jit(solution)/shard_map/ppermute | solution.py:25
  96.0 22.5 %copy-start.14 = (f32[768]{0:T(1024)S(1)}, f32[768]{0:T(1024)}, u32[]{:S(2)}) copy-start(f32[768]{0:T(1024)} %refs_5_.7) | copy-start | bytes 9220
  96.0 22.5 %copy-start.15 = (f32[768]{0:T(1024)S(1)}, f32[768]{0:T(1024)}, u32[]{:S(2)}) copy-start(f32[768]{0:T(1024)} %refs_8_.3) | copy-start | bytes 9220
  96.1 16.4 %collective-permute-start.20 = (bf16[256,768]{1,0:T(8,128)(2,1)S(1)}, bf16[256,768]{1,0:T(8,128)(2,1)S(1)}, u32[]{:S(2)}, u32[]{:S(2)}) collective-permute-start(bf16[256,768]{1,0:T(8,128)(2,1)S(1)} %get-tuple-element.233), channel_id=1, source_target_pairs={{0,2},{1,3},{2,0},{3,1},{4,6},{5,7},{6,4},{7,5},{8,10},{9,11},{10,... | collective-permute-start | bytes 1179656 | tf_op jit(solution)/shard_map/ppermute | solution.py:25
  96.7 15.1 %collective-permute-start.21 = (bf16[192,768]{1,0:T(8,128)(2,1)S(1)}, bf16[192,768]{1,0:T(8,128)(2,1)S(1)}, u32[]{:S(2)}, u32[]{:S(2)}) collective-permute-start(bf16[192,768]{1,0:T(8,128)(2,1)S(1)} %get-tuple-element.234.refs_1_), channel_id=1, source_target_pairs={{0,16},{4,20},{8,24},{12,28},{16,0},{20,4},{24,8},{28,12},{1,17},{... | collective-permute-start | bytes 884744 | tf_op jit(solution)/shard_map/ppermute | solution.py:25
  96.7 15.9 %collective-permute-start.23 = (bf16[224,768]{1,0:T(8,128)(2,1)S(1)}, bf16[224,768]{1,0:T(8,128)(2,1)S(1)}, u32[]{:S(2)}, u32[]{:S(2)}) collective-permute-start(bf16[224,768]{1,0:T(8,128)(2,1)S(1)} %get-tuple-element.241), channel_id=1, source_target_pairs={{0,4},{4,0},{8,12},{12,8},{16,20},{20,16},{24,28},{28,24},{1,5},{5... | collective-permute-start | bytes 1032200 | tf_op jit(solution)/shard_map/ppermute | solution.py:25
  98.1 15.6 %collective-permute-start.24 = (bf16[224,768]{1,0:T(8,128)(2,1)S(1)}, bf16[224,768]{1,0:T(8,128)(2,1)S(1)}, u32[]{:S(2)}, u32[]{:S(2)}) collective-permute-start(bf16[224,768]{1,0:T(8,128)(2,1)S(1)} %get-tuple-element.242), channel_id=1, source_target_pairs={{0,8},{4,12},{8,0},{12,4},{16,24},{20,28},{24,16},{28,20},{1,9},{5... | collective-permute-start | bytes 1032200 | tf_op jit(solution)/shard_map/ppermute | solution.py:25
  112.5 6.1 %collective-permute-start.22 = (bf16[256,768]{1,0:T(8,128)(2,1)S(1)}, bf16[256,768]{1,0:T(8,128)(2,1)S(1)}, u32[]{:S(2)}, u32[]{:S(2)}) collective-permute-start(bf16[256,768]{1,0:T(8,128)(2,1)S(1)} %get-tuple-element.237.refs_2_), channel_id=1, source_target_pairs={{0,1},{1,0},{2,3},{3,2},{4,5},{5,4},{6,7},{7,6},{8,9},{9,8},{10,11... | collective-permute-start | bytes 1179656 | tf_op jit(solution)/shard_map/ppermute | solution.py:25
  114.5 7.4 %collective-permute-start.25 = (bf16[112,768]{1,0:T(8,128)(2,1)S(1)}, bf16[112,768]{1,0:T(8,128)(2,1)S(1)}, u32[]{:S(2)}, u32[]{:S(2)}) collective-permute-start(bf16[112,768]{1,0:T(8,128)(2,1)S(1)} %get-tuple-element.249), channel_id=1, source_target_pairs={{0,8},{4,12},{8,0},{12,4},{16,24},{20,28},{24,16},{28,20},{1,9},{5... | collective-permute-start | bytes 516104 | tf_op jit(solution)/shard_map/ppermute | solution.py:25
  114.5 7.3 %collective-permute-start.26 = (bf16[112,768]{1,0:T(8,128)(2,1)S(1)}, bf16[112,768]{1,0:T(8,128)(2,1)S(1)}, u32[]{:S(2)}, u32[]{:S(2)}) collective-permute-start(bf16[112,768]{1,0:T(8,128)(2,1)S(1)} %get-tuple-element.250), channel_id=1, source_target_pairs={{0,4},{4,0},{8,12},{12,8},{16,20},{20,16},{24,28},{28,24},{1,5},{5... | collective-permute-start | bytes 516104 | tf_op jit(solution)/shard_map/ppermute | solution.py:25
  115.4 20.2 %collective-permute-start.29 = (bf16[192,768]{1,0:T(8,128)(2,1)S(1)}, bf16[192,768]{1,0:T(8,128)(2,1)S(1)}, u32[]{:S(2)}, u32[]{:S(2)}) collective-permute-start(bf16[192,768]{1,0:T(8,128)(2,1)S(1)} %get-tuple-element.259.refs_1_), channel_id=1, source_target_pairs={{0,8},{4,12},{8,0},{12,4},{16,24},{20,28},{24,16},{28,20},{1,9},{5... | collective-permute-start | bytes 884744 | tf_op jit(solution)/shard_map/ppermute | solution.py:25
  117.4 18.3 %collective-permute-start.30 = (bf16[192,768]{1,0:T(8,128)(2,1)S(1)}, bf16[192,768]{1,0:T(8,128)(2,1)S(1)}, u32[]{:S(2)}, u32[]{:S(2)}) collective-permute-start(bf16[192,768]{1,0:T(8,128)(2,1)S(1)} %get-tuple-element.260.refs_2_), channel_id=1, source_target_pairs={{0,4},{4,0},{8,12},{12,8},{16,20},{20,16},{24,28},{28,24},{1,5},{5... | collective-permute-start | bytes 884744 | tf_op jit(solution)/shard_map/ppermute | solution.py:25
  122.5 13.0 %collective-permute-start.27 = (bf16[120,768]{1,0:T(8,128)(2,1)S(1)}, bf16[120,768]{1,0:T(8,128)(2,1)S(1)}, u32[]{:S(2)}, u32[]{:S(2)}) collective-permute-start(bf16[120,768]{1,0:T(8,128)(2,1)S(1)} %get-tuple-element.255), channel_id=1, source_target_pairs={{0,16},{4,20},{8,24},{12,28},{16,0},{20,4},{24,8},{28,12},{1,17},{... | collective-permute-start | bytes 552968 | tf_op jit(solution)/shard_map/ppermute | solution.py:25
  135.6 7.6 %collective-permute-start.28 = (bf16[112,768]{1,0:T(8,128)(2,1)S(1)}, bf16[112,768]{1,0:T(8,128)(2,1)S(1)}, u32[]{:S(2)}, u32[]{:S(2)}) collective-permute-start(bf16[112,768]{1,0:T(8,128)(2,1)S(1)} %get-tuple-element.257.refs_1_), channel_id=1, source_target_pairs={{0,16},{4,20},{8,24},{12,28},{16,0},{20,4},{24,8},{28,12},{1,17},{... | collective-permute-start | bytes 516104 | tf_op jit(solution)/shard_map/ppermute | solution.py:25
  136.5 20.8 %collective-permute-start.35 = (bf16[384,768]{1,0:T(8,128)(2,1)S(1)}, bf16[384,768]{1,0:T(8,128)(2,1)S(1)}, u32[]{:S(2)}, u32[]{:S(2)}) collective-permute-start(bf16[384,768]{1,0:T(8,128)(2,1)S(1)} %get-tuple-element.268.refs_1_), channel_id=1, source_target_pairs={{0,4},{4,0},{8,12},{12,8},{16,20},{20,16},{24,28},{28,24},{1,5},{5... | collective-permute-start | bytes 1769480 | tf_op jit(solution)/shard_map/ppermute | solution.py:25
  136.6 20.8 %collective-permute-start.36 = (bf16[384,768]{1,0:T(8,128)(2,1)S(1)}, bf16[384,768]{1,0:T(8,128)(2,1)S(1)}, u32[]{:S(2)}, u32[]{:S(2)}) collective-permute-start(bf16[384,768]{1,0:T(8,128)(2,1)S(1)} %get-tuple-element.269.refs_3_), channel_id=1, source_target_pairs={{0,8},{4,12},{8,0},{12,4},{16,24},{20,28},{24,16},{28,20},{1,9},{5... | collective-permute-start | bytes 1769480 | tf_op jit(solution)/shard_map/ppermute | solution.py:25
  143.8 10.8 %collective-permute-start.31 = (bf16[120,768]{1,0:T(8,128)(2,1)S(1)}, bf16[120,768]{1,0:T(8,128)(2,1)S(1)}, u32[]{:S(2)}, u32[]{:S(2)}) collective-permute-start(bf16[120,768]{1,0:T(8,128)(2,1)S(1)} %get-tuple-element.263.refs_1_), channel_id=1, source_target_pairs={{0,8},{4,12},{8,0},{12,4},{16,24},{20,28},{24,16},{28,20},{1,9},{5... | collective-permute-start | bytes 552968 | tf_op jit(solution)/shard_map/ppermute | solution.py:25
  143.9 6.9 %collective-permute-start.32 = (bf16[112,768]{1,0:T(8,128)(2,1)S(1)}, bf16[112,768]{1,0:T(8,128)(2,1)S(1)}, u32[]{:S(2)}, u32[]{:S(2)}) collective-permute-start(bf16[112,768]{1,0:T(8,128)(2,1)S(1)} %get-tuple-element.264.refs_2_), channel_id=1, source_target_pairs={{0,4},{4,0},{8,12},{12,8},{16,20},{20,16},{24,28},{28,24},{1,5},{5... | collective-permute-start | bytes 516104 | tf_op jit(solution)/shard_map/ppermute | solution.py:25
  155.4 9.2 %collective-permute-start.33 = (bf16[232,768]{1,0:T(8,128)(2,1)S(1)}, bf16[232,768]{1,0:T(8,128)(2,1)S(1)}, u32[]{:S(2)}, u32[]{:S(2)}) collective-permute-start(bf16[232,768]{1,0:T(8,128)(2,1)S(1)} %get-tuple-element.266.refs_1_), channel_id=1, source_target_pairs={{0,4},{4,0},{8,12},{12,8},{16,20},{20,16},{24,28},{28,24},{1,5},{5... | collective-permute-start | bytes 1069064 | tf_op jit(solution)/shard_map/ppermute | solution.py:25
  157.3 7.2 %collective-permute-start.34 = (bf16[224,768]{1,0:T(8,128)(2,1)S(1)}, bf16[224,768]{1,0:T(8,128)(2,1)S(1)}, u32[]{:S(2)}, u32[]{:S(2)}) collective-permute-start(bf16[224,768]{1,0:T(8,128)(2,1)S(1)} %get-tuple-element.267.refs_3_), channel_id=1, source_target_pairs={{0,8},{4,12},{8,0},{12,4},{16,24},{20,28},{24,16},{28,20},{1,9},{5... | collective-permute-start | bytes 1032200 | tf_op jit(solution)/shard_map/ppermute | solution.py:25
  (9 other events, 88.8 us)
